TPU v7x, 32 devices: a whole 2x2x4 slice. The times are simulated.
32 devices in a mesh: col: 16 (over z, x, core), row: 2 (over y).
Axes of the slice: x: 2, y: 2, z: 4, core: 2. Of those that a mesh axis runs over, the one named last changes fastest.
Arguments:
- matrix: float32 [2048, 2048], P('row', 'col'), as said below
- row_diag: float32 [2, 2048], P(None, 'row'), may hold values from 0.8 to 1.2
- col_diag: float32 [2, 2048], P(None, 'col'), may hold values from 0.8 to 1.2
Outputs:
- factored: float32 [2048, 2048], P('row', 'col')
Inputs may be any that keep to these rules, and one draw needn't show every extreme that they name: `matrix`: off the diagonal the entries lie within -6 and 6; the diagonal entries exceed 1.5 * sqrt(512) - 6.
All inputs are finite; a program needn't handle non-finite values.
Results may differ from a plain program's by a relative error of at most 0.0001.
Values sent between devices are 32-bit elements; how exact they have to be, the bound alone decides.
No kernel may reach another device: no remote copies, remote signals or barrier semaphores. Data moves between devices by JAX's collectives and lax.ppermute only.
A program may use at most 64 MiB of HBM per device.

v0:
```python
import jax
import jax.numpy as jnp
from jax import lax
from jax.sharding import PartitionSpec as P

PW = 256
PANELS = 2


inv_root = 0.7071067811865476


def swapped(x, axis, distance):
    return lax.ppermute(x, axis, [(i, i ^ 1 << distance) for i in range(lax.axis_size(axis))])


def from_root(x, axis, root):
    mine = lax.axis_index(axis) == root
    return lax.psum(jnp.where(mine, x, jnp.zeros_like(x)), axis)


def lu_block(block):
    size = block.shape[0]
    places = jnp.arange(size)

    def eliminate(step, current):
        pivot = current[step, step]
        below = places > step
        column = jnp.where(below, current[:, step] / pivot, 0.0)
        across = jnp.where(below, current[step, :], 0.0)
        current = current - column[:, None] * across[None, :]
        return jnp.where((places == step)[None, :] & below[:, None], column[:, None], current)

    return lax.fori_loop(0, size, eliminate, block)


def hdot(left, right):
    return jnp.dot(left, right, precision=lax.Precision.HIGHEST, preferred_element_type=jnp.float32)


def strict_inverse(strict):
    size = strict.shape[0]
    identity = jnp.eye(size, dtype=strict.dtype)
    result = identity - strict
    power = strict
    exponent = 1
    while exponent * 2 < size:
        power = hdot(power, power)
        exponent = exponent * 2
        result = hdot(result, identity + power)
    return result


def inverses(packed):
    upper_factor = jnp.triu(packed)
    lower_inverse = strict_inverse(jnp.tril(packed, -1))
    pivots = jnp.diagonal(packed)
    scaled = jnp.triu(packed, 1) / pivots[:, None]
    upper_inverse = strict_inverse(scaled) / pivots[None, :]
    return (lower_inverse, upper_inverse, upper_factor)


def pair_mix(own, partner, is_first, scales):
    return scales * jnp.where(is_first, own + partner, partner - own) * inv_root


def shards(matrix, row_diag, col_diag):
    height, width = matrix.shape
    row_pos = lax.axis_index("row")
    col_pos = lax.axis_index("col")
    first_row = row_pos * height
    first_col = col_pos * width
    rows = first_row + jnp.arange(height, dtype=jnp.int32)[:, None]
    cols = first_col + jnp.arange(width, dtype=jnp.int32)[None, :]
    partner = swapped(matrix, "row", 0)
    current = pair_mix(matrix, partner, row_pos == 0, row_diag[0][:, None])
    half = height // 2
    upper_part, lower_part = (current[:half], current[half:])
    current = jnp.concatenate(
        [
            row_diag[1][:half, None] * (upper_part + lower_part) * inv_root,
            row_diag[1][half:, None] * (upper_part - lower_part) * inv_root,
        ],
        0,
    )
    top_bit = lax.axis_size("col").bit_length() - 2
    partner = swapped(current, "col", top_bit)
    current = pair_mix(current, partner, col_pos // 2**top_bit % 2 == 0, col_diag[0][None, :])
    partner = swapped(current, "col", top_bit - 1)
    current = pair_mix(
        current, partner, col_pos // 2 ** (top_bit - 1) % 2 == 0, col_diag[1][None, :]
    )
    count = PW // width
    for panel in range(PANELS):
        start = panel * PW
        stop = start + PW
        owner = start // width
        offset = jnp.clip(start - first_row, 0, height - PW)
        band_local = lax.dynamic_slice_in_dim(current, offset, PW, 0)
        panel_parts = []
        for piece in range(count):
            panel_parts.append(from_root(current, "col", owner + piece))
        panel_block = jnp.concatenate(panel_parts, 1)
        diag_local = lax.dynamic_slice_in_dim(panel_block, offset, PW, 0)
        diag_block, band_rows = (from_root(diag_local, "row", 0), from_root(band_local, "row", 0))
        packed = lu_block(diag_block)
        lower_inverse, upper_inverse, upper_factor = inverses(packed)
        lower_rows = hdot(panel_block, upper_inverse)
        upper_cols = hdot(lower_inverse, band_rows)
        below = rows >= stop
        right = cols >= stop
        inside = (cols >= start) & (cols < stop)
        updated = current - hdot(
            jnp.where(below, lower_rows, 0.0), jnp.where(right, upper_cols, 0.0)
        )
        col_offset = jnp.clip(first_col - start, 0, PW - width)
        lower_cols = lax.dynamic_slice_in_dim(lower_rows, col_offset, width, 1)
        updated = jnp.where(below & inside, lower_cols, updated)
        packed_cols = lax.dynamic_slice_in_dim(packed, col_offset, width, 1)
        new_band = jnp.where(right, upper_cols, jnp.where(inside, packed_cols, band_rows))
        placed = lax.dynamic_update_slice_in_dim(updated, new_band, offset, 0)
        in_band = (rows >= start) & (rows < stop)
        current = jnp.where(in_band, placed, updated)
    return current


def solution(mesh):
    in_specs = (P("row", "col"), P(None, "row"), P(None, "col"))
    out_specs = P("row", "col")
    return jax.shard_map(shards, mesh=mesh, in_specs=in_specs, out_specs=out_specs, check_vma=False)
```

profile of v0, /device:TPU:0, one launch (start us, length us, event | category | flops | bytes accessed | tf_op | source)
XLA Modules:
  0.0 1171.0 jit_solution(15443678754477894416)
XLA Ops:
  6.5 3.0 collective-permute-start
  9.6 12.1 %collective-permute-done = f32[1024,128]{1,0:T(8,128)S(1)} collective-permute-done((f32[1024,128]{1,0:T(8,128)}, f32[1024,128]{1,0:T(8,128)S(1)}, u32[]{:S(2)}, u32[]{:S(2)}) %collective-permute-start) | collective-permute-done | bytes 524320 | tf_op jit(solution)/shard_map/ppermute | solution.py:14
  21.7 1.2 multiply_multiply_fusion.2
  23.2 2.9 collective-permute-start.1
  26.0 0.7 copy-done.6
  26.7 21.7 %collective-permute-done.1 = f32[1024,128]{1,0:T(8,128)S(1)} collective-permute-done((f32[1024,128]{1,0:T(8,128)S(1)}, f32[1024,128]{1,0:T(8,128)S(1)}, u32[]{:S(2)}, u32[]{:S(2)}) %collective-permute-start.1) | collective-permute-done | bytes 524320 | tf_op jit(solution)/shard_map/ppermute | solution.py:14
  48.5 0.7 collective-permute-start.2
  49.2 12.3 %collective-permute-done.2 = f32[1024,128]{1,0:T(8,128)S(1)} collective-permute-done((f32[1024,128]{1,0:T(8,128)S(1)}, f32[1024,128]{1,0:T(8,128)S(1)}, u32[]{:S(2)}, u32[]{:S(2)}) %collective-permute-start.2) | collective-permute-done | bytes 524320 | tf_op jit(solution)/shard_map/ppermute | solution.py:14
  61.5 0.9 broadcast_select_fusion.2
  62.4 0.9 broadcast_select_fusion.3
  63.5 0.7 dynamic-slice_select_fusion.5
  64.1 95.2 %all-reduce.11.cloned.1.call-done = (f32[1024,128]{1,0:T(8,128)}, f32[1024,128]{1,0:T(8,128)}) async-done(((f32[1024,128]{1,0:T(8,128)}, f32[1024,128]{1,0:T(8,128)}), (f32[1024,128]{1,0:T(8,128)}, f32[1024,128]{1,0:T(8,128)})) %all-reduce.11.cloned.1.call-update) | async-done | bytes 1048592 | tf_op jit(solution)/shard_map/psum | solution.py:19
  159.3 1.1 constant_dynamic-update-slice_fusion.1
  160.6 0.7 dynamic-slice_select_fusion.1
  161.4 25.2 %all-reduce.15.cloned.1.call-done = (f32[256,256]{1,0:T(8,128)}, f32[256,128]{1,0:T(8,128)}) async-done(((f32[256,256]{1,0:T(8,128)}, f32[256,128]{1,0:T(8,128)}), (f32[256,256]{1,0:T(8,128)}, f32[256,128]{1,0:T(8,128)})) %all-reduce.15.cloned.1.call-update) | async-done | bytes 393232 | tf_op jit(solution)/shard_map/psum | solution.py:19
  186.7 1.1 copy.16
  187.7 407.8 %while.30 = (s32[]{:T(128)}, f32[256,256]{0,1:T(8,128)S(1)}, s32[]{:T(128)}) while((s32[]{:T(128)}, f32[256,256]{0,1:T(8,128)S(1)}, s32[]{:T(128)}) %tuple.81), condition=%wide.region_4.5_spmd.clone.clone, body=%wide.region_3.4_spmd.clone.clone.sunk | while | flops 263426 | bytes 1056337 | solution.py:34
  188.5 0.7 reshape_select_fusion.9
  190.1 0.7 reshape_select_fusion.9
  191.7 0.7 reshape_select_fusion.9
  193.3 0.7 reshape_select_fusion.9
  201.3 0.7 reshape_select_fusion.9
  202.9 0.7 reshape_select_fusion.9
  204.4 0.7 reshape_select_fusion.9
  206.0 0.7 reshape_select_fusion.9
  207.6 0.7 reshape_select_fusion.9
  217.2 0.7 reshape_select_fusion.9
  218.8 0.7 reshape_select_fusion.9
  220.4 0.7 reshape_select_fusion.9
  222.0 0.7 reshape_select_fusion.9
  223.6 0.7 reshape_select_fusion.9
  231.5 0.7 reshape_select_fusion.9
  233.1 0.7 reshape_select_fusion.9
  234.7 0.7 reshape_select_fusion.9
  236.3 0.7 reshape_select_fusion.9
  237.9 0.7 reshape_select_fusion.9
  247.5 0.7 reshape_select_fusion.9
  249.1 0.7 reshape_select_fusion.9
  250.7 0.7 reshape_select_fusion.9
  252.2 0.7 reshape_select_fusion.9
  253.8 0.7 reshape_select_fusion.9
  261.8 0.7 reshape_select_fusion.9
  263.4 0.7 reshape_select_fusion.9
  265.0 0.7 reshape_select_fusion.9
  266.6 0.7 reshape_select_fusion.9
  268.2 0.7 reshape_select_fusion.9
  277.7 0.7 reshape_select_fusion.9
  279.3 0.7 reshape_select_fusion.9
  595.7 2.5 gather_fusion
  605.3 1.0 fusion.80
  611.5 1.0 fusion.4
  612.7 1.0 select_n.267
  613.7 1.1 broadcast_select_fusion
  614.9 0.7 dynamic-slice_select_fusion.3
  615.5 93.4 %all-reduce.9.cloned.1.call-done = (f32[1024,128]{1,0:T(8,128)}, f32[1024,128]{1,0:T(8,128)}) async-done(((f32[1024,128]{1,0:T(8,128)}, f32[1024,128]{1,0:T(8,128)}), (f32[1024,128]{1,0:T(8,128)}, f32[1024,128]{1,0:T(8,128)})) %all-reduce.9.cloned.1.call-update) | async-done | bytes 1048592 | tf_op jit(solution)/shard_map/psum | solution.py:19
  708.9 1.1 constant_dynamic-update-slice_fusion.3
  710.2 0.7 dynamic-slice_select_fusion
  711.0 25.1 %all-reduce.13.cloned.1.call-done = (f32[256,256]{1,0:T(8,128)}, f32[256,128]{1,0:T(8,128)}) async-done(((f32[256,256]{1,0:T(8,128)}, f32[256,128]{1,0:T(8,128)}), (f32[256,256]{1,0:T(8,128)}, f32[256,128]{1,0:T(8,128)})) %all-reduce.13.cloned.1.call-update) | async-done | bytes 393232 | tf_op jit(solution)/shard_map/psum | solution.py:19
  736.1 1.1 copy.20
  737.2 407.8 %while.31 = (s32[]{:T(128)}, f32[256,256]{0,1:T(8,128)S(1)}, s32[]{:T(128)}) while((s32[]{:T(128)}, f32[256,256]{0,1:T(8,128)S(1)}, s32[]{:T(128)}) %tuple.84), condition=%wide.region_10.11_spmd.clone.clone, body=%wide.region_9.10_spmd.clone.clone.sunk | while | flops 263426 | bytes 1056337 | solution.py:34
  1145.2 2.6 gather_fusion.1
  1154.8 1.0 fusion.93
  1161.0 1.0 fusion.5
  1162.8 1.7 select_n.284
  (3141 shorter events, 794.8 us)
Async XLA Ops:
  6.5 3.0 copy-start.5
  6.5 152.8 %all-reduce.11.cloned.1.call-start = ((), (), s32[]{:S(2)}) async-start(), calls=%async_computation.1 | async-start | bytes 2097152 | tf_op jit(solution)/shard_map/psum | solution.py:19
  6.5 15.1 %collective-permute-start = (f32[1024,128]{1,0:T(8,128)}, f32[1024,128]{1,0:T(8,128)S(1)}, u32[]{:S(2)}, u32[]{:S(2)}) collective-permute-start(f32[1024,128]{1,0:T(8,128)} %param.7), channel_id=1, source_target_pairs={{0,1},{1,0},{2,3},{3,2},{4,5},{5,4},{6,7},{7,6},{8,9},{9,8},{10,11... | collective-permute-start | bytes 1572872 | tf_op jit(solution)/shard_map/ppermute | solution.py:14
  9.5 12.1 %slice-start = ((f32[2,1024]{1,0:T(2,128)}), f32[1,1024]{1,0:T(1,128)S(1)}, s32[]{:S(2)}) async-start(f32[2,1024]{1,0:T(2,128)} %param.8), calls=%async_computation.4 | async-start | bytes 8192 | tf_op jit(solution)/shard_map/slice | solution.py:76
  23.2 25.3 %collective-permute-start.1 = (f32[1024,128]{1,0:T(8,128)S(1)}, f32[1024,128]{1,0:T(8,128)S(1)}, u32[]{:S(2)}, u32[]{:S(2)}) collective-permute-start(f32[1024,128]{1,0:T(8,128)S(1)} %pad_maximum_fusion), channel_id=1, source_target_pairs={{0,16},{2,18},{4,20},{6,22},{8,24},{10,26},{12,28},{14,30},{16,0},... | collective-permute-start | bytes 1572872 | tf_op jit(solution)/shard_map/ppermute | solution.py:14
  26.0 0.7 copy-start.6
  48.5 13.0 %collective-permute-start.2 = (f32[1024,128]{1,0:T(8,128)S(1)}, f32[1024,128]{1,0:T(8,128)S(1)}, u32[]{:S(2)}, u32[]{:S(2)}) collective-permute-start(f32[1024,128]{1,0:T(8,128)S(1)} %multiply_multiply_fusion.1), channel_id=1, source_target_pairs={{0,8},{2,10},{4,12},{6,14},{8,0},{10,2},{12,4},{14,6},{16,24},{18,... | collective-permute-start | bytes 1572872 | tf_op jit(solution)/shard_map/ppermute | solution.py:14
  63.3 123.4 %all-reduce.15.cloned.1.call-start = ((), (), s32[]{:S(2)}) async-start(), calls=%async_computation.3 | async-start | bytes 786432 | tf_op jit(solution)/shard_map/psum | solution.py:19
  159.3 1.2 copy-start.1
  161.3 547.6 %all-reduce.9.cloned.1.call-start = ((), (), s32[]{:S(2)}) async-start(), calls=%async_computation | async-start | bytes 2097152 | tf_op jit(solution)/shard_map/psum | solution.py:19
  610.2 0.9 copy-start.4
  614.8 121.3 %all-reduce.13.cloned.1.call-start = ((), (), s32[]{:S(2)}) async-start(), calls=%async_computation.2 | async-start | bytes 786432 | tf_op jit(solution)/shard_map/psum | solution.py:19
  708.9 1.2 copy-start.2
  1159.7 0.9 copy-start.3
  1162.0 0.8 copy-start
Sparse Core Ops, SparseCore 0:
  63.4 95.8 all-reduce.10
  161.7 24.8 all-reduce.14
  615.0 93.9 all-reduce.8
  711.2 24.8 all-reduce.12
where the time goes:
time: 1180 us; the launch traced here: 1170 us
  other arithmetic  427 us (36%)
  local copies, waits for them, and re-layouts  384 us (33%)
  waiting for transfers between devices  285 us (24%)
  matrix products  27 us (2%)
  loops' own time  26.7 us (2%)
  between operations  13.9 us (1%)
    select_n x512, other arithmetic, eliminate(): column = jnp.where(below, current[:, step] / pivot, 0.0)  335 us
    dynamic_slice x512, local copies, waits for them, and re-layouts, eliminate(): pivot = current[step, step]  303 us
    psum x4, waiting for transfers between devices, from_root(): return lax.psum(jnp.where(mine, x, jnp.zeros_like(x)), axis)  239 us
    select_n x512, other arithmetic, eliminate(): jnp.where((places == step)[None, :] & below[:, None], column[:, None], cu...  75.5 us
    while x512, local copies, waits for them, and re-layouts  65.8 us
    ppermute x3, waiting for transfers between devices, swapped(): lax.ppermute(x, axis, [(i, i ^ 1 << distance) for i in range(lax.axis_siz...  46.1 us
    dot_general x62, matrix products, hdot(): jnp.dot(left, right, precision=lax.Precision.HIGHEST, preferred_element_t...  27 us
    another operation x2, loops' own time, lu_block(): return lax.fori_loop(0, size, eliminate, block)  26.7 us
  transfers between devices with their start and end apart: 7, of which 7 were waited for; matrix products, arithmetic and copies ran while one was open for 0% of the time, Pallas kernels for 0%

commit v1 on v0

v1 whole, which is shorter than its diff:
```python
import jax
import jax.numpy as jnp
from jax import lax
from jax.experimental import pallas as pl
from jax.experimental.pallas import tpu as pltpu
from jax.sharding import PartitionSpec as P

PW = 256
PANELS = 2
LEAD = PW * PANELS

inv_root = 0.7071067811865476

SUB = 8
BLK = 128


def swapped(x, axis, mask):
    return lax.ppermute(x, axis, [(i, i ^ mask) for i in range(lax.axis_size(axis))])


def hdot(left, right):
    return jnp.dot(left, right, precision=lax.Precision.HIGHEST, preferred_element_type=jnp.float32)


def tree_sum(terms):
    while len(terms) > 1:
        terms = [terms[i] + terms[i + 1] if i + 1 < len(terms) else terms[i] for i in range(0, len(terms), 2)]
    return terms[0]


def factor(block):
    count = BLK // SUB
    shape = (SUB, BLK)
    sub = lax.broadcasted_iota(jnp.int32, shape, 0)
    lane = lax.broadcasted_iota(jnp.int32, shape, 1)

    def row(x, j):
        return jnp.broadcast_to(x[j : j + 1, :], shape)

    def col(x, j):
        return jnp.broadcast_to(x[:, j : j + 1], shape)

    strips = [block[SUB * i : SUB * (i + 1)] for i in range(count)]
    extra = [jnp.where(lane == sub + SUB * i, 1.0, 0.0) for i in range(count)]
    pending = [jnp.zeros(shape, jnp.float32) for _ in range(count)]
    upper = []
    small = []
    for t in range(count):
        base = SUB * t
        inside = (lane >= base) & (lane < base + SUB)
        for i in range(t, count):
            pending[i] = jnp.where(inside, strips[i], pending[i])
        c = [col(strips[t], base + m) for m in range(SUB)]
        w, x, forward = strips[t], extra[t], strips[t]
        g = jnp.where(lane == sub + base, 1.0, 0.0)
        for j in range(SUB):
            r = 1.0 / row(c[j], j)
            here = sub == j
            cj = c[j]
            for m in range(j + 1, SUB):
                scaled = row(c[m], j) * r
                c[m] = jnp.where(here, scaled, c[m] - cj * scaled)
            scaled = row(w, j) * r
            w = jnp.where(here, scaled, w - cj * scaled)
            scaled = row(x, j) * r
            x = jnp.where(here, scaled, x - cj * scaled)
            scaled = row(g, j) * r
            g = jnp.where(sub > j, g, jnp.where(here, scaled, g - cj * scaled))
            if j < SUB - 1:
                forward = jnp.where(sub > j, forward - (cj * r) * row(forward, j), forward)
        upper.append(forward)
        small.append(g)
        w_rows = [row(w, m) for m in range(SUB)]
        x_rows = [row(x, m) for m in range(SUB)]
        for i in list(range(t + 1, count)) + list(range(t)):
            b = [col(strips[i], base + m) for m in range(SUB)]
            strips[i] = strips[i] - tree_sum([b[m] * w_rows[m] for m in range(SUB)])
            extra[i] = extra[i] - tree_sum([b[m] * x_rows[m] for m in range(SUB)])
        strips[t], extra[t] = w, x
    upper, pending, small, inverse = (jnp.concatenate(v, 0) for v in (upper, pending, small, extra))
    return upper, hdot(pending, small), inverse


def lu_kernel(info, *refs):
    blocks = LEAD // BLK
    panel_refs = refs[:blocks]
    own_top, own, out, work, rhs, packed, reduced = refs[blocks:]
    is_panel = info[0] == 1
    slot = info[1]
    is_top = info[2] == 1
    for j in range(blocks):
        work[j] = panel_refs[j][0:LEAD, :]
    rhs[...] = own_top[...]
    for k in range(blocks):
        here = pl.ds(BLK * k, BLK)
        upper, lower, inverse = factor(work[k, here, :])
        size = (BLK, BLK)
        above = lax.broadcasted_iota(jnp.int32, size, 0) <= lax.broadcasted_iota(jnp.int32, size, 1)
        upper = jnp.where(above, upper, 0.0)
        packed[k, here, :] = jnp.where(above, upper, lower)
        upper_inverse = hdot(inverse, lower)
        solved = [hdot(inverse, work[j, here, :]) for j in range(k + 1, blocks)]
        solved_rhs = hdot(inverse, rhs[here, :])
        if k + 1 < blocks:
            rest = pl.ds(BLK * (k + 1), LEAD - BLK * (k + 1))
            left = work[k, rest, :]
            for n, j in enumerate(range(k + 1, blocks)):
                work[j, rest, :] = work[j, rest, :] - hdot(left, solved[n])
            rhs[rest, :] = rhs[rest, :] - hdot(left, solved_rhs)
            packed[k, rest, :] = hdot(left, upper_inverse)
        for n, j in enumerate(range(k + 1, blocks)):
            packed[j, here, :] = hdot(upper, solved[n])
            work[j, here, :] = solved[n]
        out[here, :] = hdot(upper, solved_rhs)
        mine = jnp.where(slot == k, upper_inverse, 0.0)
        reduced[here, :] = jnp.where(is_panel, mine, solved_rhs)
    for k in range(blocks - 2, -1, -1):
        here = pl.ds(BLK * k, BLK)
        terms = [hdot(work[j, here, :], reduced[pl.ds(BLK * j, BLK), :]) for j in range(k + 1, blocks)]
        reduced[here, :] = reduced[here, :] - tree_sum(terms)
    top = jnp.where(is_panel, packed[slot], out[0:LEAD, :])
    height = out.shape[0]

    def below(first, rows):
        where = pl.ds(first, rows)
        terms = [
            hdot(panel_refs[j][pl.ds(LEAD + first, rows), :], reduced[pl.ds(BLK * j, BLK), :]) for j in range(blocks)
        ]
        total = tree_sum(terms)
        return jnp.where(is_panel, total, own[where, :] - total)

    for first in range(0, LEAD, 256):
        part = below(first, 256)
        out[pl.ds(first, 256), :] = jnp.where(is_top, top[first : first + 256], part)
    if height - LEAD <= 512:
        for first in range(LEAD, height, 256):
            out[pl.ds(first, 256), :] = below(first, 256)
    else:

        def step(n, carry):
            first = pl.multiple_of(LEAD + n * 256, 256)
            out[pl.ds(first, 256), :] = below(first, 256)
            return carry

        lax.fori_loop(0, (height - LEAD) // 256, step, 0)


def shards(matrix, row_diag, col_diag):
    height, width = matrix.shape
    row_pos = lax.axis_index("row")
    col_pos = lax.axis_index("col")
    half = height // 2
    blocks = LEAD // width
    block_bits = blocks.bit_length() - 1
    high_bit = lax.axis_size("col").bit_length() - 2
    high, low = 2**high_bit, 2 ** (high_bit - 1)
    is_first = row_pos == 0

    partner = swapped(matrix, "row", 1)
    other_rows = swapped(row_diag, "row", 1)
    others = {mask: swapped(col_diag, "col", mask) for mask in (low, high, high | low)}
    first_diag = jnp.where(is_first, row_diag, other_rows)
    total = matrix + partner
    mixed = row_diag[0][:, None] * jnp.where(is_first, total, partner - matrix) * inv_root
    upper_part, lower_part = mixed[:half], mixed[half:]
    first_mixed = first_diag[0][:, None] * total * inv_root
    top_rows = first_diag[1][:LEAD, None] * (first_mixed[:LEAD] + first_mixed[half : half + LEAD]) * inv_root
    current = jnp.concatenate(
        [
            top_rows,
            row_diag[1][:half, None] * (upper_part + lower_part) * inv_root,
            row_diag[1][half:, None] * (upper_part - lower_part) * inv_root,
        ],
        0,
    )

    in_high = (col_pos & high) != 0
    in_low = (col_pos & low) != 0
    by_mask = {0: col_diag, **others}

    def diag_of(h, l):
        mask = jnp.where(in_high != h, high, 0) + jnp.where(in_low != l, low, 0)
        picked = col_diag
        for m, value in others.items():
            picked = jnp.where(mask == m, value, picked)
        return picked

    partner = swapped(current, "col", low)
    even = jnp.where(in_low, partner, current)
    odd = jnp.where(in_low, current, partner)

    def contribution(h, l):
        scale_even = diag_of(h, jnp.bool_(False))[0]
        scale_odd = diag_of(h, jnp.bool_(True))[0]
        sign = jnp.where(in_high & h, -0.5, 0.5)
        return (sign * scale_even) * even + (jnp.where(l, -sign, sign) * scale_odd) * odd

    none = jnp.bool_(False)
    sent = contribution(~in_high, ~in_low)
    kept = contribution(in_high, in_low)
    lead = contribution(none, none)
    received = swapped(sent, "col", high | low)
    received_lead = swapped(lead, "col", high | low)
    own = col_diag[1] * (kept + received)
    panel = diag_of(none, none)[1] * (lead + received_lead)

    for bit in range(block_bits, high_bit - 1):
        arrived = swapped(panel, "col", 2**bit)
        panel = jnp.where((col_pos & 2**bit) != 0, arrived, panel)
    pieces = [panel]
    for bit in range(block_bits - 1, -1, -1):
        arrived = [swapped(p, "col", 2**bit) for p in pieces]
        second = (col_pos & 2**bit) != 0
        pieces = [
            piece
            for a, b in zip(pieces, arrived)
            for piece in (jnp.where(second, b, a), jnp.where(second, a, b))
        ]

    info = jnp.stack(
        [(col_pos < blocks).astype(jnp.int32), jnp.minimum(col_pos, blocks - 1).astype(jnp.int32), is_first.astype(jnp.int32)]
    )
    vmem = pl.BlockSpec(memory_space=pltpu.VMEM)
    return pl.pallas_call(
        lu_kernel,
        out_shape=jax.ShapeDtypeStruct((height, width), jnp.float32),
        in_specs=[pl.BlockSpec(memory_space=pltpu.SMEM)] + [vmem] * (blocks + 2),
        out_specs=vmem,
        scratch_shapes=[
            pltpu.VMEM((blocks, LEAD, width), jnp.float32),
            pltpu.VMEM((LEAD, width), jnp.float32),
            pltpu.VMEM((blocks, LEAD, width), jnp.float32),
            pltpu.VMEM((LEAD, width), jnp.float32),
        ],
        name="panel_lu",
    )(info, *pieces, own[:LEAD], own[LEAD:])


def solution(mesh):
    in_specs = (P("row", "col"), P(None, "row"), P(None, "col"))
    out_specs = P("row", "col")
    return jax.shard_map(shards, mesh=mesh, in_specs=in_specs, out_specs=out_specs, check_vma=False)
```

time: 1180 us -> 154 us (0.13)
  the two profiles are of different devices: /device:TPU:0 before, /device:TPU:9 now
where the time goes in v1:
time: 154 us
  waiting for transfers between devices  107 us (69%)
  Pallas kernels  24.6 us (16%)
  starting transfers between devices  11.6 us (8%)
  other arithmetic  7.84 us (5%)
  local copies, waits for them, and re-layouts  2.62 us (2%)
    ppermute x11, waiting for transfers between devices, swapped(): lax.ppermute(x, axis, [(i, i ^ mask) for i in range(lax.axis_size(axis))])  107 us
    pallas_call x1, Pallas kernels, shards(): pl.pallas_call(lu_kernel, out_shape=jax.ShapeDtypeStruct((height, width),...  24.6 us
    ppermute x11, starting transfers between devices, swapped(): lax.ppermute(x, axis, [(i, i ^ mask) for i in range(lax.axis_size(axis))])  11.6 us
    select_n x3, other arithmetic, shards(): jnp.where(second, a, b)  4.93 us
  transfers between devices with their start and end apart: 11, of which 6 were waited for; matrix products, arithmetic and copies ran while one was open for 3% of the time, Pallas kernels for 0%

profile of v1, /device:TPU:9, one launch (start us, length us, event | category | flops | bytes accessed | tf_op | source)
XLA Modules:
  0.0 154.2 jit_solution(8390644461439303792)
XLA Ops:
  0.0 0.0 copy-start
  0.0 1.2 collective-permute-start.4
  1.2 0.2 collective-permute-start.3
  1.5 0.7 fusion.2
  2.2 0.0 copy-done
  2.2 11.0 %collective-permute-done.3 = f32[2,1024]{1,0:T(2,128)S(1)} collective-permute-done((f32[2,1024]{1,0:T(2,128)}, f32[2,1024]{1,0:T(2,128)S(1)}, u32[]{:S(2)}, u32[]{:S(2)}) %collective-permute-start.3) | collective-permute-done | bytes 8224 | tf_op jit(solution)/shard_map/ppermute | solution.py:19
  13.2 0.0 collective-permute-done.4
  13.2 1.4 multiply_multiply_fusion.1
  14.6 0.1 fusion.1
  14.8 0.2 multiply_multiply_fusion.3
  15.0 0.0 copy-start.1
  15.0 0.1 pad_maximum_fusion
  15.0 0.3 collective-permute-start.5
  15.3 0.3 copy-done.1
  15.6 0.9 collective-permute-start.2
  16.6 2.3 %collective-permute-start.1 = (f32[2,128]{1,0:T(2,128)S(1)}, f32[2,128]{1,0:T(2,128)S(1)}, u32[]{:S(2)}, u32[]{:S(2)}) collective-permute-start(f32[2,128]{1,0:T(2,128)S(1)} %copy-done.1), channel_id=1, source_target_pairs={{0,16},{2,18},{4,20},{6,22},{8,24},{10,26},{12,28},{14,30},{16,0},... | collective-permute-start | bytes 3080 | tf_op jit(solution)/shard_map/ppermute | solution.py:19
  18.9 0.0 collective-permute-start
  18.9 13.8 %collective-permute-done.2 = f32[2,128]{1,0:T(2,128)S(1)} collective-permute-done((f32[2,128]{1,0:T(2,128)S(1)}, f32[2,128]{1,0:T(2,128)S(1)}, u32[]{:S(2)}, u32[]{:S(2)}) %collective-permute-start.2) | collective-permute-done | bytes 1056 | tf_op jit(solution)/shard_map/ppermute | solution.py:19
  32.7 0.7 collective-permute-done.1
  33.4 0.0 collective-permute-done
  33.5 0.0 collective-permute-done.5
  33.5 0.2 multiply_add_fusion
  33.7 0.6 collective-permute-start.10
  34.3 50.8 %collective-permute-done.10 = f32[1536,128]{1,0:T(8,128)S(1)} collective-permute-done((f32[1536,128]{1,0:T(8,128)S(1)}, f32[1536,128]{1,0:T(8,128)S(1)}, u32[]{:S(2)}, u32[]{:S(2)}) %collective-permute-start.10) | collective-permute-done | bytes 786464 | tf_op jit(solution)/shard_map/ppermute | solution.py:19
  85.1 0.2 add_multiply_fusion
  85.3 0.5 collective-permute-start.6
  85.8 16.4 %collective-permute-done.6 = f32[1536,128]{1,0:T(8,128)S(1)} collective-permute-done((f32[1536,128]{1,0:T(8,128)S(1)}, f32[1536,128]{1,0:T(8,128)S(1)}, u32[]{:S(2)}, u32[]{:S(2)}) %collective-permute-start.6) | collective-permute-done | bytes 786464 | tf_op jit(solution)/shard_map/ppermute | solution.py:19
  102.1 0.1 add_multiply_fusion.1
  102.3 1.3 collective-permute-start.7
  103.5 14.8 %collective-permute-done.7 = f32[1536,128]{1,0:T(8,128)} collective-permute-done((f32[1536,128]{1,0:T(8,128)S(1)}, f32[1536,128]{1,0:T(8,128)}, u32[]{:S(2)}, u32[]{:S(2)}) %collective-permute-start.7) | collective-permute-done | bytes 786464 | tf_op jit(solution)/shard_map/ppermute | solution.py:19
  118.4 1.2 broadcast_select_fusion.2
  119.6 4.1 %collective-permute-start.9 = (f32[1536,128]{1,0:T(8,128)S(1)}, f32[1536,128]{1,0:T(8,128)}, u32[]{:S(2)}, u32[]{:S(2)}) collective-permute-start(f32[1536,128]{1,0:T(8,128)S(1)} %get-tuple-element.12), channel_id=1, source_target_pairs={{0,2},{2,0},{4,6},{6,4},{8,10},{10,8},{12,14},{14,12},{16,18},{18,... | collective-permute-start | bytes 2359304 | tf_op jit(solution)/shard_map/ppermute | solution.py:19
  123.7 0.1 collective-permute-start.8
  123.8 0.6 pad_add_fusion.info
  124.4 0.7 slice.91.refs_4_
  125.1 0.8 slice.92.refs_5_
  125.9 0.0 collective-permute-done.9
  125.9 2.4 %broadcast_select_fusion.4 = (f32[1536,128]{1,0:T(8,128)}, f32[1536,128]{1,0:T(8,128)}) fusion(f32[1536,128]{1,0:T(8,128)S(1)} %get-tuple-element.12, f32[1536,128]{1,0:T(8,128)} %collective-permute-done.9, pred[]{:T(512)S(6)} %ne.21), kind=kLoop, calls=%fused_computation.11 | loop fusion | flops 393216 | bytes 3145729 | tf_op jit(solution)/shard_map/jit(_where)/select_n | solution.py:218
  128.4 0.0 collective-permute-done.8
  128.4 1.3 broadcast_select_fusion.6
  129.6 24.6 %panel_lu.1 = f32[1024,128]{1,0:T(8,128)} custom-call(s32[3]{0:T(128)} %pad_add_fusion.info, f32[1536,128]{1,0:T(8,128)} %get-tuple-element.15.refs_0_, f32[1536,128]{1,0:T(8,128)} %get-tuple-element.14.refs_1_, f32[1536,128]{1,0:T(8,128)} %get-tuple-element.11.refs_2_, f32[1536,128]{1,0:T(8,128)} %get-tuple-element.10.refs_3_, f32[512,128]{1,0:T(8,128)} %slice.91.refs_4_, ...), custom_call_target="tpu_custom_call" | custom-call | tf_op jit(solution)/shard_map/panel_lu/pallas_call | solution.py:225
  (11 shorter events, 0.1 us)
Async XLA Ops:
  0.0 2.2 %copy-start = (f32[2,1024]{1,0:T(2,128)S(1)}, f32[2,1024]{1,0:T(2,128)}, u32[]{:S(2)}) copy-start(f32[2,1024]{1,0:T(2,128)} %param.4) | copy-start | bytes 24580
  0.0 13.2 %collective-permute-start.4 = (f32[1024,128]{1,0:T(8,128)}, f32[1024,128]{1,0:T(8,128)S(1)}, u32[]{:S(2)}, u32[]{:S(2)}) collective-permute-start(f32[1024,128]{1,0:T(8,128)} %param.3), channel_id=1, source_target_pairs={{0,1},{1,0},{2,3},{3,2},{4,5},{5,4},{6,7},{7,6},{8,9},{9,8},{10,11... | collective-permute-start | bytes 1572872 | tf_op jit(solution)/shard_map/ppermute | solution.py:19
  1.2 12.0 %collective-permute-start.3 = (f32[2,1024]{1,0:T(2,128)}, f32[2,1024]{1,0:T(2,128)S(1)}, u32[]{:S(2)}, u32[]{:S(2)}) collective-permute-start(f32[2,1024]{1,0:T(2,128)} %param.4), channel_id=1, source_target_pairs={{0,1},{1,0},{2,3},{3,2},{4,5},{5,4},{6,7},{7,6},{8,9},{9,8},{10,11... | collective-permute-start | bytes 24584 | tf_op jit(solution)/shard_map/ppermute | solution.py:19
  15.0 0.7 copy-start.1
  15.0 18.4 %collective-permute-start.5 = (f32[1536,128]{1,0:T(8,128)S(1)}, f32[1536,128]{1,0:T(8,128)S(1)}, u32[]{:S(2)}, u32[]{:S(2)}) collective-permute-start(f32[1536,128]{1,0:T(8,128)S(1)} %pad_maximum_fusion), channel_id=1, source_target_pairs={{0,8},{2,10},{4,12},{6,14},{8,0},{10,2},{12,4},{14,6},{16,24},{18,... | collective-permute-start | bytes 2359304 | tf_op jit(solution)/shard_map/ppermute | solution.py:19
  15.6 17.0 %collective-permute-start.2 = (f32[2,128]{1,0:T(2,128)S(1)}, f32[2,128]{1,0:T(2,128)S(1)}, u32[]{:S(2)}, u32[]{:S(2)}) collective-permute-start(f32[2,128]{1,0:T(2,128)S(1)} %copy-done.1), channel_id=1, source_target_pairs={{0,8},{2,10},{4,12},{6,14},{8,0},{10,2},{12,4},{14,6},{16,24},{18,... | collective-permute-start | bytes 3080 | tf_op jit(solution)/shard_map/ppermute | solution.py:19
  16.6 16.9 %collective-permute-start.1 = (f32[2,128]{1,0:T(2,128)S(1)}, f32[2,128]{1,0:T(2,128)S(1)}, u32[]{:S(2)}, u32[]{:S(2)}) collective-permute-start(f32[2,128]{1,0:T(2,128)S(1)} %copy-done.1), channel_id=1, source_target_pairs={{0,16},{2,18},{4,20},{6,22},{8,24},{10,26},{12,28},{14,30},{16,0},... | collective-permute-start | bytes 3080 | tf_op jit(solution)/shard_map/ppermute | solution.py:19
  18.9 14.6 %collective-permute-start = (f32[2,128]{1,0:T(2,128)S(1)}, f32[2,128]{1,0:T(2,128)S(1)}, u32[]{:S(2)}, u32[]{:S(2)}) collective-permute-start(f32[2,128]{1,0:T(2,128)S(1)} %copy-done.1), channel_id=1, source_target_pairs={{0,24},{2,26},{4,28},{6,30},{8,16},{10,18},{12,20},{14,22},{16,8},... | collective-permute-start | bytes 3080 | tf_op jit(solution)/shard_map/ppermute | solution.py:19
  33.7 51.4 %collective-permute-start.10 = (f32[1536,128]{1,0:T(8,128)S(1)}, f32[1536,128]{1,0:T(8,128)S(1)}, u32[]{:S(2)}, u32[]{:S(2)}) collective-permute-start(f32[1536,128]{1,0:T(8,128)S(1)} %get-tuple-element.5), channel_id=1, source_target_pairs={{0,24},{2,26},{4,28},{6,30},{8,16},{10,18},{12,20},{14,22},{16,8},... | collective-permute-start | bytes 2359304 | tf_op jit(solution)/shard_map/ppermute | solution.py:19
  85.3 16.9 %collective-permute-start.6 = (f32[1536,128]{1,0:T(8,128)S(1)}, f32[1536,128]{1,0:T(8,128)S(1)}, u32[]{:S(2)}, u32[]{:S(2)}) collective-permute-start(f32[1536,128]{1,0:T(8,128)S(1)} %get-tuple-element.9), channel_id=1, source_target_pairs={{0,24},{2,26},{4,28},{6,30},{8,16},{10,18},{12,20},{14,22},{16,8},... | collective-permute-start | bytes 2359304 | tf_op jit(solution)/shard_map/ppermute | solution.py:19
  102.3 16.1 %collective-permute-start.7 = (f32[1536,128]{1,0:T(8,128)S(1)}, f32[1536,128]{1,0:T(8,128)}, u32[]{:S(2)}, u32[]{:S(2)}) collective-permute-start(f32[1536,128]{1,0:T(8,128)S(1)} %add_multiply_fusion.1), channel_id=1, source_target_pairs={{0,4},{2,6},{4,0},{6,2},{8,12},{10,14},{12,8},{14,10},{16,20},{18,... | collective-permute-start | bytes 2359304 | tf_op jit(solution)/shard_map/ppermute | solution.py:19
  119.6 6.3 %collective-permute-start.9 = (f32[1536,128]{1,0:T(8,128)S(1)}, f32[1536,128]{1,0:T(8,128)}, u32[]{:S(2)}, u32[]{:S(2)}) collective-permute-start(f32[1536,128]{1,0:T(8,128)S(1)} %get-tuple-element.12), channel_id=1, source_target_pairs={{0,2},{2,0},{4,6},{6,4},{8,10},{10,8},{12,14},{14,12},{16,18},{18,... | collective-permute-start | bytes 2359304 | tf_op jit(solution)/shard_map/ppermute | solution.py:19
  123.7 4.7 %collective-permute-start.8 = (f32[1536,128]{1,0:T(8,128)S(1)}, f32[1536,128]{1,0:T(8,128)S(1)}, u32[]{:S(2)}, u32[]{:S(2)}) collective-permute-start(f32[1536,128]{1,0:T(8,128)S(1)} %get-tuple-element.13), channel_id=1, source_target_pairs={{0,2},{2,0},{4,6},{6,4},{8,10},{10,8},{12,14},{14,12},{16,18},{18,... | collective-permute-start | bytes 2359304 | tf_op jit(solution)/shard_map/ppermute | solution.py:19

commit v2 on v1

v2 whole, which is shorter than its diff:
```python
import functools

import jax
import jax.numpy as jnp
from jax import lax
from jax.experimental import pallas as pl
from jax.experimental.pallas import tpu as pltpu
from jax.sharding import PartitionSpec as P

PW = 256
PANELS = 2
LEAD = PW * PANELS

SUB = 8
BLK = 128


def swapped(x, axis, mask):
    return lax.ppermute(x, axis, [(i, i ^ mask) for i in range(lax.axis_size(axis))])


def hdot(left, right):
    return jnp.dot(left, right, precision=lax.Precision.HIGHEST, preferred_element_type=jnp.float32)


def tree_sum(terms):
    while len(terms) > 1:
        terms = [terms[i] + terms[i + 1] if i + 1 < len(terms) else terms[i] for i in range(0, len(terms), 2)]
    return terms[0]


def factor(block):
    count = BLK // SUB
    shape = (SUB, BLK)
    sub = lax.broadcasted_iota(jnp.int32, shape, 0)
    lane = lax.broadcasted_iota(jnp.int32, shape, 1)

    def row(x, j):
        return jnp.broadcast_to(x[j : j + 1, :], shape)

    def col(x, j):
        return jnp.broadcast_to(x[:, j : j + 1], shape)

    strips = [block[SUB * i : SUB * (i + 1)] for i in range(count)]
    extra = [jnp.where(lane == sub + SUB * i, 1.0, 0.0) for i in range(count)]
    pending = [jnp.zeros(shape, jnp.float32) for _ in range(count)]
    upper = []
    small = []
    for t in range(count):
        base = SUB * t
        inside = (lane >= base) & (lane < base + SUB)
        for i in range(t, count):
            pending[i] = jnp.where(inside, strips[i], pending[i])
        c = [col(strips[t], base + m) for m in range(SUB)]
        w, x, forward = strips[t], extra[t], strips[t]
        g = jnp.where(lane == sub + base, 1.0, 0.0)
        for j in range(SUB):
            r = 1.0 / row(c[j], j)
            here = sub == j
            cj = c[j]
            for m in range(j + 1, SUB):
                scaled = row(c[m], j) * r
                c[m] = jnp.where(here, scaled, c[m] - cj * scaled)
            scaled = row(w, j) * r
            w = jnp.where(here, scaled, w - cj * scaled)
            scaled = row(x, j) * r
            x = jnp.where(here, scaled, x - cj * scaled)
            scaled = row(g, j) * r
            g = jnp.where(sub > j, g, jnp.where(here, scaled, g - cj * scaled))
            if j < SUB - 1:
                forward = jnp.where(sub > j, forward - (cj * r) * row(forward, j), forward)
        upper.append(forward)
        small.append(g)
        w_rows = [row(w, m) for m in range(SUB)]
        x_rows = [row(x, m) for m in range(SUB)]
        for i in list(range(t + 1, count)) + list(range(t)):
            b = [col(strips[i], base + m) for m in range(SUB)]
            strips[i] = strips[i] - tree_sum([b[m] * w_rows[m] for m in range(SUB)])
            extra[i] = extra[i] - tree_sum([b[m] * x_rows[m] for m in range(SUB)])
        strips[t], extra[t] = w, x
    upper, pending, small, inverse = (jnp.concatenate(v, 0) for v in (upper, pending, small, extra))
    return upper, hdot(pending, small), inverse


def eliminate_block(k, work, packed, inverted):
    blocks = LEAD // BLK
    here = pl.ds(BLK * k, BLK)
    upper, lower, inverse = factor(work[k, here, :])
    size = (BLK, BLK)
    above = lax.broadcasted_iota(jnp.int32, size, 0) <= lax.broadcasted_iota(jnp.int32, size, 1)
    upper = jnp.where(above, upper, 0.0)
    packed[k, here, :] = jnp.where(above, upper, lower)
    upper_inverse = hdot(inverse, lower)
    inverted[here, :] = upper_inverse
    work[k, here, :] = inverse
    later = range(k + 1, blocks)
    solved = {j: hdot(inverse, work[j, here, :]) for j in later}
    if k + 1 < blocks:
        rest = pl.ds(BLK * (k + 1), LEAD - BLK * (k + 1))
        left = work[k, rest, :]
        for j in later:
            work[j, rest, :] = work[j, rest, :] - hdot(left, solved[j])
        packed[k, rest, :] = hdot(left, upper_inverse)
    for j in later:
        packed[j, here, :] = hdot(upper, solved[j])
        work[j, here, :] = solved[j]


def first_kernel(*refs):
    blocks = LEAD // BLK
    pieces, (work, packed, inverted) = refs[:blocks], refs[blocks:]
    for j in range(blocks):
        work[j] = pieces[j][...]
    eliminate_block(0, work, packed, inverted)


def next_kernel(k, old_work, old_packed, old_inverted, work, packed, inverted):
    eliminate_block(k, work, packed, inverted)


def last_kernel(info, work, packed, inverted, own_top, own, *refs):
    blocks = LEAD // BLK
    pieces, (out, rhs, reduced, top) = refs[:blocks], refs[blocks:]
    is_panel = info[0] == 1
    slot = info[1]
    is_top = info[2] == 1
    rhs[...] = own_top[...]
    size = (BLK, BLK)
    above = lax.broadcasted_iota(jnp.int32, size, 0) <= lax.broadcasted_iota(jnp.int32, size, 1)
    for k in range(blocks):
        here = pl.ds(BLK * k, BLK)
        solved = hdot(work[k, here, :], rhs[here, :])
        for i in range(k + 1, blocks):
            there = pl.ds(BLK * i, BLK)
            rhs[there, :] = rhs[there, :] - hdot(work[k, there, :], solved)
        upper = jnp.where(above, packed[k, here, :], 0.0)
        top[here, :] = jnp.where(is_panel, packed[slot, here, :], hdot(upper, solved))
        mine = jnp.where(slot == k, inverted[here, :], 0.0)
        reduced[here, :] = jnp.where(is_panel, mine, solved)
    for k in range(blocks - 2, -1, -1):
        here = pl.ds(BLK * k, BLK)
        terms = [hdot(work[j, here, :], reduced[pl.ds(BLK * j, BLK), :]) for j in range(k + 1, blocks)]
        reduced[here, :] = reduced[here, :] - tree_sum(terms)
    height = out.shape[0]

    def below(first, rows):
        where = pl.ds(first, rows)
        terms = [hdot(pieces[j][where, :], reduced[pl.ds(BLK * j, BLK), :]) for j in range(blocks)]
        total = tree_sum(terms)
        return jnp.where(is_panel, total, own[where, :] - total)

    for first in range(0, LEAD, 256):
        out[pl.ds(first, 256), :] = jnp.where(is_top, top[pl.ds(first, 256), :], below(first, 256))

    def step(n, carry):
        first = pl.multiple_of(LEAD + n * 256, 256)
        out[pl.ds(first, 256), :] = below(first, 256)
        return carry

    lax.fori_loop(0, (height - LEAD) // 256, step, 0)


def shards(matrix, row_diag, col_diag):
    height, width = matrix.shape
    row_pos = lax.axis_index("row")
    col_pos = lax.axis_index("col")
    half = height // 2
    blocks = LEAD // width
    block_bits = blocks.bit_length() - 1
    high_bit = lax.axis_size("col").bit_length() - 2
    high, low = 2**high_bit, 2 ** (high_bit - 1)
    is_first = row_pos == 0
    in_high = (col_pos & high) != 0
    in_low = (col_pos & low) != 0

    partner = swapped(matrix, "row", 1)
    other_rows = swapped(row_diag, "row", 1)
    pair = jnp.concatenate([col_diag, swapped(col_diag, "col", low)], 0)
    far_pair = swapped(pair, "col", high)

    def diag_of(h, l):
        near = in_high == h
        chosen = jnp.where(near, pair, far_pair)
        return jnp.where(in_low == l, chosen[:2], chosen[2:])

    first_diag = jnp.where(is_first, row_diag, other_rows)
    total = matrix + partner
    lead_sum = [first_diag[0][a : a + LEAD, None] * total[a : a + LEAD] for a in (0, half)]
    top_rows = (0.5 * first_diag[1][:LEAD])[:, None] * (lead_sum[0] + lead_sum[1])
    mixed = row_diag[0][:, None] * jnp.where(is_first, total, partner - matrix)
    upper_part, lower_part = mixed[:half], mixed[half:]
    own_rows = jnp.concatenate(
        [
            (0.5 * row_diag[1][:half])[:, None] * (upper_part + lower_part),
            (0.5 * row_diag[1][half:])[:, None] * (upper_part - lower_part),
        ],
        0,
    )

    none, yes = jnp.bool_(False), jnp.bool_(True)

    def halves(values):
        other = swapped(values, "col", low)
        return jnp.where(in_low, other, values), jnp.where(in_low, values, other)

    def contribution(parts, h, l):
        even, odd = parts
        sign = jnp.where(in_high & h, -0.5, 0.5)
        scale_even = sign * diag_of(h, none)[0]
        scale_odd = jnp.where(l, -sign, sign) * diag_of(h, yes)[0]
        return scale_even * even + scale_odd * odd

    def spread(values):
        for bit in range(block_bits, high_bit - 1):
            arrived = swapped(values, "col", 2**bit)
            values = jnp.where((col_pos & 2**bit) != 0, arrived, values)
        return values

    def gather(pieces, bit):
        arrived = [swapped(p, "col", 2**bit) for p in pieces]
        second = (col_pos & 2**bit) != 0
        return [
            piece
            for a, b in zip(pieces, arrived)
            for piece in (jnp.where(second, b, a), jnp.where(second, a, b))
        ]

    lead_scale = diag_of(none, none)[1]
    top_parts = halves(top_rows)
    lead = contribution(top_parts, none, none)
    lead = spread(lead_scale * (lead + swapped(lead, "col", high)))
    own_parts = halves(own_rows)
    lead_pieces = [lead]
    for bit in range(block_bits - 1, -1, -1):
        lead_pieces = gather(lead_pieces, bit)

    panel = contribution(own_parts, none, none)
    panel_half = jnp.where(in_low, panel[half:], panel[:half])
    far_half, _ = lax.optimization_barrier((swapped(panel_half, "col", high), lead))
    panel_half = lead_scale * (panel_half + far_half)
    sent = jnp.concatenate(
        [contribution(top_parts, ~in_high, in_low), contribution(own_parts, ~in_high, in_low)], 0
    )
    kept = jnp.concatenate([contribution(top_parts, in_high, in_low), contribution(own_parts, in_high, in_low)], 0)
    received = swapped(sent, "col", high)
    other_half = swapped(panel_half, "col", low)
    panel = spread(
        jnp.where(
            in_low,
            jnp.concatenate([other_half, panel_half], 0),
            jnp.concatenate([panel_half, other_half], 0),
        )
    )
    panel_pieces = [panel]

    vmem = pl.BlockSpec(memory_space=pltpu.VMEM)
    cost = pl.CostEstimate(flops=4_000_000_000, bytes_accessed=12_000_000, transcendentals=0)
    size = 4 * width * (5 * blocks * LEAD + (blocks + 4) * (height + LEAD))
    params = pltpu.CompilerParams(vmem_limit_bytes=2 * size)
    stack = jax.ShapeDtypeStruct((blocks, LEAD, width), jnp.float32)
    state_shapes = (stack, stack, jax.ShapeDtypeStruct((LEAD, width), jnp.float32))
    state = pl.pallas_call(
        first_kernel,
        out_shape=state_shapes,
        in_specs=[vmem] * blocks,
        out_specs=(vmem,) * 3,
        cost_estimate=cost,
        compiler_params=params,
        name="eliminate_0",
    )(*lead_pieces)
    for k in range(1, blocks):
        state = pl.pallas_call(
            functools.partial(next_kernel, k),
            out_shape=state_shapes,
            in_specs=[vmem] * 3,
            out_specs=(vmem,) * 3,
            input_output_aliases={0: 0, 1: 1, 2: 2},
            cost_estimate=cost,
            compiler_params=params,
            name=f"eliminate_{k}",
        )(*state)

    for bit in range(block_bits - 1, -1, -1):
        panel_pieces = gather(panel_pieces, bit)
    whole = diag_of(in_high, in_low)[1] * (kept + received)

    info = jnp.stack(
        [
            (col_pos < blocks).astype(jnp.int32),
            jnp.minimum(col_pos, blocks - 1).astype(jnp.int32),
            is_first.astype(jnp.int32),
        ]
    )
    return pl.pallas_call(
        last_kernel,
        out_shape=jax.ShapeDtypeStruct((height, width), jnp.float32),
        in_specs=[pl.BlockSpec(memory_space=pltpu.SMEM)] + [vmem] * (blocks + 5),
        out_specs=vmem,
        scratch_shapes=[pltpu.VMEM((LEAD, width), jnp.float32)] * 3,
        cost_estimate=cost,
        compiler_params=params,
        name="own_columns",
    )(info, *state, whole[:LEAD], whole[LEAD:], *panel_pieces)


def solution(mesh):
    in_specs = (P("row", "col"), P(None, "row"), P(None, "col"))
    out_specs = P("row", "col")
    return jax.shard_map(shards, mesh=mesh, in_specs=in_specs, out_specs=out_specs, check_vma=False)
```

time: 154 us -> 101 us (0.66)
  the two profiles are of different devices: /device:TPU:9 before, /device:TPU:0 now
where the time goes in v2:
time: 101 us
  waiting for transfers between devices  47.2 us (47%)
  Pallas kernels  27.1 us (27%)
  starting transfers between devices  21.5 us (21%)
  other arithmetic  3.24 us (3%)
  local copies, waits for them, and re-layouts  1.45 us (1%)
    ppermute x16, waiting for transfers between devices, swapped(): lax.ppermute(x, axis, [(i, i ^ mask) for i in range(lax.axis_size(axis))])  47.2 us
    ppermute x16, starting transfers between devices, swapped(): lax.ppermute(x, axis, [(i, i ^ mask) for i in range(lax.axis_size(axis))])  21.5 us
    pallas_call x3, Pallas kernels, shards(): pl.pallas_call(functools.partial(next_kernel, k), out_shape=state_shapes,...  15 us
    pallas_call x1, Pallas kernels, shards(): pl.pallas_call(first_kernel, out_shape=state_shapes, in_specs=[vmem] * bl...  6.35 us
    pallas_call x1, Pallas kernels, shards(): pl.pallas_call(last_kernel, out_shape=jax.ShapeDtypeStruct((height, width...  5.75 us
  transfers between devices with their start and end apart: 16, of which 8 were waited for; matrix products, arithmetic and copies ran while one was open for 2% of the time, Pallas kernels for 21%

profile of v2, /device:TPU:0, one launch (start us, length us, event | category | flops | bytes accessed | tf_op | source)
XLA Modules:
  0.0 100.8 jit_solution(7959019760154529026)
XLA Ops:
  0.0 3.1 %collective-permute-start = (f32[2,128]{1,0:T(2,128)}, f32[2,128]{1,0:T(2,128)S(1)}, u32[]{:S(2)}, u32[]{:S(2)}) collective-permute-start(f32[2,128]{1,0:T(2,128)} %param.5), channel_id=1, source_target_pairs={{0,8},{2,10},{4,12},{6,14},{8,0},{10,2},{12,4},{14,6},{16,24},{18,... | collective-permute-start | bytes 3080 | tf_op jit(solution)/shard_map/ppermute | solution.py:19
  3.1 1.5 %collective-permute-start.3 = (f32[1024,128]{1,0:T(8,128)}, f32[1024,128]{1,0:T(8,128)S(1)}, u32[]{:S(2)}, u32[]{:S(2)}) collective-permute-start(f32[1024,128]{1,0:T(8,128)} %param.3), channel_id=1, source_target_pairs={{0,1},{1,0},{2,3},{3,2},{4,5},{5,4},{6,7},{7,6},{8,9},{9,8},{10,11... | collective-permute-start | bytes 1572872 | tf_op jit(solution)/shard_map/ppermute | solution.py:19
  4.6 0.5 collective-permute-start.2
  5.1 0.0 copy-start
  5.1 0.7 copy-done
  5.9 0.0 copy-start.1
  5.9 0.0 collective-permute-done
  5.9 0.7 copy-done.1
  6.6 2.6 %collective-permute-start.1 = (f32[4,128]{1,0:T(4,128)S(1)}, f32[4,128]{1,0:T(4,128)S(1)}, u32[]{:S(2)}, u32[]{:S(2)}) collective-permute-start(f32[4,128]{1,0:T(4,128)S(1)} %pad_maximum_fusion.2), channel_id=1, source_target_pairs={{0,16},{2,18},{4,20},{6,22},{8,24},{10,26},{12,28},{14,30},{16,0},... | collective-permute-start | bytes 6152 | tf_op jit(solution)/shard_map/ppermute | solution.py:19
  9.2 1.9 %collective-permute-done.1 = f32[4,128]{1,0:T(4,128)S(1)} collective-permute-done((f32[4,128]{1,0:T(4,128)S(1)}, f32[4,128]{1,0:T(4,128)S(1)}, u32[]{:S(2)}, u32[]{:S(2)}) %collective-permute-start.1) | collective-permute-done | bytes 2080 | tf_op jit(solution)/shard_map/ppermute | solution.py:19
  11.1 5.7 %collective-permute-done.2 = f32[2,1024]{1,0:T(2,128)S(1)} collective-permute-done((f32[2,1024]{1,0:T(2,128)}, f32[2,1024]{1,0:T(2,128)S(1)}, u32[]{:S(2)}, u32[]{:S(2)}) %collective-permute-start.2) | collective-permute-done | bytes 8224 | tf_op jit(solution)/shard_map/ppermute | solution.py:19
  16.8 0.0 collective-permute-done.3
  16.9 1.3 %select_multiply_fusion = (f32[1024,128]{1,0:T(8,128)S(1)}, f32[1024,128]{1,0:T(8,128)S(1)}) fusion(f32[1024,128]{1,0:T(8,128)S(1)} %collective-permute-done.3, f32[1024,128]{1,0:T(8,128)} %param.3, f32[1024]{0:T(1024)S(1)} %bitcast.31, pred[]{:T(512)S(6)} %eq.8), kind=kLoop, calls=%fused_computation.8 | loop fusion | flops 524288 | bytes 2101249 | tf_op jit(solution)/shard_map/mul | solution.py:190
  18.1 0.3 fusion.2
  18.4 0.3 collective-permute-start.4
  18.7 0.2 add_multiply_fusion.1
  19.0 1.8 %collective-permute-start.9 = (f32[1024,128]{1,0:T(8,128)S(1)}, f32[1024,128]{1,0:T(8,128)S(1)}, u32[]{:S(2)}, u32[]{:S(2)}) collective-permute-start(f32[1024,128]{1,0:T(8,128)S(1)} %pad_maximum_fusion.1), channel_id=1, source_target_pairs={{0,8},{2,10},{4,12},{6,14},{8,0},{10,2},{12,4},{14,6},{16,24},{18,... | collective-permute-start | bytes 1572872 | tf_op jit(solution)/shard_map/ppermute | solution.py:19
  20.8 9.6 %collective-permute-done.4 = f32[512,128]{1,0:T(8,128)S(1)} collective-permute-done((f32[512,128]{1,0:T(8,128)S(1)}, f32[512,128]{1,0:T(8,128)S(1)}, u32[]{:S(2)}, u32[]{:S(2)}) %collective-permute-start.4) | collective-permute-done | bytes 262176 | tf_op jit(solution)/shard_map/ppermute | solution.py:19
  30.4 0.3 multiply_add_fusion.4
  30.7 0.1 multiply_add_fusion.3
  30.8 0.5 collective-permute-start.5
  31.3 0.1 pad_add_fusion.info
  31.4 9.0 %collective-permute-done.5 = f32[512,128]{1,0:T(8,128)S(1)} collective-permute-done((f32[512,128]{1,0:T(8,128)S(1)}, f32[512,128]{1,0:T(8,128)S(1)}, u32[]{:S(2)}, u32[]{:S(2)}) %collective-permute-start.5) | collective-permute-done | bytes 262176 | tf_op jit(solution)/shard_map/ppermute | solution.py:19
  40.4 1.4 %collective-permute-start.6 = (f32[512,128]{1,0:T(8,128)S(1)}, f32[512,128]{1,0:T(8,128)S(1)}, u32[]{:S(2)}, u32[]{:S(2)}) collective-permute-start(f32[512,128]{1,0:T(8,128)S(1)} %add_multiply_fusion.2), channel_id=1, source_target_pairs={{0,4},{2,6},{4,0},{6,2},{8,12},{10,14},{12,8},{14,10},{16,20},{18,... | collective-permute-start | bytes 786440 | tf_op jit(solution)/shard_map/ppermute | solution.py:19
  41.8 0.4 collective-permute-done.9
  42.2 0.1 multiply_add_fusion
  42.4 3.1 %collective-permute-start.11 = (f32[512,128]{1,0:T(8,128)S(1)}, f32[512,128]{1,0:T(8,128)S(1)}, u32[]{:S(2)}, u32[]{:S(2)}) collective-permute-start(f32[512,128]{1,0:T(8,128)S(1)} %slice_select_fusion), channel_id=1, source_target_pairs={{0,16},{2,18},{4,20},{6,22},{8,24},{10,26},{12,28},{14,30},{16,0},... | collective-permute-start | bytes 786440 | tf_op jit(solution)/shard_map/ppermute | solution.py:19
  45.5 0.1 multiply_add_fusion.2
  45.6 9.9 %collective-permute-done.11 = f32[512,128]{1,0:T(8,128)S(1)} collective-permute-done((f32[512,128]{1,0:T(8,128)S(1)}, f32[512,128]{1,0:T(8,128)S(1)}, u32[]{:S(2)}, u32[]{:S(2)}) %collective-permute-start.11) | collective-permute-done | bytes 262176 | tf_op jit(solution)/shard_map/ppermute | solution.py:19
  55.5 0.1 add_multiply_fusion
  55.6 0.4 collective-permute-start.12
  55.9 0.0 collective-permute-done.6
  56.0 0.1 collective-permute-start.7
  56.1 0.1 pad_maximum_fusion
  56.1 3.4 %collective-permute-start.10 = (f32[1536,128]{1,0:T(8,128)S(1)}, f32[1536,128]{1,0:T(8,128)S(1)}, u32[]{:S(2)}, u32[]{:S(2)}) collective-permute-start(f32[1536,128]{1,0:T(8,128)S(1)} %pad_maximum_fusion), channel_id=1, source_target_pairs={{0,16},{2,18},{4,20},{6,22},{8,24},{10,26},{12,28},{14,30},{16,0},... | collective-permute-start | bytes 2359304 | tf_op jit(solution)/shard_map/ppermute | solution.py:19
  59.6 0.2 collective-permute-start.8
  59.8 5.5 %collective-permute-done.12 = f32[512,128]{1,0:T(8,128)S(1)} collective-permute-done((f32[512,128]{1,0:T(8,128)S(1)}, f32[512,128]{1,0:T(8,128)S(1)}, u32[]{:S(2)}, u32[]{:S(2)}) %collective-permute-start.12) | collective-permute-done | bytes 262176 | tf_op jit(solution)/shard_map/ppermute | solution.py:19
  65.4 2.0 %collective-permute-start.13 = (f32[1024,128]{1,0:T(8,128)S(1)}, f32[1024,128]{1,0:T(8,128)S(1)}, u32[]{:S(2)}, u32[]{:S(2)}) collective-permute-start(f32[1024,128]{1,0:T(8,128)S(1)} %maximum_select_fusion), channel_id=1, source_target_pairs={{0,4},{2,6},{4,0},{6,2},{8,12},{10,14},{12,8},{14,10},{16,20},{18,... | collective-permute-start | bytes 1572872 | tf_op jit(solution)/shard_map/ppermute | solution.py:19
  67.3 0.0 collective-permute-done.7
  67.4 0.0 collective-permute-done.8
  67.4 6.3 %eliminate_0.1 = (f32[4,512,128]{2,1,0:T(8,128)S(1)}, f32[4,512,128]{2,1,0:T(8,128)S(1)}, f32[512,128]{1,0:T(8,128)S(1)}) custom-call(f32[512,128]{1,0:T(8,128)S(1)} %get-tuple-element.56.refs_0_, f32[512,128]{1,0:T(8,128)S(1)} %get-tuple-element.55.refs_1_, f32[512,128]{1,0:T(8,128)S(1)} %get-tuple-element.52.refs_2_, f32[512,128]{1,0:T(8,128)S(1)} %get-tuple-element.51.refs_3_), custom_call_target="tpu_custom_call" | custom-call | flops 4000000000 | bytes 12000000 | tf_op jit(solution)/shard_map/eliminate_0/pallas_call | solution.py:262
  73.8 5.8 %eliminate_1.1 = (f32[4,512,128]{2,1,0:T(8,128)S(1)}, f32[4,512,128]{2,1,0:T(8,128)S(1)}, f32[512,128]{1,0:T(8,128)S(1)}) custom-call(f32[4,512,128]{2,1,0:T(8,128)S(1)} %get-tuple-element.18.old_work, f32[4,512,128]{2,1,0:T(8,128)S(1)} %get-tuple-element.19.old_packed, ...), custom_call_target="tpu_custom_call", output_to_operand_aliasing={{0}: (0, {}), {1}: (1, {}), {2}: (2, {})} | custom-call | flops 4000000000 | bytes 12000000 | tf_op jit(solution)/shard_map/eliminate_1/pallas_call | solution.py:272
  79.6 4.7 %eliminate_2.1 = (f32[4,512,128]{2,1,0:T(8,128)S(1)}, f32[4,512,128]{2,1,0:T(8,128)S(1)}, f32[512,128]{1,0:T(8,128)S(1)}) custom-call(f32[4,512,128]{2,1,0:T(8,128)S(1)} %get-tuple-element.21.old_work, f32[4,512,128]{2,1,0:T(8,128)S(1)} %get-tuple-element.22.old_packed, ...), custom_call_target="tpu_custom_call", output_to_operand_aliasing={{0}: (0, {}), {1}: (1, {}), {2}: (2, {})} | custom-call | flops 4000000000 | bytes 12000000 | tf_op jit(solution)/shard_map/eliminate_2/pallas_call | solution.py:272
  84.3 0.0 collective-permute-done.13
  84.4 0.1 broadcast_select_fusion
  84.5 0.1 collective-permute-start.14
  84.6 4.4 %eliminate_3.1 = (f32[4,512,128]{2,1,0:T(8,128)S(1)}, f32[4,512,128]{2,1,0:T(8,128)S(1)}, f32[512,128]{1,0:T(8,128)S(1)}) custom-call(f32[4,512,128]{2,1,0:T(8,128)S(1)} %get-tuple-element.24.old_work, f32[4,512,128]{2,1,0:T(8,128)S(1)} %get-tuple-element.25.old_packed, ...), custom_call_target="tpu_custom_call", output_to_operand_aliasing={{0}: (0, {}), {1}: (1, {}), {2}: (2, {})} | custom-call | flops 4000000000 | bytes 12000000 | tf_op jit(solution)/shard_map/eliminate_3/pallas_call | solution.py:272
  89.0 0.6 collective-permute-start.15
  89.6 5.1 %collective-permute-done.10 = f32[1536,128]{1,0:T(8,128)S(1)} collective-permute-done((f32[1536,128]{1,0:T(8,128)S(1)}, f32[1536,128]{1,0:T(8,128)S(1)}, u32[]{:S(2)}, u32[]{:S(2)}) %collective-permute-start.10) | collective-permute-done | bytes 786464 | tf_op jit(solution)/shard_map/ppermute | solution.py:19
  94.7 0.1 fusion
  94.8 0.0 collective-permute-done.14
  94.8 0.1 broadcast_select_fusion.4
  95.0 0.0 collective-permute-done.15
  95.0 0.1 broadcast_select_fusion.2
  95.1 5.7 %own_columns.1 = f32[1024,128]{1,0:T(8,128)} custom-call(s32[3]{0:T(128)S(1)} %pad_add_fusion.info, f32[4,512,128]{2,1,0:T(8,128)S(1)} %get-tuple-element.27.work, f32[4,512,128]{2,1,0:T(8,128)S(1)} %get-tuple-element.28.packed, f32[512,128]{1,0:T(8,128)S(1)} %get-tuple-element.29.inverted, f32[512,128]{1,0:T(8,128)S(1)} %slice.156.own_top, ...), custom_call_target="tpu_custom_call" | custom-call | flops 4000000000 | bytes 12000000 | tf_op jit(solution)/shard_map/own_columns/pallas_call | solution.py:294
  (23 shorter events, 0.4 us)
Async XLA Ops:
  0.0 5.9 %collective-permute-start = (f32[2,128]{1,0:T(2,128)}, f32[2,128]{1,0:T(2,128)S(1)}, u32[]{:S(2)}, u32[]{:S(2)}) collective-permute-start(f32[2,128]{1,0:T(2,128)} %param.5), channel_id=1, source_target_pairs={{0,8},{2,10},{4,12},{6,14},{8,0},{10,2},{12,4},{14,6},{16,24},{18,... | collective-permute-start | bytes 3080 | tf_op jit(solution)/shard_map/ppermute | solution.py:19
  3.1 13.8 %collective-permute-start.3 = (f32[1024,128]{1,0:T(8,128)}, f32[1024,128]{1,0:T(8,128)S(1)}, u32[]{:S(2)}, u32[]{:S(2)}) collective-permute-start(f32[1024,128]{1,0:T(8,128)} %param.3), channel_id=1, source_target_pairs={{0,1},{1,0},{2,3},{3,2},{4,5},{5,4},{6,7},{7,6},{8,9},{9,8},{10,11... | collective-permute-start | bytes 1572872 | tf_op jit(solution)/shard_map/ppermute | solution.py:19
  4.6 12.2 %collective-permute-start.2 = (f32[2,1024]{1,0:T(2,128)}, f32[2,1024]{1,0:T(2,128)S(1)}, u32[]{:S(2)}, u32[]{:S(2)}) collective-permute-start(f32[2,1024]{1,0:T(2,128)} %param.4), channel_id=1, source_target_pairs={{0,1},{1,0},{2,3},{3,2},{4,5},{5,4},{6,7},{7,6},{8,9},{9,8},{10,11... | collective-permute-start | bytes 24584 | tf_op jit(solution)/shard_map/ppermute | solution.py:19
  5.1 0.7 copy-start
  5.9 0.7 copy-start.1
  6.6 4.5 %collective-permute-start.1 = (f32[4,128]{1,0:T(4,128)S(1)}, f32[4,128]{1,0:T(4,128)S(1)}, u32[]{:S(2)}, u32[]{:S(2)}) collective-permute-start(f32[4,128]{1,0:T(4,128)S(1)} %pad_maximum_fusion.2), channel_id=1, source_target_pairs={{0,16},{2,18},{4,20},{6,22},{8,24},{10,26},{12,28},{14,30},{16,0},... | collective-permute-start | bytes 6152 | tf_op jit(solution)/shard_map/ppermute | solution.py:19
  18.4 12.1 %collective-permute-start.4 = (f32[512,128]{1,0:T(8,128)S(1)}, f32[512,128]{1,0:T(8,128)S(1)}, u32[]{:S(2)}, u32[]{:S(2)}) collective-permute-start(f32[512,128]{1,0:T(8,128)S(1)} %fusion.2), channel_id=1, source_target_pairs={{0,8},{2,10},{4,12},{6,14},{8,0},{10,2},{12,4},{14,6},{16,24},{18,... | collective-permute-start | bytes 786440 | tf_op jit(solution)/shard_map/ppermute | solution.py:19
  19.0 23.2 %collective-permute-start.9 = (f32[1024,128]{1,0:T(8,128)S(1)}, f32[1024,128]{1,0:T(8,128)S(1)}, u32[]{:S(2)}, u32[]{:S(2)}) collective-permute-start(f32[1024,128]{1,0:T(8,128)S(1)} %pad_maximum_fusion.1), channel_id=1, source_target_pairs={{0,8},{2,10},{4,12},{6,14},{8,0},{10,2},{12,4},{14,6},{16,24},{18,... | collective-permute-start | bytes 1572872 | tf_op jit(solution)/shard_map/ppermute | solution.py:19
  30.8 9.5 %collective-permute-start.5 = (f32[512,128]{1,0:T(8,128)S(1)}, f32[512,128]{1,0:T(8,128)S(1)}, u32[]{:S(2)}, u32[]{:S(2)}) collective-permute-start(f32[512,128]{1,0:T(8,128)S(1)} %get-tuple-element.48), channel_id=1, source_target_pairs={{0,16},{2,18},{4,20},{6,22},{8,24},{10,26},{12,28},{14,30},{16,0},... | collective-permute-start | bytes 786440 | tf_op jit(solution)/shard_map/ppermute | solution.py:19
  40.4 15.6 %collective-permute-start.6 = (f32[512,128]{1,0:T(8,128)S(1)}, f32[512,128]{1,0:T(8,128)S(1)}, u32[]{:S(2)}, u32[]{:S(2)}) collective-permute-start(f32[512,128]{1,0:T(8,128)S(1)} %add_multiply_fusion.2), channel_id=1, source_target_pairs={{0,4},{2,6},{4,0},{6,2},{8,12},{10,14},{12,8},{14,10},{16,20},{18,... | collective-permute-start | bytes 786440 | tf_op jit(solution)/shard_map/ppermute | solution.py:19
  42.4 13.1 %collective-permute-start.11 = (f32[512,128]{1,0:T(8,128)S(1)}, f32[512,128]{1,0:T(8,128)S(1)}, u32[]{:S(2)}, u32[]{:S(2)}) collective-permute-start(f32[512,128]{1,0:T(8,128)S(1)} %slice_select_fusion), channel_id=1, source_target_pairs={{0,16},{2,18},{4,20},{6,22},{8,24},{10,26},{12,28},{14,30},{16,0},... | collective-permute-start | bytes 786440 | tf_op jit(solution)/shard_map/ppermute | solution.py:19
  55.6 9.8 %collective-permute-start.12 = (f32[512,128]{1,0:T(8,128)S(1)}, f32[512,128]{1,0:T(8,128)S(1)}, u32[]{:S(2)}, u32[]{:S(2)}) collective-permute-start(f32[512,128]{1,0:T(8,128)S(1)} %add_multiply_fusion), channel_id=1, source_target_pairs={{0,8},{2,10},{4,12},{6,14},{8,0},{10,2},{12,4},{14,6},{16,24},{18,... | collective-permute-start | bytes 786440 | tf_op jit(solution)/shard_map/ppermute | solution.py:19
  56.0 11.3 %collective-permute-start.7 = (f32[512,128]{1,0:T(8,128)S(1)}, f32[512,128]{1,0:T(8,128)S(1)}, u32[]{:S(2)}, u32[]{:S(2)}) collective-permute-start(f32[512,128]{1,0:T(8,128)S(1)} %get-tuple-element.54), channel_id=1, source_target_pairs={{0,2},{2,0},{4,6},{6,4},{8,10},{10,8},{12,14},{14,12},{16,18},{18,... | collective-permute-start | bytes 786440 | tf_op jit(solution)/shard_map/ppermute | solution.py:19
  56.1 38.5 %collective-permute-start.10 = (f32[1536,128]{1,0:T(8,128)S(1)}, f32[1536,128]{1,0:T(8,128)S(1)}, u32[]{:S(2)}, u32[]{:S(2)}) collective-permute-start(f32[1536,128]{1,0:T(8,128)S(1)} %pad_maximum_fusion), channel_id=1, source_target_pairs={{0,16},{2,18},{4,20},{6,22},{8,24},{10,26},{12,28},{14,30},{16,0},... | collective-permute-start | bytes 2359304 | tf_op jit(solution)/shard_map/ppermute | solution.py:19
  59.6 7.8 %collective-permute-start.8 = (f32[512,128]{1,0:T(8,128)S(1)}, f32[512,128]{1,0:T(8,128)S(1)}, u32[]{:S(2)}, u32[]{:S(2)}) collective-permute-start(f32[512,128]{1,0:T(8,128)S(1)} %get-tuple-element.53), channel_id=1, source_target_pairs={{0,2},{2,0},{4,6},{6,4},{8,10},{10,8},{12,14},{14,12},{16,18},{18,... | collective-permute-start | bytes 786440 | tf_op jit(solution)/shard_map/ppermute | solution.py:19
  65.4 19.0 %collective-permute-start.13 = (f32[1024,128]{1,0:T(8,128)S(1)}, f32[1024,128]{1,0:T(8,128)S(1)}, u32[]{:S(2)}, u32[]{:S(2)}) collective-permute-start(f32[1024,128]{1,0:T(8,128)S(1)} %maximum_select_fusion), channel_id=1, source_target_pairs={{0,4},{2,6},{4,0},{6,2},{8,12},{10,14},{12,8},{14,10},{16,20},{18,... | collective-permute-start | bytes 1572872 | tf_op jit(solution)/shard_map/ppermute | solution.py:19
  84.5 10.3 %collective-permute-start.14 = (f32[1024,128]{1,0:T(8,128)S(1)}, f32[1024,128]{1,0:T(8,128)S(1)}, u32[]{:S(2)}, u32[]{:S(2)}) collective-permute-start(f32[1024,128]{1,0:T(8,128)S(1)} %get-tuple-element.42), channel_id=1, source_target_pairs={{0,2},{2,0},{4,6},{6,4},{8,10},{10,8},{12,14},{14,12},{16,18},{18,... | collective-permute-start | bytes 1572872 | tf_op jit(solution)/shard_map/ppermute | solution.py:19
  89.0 6.0 %collective-permute-start.15 = (f32[1024,128]{1,0:T(8,128)S(1)}, f32[1024,128]{1,0:T(8,128)S(1)}, u32[]{:S(2)}, u32[]{:S(2)}) collective-permute-start(f32[1024,128]{1,0:T(8,128)S(1)} %get-tuple-element.41), channel_id=1, source_target_pairs={{0,2},{2,0},{4,6},{6,4},{8,10},{10,8},{12,14},{14,12},{16,18},{18,... | collective-permute-start | bytes 1572872 | tf_op jit(solution)/shard_map/ppermute | solution.py:19

commit v3 on v2

--- a/solution.py
+++ b/solution.py
@@ -187,7 +187,42 @@
     total = matrix + partner
     lead_sum = [first_diag[0][a : a + LEAD, None] * total[a : a + LEAD] for a in (0, half)]
     top_rows = (0.5 * first_diag[1][:LEAD])[:, None] * (lead_sum[0] + lead_sum[1])
-    mixed = row_diag[0][:, None] * jnp.where(is_first, total, partner - matrix)
+    none, yes = jnp.bool_(False), jnp.bool_(True)
+
+    def halves(values):
+        other = swapped(values, "col", low)
+        return jnp.where(in_low, other, values), jnp.where(in_low, values, other)
+
+    def contribution(parts, h, l):
+        even, odd = parts
+        sign = jnp.where(in_high & h, -0.5, 0.5)
+        scale_even = sign * diag_of(h, none)[0]
+        scale_odd = jnp.where(l, -sign, sign) * diag_of(h, yes)[0]
+        return scale_even * even + scale_odd * odd
+
+    def spread(values):
+        for bit in range(block_bits, high_bit - 1):
+            arrived = swapped(values, "col", 2**bit)
+            values = jnp.where((col_pos & 2**bit) != 0, arrived, values)
+        return values
+
+    def gather(pieces, bit):
+        return joined(pieces, [swapped(p, "col", 2**bit) for p in pieces], bit)
+
+    def joined(pieces, arrived, bit):
+        second = (col_pos & 2**bit) != 0
+        return [
+            piece
+            for a, b in zip(pieces, arrived)
+            for piece in (jnp.where(second, b, a), jnp.where(second, a, b))
+        ]
+
+    lead_scale = diag_of(none, none)[1]
+    top_parts = halves(top_rows)
+    *top_parts, local, remote = lax.optimization_barrier((*top_parts, matrix, partner))
+    lead = contribution(top_parts, none, none)
+    lead = spread(lead_scale * (lead + swapped(lead, "col", high)))
+    mixed = row_diag[0][:, None] * jnp.where(is_first, local + remote, remote - local)
     upper_part, lower_part = mixed[:half], mixed[half:]
     own_rows = jnp.concatenate(
         [
@@ -197,38 +232,6 @@
         0,
     )
 
-    none, yes = jnp.bool_(False), jnp.bool_(True)
-
-    def halves(values):
-        other = swapped(values, "col", low)
-        return jnp.where(in_low, other, values), jnp.where(in_low, values, other)
-
-    def contribution(parts, h, l):
-        even, odd = parts
-        sign = jnp.where(in_high & h, -0.5, 0.5)
-        scale_even = sign * diag_of(h, none)[0]
-        scale_odd = jnp.where(l, -sign, sign) * diag_of(h, yes)[0]
-        return scale_even * even + scale_odd * odd
-
-    def spread(values):
-        for bit in range(block_bits, high_bit - 1):
-            arrived = swapped(values, "col", 2**bit)
-            values = jnp.where((col_pos & 2**bit) != 0, arrived, values)
-        return values
-
-    def gather(pieces, bit):
-        arrived = [swapped(p, "col", 2**bit) for p in pieces]
-        second = (col_pos & 2**bit) != 0
-        return [
-            piece
-            for a, b in zip(pieces, arrived)
-            for piece in (jnp.where(second, b, a), jnp.where(second, a, b))
-        ]
-
-    lead_scale = diag_of(none, none)[1]
-    top_parts = halves(top_rows)
-    lead = contribution(top_parts, none, none)
-    lead = spread(lead_scale * (lead + swapped(lead, "col", high)))
     own_parts = halves(own_rows)
     lead_pieces = [lead]
     for bit in range(block_bits - 1, -1, -1):
@@ -236,23 +239,12 @@
 
     panel = contribution(own_parts, none, none)
     panel_half = jnp.where(in_low, panel[half:], panel[:half])
-    far_half, _ = lax.optimization_barrier((swapped(panel_half, "col", high), lead))
-    panel_half = lead_scale * (panel_half + far_half)
+    far_half = swapped(panel_half, "col", high)
     sent = jnp.concatenate(
         [contribution(top_parts, ~in_high, in_low), contribution(own_parts, ~in_high, in_low)], 0
     )
     kept = jnp.concatenate([contribution(top_parts, in_high, in_low), contribution(own_parts, in_high, in_low)], 0)
     received = swapped(sent, "col", high)
-    other_half = swapped(panel_half, "col", low)
-    panel = spread(
-        jnp.where(
-            in_low,
-            jnp.concatenate([other_half, panel_half], 0),
-            jnp.concatenate([panel_half, other_half], 0),
-        )
-    )
-    panel_pieces = [panel]
-
     vmem = pl.BlockSpec(memory_space=pltpu.VMEM)
     cost = pl.CostEstimate(flops=4_000_000_000, bytes_accessed=12_000_000, transcendentals=0)
     size = 4 * width * (5 * blocks * LEAD + (blocks + 4) * (height + LEAD))
@@ -268,6 +260,11 @@
         compiler_params=params,
         name="eliminate_0",
     )(*lead_pieces)
+    far_half, *state = lax.optimization_barrier((far_half, *state))
+    panel_half = lead_scale * (panel_half + far_half)
+    other_half = swapped(panel_half, "col", low)
+    panel_pieces = []
+
     for k in range(1, blocks):
         state = pl.pallas_call(
             functools.partial(next_kernel, k),
@@ -279,9 +276,20 @@
             compiler_params=params,
             name=f"eliminate_{k}",
         )(*state)
-
-    for bit in range(block_bits - 1, -1, -1):
-        panel_pieces = gather(panel_pieces, bit)
+        bit = block_bits - k + 1
+        arrived = [other_half] if k == 1 else [swapped(p, "col", 2**bit) for p in panel_pieces]
+        if k == blocks - 1:
+            arrived.append(received)
+        *arrived, state0, state1, state2 = lax.optimization_barrier((*arrived, *state))
+        state = (state0, state1, state2)
+        if k == blocks - 1:
+            received = arrived.pop()
+        if k == 1:
+            ordered = jnp.where(in_low, arrived[0], panel_half), jnp.where(in_low, panel_half, arrived[0])
+            panel_pieces = [spread(jnp.concatenate(ordered, 0))]
+        else:
+            panel_pieces = joined(panel_pieces, arrived, bit)
+
     whole = diag_of(in_high, in_low)[1] * (kept + received)
 
     info = jnp.stack(

time: 101 us -> 120 us (1.19)
  waiting for transfers between devices: 47.2 us -> 65.6 us
  other arithmetic: 3.24 us -> 9.48 us
  starting transfers between devices: 21.5 us -> 16.2 us
    ppermute x16, waiting for transfers between devices: 47.2 us -> 65.6 us  [swapped(): lax.ppermute(x, axis, [(i, i ^ mask) for i in range(lax.axis_size(axis))])]
    ppermute x16, starting transfers between devices: 21.5 us -> 16.2 us  [swapped(): lax.ppermute(x, axis, [(i, i ^ mask) for i in range(lax.axis_size(axis))])]
    select_n x7 -> x8, other arithmetic: 0.49 us -> 2.72 us  [the longest x6 2.41 us: joined(): jnp.where(second, a, b)]
    add x4 -> x3, other arithmetic: 0.57 us -> 1.82 us  [contribution(): return scale_even * even + scale_odd * odd]
  transfers between devices with their start and end apart: 16 -> 16, of which waited for: 8 -> 10; matrix products, arithmetic and copies ran while one was open for 2% -> 3% of each run, Pallas kernels for 21% -> 18%
where the time goes in v3:
time: 120 us
  waiting for transfers between devices  65.6 us (55%)
  Pallas kernels  27.1 us (23%)
  starting transfers between devices  16.2 us (14%)
  other arithmetic  9.48 us (8%)
  local copies, waits for them, and re-layouts  1.43 us (1%)
    ppermute x16, waiting for transfers between devices, swapped(): lax.ppermute(x, axis, [(i, i ^ mask) for i in range(lax.axis_size(axis))])  65.6 us
    ppermute x16, starting transfers between devices, swapped(): lax.ppermute(x, axis, [(i, i ^ mask) for i in range(lax.axis_size(axis))])  16.2 us
    pallas_call x3, Pallas kernels, shards(): pl.pallas_call(functools.partial(next_kernel, k), out_shape=state_shapes,...  15 us
    pallas_call x1, Pallas kernels, shards(): pl.pallas_call(first_kernel, out_shape=state_shapes, in_specs=[vmem] * bl...  6.35 us
    pallas_call x1, Pallas kernels, shards(): pl.pallas_call(last_kernel, out_shape=jax.ShapeDtypeStruct((height, width...  5.74 us
    select_n x6, other arithmetic, joined(): jnp.where(second, a, b)  2.41 us
  transfers between devices with their start and end apart: 16, of which 10 were waited for; matrix products, arithmetic and copies ran while one was open for 3% of the time, Pallas kernels for 18%

profile of v3, /device:TPU:0, one launch (start us, length us, event | category | flops | bytes accessed | tf_op | source)
XLA Modules:
  0.0 120.0 jit_solution(17661037044544600200)
XLA Ops:
  0.0 3.1 %collective-permute-start = (f32[2,128]{1,0:T(2,128)}, f32[2,128]{1,0:T(2,128)S(1)}, u32[]{:S(2)}, u32[]{:S(2)}) collective-permute-start(f32[2,128]{1,0:T(2,128)} %param.5), channel_id=1, source_target_pairs={{0,8},{2,10},{4,12},{6,14},{8,0},{10,2},{12,4},{14,6},{16,24},{18,... | collective-permute-start | bytes 3080 | tf_op jit(solution)/shard_map/ppermute | solution.py:19
  3.1 1.5 %collective-permute-start.2 = (f32[2,1024]{1,0:T(2,128)}, f32[2,1024]{1,0:T(2,128)S(1)}, u32[]{:S(2)}, u32[]{:S(2)}) collective-permute-start(f32[2,1024]{1,0:T(2,128)} %param.4), channel_id=1, source_target_pairs={{0,1},{1,0},{2,3},{3,2},{4,5},{5,4},{6,7},{7,6},{8,9},{9,8},{10,11... | collective-permute-start | bytes 24584 | tf_op jit(solution)/shard_map/ppermute | solution.py:19
  4.6 0.5 collective-permute-start.3
  5.1 0.7 slice_multiply_fusion.4
  5.8 0.0 copy-start.3
  5.8 0.7 copy-done.3
  6.5 0.0 copy-start.4
  6.5 0.0 collective-permute-done
  6.5 0.7 copy-done.4
  7.2 2.6 %collective-permute-start.1 = (f32[4,128]{1,0:T(4,128)S(1)}, f32[4,128]{1,0:T(4,128)S(1)}, u32[]{:S(2)}, u32[]{:S(2)}) collective-permute-start(f32[4,128]{1,0:T(4,128)S(1)} %pad_maximum_fusion.3), channel_id=1, source_target_pairs={{0,16},{2,18},{4,20},{6,22},{8,24},{10,26},{12,28},{14,30},{16,0},... | collective-permute-start | bytes 6152 | tf_op jit(solution)/shard_map/ppermute | solution.py:19
  9.8 1.9 %collective-permute-done.1 = f32[4,128]{1,0:T(4,128)S(1)} collective-permute-done((f32[4,128]{1,0:T(4,128)S(1)}, f32[4,128]{1,0:T(4,128)S(1)}, u32[]{:S(2)}, u32[]{:S(2)}) %collective-permute-start.1) | collective-permute-done | bytes 2080 | tf_op jit(solution)/shard_map/ppermute | solution.py:19
  11.7 0.0 collective-permute-done.2
  11.8 6.2 %collective-permute-done.3 = f32[1024,128]{1,0:T(8,128)S(1)} collective-permute-done((f32[1024,128]{1,0:T(8,128)}, f32[1024,128]{1,0:T(8,128)S(1)}, u32[]{:S(2)}, u32[]{:S(2)}) %collective-permute-start.3) | collective-permute-done | bytes 524320 | tf_op jit(solution)/shard_map/ppermute | solution.py:19
  18.0 1.1 add.39
  19.1 0.3 fusion.2
  19.4 0.4 collective-permute-start.4
  19.8 6.3 %collective-permute-done.4 = f32[512,128]{1,0:T(8,128)S(1)} collective-permute-done((f32[512,128]{1,0:T(8,128)S(1)}, f32[512,128]{1,0:T(8,128)S(1)}, u32[]{:S(2)}, u32[]{:S(2)}) %collective-permute-start.4) | collective-permute-done | bytes 262176 | tf_op jit(solution)/shard_map/ppermute | solution.py:19
  26.1 0.3 broadcast_select_fusion.16
  26.4 0.0 copy-start
  26.4 0.8 multiply_add_fusion.3
  27.2 2.6 %collective-permute-start.7 = (f32[512,128]{1,0:T(8,128)S(1)}, f32[512,128]{1,0:T(8,128)S(1)}, u32[]{:S(2)}, u32[]{:S(2)}) collective-permute-start(f32[512,128]{1,0:T(8,128)S(1)} %get-tuple-element.86), channel_id=1, source_target_pairs={{0,16},{2,18},{4,20},{6,22},{8,24},{10,26},{12,28},{14,30},{16,0},... | collective-permute-start | bytes 786440 | tf_op jit(solution)/shard_map/ppermute | solution.py:19
  29.8 0.0 copy-done
  29.8 0.2 select_multiply_fusion
  30.0 0.2 add_multiply_fusion.2
  30.3 0.5 collective-permute-start.5
  30.8 8.6 %collective-permute-done.7 = f32[512,128]{1,0:T(8,128)S(1)} collective-permute-done((f32[512,128]{1,0:T(8,128)S(1)}, f32[512,128]{1,0:T(8,128)S(1)}, u32[]{:S(2)}, u32[]{:S(2)}) %collective-permute-start.7) | collective-permute-done | bytes 262176 | tf_op jit(solution)/shard_map/ppermute | solution.py:19
  39.5 1.6 %collective-permute-start.8 = (f32[512,128]{1,0:T(8,128)S(1)}, f32[512,128]{1,0:T(8,128)S(1)}, u32[]{:S(2)}, u32[]{:S(2)}) collective-permute-start(f32[512,128]{1,0:T(8,128)S(1)} %add_multiply_fusion.1), channel_id=1, source_target_pairs={{0,4},{2,6},{4,0},{6,2},{8,12},{10,14},{12,8},{14,10},{16,20},{18,... | collective-permute-start | bytes 786440 | tf_op jit(solution)/shard_map/ppermute | solution.py:19
  41.1 6.2 %collective-permute-done.8 = f32[512,128]{1,0:T(8,128)S(1)} collective-permute-done((f32[512,128]{1,0:T(8,128)S(1)}, f32[512,128]{1,0:T(8,128)S(1)}, u32[]{:S(2)}, u32[]{:S(2)}) %collective-permute-start.8) | collective-permute-done | bytes 262176 | tf_op jit(solution)/shard_map/ppermute | solution.py:19
  47.3 0.1 collective-permute-start.10
  47.4 0.5 collective-permute-start.9
  47.9 0.0 collective-permute-done.5
  47.9 0.9 multiply_add_fusion
  48.8 0.1 multiply_add_fusion.1
  49.0 0.1 collective-permute-start.6
  49.1 0.0 collective-permute-done.10
  49.1 0.2 collective-permute-done.9
  49.4 6.3 %eliminate_0.1 = (f32[4,512,128]{2,1,0:T(8,128)S(1)}, f32[4,512,128]{2,1,0:T(8,128)S(1)}, f32[512,128]{1,0:T(8,128)S(1)}) custom-call(f32[512,128]{1,0:T(8,128)S(1)} %get-tuple-element.94.refs_0_, f32[512,128]{1,0:T(8,128)S(1)} %get-tuple-element.93.refs_1_, f32[512,128]{1,0:T(8,128)S(1)} %get-tuple-element.90.refs_2_, f32[512,128]{1,0:T(8,128)S(1)} %get-tuple-element.89.refs_3_), custom_call_target="tpu_custom_call" | custom-call | flops 4000000000 | bytes 12000000 | tf_op jit(solution)/shard_map/eliminate_0/pallas_call | solution.py:254
  55.7 7.7 %collective-permute-done.6 = f32[512,128]{1,0:T(8,128)S(1)} collective-permute-done((f32[512,128]{1,0:T(8,128)S(1)}, f32[512,128]{1,0:T(8,128)S(1)}, u32[]{:S(2)}, u32[]{:S(2)}) %collective-permute-start.6) | collective-permute-done | bytes 262176 | tf_op jit(solution)/shard_map/ppermute | solution.py:19
  63.4 0.1 collective-permute-start.11
  63.5 5.8 %eliminate_1.1 = (f32[4,512,128]{2,1,0:T(8,128)S(1)}, f32[4,512,128]{2,1,0:T(8,128)S(1)}, f32[512,128]{1,0:T(8,128)S(1)}) custom-call(f32[4,512,128]{2,1,0:T(8,128)S(1)} %get-tuple-element.47.old_work, f32[4,512,128]{2,1,0:T(8,128)S(1)} %get-tuple-element.48.old_packed, ...), custom_call_target="tpu_custom_call", output_to_operand_aliasing={{0}: (0, {}), {1}: (1, {}), {2}: (2, {})} | custom-call | flops 4000000000 | bytes 12000000 | tf_op jit(solution)/shard_map/eliminate_1/pallas_call | solution.py:269
  69.3 2.4 %collective-permute-done.11 = f32[512,128]{1,0:T(8,128)S(1)} collective-permute-done((f32[512,128]{1,0:T(8,128)S(1)}, f32[512,128]{1,0:T(8,128)S(1)}, u32[]{:S(2)}, u32[]{:S(2)}) %collective-permute-start.11) | collective-permute-done | bytes 262176 | tf_op jit(solution)/shard_map/ppermute | solution.py:19
  71.8 1.6 %collective-permute-start.12 = (f32[1024,128]{1,0:T(8,128)S(1)}, f32[1024,128]{1,0:T(8,128)S(1)}, u32[]{:S(2)}, u32[]{:S(2)}) collective-permute-start(f32[1024,128]{1,0:T(8,128)S(1)} %pad_maximum_fusion.2), channel_id=1, source_target_pairs={{0,4},{2,6},{4,0},{6,2},{8,12},{10,14},{12,8},{14,10},{16,20},{18,... | collective-permute-start | bytes 1572872 | tf_op jit(solution)/shard_map/ppermute | solution.py:19
  73.4 0.9 pad_maximum_fusion
  74.3 0.5 collective-permute-start.15
  74.8 4.7 %eliminate_2.1 = (f32[4,512,128]{2,1,0:T(8,128)S(1)}, f32[4,512,128]{2,1,0:T(8,128)S(1)}, f32[512,128]{1,0:T(8,128)S(1)}) custom-call(f32[4,512,128]{2,1,0:T(8,128)S(1)} %get-tuple-element.54.old_work, f32[4,512,128]{2,1,0:T(8,128)S(1)} %get-tuple-element.55.old_packed, ...), custom_call_target="tpu_custom_call", output_to_operand_aliasing={{0}: (0, {}), {1}: (1, {}), {2}: (2, {})} | custom-call | flops 4000000000 | bytes 12000000 | tf_op jit(solution)/shard_map/eliminate_2/pallas_call | solution.py:269
  79.5 5.3 %collective-permute-done.12 = f32[1024,128]{1,0:T(8,128)S(1)} collective-permute-done((f32[1024,128]{1,0:T(8,128)S(1)}, f32[1024,128]{1,0:T(8,128)S(1)}, u32[]{:S(2)}, u32[]{:S(2)}) %collective-permute-start.12) | collective-permute-done | bytes 524320 | tf_op jit(solution)/shard_map/ppermute | solution.py:19
  84.9 0.1 broadcast_select_fusion.6
  85.0 0.1 collective-permute-start.13
  85.0 0.5 collective-permute-start.14
  85.5 0.1 pad_add_fusion.info
  85.6 0.0 copy-start.1
  85.6 0.0 copy-start.2
  85.6 4.4 %eliminate_3.1 = (f32[4,512,128]{2,1,0:T(8,128)S(1)}, f32[4,512,128]{2,1,0:T(8,128)S(1)}, f32[512,128]{1,0:T(8,128)S(1)}) custom-call(f32[4,512,128]{2,1,0:T(8,128)S(1)} %get-tuple-element.61.old_work, f32[4,512,128]{2,1,0:T(8,128)S(1)} %get-tuple-element.62.old_packed, ...), custom_call_target="tpu_custom_call", output_to_operand_aliasing={{0}: (0, {}), {1}: (1, {}), {2}: (2, {})} | custom-call | flops 4000000000 | bytes 12000000 | tf_op jit(solution)/shard_map/eliminate_3/pallas_call | solution.py:269
  90.0 20.7 %collective-permute-done.15 = f32[1536,128]{1,0:T(8,128)} collective-permute-done((f32[1536,128]{1,0:T(8,128)}, f32[1536,128]{1,0:T(8,128)}, u32[]{:S(2)}, u32[]{:S(2)}) %collective-permute-start.15) | collective-permute-done | bytes 786464 | tf_op jit(solution)/shard_map/ppermute | solution.py:19
  110.7 0.0 collective-permute-done.13
  110.7 0.0 collective-permute-done.14
  110.7 0.0 copy-done.1
  110.7 0.0 copy-done.2
  110.7 1.2 %fusion = f32[1536,128]{1,0:T(8,128)S(1)} fusion(f32[1536,128]{1,0:T(8,128)} %collective-permute-done.15, f32[1024,128]{1,0:T(8,128)S(1)} %copy-done.1, f32[512,128]{1,0:T(8,128)S(1)} %copy-done.2, f32[128]{0:T(128)S(1)} %slice_bitcast_fusion), kind=kLoop, calls=%fused_computation.2 | loop fusion | flops 589824 | bytes 2359808 | tf_op jit(solution)/shard_map/mul | solution.py:293
  112.0 1.1 broadcast_select_fusion
  113.1 1.1 broadcast_select_fusion.2
  114.3 5.7 %own_columns.1 = f32[1024,128]{1,0:T(8,128)} custom-call(s32[3]{0:T(128)S(1)} %pad_add_fusion.info, f32[4,512,128]{2,1,0:T(8,128)S(1)} %get-tuple-element.67.work, f32[4,512,128]{2,1,0:T(8,128)S(1)} %get-tuple-element.68.packed, f32[512,128]{1,0:T(8,128)S(1)} %get-tuple-element.69.inverted, f32[512,128]{1,0:T(8,128)S(1)} %slice.158.own_top, ...), custom_call_target="tpu_custom_call" | custom-call | flops 4000000000 | bytes 12000000 | tf_op jit(solution)/shard_map/own_columns/pallas_call | solution.py:302
  (24 shorter events, 0.4 us)
Async XLA Ops:
  0.0 6.5 %collective-permute-start = (f32[2,128]{1,0:T(2,128)}, f32[2,128]{1,0:T(2,128)S(1)}, u32[]{:S(2)}, u32[]{:S(2)}) collective-permute-start(f32[2,128]{1,0:T(2,128)} %param.5), channel_id=1, source_target_pairs={{0,8},{2,10},{4,12},{6,14},{8,0},{10,2},{12,4},{14,6},{16,24},{18,... | collective-permute-start | bytes 3080 | tf_op jit(solution)/shard_map/ppermute | solution.py:19
  3.1 8.7 %collective-permute-start.2 = (f32[2,1024]{1,0:T(2,128)}, f32[2,1024]{1,0:T(2,128)S(1)}, u32[]{:S(2)}, u32[]{:S(2)}) collective-permute-start(f32[2,1024]{1,0:T(2,128)} %param.4), channel_id=1, source_target_pairs={{0,1},{1,0},{2,3},{3,2},{4,5},{5,4},{6,7},{7,6},{8,9},{9,8},{10,11... | collective-permute-start | bytes 24584 | tf_op jit(solution)/shard_map/ppermute | solution.py:19
  4.6 13.4 %collective-permute-start.3 = (f32[1024,128]{1,0:T(8,128)}, f32[1024,128]{1,0:T(8,128)S(1)}, u32[]{:S(2)}, u32[]{:S(2)}) collective-permute-start(f32[1024,128]{1,0:T(8,128)} %param.3), channel_id=1, source_target_pairs={{0,1},{1,0},{2,3},{3,2},{4,5},{5,4},{6,7},{7,6},{8,9},{9,8},{10,11... | collective-permute-start | bytes 1572872 | tf_op jit(solution)/shard_map/ppermute | solution.py:19
  5.8 0.7 copy-start.3
  6.5 0.7 copy-start.4
  7.2 4.5 %collective-permute-start.1 = (f32[4,128]{1,0:T(4,128)S(1)}, f32[4,128]{1,0:T(4,128)S(1)}, u32[]{:S(2)}, u32[]{:S(2)}) collective-permute-start(f32[4,128]{1,0:T(4,128)S(1)} %pad_maximum_fusion.3), channel_id=1, source_target_pairs={{0,16},{2,18},{4,20},{6,22},{8,24},{10,26},{12,28},{14,30},{16,0},... | collective-permute-start | bytes 6152 | tf_op jit(solution)/shard_map/ppermute | solution.py:19
  19.4 6.8 %collective-permute-start.4 = (f32[512,128]{1,0:T(8,128)S(1)}, f32[512,128]{1,0:T(8,128)S(1)}, u32[]{:S(2)}, u32[]{:S(2)}) collective-permute-start(f32[512,128]{1,0:T(8,128)S(1)} %fusion.2), channel_id=1, source_target_pairs={{0,8},{2,10},{4,12},{6,14},{8,0},{10,2},{12,4},{14,6},{16,24},{18,... | collective-permute-start | bytes 786440 | tf_op jit(solution)/shard_map/ppermute | solution.py:19
  26.4 3.4 %copy-start = (f32[1024,128]{1,0:T(8,128)S(1)}, f32[1024,128]{1,0:T(8,128)}, u32[]{:S(2)}) copy-start(f32[1024,128]{1,0:T(8,128)} %param.3) | copy-start | bytes 1572868
  27.2 12.2 %collective-permute-start.7 = (f32[512,128]{1,0:T(8,128)S(1)}, f32[512,128]{1,0:T(8,128)S(1)}, u32[]{:S(2)}, u32[]{:S(2)}) collective-permute-start(f32[512,128]{1,0:T(8,128)S(1)} %get-tuple-element.86), channel_id=1, source_target_pairs={{0,16},{2,18},{4,20},{6,22},{8,24},{10,26},{12,28},{14,30},{16,0},... | collective-permute-start | bytes 786440 | tf_op jit(solution)/shard_map/ppermute | solution.py:19
  30.3 17.6 %collective-permute-start.5 = (f32[1024,128]{1,0:T(8,128)S(1)}, f32[1024,128]{1,0:T(8,128)S(1)}, u32[]{:S(2)}, u32[]{:S(2)}) collective-permute-start(f32[1024,128]{1,0:T(8,128)S(1)} %pad_maximum_fusion.1), channel_id=1, source_target_pairs={{0,8},{2,10},{4,12},{6,14},{8,0},{10,2},{12,4},{14,6},{16,24},{18,... | collective-permute-start | bytes 1572872 | tf_op jit(solution)/shard_map/ppermute | solution.py:19
  39.5 7.8 %collective-permute-start.8 = (f32[512,128]{1,0:T(8,128)S(1)}, f32[512,128]{1,0:T(8,128)S(1)}, u32[]{:S(2)}, u32[]{:S(2)}) collective-permute-start(f32[512,128]{1,0:T(8,128)S(1)} %add_multiply_fusion.1), channel_id=1, source_target_pairs={{0,4},{2,6},{4,0},{6,2},{8,12},{10,14},{12,8},{14,10},{16,20},{18,... | collective-permute-start | bytes 786440 | tf_op jit(solution)/shard_map/ppermute | solution.py:19
  47.3 1.7 %collective-permute-start.10 = (f32[512,128]{1,0:T(8,128)S(1)}, f32[512,128]{1,0:T(8,128)S(1)}, u32[]{:S(2)}, u32[]{:S(2)}) collective-permute-start(f32[512,128]{1,0:T(8,128)S(1)} %get-tuple-element.91), channel_id=1, source_target_pairs={{0,2},{2,0},{4,6},{6,4},{8,10},{10,8},{12,14},{14,12},{16,18},{18,... | collective-permute-start | bytes 786440 | tf_op jit(solution)/shard_map/ppermute | solution.py:19
  47.4 1.9 %collective-permute-start.9 = (f32[512,128]{1,0:T(8,128)S(1)}, f32[512,128]{1,0:T(8,128)S(1)}, u32[]{:S(2)}, u32[]{:S(2)}) collective-permute-start(f32[512,128]{1,0:T(8,128)S(1)} %get-tuple-element.92), channel_id=1, source_target_pairs={{0,2},{2,0},{4,6},{6,4},{8,10},{10,8},{12,14},{14,12},{16,18},{18,... | collective-permute-start | bytes 786440 | tf_op jit(solution)/shard_map/ppermute | solution.py:19
  49.0 14.4 %collective-permute-start.6 = (f32[512,128]{1,0:T(8,128)S(1)}, f32[512,128]{1,0:T(8,128)S(1)}, u32[]{:S(2)}, u32[]{:S(2)}) collective-permute-start(f32[512,128]{1,0:T(8,128)S(1)} %slice_select_fusion), channel_id=1, source_target_pairs={{0,16},{2,18},{4,20},{6,22},{8,24},{10,26},{12,28},{14,30},{16,0},... | collective-permute-start | bytes 786440 | tf_op jit(solution)/shard_map/ppermute | solution.py:19
  63.4 8.3 %collective-permute-start.11 = (f32[512,128]{1,0:T(8,128)S(1)}, f32[512,128]{1,0:T(8,128)S(1)}, u32[]{:S(2)}, u32[]{:S(2)}) collective-permute-start(f32[512,128]{1,0:T(8,128)S(1)} %add_multiply_fusion), channel_id=1, source_target_pairs={{0,8},{2,10},{4,12},{6,14},{8,0},{10,2},{12,4},{14,6},{16,24},{18,... | collective-permute-start | bytes 786440 | tf_op jit(solution)/shard_map/ppermute | solution.py:19
  71.8 13.1 %collective-permute-start.12 = (f32[1024,128]{1,0:T(8,128)S(1)}, f32[1024,128]{1,0:T(8,128)S(1)}, u32[]{:S(2)}, u32[]{:S(2)}) collective-permute-start(f32[1024,128]{1,0:T(8,128)S(1)} %pad_maximum_fusion.2), channel_id=1, source_target_pairs={{0,4},{2,6},{4,0},{6,2},{8,12},{10,14},{12,8},{14,10},{16,20},{18,... | collective-permute-start | bytes 1572872 | tf_op jit(solution)/shard_map/ppermute | solution.py:19
  74.3 36.4 %collective-permute-start.15 = (f32[1536,128]{1,0:T(8,128)}, f32[1536,128]{1,0:T(8,128)}, u32[]{:S(2)}, u32[]{:S(2)}) collective-permute-start(f32[1536,128]{1,0:T(8,128)} %pad_maximum_fusion), channel_id=1, source_target_pairs={{0,16},{2,18},{4,20},{6,22},{8,24},{10,26},{12,28},{14,30},{16,0},... | collective-permute-start | bytes 2359304 | tf_op jit(solution)/shard_map/ppermute | solution.py:19
  85.0 25.8 %collective-permute-start.13 = (f32[1024,128]{1,0:T(8,128)S(1)}, f32[1024,128]{1,0:T(8,128)}, u32[]{:S(2)}, u32[]{:S(2)}) collective-permute-start(f32[1024,128]{1,0:T(8,128)S(1)} %get-tuple-element.83), channel_id=1, source_target_pairs={{0,2},{2,0},{4,6},{6,4},{8,10},{10,8},{12,14},{14,12},{16,18},{18,... | collective-permute-start | bytes 1572872 | tf_op jit(solution)/shard_map/ppermute | solution.py:19
  85.0 25.7 %collective-permute-start.14 = (f32[1024,128]{1,0:T(8,128)S(1)}, f32[1024,128]{1,0:T(8,128)}, u32[]{:S(2)}, u32[]{:S(2)}) collective-permute-start(f32[1024,128]{1,0:T(8,128)S(1)} %get-tuple-element.82), channel_id=1, source_target_pairs={{0,2},{2,0},{4,6},{6,4},{8,10},{10,8},{12,14},{14,12},{16,18},{18,... | collective-permute-start | bytes 1572872 | tf_op jit(solution)/shard_map/ppermute | solution.py:19
  85.6 25.1 %copy-start.1 = (f32[1024,128]{1,0:T(8,128)S(1)}, f32[1024,128]{1,0:T(8,128)}, u32[]{:S(2)}) copy-start(f32[1024,128]{1,0:T(8,128)} %get-tuple-element.73) | copy-start | bytes 1572868
  85.6 25.1 %copy-start.2 = (f32[512,128]{1,0:T(8,128)S(1)}, f32[512,128]{1,0:T(8,128)}, u32[]{:S(2)}) copy-start(f32[512,128]{1,0:T(8,128)} %get-tuple-element.84) | copy-start | bytes 786436

commit v4 on v3

--- a/solution.py
+++ b/solution.py
@@ -1,4 +1,5 @@
 import functools
+
 
 import jax
 import jax.numpy as jnp
@@ -10,6 +11,7 @@
 PW = 256
 PANELS = 2
 LEAD = PW * PANELS
+SPLIT = LEAD // 2
 
 SUB = 8
 BLK = 128
@@ -118,9 +120,10 @@
     eliminate_block(k, work, packed, inverted)
 
 
-def last_kernel(info, work, packed, inverted, own_top, own, *refs):
+def last_kernel(info, work, packed, inverted, own_top, *refs):
     blocks = LEAD // BLK
-    pieces, (out, rhs, reduced, top) = refs[:blocks], refs[blocks:]
+    own, pieces = refs[:2], refs[2 : 2 + 2 * blocks]
+    out, rhs, reduced, top = refs[2 + 2 * blocks :]
     is_panel = info[0] == 1
     slot = info[1]
     is_top = info[2] == 1
@@ -141,23 +144,29 @@
         here = pl.ds(BLK * k, BLK)
         terms = [hdot(work[j, here, :], reduced[pl.ds(BLK * j, BLK), :]) for j in range(k + 1, blocks)]
         reduced[here, :] = reduced[here, :] - tree_sum(terms)
-    height = out.shape[0]
-
-    def below(first, rows):
-        where = pl.ds(first, rows)
-        terms = [hdot(pieces[j][where, :], reduced[pl.ds(BLK * j, BLK), :]) for j in range(blocks)]
+    part_rows = own[0].shape[0]
+
+    def below(part, first):
+        where = pl.ds(first, SPLIT)
+        terms = [hdot(pieces[2 * j + part][where, :], reduced[pl.ds(BLK * j, BLK), :]) for j in range(blocks)]
         total = tree_sum(terms)
-        return jnp.where(is_panel, total, own[where, :] - total)
-
-    for first in range(0, LEAD, 256):
-        out[pl.ds(first, 256), :] = jnp.where(is_top, top[pl.ds(first, 256), :], below(first, 256))
+        return jnp.where(is_panel, total, own[part][where, :] - total)
+
+    for part in range(2):
+        where = pl.ds(SPLIT * part, SPLIT)
+        out[where, :] = jnp.where(is_top, top[where, :], below(part, 0))
 
     def step(n, carry):
-        first = pl.multiple_of(LEAD + n * 256, 256)
-        out[pl.ds(first, 256), :] = below(first, 256)
+        for part in range(2):
+            first = pl.multiple_of(n * SPLIT, SPLIT)
+            out[pl.ds(pl.multiple_of(n * LEAD, LEAD) + SPLIT * part, SPLIT), :] = below(part, first)
         return carry
 
-    lax.fori_loop(0, (height - LEAD) // 256, step, 0)
+    if part_rows // SPLIT <= 2:
+        for n in range(1, part_rows // SPLIT):
+            step(n, 0)
+    else:
+        lax.fori_loop(1, part_rows // SPLIT, step, 0)
 
 
 def shards(matrix, row_diag, col_diag):
@@ -172,26 +181,24 @@
     is_first = row_pos == 0
     in_high = (col_pos & high) != 0
     in_low = (col_pos & low) != 0
-
-    partner = swapped(matrix, "row", 1)
+    part_rows = half // 2
+
+    def parts_of(values):
+        grouped = values.reshape(2, half // LEAD, 2, SPLIT, *values.shape[1:])
+        return [grouped[:, :, p].reshape(2, part_rows, *values.shape[1:]) for p in range(2)]
+
+    rows_p, rows_q = parts_of(matrix)
+    other_p = swapped(rows_p, "row", 1)
+    near_q = swapped(rows_q, "col", low)
     other_rows = swapped(row_diag, "row", 1)
     pair = jnp.concatenate([col_diag, swapped(col_diag, "col", low)], 0)
     far_pair = swapped(pair, "col", high)
 
     def diag_of(h, l):
-        near = in_high == h
-        chosen = jnp.where(near, pair, far_pair)
+        chosen = jnp.where(in_high == h, pair, far_pair)
         return jnp.where(in_low == l, chosen[:2], chosen[2:])
 
-    first_diag = jnp.where(is_first, row_diag, other_rows)
-    total = matrix + partner
-    lead_sum = [first_diag[0][a : a + LEAD, None] * total[a : a + LEAD] for a in (0, half)]
-    top_rows = (0.5 * first_diag[1][:LEAD])[:, None] * (lead_sum[0] + lead_sum[1])
     none, yes = jnp.bool_(False), jnp.bool_(True)
-
-    def halves(values):
-        other = swapped(values, "col", low)
-        return jnp.where(in_low, other, values), jnp.where(in_low, values, other)
 
     def contribution(parts, h, l):
         even, odd = parts
@@ -199,6 +206,30 @@
         scale_even = sign * diag_of(h, none)[0]
         scale_odd = jnp.where(l, -sign, sign) * diag_of(h, yes)[0]
         return scale_even * even + scale_odd * odd
+
+    first_diag = jnp.where(is_first, row_diag, other_rows)
+    own_scales = [parts_of(row_diag[level]) for level in range(2)]
+    first_scales = [parts_of(first_diag[level]) for level in range(2)]
+
+    def own_mixed(part, local, remote):
+        scale0, scale1 = own_scales[0][part][..., None], own_scales[1][part][..., None]
+        mixed = scale0 * jnp.where(is_first, local + remote, remote - local)
+        return 0.5 * scale1[0] * (mixed[0] + mixed[1]), 0.5 * scale1[1] * (mixed[0] - mixed[1])
+
+    def lead_mixed(part, values):
+        scale0 = first_scales[0][part][:, :SPLIT, None]
+        scale1 = first_scales[1][part][0, :SPLIT, None]
+        return 0.5 * scale1 * (scale0[0] * values[0][:SPLIT] + scale0[1] * values[1][:SPLIT])
+
+    even_q = jnp.where(in_low, near_q, rows_q)
+    odd_q = jnp.where(in_low, rows_q, near_q)
+    lead_own = lead_mixed(0, [rows_p[i, :SPLIT] + other_p[i, :SPLIT] for i in range(2)])
+    lead_own = (0.5 * diag_of(none, in_low)[0]) * lead_own
+    lead_near = lead_mixed(1, contribution((even_q[:, :SPLIT], odd_q[:, :SPLIT]), none, none))
+    lead_p = lead_own + swapped(lead_own, "col", low)
+    lead_q = lead_near + swapped(lead_near, "row", 1)
+    lead = jnp.concatenate([lead_p, lead_q], 0)
+    lead, rows_p, other_p, even_q, odd_q = lax.optimization_barrier((lead, rows_p, other_p, even_q, odd_q))
 
     def spread(values):
         for bit in range(block_bits, high_bit - 1):
@@ -218,33 +249,27 @@
         ]
 
     lead_scale = diag_of(none, none)[1]
-    top_parts = halves(top_rows)
-    *top_parts, local, remote = lax.optimization_barrier((*top_parts, matrix, partner))
-    lead = contribution(top_parts, none, none)
-    lead = spread(lead_scale * (lead + swapped(lead, "col", high)))
-    mixed = row_diag[0][:, None] * jnp.where(is_first, local + remote, remote - local)
-    upper_part, lower_part = mixed[:half], mixed[half:]
-    own_rows = jnp.concatenate(
-        [
-            (0.5 * row_diag[1][:half])[:, None] * (upper_part + lower_part),
-            (0.5 * row_diag[1][half:])[:, None] * (upper_part - lower_part),
-        ],
-        0,
-    )
-
-    own_parts = halves(own_rows)
-    lead_pieces = [lead]
+    far_lead = swapped(lead, "col", high)
+    lead_pieces = [spread(lead_scale * (lead + far_lead))]
     for bit in range(block_bits - 1, -1, -1):
         lead_pieces = gather(lead_pieces, bit)
 
-    panel = contribution(own_parts, none, none)
-    panel_half = jnp.where(in_low, panel[half:], panel[:half])
+    own_p = jnp.stack(own_mixed(0, rows_p, other_p))
+    near_p = swapped(own_p, "col", low)
+    even_p = jnp.where(in_low, near_p, own_p)
+    odd_p = jnp.where(in_low, own_p, near_p)
+    other_even, other_odd = swapped(even_q, "row", 1), swapped(odd_q, "row", 1)
+    even_q = jnp.stack(own_mixed(1, even_q, other_even))
+    odd_q = jnp.stack(own_mixed(1, odd_q, other_odd))
+    flat = lambda values: values.reshape(2 * part_rows, width)
+    both = [(flat(even_p), flat(odd_p)), (flat(even_q), flat(odd_q))]
+
+    mine = [jnp.where(in_low, q, p) for p, q in zip(*both)]
+    panel_half = contribution(mine, none, none)
     far_half = swapped(panel_half, "col", high)
-    sent = jnp.concatenate(
-        [contribution(top_parts, ~in_high, in_low), contribution(own_parts, ~in_high, in_low)], 0
-    )
-    kept = jnp.concatenate([contribution(top_parts, in_high, in_low), contribution(own_parts, in_high, in_low)], 0)
-    received = swapped(sent, "col", high)
+    received = [swapped(contribution(v, ~in_high, in_low), "col", high) for v in both]
+    kept = [contribution(v, in_high, in_low) for v in both]
+
     vmem = pl.BlockSpec(memory_space=pltpu.VMEM)
     cost = pl.CostEstimate(flops=4_000_000_000, bytes_accessed=12_000_000, transcendentals=0)
     size = 4 * width * (5 * blocks * LEAD + (blocks + 4) * (height + LEAD))
@@ -264,6 +289,7 @@
     panel_half = lead_scale * (panel_half + far_half)
     other_half = swapped(panel_half, "col", low)
     panel_pieces = []
+    own_top = own_parts = None
 
     for k in range(1, blocks):
         state = pl.pallas_call(
@@ -274,23 +300,33 @@
             input_output_aliases={0: 0, 1: 1, 2: 2},
             cost_estimate=cost,
             compiler_params=params,
-            name=f"eliminate_{k}",
         )(*state)
         bit = block_bits - k + 1
         arrived = [other_half] if k == 1 else [swapped(p, "col", 2**bit) for p in panel_pieces]
+        count = len(arrived)
+        if k == blocks - 2:
+            arrived += received
         if k == blocks - 1:
-            arrived.append(received)
+            arrived += [far_top]
         *arrived, state0, state1, state2 = lax.optimization_barrier((*arrived, *state))
         state = (state0, state1, state2)
+        arrived, extra = arrived[:count], arrived[count:]
+        if k == blocks - 2:
+            scale = diag_of(in_high, in_low)[1]
+            own_parts = [scale * (a + b) for a, b in zip(kept, extra)]
+            own_top = jnp.concatenate([v[:SPLIT] for v in own_parts], 0)
+            far_top = lax.ppermute(own_top, "row", [(0, 1)])
         if k == blocks - 1:
-            received = arrived.pop()
+            own_top = jnp.where(is_first, own_top, extra[0])
         if k == 1:
-            ordered = jnp.where(in_low, arrived[0], panel_half), jnp.where(in_low, panel_half, arrived[0])
-            panel_pieces = [spread(jnp.concatenate(ordered, 0))]
+            panel_pieces = [
+                spread(jnp.where(in_low, arrived[0], panel_half)),
+                spread(jnp.where(in_low, panel_half, arrived[0])),
+            ]
         else:
-            panel_pieces = joined(panel_pieces, arrived, bit)
-
-    whole = diag_of(in_high, in_low)[1] * (kept + received)
+            first = joined(panel_pieces[0::2], arrived[0::2], bit)
+            second = joined(panel_pieces[1::2], arrived[1::2], bit)
+            panel_pieces = [v for pq in zip(first, second) for v in pq]
 
     info = jnp.stack(
         [
@@ -302,16 +338,17 @@
     return pl.pallas_call(
         last_kernel,
         out_shape=jax.ShapeDtypeStruct((height, width), jnp.float32),
-        in_specs=[pl.BlockSpec(memory_space=pltpu.SMEM)] + [vmem] * (blocks + 5),
+        in_specs=[pl.BlockSpec(memory_space=pltpu.SMEM)] + [vmem] * (2 * blocks + 6),
         out_specs=vmem,
         scratch_shapes=[pltpu.VMEM((LEAD, width), jnp.float32)] * 3,
         cost_estimate=cost,
         compiler_params=params,
         name="own_columns",
-    )(info, *state, whole[:LEAD], whole[LEAD:], *panel_pieces)
+    )(info, *state, own_top, *own_parts, *panel_pieces)
 
 
 def solution(mesh):
     in_specs = (P("row", "col"), P(None, "row"), P(None, "col"))
     out_specs = P("row", "col")
+
     return jax.shard_map(shards, mesh=mesh, in_specs=in_specs, out_specs=out_specs, check_vma=False)

time: 120 us -> 110 us (0.917)
  waiting for transfers between devices: 65.6 us -> 49.2 us
  starting transfers between devices: 16.2 us -> 29.6 us
  other arithmetic: 9.48 us -> 2.2 us
    ppermute x16 -> x24, waiting for transfers between devices: 65.6 us -> 49.2 us  [swapped(): lax.ppermute(x, axis, [(i, i ^ mask) for i in range(lax.axis_size(axis))])]
    ppermute x16 -> x24, starting transfers between devices: 16.2 us -> 27 us  [swapped(): lax.ppermute(x, axis, [(i, i ^ mask) for i in range(lax.axis_size(axis))])]
    ppermute x0 -> x1, starting transfers between devices: none -> 2.65 us  [shards(): far_top = lax.ppermute(own_top, 'row', [(0, 1)])]
    select_n x6 -> x9, other arithmetic: 2.41 us -> 0.34 us  [joined(): jnp.where(second, a, b)]
    add x3 -> x2, other arithmetic: 1.82 us -> 0.2 us  [contribution(): return scale_even * even + scale_odd * odd]
    mul x7 -> x12, other arithmetic: 2.65 us -> 1.07 us  [the longest x2 0.29 us: own_mixed(): mixed = scale0 * jnp.where(is_first, local + remote, remote - local)]
  transfers between devices with their start and end apart: 16 -> 25, of which waited for: 10 -> 9; matrix products, arithmetic and copies ran while one was open for 3% -> 3% of each run, Pallas kernels for 18% -> 19%
where the time goes in v4:
time: 110 us
  waiting for transfers between devices  49.2 us (45%)
  starting transfers between devices  29.6 us (27%)
  Pallas kernels  26.7 us (24%)
  other arithmetic  2.2 us (2%)
  local copies, waits for them, and re-layouts  1.93 us (2%)
    ppermute x24, waiting for transfers between devices, swapped(): lax.ppermute(x, axis, [(i, i ^ mask) for i in range(lax.axis_size(axis))])  49.2 us
    ppermute x24, starting transfers between devices, swapped(): lax.ppermute(x, axis, [(i, i ^ mask) for i in range(lax.axis_size(axis))])  27 us
    pallas_call x3, Pallas kernels, shards(): pl.pallas_call(functools.partial(next_kernel, k), out_shape=state_shapes,...  15 us
    pallas_call x1, Pallas kernels, shards(): pl.pallas_call(first_kernel, out_shape=state_shapes, in_specs=[vmem] * bl...  6.35 us
    pallas_call x1, Pallas kernels, shards(): pl.pallas_call(last_kernel, out_shape=jax.ShapeDtypeStruct((height, width...  5.42 us
    ppermute x1, starting transfers between devices, shards(): far_top = lax.ppermute(own_top, 'row', [(0, 1)])  2.65 us
  transfers between devices with their start and end apart: 25, of which 9 were waited for; matrix products, arithmetic and copies ran while one was open for 3% of the time, Pallas kernels for 19%

profile of v4, /device:TPU:0, one launch (start us, length us, event | category | flops | bytes accessed | tf_op | source)
XLA Modules:
  0.0 110.2 jit_solution(16818056510776358887)
XLA Ops:
  0.0 3.1 %collective-permute-start = (f32[2,128]{1,0:T(2,128)}, f32[2,128]{1,0:T(2,128)S(1)}, u32[]{:S(2)}, u32[]{:S(2)}) collective-permute-start(f32[2,128]{1,0:T(2,128)} %param.5), channel_id=1, source_target_pairs={{0,8},{2,10},{4,12},{6,14},{8,0},{10,2},{12,4},{14,6},{16,24},{18,... | collective-permute-start | bytes 3080 | tf_op jit(solution)/shard_map/ppermute | solution.py:21
  3.1 1.1 %slice_bitcast_fusion.1 = (f32[2,256,128]{2,1,0:T(8,128)S(1)}, f32[2,256,128]{2,1,0:T(8,128)S(1)}) fusion(f32[2,1,2,256,128]{4,3,2,0,1:T(8,128)} %bitcast.148), kind=kLoop, calls=%fused_computation.1 | loop fusion | bytes 1048576 | tf_op jit(solution)/shard_map/reshape;squeeze | solution.py:188
  4.2 0.1 collective-permute-start.5
  4.3 1.9 %collective-permute-start.2 = (f32[2,1024]{1,0:T(2,128)S(1)}, f32[2,1024]{1,0:T(2,128)S(1)}, u32[]{:S(2)}, u32[]{:S(2)}) collective-permute-start(f32[2,1024]{1,0:T(2,128)S(1)} %copy-done.1), channel_id=1, source_target_pairs={{0,1},{1,0},{2,3},{3,2},{4,5},{5,4},{6,7},{7,6},{8,9},{9,8},{10,11... | collective-permute-start | bytes 24584 | tf_op jit(solution)/shard_map/ppermute | solution.py:21
  6.2 0.1 collective-permute-start.3
  6.4 0.0 copy-start.2
  6.4 0.7 copy-done.2
  7.2 0.1 pad_add_fusion.info
  7.2 0.0 collective-permute-done
  7.3 3.0 %collective-permute-start.1 = (f32[4,128]{1,0:T(4,128)S(1)}, f32[4,128]{1,0:T(4,128)S(1)}, u32[]{:S(2)}, u32[]{:S(2)}) collective-permute-start(f32[4,128]{1,0:T(4,128)S(1)} %pad_maximum_fusion.5), channel_id=1, source_target_pairs={{0,16},{2,18},{4,20},{6,22},{8,24},{10,26},{12,28},{14,30},{16,0},... | collective-permute-start | bytes 6152 | tf_op jit(solution)/shard_map/ppermute | solution.py:21
  10.3 1.7 %collective-permute-done.1 = f32[4,128]{1,0:T(4,128)S(1)} collective-permute-done((f32[4,128]{1,0:T(4,128)S(1)}, f32[4,128]{1,0:T(4,128)S(1)}, u32[]{:S(2)}, u32[]{:S(2)}) %collective-permute-start.1) | collective-permute-done | bytes 2080 | tf_op jit(solution)/shard_map/ppermute | solution.py:21
  12.0 0.0 collective-permute-done.2
  12.2 0.0 collective-permute-done.5
  12.2 0.1 multiply_add_fusion
  12.2 0.2 fusion.13
  12.4 1.8 %collective-permute-start.6 = (f32[256,128]{1,0:T(8,128)S(1)}, f32[256,128]{1,0:T(8,128)S(1)}, u32[]{:S(2)}, u32[]{:S(2)}) collective-permute-start(f32[256,128]{1,0:T(8,128)S(1)} %fusion.13), channel_id=1, source_target_pairs={{0,1},{1,0},{2,3},{3,2},{4,5},{5,4},{6,7},{7,6},{8,9},{9,8},{10,11... | collective-permute-start | bytes 393224 | tf_op jit(solution)/shard_map/ppermute | solution.py:21
  14.2 0.2 fusion.19
  14.4 2.5 %collective-permute-start.4 = (f32[256,128]{1,0:T(8,128)S(1)}, f32[256,128]{1,0:T(8,128)S(1)}, u32[]{:S(2)}, u32[]{:S(2)}) collective-permute-start(f32[256,128]{1,0:T(8,128)S(1)} %fusion.19), channel_id=1, source_target_pairs={{0,8},{2,10},{4,12},{6,14},{8,0},{10,2},{12,4},{14,6},{16,24},{18,... | collective-permute-start | bytes 393224 | tf_op jit(solution)/shard_map/ppermute | solution.py:21
  17.0 0.5 collective-permute-done.6
  17.5 0.2 fusion.24
  17.6 2.3 %collective-permute-done.4 = f32[256,128]{1,0:T(8,128)S(1)} collective-permute-done((f32[256,128]{1,0:T(8,128)S(1)}, f32[256,128]{1,0:T(8,128)S(1)}, u32[]{:S(2)}, u32[]{:S(2)}) %collective-permute-start.4) | collective-permute-done | bytes 131104 | tf_op jit(solution)/shard_map/ppermute | solution.py:21
  19.9 2.2 %collective-permute-start.11 = (f32[512,128]{1,0:T(8,128)S(1)}, f32[512,128]{1,0:T(8,128)S(1)}, u32[]{:S(2)}, u32[]{:S(2)}) collective-permute-start(f32[512,128]{1,0:T(8,128)S(1)} %pad_maximum_fusion), channel_id=1, source_target_pairs={{0,16},{2,18},{4,20},{6,22},{8,24},{10,26},{12,28},{14,30},{16,0},... | collective-permute-start | bytes 786440 | tf_op jit(solution)/shard_map/ppermute | solution.py:21
  22.1 0.5 collective-permute-start.7
  22.7 1.5 %collective-permute-start.9 = (f32[2,256,128]{2,1,0:T(8,128)S(1)}, f32[2,256,128]{2,1,0:T(8,128)S(1)}, u32[]{:S(2)}, u32[]{:S(2)}) collective-permute-start(f32[2,256,128]{2,1,0:T(8,128)S(1)} %get-tuple-element.48), channel_id=1, source_target_pairs={{0,1},{1,0},{2,3},{3,2},{4,5},{5,4},{6,7},{7,6},{8,9},{9,8},{10,11... | collective-permute-start | bytes 786440 | tf_op jit(solution)/shard_map/ppermute | solution.py:21
  24.2 0.1 select_multiply_fusion.1
  24.3 0.1 add_multiply_fusion.3
  24.5 1.7 %collective-permute-start.8 = (f32[2,256,128]{2,1,0:T(8,128)S(1)}, f32[2,256,128]{2,1,0:T(8,128)S(1)}, u32[]{:S(2)}, u32[]{:S(2)}) collective-permute-start(f32[2,256,128]{2,1,0:T(8,128)S(1)} %pad_maximum_fusion.2), channel_id=1, source_target_pairs={{0,8},{2,10},{4,12},{6,14},{8,0},{10,2},{12,4},{14,6},{16,24},{18,... | collective-permute-start | bytes 786440 | tf_op jit(solution)/shard_map/ppermute | solution.py:21
  26.1 6.3 %collective-permute-done.11 = f32[512,128]{1,0:T(8,128)S(1)} collective-permute-done((f32[512,128]{1,0:T(8,128)S(1)}, f32[512,128]{1,0:T(8,128)S(1)}, u32[]{:S(2)}, u32[]{:S(2)}) %collective-permute-start.11) | collective-permute-done | bytes 262176 | tf_op jit(solution)/shard_map/ppermute | solution.py:21
  32.4 1.6 %collective-permute-start.12 = (f32[512,128]{1,0:T(8,128)S(1)}, f32[512,128]{1,0:T(8,128)S(1)}, u32[]{:S(2)}, u32[]{:S(2)}) collective-permute-start(f32[512,128]{1,0:T(8,128)S(1)} %add_multiply_fusion.1), channel_id=1, source_target_pairs={{0,4},{2,6},{4,0},{6,2},{8,12},{10,14},{12,8},{14,10},{16,20},{18,... | collective-permute-start | bytes 786440 | tf_op jit(solution)/shard_map/ppermute | solution.py:21
  34.0 0.0 collective-permute-done.7
  34.0 0.2 select_multiply_fusion.2
  34.2 0.1 add_multiply_fusion.2
  34.3 0.0 collective-permute-done.8
  34.4 5.0 %collective-permute-done.12 = f32[512,128]{1,0:T(8,128)S(1)} collective-permute-done((f32[512,128]{1,0:T(8,128)S(1)}, f32[512,128]{1,0:T(8,128)S(1)}, u32[]{:S(2)}, u32[]{:S(2)}) %collective-permute-start.12) | collective-permute-done | bytes 262176 | tf_op jit(solution)/shard_map/ppermute | solution.py:21
  39.5 0.1 collective-permute-start.14
  39.6 0.5 collective-permute-start.13
  40.1 0.1 fusion.6
  40.2 0.1 collective-permute-start.10
  40.3 2.9 %collective-permute-start.18 = (f32[512,128]{1,0:T(8,128)S(1)}, f32[512,128]{1,0:T(8,128)S(1)}, u32[]{:S(2)}, u32[]{:S(2)}) collective-permute-start(f32[512,128]{1,0:T(8,128)S(1)} %get-tuple-element.106), channel_id=1, source_target_pairs={{0,16},{2,18},{4,20},{6,22},{8,24},{10,26},{12,28},{14,30},{16,0},... | collective-permute-start | bytes 786440 | tf_op jit(solution)/shard_map/ppermute | solution.py:21
  43.2 0.1 collective-permute-start.19
  43.3 0.0 collective-permute-done.14
  43.4 6.4 %eliminate_0.1 = (f32[4,512,128]{2,1,0:T(8,128)S(1)}, f32[4,512,128]{2,1,0:T(8,128)S(1)}, f32[512,128]{1,0:T(8,128)S(1)}) custom-call(f32[512,128]{1,0:T(8,128)S(1)} %get-tuple-element.114.refs_0_, f32[512,128]{1,0:T(8,128)S(1)} %get-tuple-element.113.refs_1_, f32[512,128]{1,0:T(8,128)S(1)} %get-tuple-element.110.refs_2_, ...), custom_call_target="tpu_custom_call" | custom-call | flops 4000000000 | bytes 12000000 | tf_op jit(solution)/shard_map/eliminate_0/pallas_call | solution.py:279
  49.7 15.5 %collective-permute-done.10 = f32[512,128]{1,0:T(8,128)S(1)} collective-permute-done((f32[512,128]{1,0:T(8,128)S(1)}, f32[512,128]{1,0:T(8,128)S(1)}, u32[]{:S(2)}, u32[]{:S(2)}) %collective-permute-start.10) | collective-permute-done | bytes 262176 | tf_op jit(solution)/shard_map/ppermute | solution.py:21
  65.3 0.1 collective-permute-start.15
  65.3 5.8 %shard_map.37 = (f32[4,512,128]{2,1,0:T(8,128)S(1)}, f32[4,512,128]{2,1,0:T(8,128)S(1)}, f32[512,128]{1,0:T(8,128)S(1)}) custom-call(f32[4,512,128]{2,1,0:T(8,128)S(1)} %get-tuple-element.54.old_work, f32[4,512,128]{2,1,0:T(8,128)S(1)} %get-tuple-element.55.old_packed, ...), custom_call_target="tpu_custom_call", output_to_operand_aliasing={{0}: (0, {}), {1}: (1, {}), {2}: (2, {})} | custom-call | flops 4000000000 | bytes 12000000 | tf_op jit(solution)/shard_map/pallas_call | solution.py:295
  71.2 10.8 %collective-permute-done.15 = f32[512,128]{1,0:T(8,128)S(1)} collective-permute-done((f32[512,128]{1,0:T(8,128)S(1)}, f32[512,128]{1,0:T(8,128)S(1)}, u32[]{:S(2)}, u32[]{:S(2)}) %collective-permute-start.15) | collective-permute-done | bytes 262176 | tf_op jit(solution)/shard_map/ppermute | solution.py:21
  82.0 0.1 broadcast_select_fusion.18
  82.1 1.6 %collective-permute-start.16 = (f32[512,128]{1,0:T(8,128)S(1)}, f32[512,128]{1,0:T(8,128)S(1)}, u32[]{:S(2)}, u32[]{:S(2)}) collective-permute-start(f32[512,128]{1,0:T(8,128)S(1)} %get-tuple-element.108), channel_id=1, source_target_pairs={{0,4},{2,6},{4,0},{6,2},{8,12},{10,14},{12,8},{14,10},{16,20},{18,... | collective-permute-start | bytes 786440 | tf_op jit(solution)/shard_map/ppermute | solution.py:21
  83.6 0.5 collective-permute-start.17
  84.2 4.7 %shard_map.38 = (f32[4,512,128]{2,1,0:T(8,128)S(1)}, f32[4,512,128]{2,1,0:T(8,128)S(1)}, f32[512,128]{1,0:T(8,128)S(1)}) custom-call(f32[4,512,128]{2,1,0:T(8,128)S(1)} %get-tuple-element.61.old_work, f32[4,512,128]{2,1,0:T(8,128)S(1)} %get-tuple-element.62.old_packed, ...), custom_call_target="tpu_custom_call", output_to_operand_aliasing={{0}: (0, {}), {1}: (1, {}), {2}: (2, {})} | custom-call | flops 4000000000 | bytes 12000000 | tf_op jit(solution)/shard_map/pallas_call | solution.py:295
  88.9 0.0 collective-permute-done.18
  88.9 2.4 %collective-permute-done.16 = f32[512,128]{1,0:T(8,128)S(1)} collective-permute-done((f32[512,128]{1,0:T(8,128)S(1)}, f32[512,128]{1,0:T(8,128)S(1)}, u32[]{:S(2)}, u32[]{:S(2)}) %collective-permute-start.16) | collective-permute-done | bytes 262176 | tf_op jit(solution)/shard_map/ppermute | solution.py:21
  91.3 4.7 %collective-permute-done.17 = f32[512,128]{1,0:T(8,128)S(1)} collective-permute-done((f32[512,128]{1,0:T(8,128)S(1)}, f32[512,128]{1,0:T(8,128)S(1)}, u32[]{:S(2)}, u32[]{:S(2)}) %collective-permute-start.17) | collective-permute-done | bytes 262176 | tf_op jit(solution)/shard_map/ppermute | solution.py:21
  96.0 0.1 fusion.5
  96.2 2.6 %collective-permute-start.24 = (f32[512,128]{1,0:T(8,128)S(1)}, f32[512,128]{1,0:T(8,128)S(1)}, u32[]{:S(2)}, u32[]{:S(2)}) collective-permute-start(f32[512,128]{1,0:T(8,128)S(1)} %pad_maximum_fusion.4), channel_id=1, source_target_pairs={{0,1},{2,3},{4,5},{6,7},{8,9},{10,11},{12,13},{14,15},{16,17},{18,... | collective-permute-start | bytes 786440 | tf_op jit(solution)/shard_map/ppermute | solution.py:318
  98.9 0.1 collective-permute-start.21
  98.9 0.5 collective-permute-start.23
  99.5 0.1 collective-permute-start.20
  99.6 0.4 collective-permute-start.22
  100.0 4.4 %shard_map.39 = (f32[4,512,128]{2,1,0:T(8,128)S(1)}, f32[4,512,128]{2,1,0:T(8,128)S(1)}, f32[512,128]{1,0:T(8,128)S(1)}) custom-call(f32[4,512,128]{2,1,0:T(8,128)S(1)} %get-tuple-element.71.old_work, f32[4,512,128]{2,1,0:T(8,128)S(1)} %get-tuple-element.72.old_packed, ...), custom_call_target="tpu_custom_call", output_to_operand_aliasing={{0}: (0, {}), {1}: (1, {}), {2}: (2, {})} | custom-call | flops 4000000000 | bytes 12000000 | tf_op jit(solution)/shard_map/pallas_call | solution.py:295
  104.5 0.0 collective-permute-done.24
  104.5 0.0 collective-permute-done.23
  104.5 0.0 collective-permute-done.20
  104.8 5.4 %own_columns.1 = f32[1024,128]{1,0:T(8,128)} custom-call(s32[3]{0:T(128)S(1)} %pad_add_fusion.info, f32[4,512,128]{2,1,0:T(8,128)S(1)} %get-tuple-element.77.work, f32[4,512,128]{2,1,0:T(8,128)S(1)} %get-tuple-element.78.packed, f32[512,128]{1,0:T(8,128)S(1)} %get-tuple-element.79.inverted, f32[512,128]{1,0:T(8,128)S(1)} %broadcast_select_fusion.own_top, ...), custom_call_target="tpu_custom_call" | custom-call | flops 4000000000 | bytes 12000000 | tf_op jit(solution)/shard_map/own_columns/pallas_call | solution.py:338
  (56 shorter events, 0.8 us)
Async XLA Ops:
  0.0 7.2 %collective-permute-start = (f32[2,128]{1,0:T(2,128)}, f32[2,128]{1,0:T(2,128)S(1)}, u32[]{:S(2)}, u32[]{:S(2)}) collective-permute-start(f32[2,128]{1,0:T(2,128)} %param.5), channel_id=1, source_target_pairs={{0,8},{2,10},{4,12},{6,14},{8,0},{10,2},{12,4},{14,6},{16,24},{18,... | collective-permute-start | bytes 3080 | tf_op jit(solution)/shard_map/ppermute | solution.py:21
  3.1 1.2 %copy-start.1 = (f32[2,1024]{1,0:T(2,128)S(1)}, f32[2,1024]{1,0:T(2,128)}, u32[]{:S(2)}) copy-start(f32[2,1024]{1,0:T(2,128)} %param.4) | copy-start | bytes 24580
  3.1 9.1 %copy-start = (f32[1024,128]{1,0:T(8,128)S(1)}, f32[1024,128]{1,0:T(8,128)}, u32[]{:S(2)}) copy-start(f32[1024,128]{1,0:T(8,128)} %param.3) | copy-start | bytes 1572868
  4.2 8.0 %collective-permute-start.5 = (f32[2,256,128]{2,1,0:T(8,128)S(1)}, f32[2,256,128]{2,1,0:T(8,128)S(1)}, u32[]{:S(2)}, u32[]{:S(2)}) collective-permute-start(f32[2,256,128]{2,1,0:T(8,128)S(1)} %get-tuple-element.118), channel_id=1, source_target_pairs={{0,8},{2,10},{4,12},{6,14},{8,0},{10,2},{12,4},{14,6},{16,24},{18,... | collective-permute-start | bytes 786440 | tf_op jit(solution)/shard_map/ppermute | solution.py:21
  4.3 7.8 %collective-permute-start.2 = (f32[2,1024]{1,0:T(2,128)S(1)}, f32[2,1024]{1,0:T(2,128)S(1)}, u32[]{:S(2)}, u32[]{:S(2)}) collective-permute-start(f32[2,1024]{1,0:T(2,128)S(1)} %copy-done.1), channel_id=1, source_target_pairs={{0,1},{1,0},{2,3},{3,2},{4,5},{5,4},{6,7},{7,6},{8,9},{9,8},{10,11... | collective-permute-start | bytes 24584 | tf_op jit(solution)/shard_map/ppermute | solution.py:21
  6.2 8.0 %collective-permute-start.3 = (f32[2,256,128]{2,1,0:T(8,128)S(1)}, f32[2,256,128]{2,1,0:T(8,128)S(1)}, u32[]{:S(2)}, u32[]{:S(2)}) collective-permute-start(f32[2,256,128]{2,1,0:T(8,128)S(1)} %get-tuple-element.46), channel_id=1, source_target_pairs={{0,1},{1,0},{2,3},{3,2},{4,5},{5,4},{6,7},{7,6},{8,9},{9,8},{10,11... | collective-permute-start | bytes 786440 | tf_op jit(solution)/shard_map/ppermute | solution.py:21
  6.4 0.7 copy-start.2
  7.3 4.7 %collective-permute-start.1 = (f32[4,128]{1,0:T(4,128)S(1)}, f32[4,128]{1,0:T(4,128)S(1)}, u32[]{:S(2)}, u32[]{:S(2)}) collective-permute-start(f32[4,128]{1,0:T(4,128)S(1)} %pad_maximum_fusion.5), channel_id=1, source_target_pairs={{0,16},{2,18},{4,20},{6,22},{8,24},{10,26},{12,28},{14,30},{16,0},... | collective-permute-start | bytes 6152 | tf_op jit(solution)/shard_map/ppermute | solution.py:21
  12.4 5.0 %collective-permute-start.6 = (f32[256,128]{1,0:T(8,128)S(1)}, f32[256,128]{1,0:T(8,128)S(1)}, u32[]{:S(2)}, u32[]{:S(2)}) collective-permute-start(f32[256,128]{1,0:T(8,128)S(1)} %fusion.13), channel_id=1, source_target_pairs={{0,1},{1,0},{2,3},{3,2},{4,5},{5,4},{6,7},{7,6},{8,9},{9,8},{10,11... | collective-permute-start | bytes 393224 | tf_op jit(solution)/shard_map/ppermute | solution.py:21
  14.4 5.5 %collective-permute-start.4 = (f32[256,128]{1,0:T(8,128)S(1)}, f32[256,128]{1,0:T(8,128)S(1)}, u32[]{:S(2)}, u32[]{:S(2)}) collective-permute-start(f32[256,128]{1,0:T(8,128)S(1)} %fusion.19), channel_id=1, source_target_pairs={{0,8},{2,10},{4,12},{6,14},{8,0},{10,2},{12,4},{14,6},{16,24},{18,... | collective-permute-start | bytes 393224 | tf_op jit(solution)/shard_map/ppermute | solution.py:21
  19.9 12.4 %collective-permute-start.11 = (f32[512,128]{1,0:T(8,128)S(1)}, f32[512,128]{1,0:T(8,128)S(1)}, u32[]{:S(2)}, u32[]{:S(2)}) collective-permute-start(f32[512,128]{1,0:T(8,128)S(1)} %pad_maximum_fusion), channel_id=1, source_target_pairs={{0,16},{2,18},{4,20},{6,22},{8,24},{10,26},{12,28},{14,30},{16,0},... | collective-permute-start | bytes 786440 | tf_op jit(solution)/shard_map/ppermute | solution.py:21
  22.1 11.8 %collective-permute-start.7 = (f32[2,256,128]{2,1,0:T(8,128)S(1)}, f32[2,256,128]{2,1,0:T(8,128)S(1)}, u32[]{:S(2)}, u32[]{:S(2)}) collective-permute-start(f32[2,256,128]{2,1,0:T(8,128)S(1)} %get-tuple-element.45), channel_id=1, source_target_pairs={{0,1},{1,0},{2,3},{3,2},{4,5},{5,4},{6,7},{7,6},{8,9},{9,8},{10,11... | collective-permute-start | bytes 786440 | tf_op jit(solution)/shard_map/ppermute | solution.py:21
  22.7 11.3 %collective-permute-start.9 = (f32[2,256,128]{2,1,0:T(8,128)S(1)}, f32[2,256,128]{2,1,0:T(8,128)S(1)}, u32[]{:S(2)}, u32[]{:S(2)}) collective-permute-start(f32[2,256,128]{2,1,0:T(8,128)S(1)} %get-tuple-element.48), channel_id=1, source_target_pairs={{0,1},{1,0},{2,3},{3,2},{4,5},{5,4},{6,7},{7,6},{8,9},{9,8},{10,11... | collective-permute-start | bytes 786440 | tf_op jit(solution)/shard_map/ppermute | solution.py:21
  24.5 9.9 %collective-permute-start.8 = (f32[2,256,128]{2,1,0:T(8,128)S(1)}, f32[2,256,128]{2,1,0:T(8,128)S(1)}, u32[]{:S(2)}, u32[]{:S(2)}) collective-permute-start(f32[2,256,128]{2,1,0:T(8,128)S(1)} %pad_maximum_fusion.2), channel_id=1, source_target_pairs={{0,8},{2,10},{4,12},{6,14},{8,0},{10,2},{12,4},{14,6},{16,24},{18,... | collective-permute-start | bytes 786440 | tf_op jit(solution)/shard_map/ppermute | solution.py:21
  32.4 7.0 %collective-permute-start.12 = (f32[512,128]{1,0:T(8,128)S(1)}, f32[512,128]{1,0:T(8,128)S(1)}, u32[]{:S(2)}, u32[]{:S(2)}) collective-permute-start(f32[512,128]{1,0:T(8,128)S(1)} %add_multiply_fusion.1), channel_id=1, source_target_pairs={{0,4},{2,6},{4,0},{6,2},{8,12},{10,14},{12,8},{14,10},{16,20},{18,... | collective-permute-start | bytes 786440 | tf_op jit(solution)/shard_map/ppermute | solution.py:21
  39.5 3.8 %collective-permute-start.14 = (f32[512,128]{1,0:T(8,128)S(1)}, f32[512,128]{1,0:T(8,128)S(1)}, u32[]{:S(2)}, u32[]{:S(2)}) collective-permute-start(f32[512,128]{1,0:T(8,128)S(1)} %get-tuple-element.111), channel_id=1, source_target_pairs={{0,2},{2,0},{4,6},{6,4},{8,10},{10,8},{12,14},{14,12},{16,18},{18,... | collective-permute-start | bytes 786440 | tf_op jit(solution)/shard_map/ppermute | solution.py:21
  39.6 3.8 %collective-permute-start.13 = (f32[512,128]{1,0:T(8,128)S(1)}, f32[512,128]{1,0:T(8,128)S(1)}, u32[]{:S(2)}, u32[]{:S(2)}) collective-permute-start(f32[512,128]{1,0:T(8,128)S(1)} %get-tuple-element.112), channel_id=1, source_target_pairs={{0,2},{2,0},{4,6},{6,4},{8,10},{10,8},{12,14},{14,12},{16,18},{18,... | collective-permute-start | bytes 786440 | tf_op jit(solution)/shard_map/ppermute | solution.py:21
  40.2 25.0 %collective-permute-start.10 = (f32[512,128]{1,0:T(8,128)S(1)}, f32[512,128]{1,0:T(8,128)S(1)}, u32[]{:S(2)}, u32[]{:S(2)}) collective-permute-start(f32[512,128]{1,0:T(8,128)S(1)} %get-tuple-element.105), channel_id=1, source_target_pairs={{0,16},{2,18},{4,20},{6,22},{8,24},{10,26},{12,28},{14,30},{16,0},... | collective-permute-start | bytes 786440 | tf_op jit(solution)/shard_map/ppermute | solution.py:21
  40.3 48.6 %collective-permute-start.18 = (f32[512,128]{1,0:T(8,128)S(1)}, f32[512,128]{1,0:T(8,128)S(1)}, u32[]{:S(2)}, u32[]{:S(2)}) collective-permute-start(f32[512,128]{1,0:T(8,128)S(1)} %get-tuple-element.106), channel_id=1, source_target_pairs={{0,16},{2,18},{4,20},{6,22},{8,24},{10,26},{12,28},{14,30},{16,0},... | collective-permute-start | bytes 786440 | tf_op jit(solution)/shard_map/ppermute | solution.py:21
  43.2 45.7 %collective-permute-start.19 = (f32[512,128]{1,0:T(8,128)S(1)}, f32[512,128]{1,0:T(8,128)S(1)}, u32[]{:S(2)}, u32[]{:S(2)}) collective-permute-start(f32[512,128]{1,0:T(8,128)S(1)} %get-tuple-element.104), channel_id=1, source_target_pairs={{0,16},{2,18},{4,20},{6,22},{8,24},{10,26},{12,28},{14,30},{16,0},... | collective-permute-start | bytes 786440 | tf_op jit(solution)/shard_map/ppermute | solution.py:21
  65.3 16.7 %collective-permute-start.15 = (f32[512,128]{1,0:T(8,128)S(1)}, f32[512,128]{1,0:T(8,128)S(1)}, u32[]{:S(2)}, u32[]{:S(2)}) collective-permute-start(f32[512,128]{1,0:T(8,128)S(1)} %add_multiply_fusion), channel_id=1, source_target_pairs={{0,8},{2,10},{4,12},{6,14},{8,0},{10,2},{12,4},{14,6},{16,24},{18,... | collective-permute-start | bytes 786440 | tf_op jit(solution)/shard_map/ppermute | solution.py:21
  82.1 9.2 %collective-permute-start.16 = (f32[512,128]{1,0:T(8,128)S(1)}, f32[512,128]{1,0:T(8,128)S(1)}, u32[]{:S(2)}, u32[]{:S(2)}) collective-permute-start(f32[512,128]{1,0:T(8,128)S(1)} %get-tuple-element.108), channel_id=1, source_target_pairs={{0,4},{2,6},{4,0},{6,2},{8,12},{10,14},{12,8},{14,10},{16,20},{18,... | collective-permute-start | bytes 786440 | tf_op jit(solution)/shard_map/ppermute | solution.py:21
  83.6 12.4 %collective-permute-start.17 = (f32[512,128]{1,0:T(8,128)S(1)}, f32[512,128]{1,0:T(8,128)S(1)}, u32[]{:S(2)}, u32[]{:S(2)}) collective-permute-start(f32[512,128]{1,0:T(8,128)S(1)} %get-tuple-element.107), channel_id=1, source_target_pairs={{0,4},{2,6},{4,0},{6,2},{8,12},{10,14},{12,8},{14,10},{16,20},{18,... | collective-permute-start | bytes 786440 | tf_op jit(solution)/shard_map/ppermute | solution.py:21
  96.2 8.3 %collective-permute-start.24 = (f32[512,128]{1,0:T(8,128)S(1)}, f32[512,128]{1,0:T(8,128)S(1)}, u32[]{:S(2)}, u32[]{:S(2)}) collective-permute-start(f32[512,128]{1,0:T(8,128)S(1)} %pad_maximum_fusion.4), channel_id=1, source_target_pairs={{0,1},{2,3},{4,5},{6,7},{8,9},{10,11},{12,13},{14,15},{16,17},{18,... | collective-permute-start | bytes 786440 | tf_op jit(solution)/shard_map/ppermute | solution.py:318
  98.9 5.6 %collective-permute-start.21 = (f32[512,128]{1,0:T(8,128)S(1)}, f32[512,128]{1,0:T(8,128)S(1)}, u32[]{:S(2)}, u32[]{:S(2)}) collective-permute-start(f32[512,128]{1,0:T(8,128)S(1)} %get-tuple-element.101), channel_id=1, source_target_pairs={{0,2},{2,0},{4,6},{6,4},{8,10},{10,8},{12,14},{14,12},{16,18},{18,... | collective-permute-start | bytes 786440 | tf_op jit(solution)/shard_map/ppermute | solution.py:21
  98.9 5.6 %collective-permute-start.23 = (f32[512,128]{1,0:T(8,128)S(1)}, f32[512,128]{1,0:T(8,128)S(1)}, u32[]{:S(2)}, u32[]{:S(2)}) collective-permute-start(f32[512,128]{1,0:T(8,128)S(1)} %get-tuple-element.100), channel_id=1, source_target_pairs={{0,2},{2,0},{4,6},{6,4},{8,10},{10,8},{12,14},{14,12},{16,18},{18,... | collective-permute-start | bytes 786440 | tf_op jit(solution)/shard_map/ppermute | solution.py:21
  99.5 5.0 %collective-permute-start.20 = (f32[512,128]{1,0:T(8,128)S(1)}, f32[512,128]{1,0:T(8,128)S(1)}, u32[]{:S(2)}, u32[]{:S(2)}) collective-permute-start(f32[512,128]{1,0:T(8,128)S(1)} %get-tuple-element.103), channel_id=1, source_target_pairs={{0,2},{2,0},{4,6},{6,4},{8,10},{10,8},{12,14},{14,12},{16,18},{18,... | collective-permute-start | bytes 786440 | tf_op jit(solution)/shard_map/ppermute | solution.py:21
  99.6 4.9 %collective-permute-start.22 = (f32[512,128]{1,0:T(8,128)S(1)}, f32[512,128]{1,0:T(8,128)S(1)}, u32[]{:S(2)}, u32[]{:S(2)}) collective-permute-start(f32[512,128]{1,0:T(8,128)S(1)} %get-tuple-element.102), channel_id=1, source_target_pairs={{0,2},{2,0},{4,6},{6,4},{8,10},{10,8},{12,14},{14,12},{16,18},{18,... | collective-permute-start | bytes 786440 | tf_op jit(solution)/shard_map/ppermute | solution.py:21

commit v5 on v4

--- a/solution.py
+++ b/solution.py
@@ -144,29 +144,32 @@
         here = pl.ds(BLK * k, BLK)
         terms = [hdot(work[j, here, :], reduced[pl.ds(BLK * j, BLK), :]) for j in range(k + 1, blocks)]
         reduced[here, :] = reduced[here, :] - tree_sum(terms)
-    part_rows = own[0].shape[0]
-
-    def below(part, first):
-        where = pl.ds(first, SPLIT)
+    quarter_runs = own[0].shape[1] // SPLIT
+
+    def below(part, run, quarter, inner):
+        where = pl.ds(pl.multiple_of(run * SPLIT, SPLIT), SPLIT)
+        local = pl.ds(pl.multiple_of(inner * SPLIT, SPLIT), SPLIT)
         terms = [hdot(pieces[2 * j + part][where, :], reduced[pl.ds(BLK * j, BLK), :]) for j in range(blocks)]
         total = tree_sum(terms)
-        return jnp.where(is_panel, total, own[part][where, :] - total)
+        return jnp.where(is_panel, total, own[quarter][part, local, :] - total)
 
     for part in range(2):
         where = pl.ds(SPLIT * part, SPLIT)
-        out[where, :] = jnp.where(is_top, top[where, :], below(part, 0))
-
-    def step(n, carry):
+        out[where, :] = jnp.where(is_top, top[where, :], below(part, 0, 0, 0))
+
+    def step(quarter, inner):
+        run = quarter * quarter_runs + inner
         for part in range(2):
-            first = pl.multiple_of(n * SPLIT, SPLIT)
-            out[pl.ds(pl.multiple_of(n * LEAD, LEAD) + SPLIT * part, SPLIT), :] = below(part, first)
-        return carry
-
-    if part_rows // SPLIT <= 2:
-        for n in range(1, part_rows // SPLIT):
-            step(n, 0)
-    else:
-        lax.fori_loop(1, part_rows // SPLIT, step, 0)
+            rows = pl.ds(pl.multiple_of(run * LEAD, LEAD) + SPLIT * part, SPLIT)
+            out[rows, :] = below(part, run, quarter, inner)
+
+    for quarter in range(2):
+        start = 1 - quarter
+        if quarter_runs - start <= 2:
+            for inner in range(start, quarter_runs):
+                step(quarter, inner)
+        else:
+            pl.loop(start, quarter_runs)(functools.partial(step, quarter))
 
 
 def shards(matrix, row_diag, col_diag):
@@ -229,7 +232,6 @@
     lead_p = lead_own + swapped(lead_own, "col", low)
     lead_q = lead_near + swapped(lead_near, "row", 1)
     lead = jnp.concatenate([lead_p, lead_q], 0)
-    lead, rows_p, other_p, even_q, odd_q = lax.optimization_barrier((lead, rows_p, other_p, even_q, odd_q))
 
     def spread(values):
         for bit in range(block_bits, high_bit - 1):
@@ -267,8 +269,16 @@
     mine = [jnp.where(in_low, q, p) for p, q in zip(*both)]
     panel_half = contribution(mine, none, none)
     far_half = swapped(panel_half, "col", high)
-    received = [swapped(contribution(v, ~in_high, in_low), "col", high) for v in both]
-    kept = [contribution(v, in_high, in_low) for v in both]
+    both, far_half, *lead_pieces = lax.optimization_barrier((both, far_half, *lead_pieces))
+    panel_half = lead_scale * (panel_half + far_half)
+    other_half = swapped(panel_half, "col", low)
+
+    def quarter(values, n):
+        return jnp.stack([v[n * part_rows : (n + 1) * part_rows] for v in values])
+
+    sent = [quarter([contribution(v, ~in_high, in_low) for v in both], n) for n in range(2)]
+    kept = [quarter([contribution(v, in_high, in_low) for v in both], n) for n in range(2)]
+    received_lead = swapped(sent[0], "col", high)
 
     vmem = pl.BlockSpec(memory_space=pltpu.VMEM)
     cost = pl.CostEstimate(flops=4_000_000_000, bytes_accessed=12_000_000, transcendentals=0)
@@ -285,13 +295,20 @@
         compiler_params=params,
         name="eliminate_0",
     )(*lead_pieces)
-    far_half, *state = lax.optimization_barrier((far_half, *state))
-    panel_half = lead_scale * (panel_half + far_half)
-    other_half = swapped(panel_half, "col", low)
-    panel_pieces = []
-    own_top = own_parts = None
+    other_half, rest, *state = lax.optimization_barrier((other_half, sent[1], *state))
+    panel_pieces = [
+        spread(jnp.where(in_low, other_half, panel_half)),
+        spread(jnp.where(in_low, panel_half, other_half)),
+    ]
+    received_rest = swapped(rest, "col", high)
+    scale = diag_of(in_high, in_low)[1]
+    own_lead = own_rest = own_top = None
 
     for k in range(1, blocks):
+        arrived = []
+        bit = block_bits - k
+        if bit >= 0:
+            arrived = [swapped(p, "col", 2**bit) for p in panel_pieces]
         state = pl.pallas_call(
             functools.partial(next_kernel, k),
             out_shape=state_shapes,
@@ -301,29 +318,23 @@
             cost_estimate=cost,
             compiler_params=params,
         )(*state)
-        bit = block_bits - k + 1
-        arrived = [other_half] if k == 1 else [swapped(p, "col", 2**bit) for p in panel_pieces]
-        count = len(arrived)
-        if k == blocks - 2:
-            arrived += received
-        if k == blocks - 1:
-            arrived += [far_top]
-        *arrived, state0, state1, state2 = lax.optimization_barrier((*arrived, *state))
+        if k == 1:
+            *arrived, received_lead, state0, state1, state2 = lax.optimization_barrier(
+                (*arrived, received_lead, *state)
+            )
+            own_lead = scale * (kept[0] + received_lead)
+            own_top = own_lead[:, :SPLIT].reshape(LEAD, width)
+            far_top = lax.ppermute(own_top, "row", [(0, 1)])
+        elif k == blocks - 1:
+            *arrived, far_top, received_rest, state0, state1, state2 = lax.optimization_barrier(
+                (*arrived, far_top, received_rest, *state)
+            )
+            own_rest = scale * (kept[1] + received_rest)
+            own_top = jnp.where(is_first, own_top, far_top)
+        else:
+            *arrived, state0, state1, state2 = lax.optimization_barrier((*arrived, *state))
         state = (state0, state1, state2)
-        arrived, extra = arrived[:count], arrived[count:]
-        if k == blocks - 2:
-            scale = diag_of(in_high, in_low)[1]
-            own_parts = [scale * (a + b) for a, b in zip(kept, extra)]
-            own_top = jnp.concatenate([v[:SPLIT] for v in own_parts], 0)
-            far_top = lax.ppermute(own_top, "row", [(0, 1)])
-        if k == blocks - 1:
-            own_top = jnp.where(is_first, own_top, extra[0])
-        if k == 1:
-            panel_pieces = [
-                spread(jnp.where(in_low, arrived[0], panel_half)),
-                spread(jnp.where(in_low, panel_half, arrived[0])),
-            ]
-        else:
+        if bit >= 0:
             first = joined(panel_pieces[0::2], arrived[0::2], bit)
             second = joined(panel_pieces[1::2], arrived[1::2], bit)
             panel_pieces = [v for pq in zip(first, second) for v in pq]
@@ -344,7 +355,7 @@
         cost_estimate=cost,
         compiler_params=params,
         name="own_columns",
-    )(info, *state, own_top, *own_parts, *panel_pieces)
+    )(info, *state, own_top, own_lead, own_rest, *panel_pieces)
 
 
 def solution(mesh):

time: 110 us -> 103 us (0.936)
  starting transfers between devices: 29.6 us -> 25.2 us
  waiting for transfers between devices: 49.2 us -> 45.8 us
    ppermute x24, starting transfers between devices: 27 us -> 22 us  [swapped(): lax.ppermute(x, axis, [(i, i ^ mask) for i in range(lax.axis_size(axis))])]
    ppermute x24, waiting for transfers between devices: 49.2 us -> 44.9 us  [swapped(): lax.ppermute(x, axis, [(i, i ^ mask) for i in range(lax.axis_size(axis))])]
  transfers between devices with their start and end apart: 25 -> 25, of which waited for: 9 -> 15; matrix products, arithmetic and copies ran while one was open for 3% -> 3% of each run, Pallas kernels for 19% -> 21%
where the time goes in v5:
time: 103 us; the launch traced here: 102 us
  waiting for transfers between devices  45.8 us (44%)
  Pallas kernels  26.8 us (26%)
  starting transfers between devices  25.2 us (24%)
  other arithmetic  2.17 us (2%)
  local copies, waits for them, and re-layouts  1.99 us (2%)
    ppermute x24, waiting for transfers between devices, swapped(): lax.ppermute(x, axis, [(i, i ^ mask) for i in range(lax.axis_size(axis))])  44.9 us
    ppermute x24, starting transfers between devices, swapped(): lax.ppermute(x, axis, [(i, i ^ mask) for i in range(lax.axis_size(axis))])  22 us
    pallas_call x3, Pallas kernels, shards(): pl.pallas_call(functools.partial(next_kernel, k), out_shape=state_shapes,...  15 us
    pallas_call x1, Pallas kernels, shards(): pl.pallas_call(first_kernel, out_shape=state_shapes, in_specs=[vmem] * bl...  6.35 us
    pallas_call x1, Pallas kernels, shards(): pl.pallas_call(last_kernel, out_shape=jax.ShapeDtypeStruct((height, width...  5.42 us
    ppermute x1, starting transfers between devices, shards(): far_top = lax.ppermute(own_top, 'row', [(0, 1)])  3.13 us
  transfers between devices with their start and end apart: 25, of which 15 were waited for; matrix products, arithmetic and copies ran while one was open for 3% of the time, Pallas kernels for 21%

profile of v5, /device:TPU:0, one launch (start us, length us, event | category | flops | bytes accessed | tf_op | source)
XLA Modules:
  0.0 102.4 jit_solution(12385993739699936129)
XLA Ops:
  0.0 3.1 %collective-permute-start = (f32[2,128]{1,0:T(2,128)}, f32[2,128]{1,0:T(2,128)S(1)}, u32[]{:S(2)}, u32[]{:S(2)}) collective-permute-start(f32[2,128]{1,0:T(2,128)} %param.5), channel_id=1, source_target_pairs={{0,8},{2,10},{4,12},{6,14},{8,0},{10,2},{12,4},{14,6},{16,24},{18,... | collective-permute-start | bytes 3080 | tf_op jit(solution)/shard_map/ppermute | solution.py:21
  3.1 1.1 %slice_bitcast_fusion.1 = (f32[2,256,128]{2,1,0:T(8,128)S(1)}, f32[2,256,128]{2,1,0:T(8,128)S(1)}) fusion(f32[2,1,2,256,128]{4,3,2,0,1:T(8,128)} %bitcast.129), kind=kLoop, calls=%fused_computation.1 | loop fusion | bytes 1048576 | tf_op jit(solution)/shard_map/reshape;squeeze | solution.py:191
  4.2 1.6 %collective-permute-start.1 = (f32[2,256,128]{2,1,0:T(8,128)S(1)}, f32[2,256,128]{2,1,0:T(8,128)S(1)}, u32[]{:S(2)}, u32[]{:S(2)}) collective-permute-start(f32[2,256,128]{2,1,0:T(8,128)S(1)} %get-tuple-element.127), channel_id=1, source_target_pairs={{0,1},{1,0},{2,3},{3,2},{4,5},{5,4},{6,7},{7,6},{8,9},{9,8},{10,11... | collective-permute-start | bytes 786440 | tf_op jit(solution)/shard_map/ppermute | solution.py:21
  5.8 0.4 collective-permute-start.3
  6.2 0.1 collective-permute-start.8
  6.3 0.0 copy-start.2
  6.4 0.7 copy-done.2
  7.1 0.1 pad_add_fusion.info
  7.2 0.0 collective-permute-done
  7.2 3.1 %collective-permute-start.6 = (f32[4,128]{1,0:T(4,128)S(1)}, f32[4,128]{1,0:T(4,128)S(1)}, u32[]{:S(2)}, u32[]{:S(2)}) collective-permute-start(f32[4,128]{1,0:T(4,128)S(1)} %pad_maximum_fusion.6), channel_id=1, source_target_pairs={{0,16},{2,18},{4,20},{6,22},{8,24},{10,26},{12,28},{14,30},{16,0},... | collective-permute-start | bytes 6152 | tf_op jit(solution)/shard_map/ppermute | solution.py:21
  10.3 1.7 %collective-permute-done.6 = f32[4,128]{1,0:T(4,128)S(1)} collective-permute-done((f32[4,128]{1,0:T(4,128)S(1)}, f32[4,128]{1,0:T(4,128)S(1)}, u32[]{:S(2)}, u32[]{:S(2)}) %collective-permute-start.6) | collective-permute-done | bytes 2080 | tf_op jit(solution)/shard_map/ppermute | solution.py:21
  12.0 0.1 collective-permute-done.8
  12.3 1.0 collective-permute-done.3
  13.3 0.1 multiply_add_fusion.4
  13.5 0.2 fusion.4
  13.6 0.8 collective-permute-start.10
  14.4 0.2 fusion.10
  14.6 2.7 %collective-permute-start.9 = (f32[256,128]{1,0:T(8,128)S(1)}, f32[256,128]{1,0:T(8,128)S(1)}, u32[]{:S(2)}, u32[]{:S(2)}) collective-permute-start(f32[256,128]{1,0:T(8,128)S(1)} %fusion.10), channel_id=1, source_target_pairs={{0,8},{2,10},{4,12},{6,14},{8,0},{10,2},{12,4},{14,6},{16,24},{18,... | collective-permute-start | bytes 393224 | tf_op jit(solution)/shard_map/ppermute | solution.py:21
  17.3 0.1 add_multiply_fusion.4
  17.4 0.1 collective-permute-start.2
  17.5 1.6 %collective-permute-start.4 = (f32[2,256,128]{2,1,0:T(8,128)S(1)}, f32[2,256,128]{2,1,0:T(8,128)S(1)}, u32[]{:S(2)}, u32[]{:S(2)}) collective-permute-start(f32[2,256,128]{2,1,0:T(8,128)S(1)} %get-tuple-element.98), channel_id=1, source_target_pairs={{0,1},{1,0},{2,3},{3,2},{4,5},{5,4},{6,7},{7,6},{8,9},{9,8},{10,11... | collective-permute-start | bytes 786440 | tf_op jit(solution)/shard_map/ppermute | solution.py:21
  19.1 0.5 collective-permute-start.5
  19.6 4.3 %collective-permute-done.9 = f32[256,128]{1,0:T(8,128)S(1)} collective-permute-done((f32[256,128]{1,0:T(8,128)S(1)}, f32[256,128]{1,0:T(8,128)S(1)}, u32[]{:S(2)}, u32[]{:S(2)}) %collective-permute-start.9) | collective-permute-done | bytes 131104 | tf_op jit(solution)/shard_map/ppermute | solution.py:21
  23.9 0.2 fusion.15
  24.1 0.1 collective-permute-start.11
  24.2 2.6 %collective-permute-done.4 = f32[2,256,128]{2,1,0:T(8,128)S(1)} collective-permute-done((f32[2,256,128]{2,1,0:T(8,128)S(1)}, f32[2,256,128]{2,1,0:T(8,128)S(1)}, u32[]{:S(2)}, u32[]{:S(2)}) %collective-permute-start.4) | collective-permute-done | bytes 262176 | tf_op jit(solution)/shard_map/ppermute | solution.py:21
  26.8 3.1 %collective-permute-done.5 = f32[2,256,128]{2,1,0:T(8,128)S(1)} collective-permute-done((f32[2,256,128]{2,1,0:T(8,128)S(1)}, f32[2,256,128]{2,1,0:T(8,128)S(1)}, u32[]{:S(2)}, u32[]{:S(2)}) %collective-permute-start.5) | collective-permute-done | bytes 262176 | tf_op jit(solution)/shard_map/ppermute | solution.py:21
  29.9 0.2 select_multiply_fusion.1
  30.1 4.3 %collective-permute-done.11 = f32[512,128]{1,0:T(8,128)S(1)} collective-permute-done((f32[512,128]{1,0:T(8,128)S(1)}, f32[512,128]{1,0:T(8,128)S(1)}, u32[]{:S(2)}, u32[]{:S(2)}) %collective-permute-start.11) | collective-permute-done | bytes 262176 | tf_op jit(solution)/shard_map/ppermute | solution.py:21
  34.4 1.6 %collective-permute-start.12 = (f32[512,128]{1,0:T(8,128)S(1)}, f32[512,128]{1,0:T(8,128)S(1)}, u32[]{:S(2)}, u32[]{:S(2)}) collective-permute-start(f32[512,128]{1,0:T(8,128)S(1)} %add_multiply_fusion.1), channel_id=1, source_target_pairs={{0,4},{2,6},{4,0},{6,2},{8,12},{10,14},{12,8},{14,10},{16,20},{18,... | collective-permute-start | bytes 786440 | tf_op jit(solution)/shard_map/ppermute | solution.py:21
  36.0 0.1 add_multiply_fusion.2
  36.1 4.7 %collective-permute-done.12 = f32[512,128]{1,0:T(8,128)S(1)} collective-permute-done((f32[512,128]{1,0:T(8,128)S(1)}, f32[512,128]{1,0:T(8,128)S(1)}, u32[]{:S(2)}, u32[]{:S(2)}) %collective-permute-start.12) | collective-permute-done | bytes 262176 | tf_op jit(solution)/shard_map/ppermute | solution.py:21
  40.9 0.1 collective-permute-start.14
  41.0 0.6 collective-permute-start.13
  41.5 0.1 multiply_add_fusion.5
  41.6 0.1 collective-permute-start.7
  41.7 0.8 collective-permute-done.14
  42.5 0.1 broadcast_select_fusion.15
  42.5 0.3 collective-permute-done.13
  42.9 12.8 %collective-permute-done.7 = f32[512,128]{1,0:T(8,128)S(1)} collective-permute-done((f32[512,128]{1,0:T(8,128)S(1)}, f32[512,128]{1,0:T(8,128)S(1)}, u32[]{:S(2)}, u32[]{:S(2)}) %collective-permute-start.7) | collective-permute-done | bytes 262176 | tf_op jit(solution)/shard_map/ppermute | solution.py:21
  55.7 0.1 multiply_add_fusion.2
  55.9 0.1 collective-permute-start.15
  56.0 2.5 %collective-permute-start.18 = (f32[2,256,128]{2,1,0:T(8,128)S(1)}, f32[2,256,128]{2,1,0:T(8,128)S(1)}, u32[]{:S(2)}, u32[]{:S(2)}) collective-permute-start(f32[2,256,128]{2,1,0:T(8,128)S(1)} %pad_maximum_fusion.5), channel_id=1, source_target_pairs={{0,16},{2,18},{4,20},{6,22},{8,24},{10,26},{12,28},{14,30},{16,0},... | collective-permute-start | bytes 786440 | tf_op jit(solution)/shard_map/ppermute | solution.py:21
  58.6 6.4 %eliminate_0.1 = (f32[4,512,128]{2,1,0:T(8,128)S(1)}, f32[4,512,128]{2,1,0:T(8,128)S(1)}, f32[512,128]{1,0:T(8,128)S(1)}) custom-call(f32[512,128]{1,0:T(8,128)S(1)} %get-tuple-element.54.refs_0_, f32[512,128]{1,0:T(8,128)S(1)} %get-tuple-element.55.refs_1_, f32[512,128]{1,0:T(8,128)S(1)} %get-tuple-element.56.refs_2_, f32[512,128]{1,0:T(8,128)S(1)} %get-tuple-element.57.refs_3_), custom_call_target="tpu_custom_call" | custom-call | flops 4000000000 | bytes 12000000 | tf_op jit(solution)/shard_map/eliminate_0/pallas_call | solution.py:289
  65.0 4.1 %collective-permute-done.15 = f32[512,128]{1,0:T(8,128)S(1)} collective-permute-done((f32[512,128]{1,0:T(8,128)S(1)}, f32[512,128]{1,0:T(8,128)S(1)}, u32[]{:S(2)}, u32[]{:S(2)}) %collective-permute-start.15) | collective-permute-done | bytes 262176 | tf_op jit(solution)/shard_map/ppermute | solution.py:21
  69.1 0.1 broadcast_select_fusion.20
  69.1 1.6 %collective-permute-start.16 = (f32[512,128]{1,0:T(8,128)S(1)}, f32[512,128]{1,0:T(8,128)S(1)}, u32[]{:S(2)}, u32[]{:S(2)}) collective-permute-start(f32[512,128]{1,0:T(8,128)S(1)} %get-tuple-element.117), channel_id=1, source_target_pairs={{0,4},{2,6},{4,0},{6,2},{8,12},{10,14},{12,8},{14,10},{16,20},{18,... | collective-permute-start | bytes 786440 | tf_op jit(solution)/shard_map/ppermute | solution.py:21
  70.7 0.5 collective-permute-start.17
  71.2 0.0 collective-permute-start.20
  71.2 5.8 %shard_map.37 = (f32[4,512,128]{2,1,0:T(8,128)S(1)}, f32[4,512,128]{2,1,0:T(8,128)S(1)}, f32[512,128]{1,0:T(8,128)S(1)}) custom-call(f32[4,512,128]{2,1,0:T(8,128)S(1)} %get-tuple-element.62.old_work, f32[4,512,128]{2,1,0:T(8,128)S(1)} %get-tuple-element.63.old_packed, ...), custom_call_target="tpu_custom_call", output_to_operand_aliasing={{0}: (0, {}), {1}: (1, {}), {2}: (2, {})} | custom-call | flops 4000000000 | bytes 12000000 | tf_op jit(solution)/shard_map/pallas_call | solution.py:312
  77.1 1.3 %collective-permute-done.16 = f32[512,128]{1,0:T(8,128)S(1)} collective-permute-done((f32[512,128]{1,0:T(8,128)S(1)}, f32[512,128]{1,0:T(8,128)S(1)}, u32[]{:S(2)}, u32[]{:S(2)}) %collective-permute-start.16) | collective-permute-done | bytes 262176 | tf_op jit(solution)/shard_map/ppermute | solution.py:21
  78.4 3.8 %collective-permute-done.17 = f32[512,128]{1,0:T(8,128)S(1)} collective-permute-done((f32[512,128]{1,0:T(8,128)S(1)}, f32[512,128]{1,0:T(8,128)S(1)}, u32[]{:S(2)}, u32[]{:S(2)}) %collective-permute-start.17) | collective-permute-done | bytes 262176 | tf_op jit(solution)/shard_map/ppermute | solution.py:21
  82.2 0.1 collective-permute-start.22
  82.3 0.5 collective-permute-start.24
  82.8 0.1 collective-permute-start.21
  83.0 0.4 collective-permute-start.23
  83.4 4.7 %shard_map.38 = (f32[4,512,128]{2,1,0:T(8,128)S(1)}, f32[4,512,128]{2,1,0:T(8,128)S(1)}, f32[512,128]{1,0:T(8,128)S(1)}) custom-call(f32[4,512,128]{2,1,0:T(8,128)S(1)} %get-tuple-element.72.old_work, f32[4,512,128]{2,1,0:T(8,128)S(1)} %get-tuple-element.73.old_packed, ...), custom_call_target="tpu_custom_call", output_to_operand_aliasing={{0}: (0, {}), {1}: (1, {}), {2}: (2, {})} | custom-call | flops 4000000000 | bytes 12000000 | tf_op jit(solution)/shard_map/pallas_call | solution.py:312
  88.2 3.1 %collective-permute-start.19 = (f32[512,128]{1,0:T(8,128)S(1)}, f32[512,128]{1,0:T(8,128)S(1)}, u32[]{:S(2)}, u32[]{:S(2)}) collective-permute-start(f32[512,128]{1,0:T(8,128)S(1)} %bitcast.128), channel_id=1, source_target_pairs={{0,1},{2,3},{4,5},{6,7},{8,9},{10,11},{12,13},{14,15},{16,17},{18,... | collective-permute-start | bytes 786440 | tf_op jit(solution)/shard_map/ppermute | solution.py:327
  91.3 0.0 collective-permute-done.24
  91.4 0.0 collective-permute-done.23
  91.5 4.4 %shard_map.39 = (f32[4,512,128]{2,1,0:T(8,128)S(1)}, f32[4,512,128]{2,1,0:T(8,128)S(1)}, f32[512,128]{1,0:T(8,128)S(1)}) custom-call(f32[4,512,128]{2,1,0:T(8,128)S(1)} %get-tuple-element.78.old_work, f32[4,512,128]{2,1,0:T(8,128)S(1)} %get-tuple-element.79.old_packed, ...), custom_call_target="tpu_custom_call", output_to_operand_aliasing={{0}: (0, {}), {1}: (1, {}), {2}: (2, {})} | custom-call | flops 4000000000 | bytes 12000000 | tf_op jit(solution)/shard_map/pallas_call | solution.py:312
  96.0 0.0 collective-permute-done.20
  96.0 0.9 collective-permute-done.19
  97.0 5.4 %own_columns.1 = f32[1024,128]{1,0:T(8,128)} custom-call(s32[3]{0:T(128)S(1)} %pad_add_fusion.info, f32[4,512,128]{2,1,0:T(8,128)S(1)} %get-tuple-element.84.work, f32[4,512,128]{2,1,0:T(8,128)S(1)} %get-tuple-element.85.packed, f32[512,128]{1,0:T(8,128)S(1)} %get-tuple-element.86.inverted, f32[512,128]{1,0:T(8,128)S(1)} %broadcast_select_fusion.own_top, ...), custom_call_target="tpu_custom_call" | custom-call | flops 4000000000 | bytes 12000000 | tf_op jit(solution)/shard_map/own_columns/pallas_call | solution.py:349
  (58 shorter events, 0.9 us)
Async XLA Ops:
  0.0 7.2 %collective-permute-start = (f32[2,128]{1,0:T(2,128)}, f32[2,128]{1,0:T(2,128)S(1)}, u32[]{:S(2)}, u32[]{:S(2)}) collective-permute-start(f32[2,128]{1,0:T(2,128)} %param.5), channel_id=1, source_target_pairs={{0,8},{2,10},{4,12},{6,14},{8,0},{10,2},{12,4},{14,6},{16,24},{18,... | collective-permute-start | bytes 3080 | tf_op jit(solution)/shard_map/ppermute | solution.py:21
  3.1 3.2 %copy-start.1 = (f32[2,1024]{1,0:T(2,128)S(1)}, f32[2,1024]{1,0:T(2,128)}, u32[]{:S(2)}) copy-start(f32[2,1024]{1,0:T(2,128)} %param.4) | copy-start | bytes 24580
  3.1 10.2 %copy-start = (f32[1024,128]{1,0:T(8,128)S(1)}, f32[1024,128]{1,0:T(8,128)}, u32[]{:S(2)}) copy-start(f32[1024,128]{1,0:T(8,128)} %param.3) | copy-start | bytes 1572868
  4.2 8.1 %collective-permute-start.1 = (f32[2,256,128]{2,1,0:T(8,128)S(1)}, f32[2,256,128]{2,1,0:T(8,128)S(1)}, u32[]{:S(2)}, u32[]{:S(2)}) collective-permute-start(f32[2,256,128]{2,1,0:T(8,128)S(1)} %get-tuple-element.127), channel_id=1, source_target_pairs={{0,1},{1,0},{2,3},{3,2},{4,5},{5,4},{6,7},{7,6},{8,9},{9,8},{10,11... | collective-permute-start | bytes 786440 | tf_op jit(solution)/shard_map/ppermute | solution.py:21
  5.8 7.5 %collective-permute-start.3 = (f32[2,256,128]{2,1,0:T(8,128)S(1)}, f32[2,256,128]{2,1,0:T(8,128)S(1)}, u32[]{:S(2)}, u32[]{:S(2)}) collective-permute-start(f32[2,256,128]{2,1,0:T(8,128)S(1)} %get-tuple-element.128), channel_id=1, source_target_pairs={{0,8},{2,10},{4,12},{6,14},{8,0},{10,2},{12,4},{14,6},{16,24},{18,... | collective-permute-start | bytes 786440 | tf_op jit(solution)/shard_map/ppermute | solution.py:21
  6.2 6.0 %collective-permute-start.8 = (f32[2,1024]{1,0:T(2,128)S(1)}, f32[2,1024]{1,0:T(2,128)S(1)}, u32[]{:S(2)}, u32[]{:S(2)}) collective-permute-start(f32[2,1024]{1,0:T(2,128)S(1)} %copy-done.1), channel_id=1, source_target_pairs={{0,1},{1,0},{2,3},{3,2},{4,5},{5,4},{6,7},{7,6},{8,9},{9,8},{10,11... | collective-permute-start | bytes 24584 | tf_op jit(solution)/shard_map/ppermute | solution.py:21
  6.3 0.7 copy-start.2
  7.2 4.7 %collective-permute-start.6 = (f32[4,128]{1,0:T(4,128)S(1)}, f32[4,128]{1,0:T(4,128)S(1)}, u32[]{:S(2)}, u32[]{:S(2)}) collective-permute-start(f32[4,128]{1,0:T(4,128)S(1)} %pad_maximum_fusion.6), channel_id=1, source_target_pairs={{0,16},{2,18},{4,20},{6,22},{8,24},{10,26},{12,28},{14,30},{16,0},... | collective-permute-start | bytes 6152 | tf_op jit(solution)/shard_map/ppermute | solution.py:21
  13.6 10.3 %collective-permute-start.10 = (f32[256,128]{1,0:T(8,128)S(1)}, f32[256,128]{1,0:T(8,128)S(1)}, u32[]{:S(2)}, u32[]{:S(2)}) collective-permute-start(f32[256,128]{1,0:T(8,128)S(1)} %fusion.4), channel_id=1, source_target_pairs={{0,1},{1,0},{2,3},{3,2},{4,5},{5,4},{6,7},{7,6},{8,9},{9,8},{10,11... | collective-permute-start | bytes 393224 | tf_op jit(solution)/shard_map/ppermute | solution.py:21
  14.6 9.3 %collective-permute-start.9 = (f32[256,128]{1,0:T(8,128)S(1)}, f32[256,128]{1,0:T(8,128)S(1)}, u32[]{:S(2)}, u32[]{:S(2)}) collective-permute-start(f32[256,128]{1,0:T(8,128)S(1)} %fusion.10), channel_id=1, source_target_pairs={{0,8},{2,10},{4,12},{6,14},{8,0},{10,2},{12,4},{14,6},{16,24},{18,... | collective-permute-start | bytes 393224 | tf_op jit(solution)/shard_map/ppermute | solution.py:21
  17.4 18.5 %collective-permute-start.2 = (f32[2,256,128]{2,1,0:T(8,128)S(1)}, f32[2,256,128]{2,1,0:T(8,128)S(1)}, u32[]{:S(2)}, u32[]{:S(2)}) collective-permute-start(f32[2,256,128]{2,1,0:T(8,128)S(1)} %pad_maximum_fusion), channel_id=1, source_target_pairs={{0,8},{2,10},{4,12},{6,14},{8,0},{10,2},{12,4},{14,6},{16,24},{18,... | collective-permute-start | bytes 786440 | tf_op jit(solution)/shard_map/ppermute | solution.py:21
  17.5 9.2 %collective-permute-start.4 = (f32[2,256,128]{2,1,0:T(8,128)S(1)}, f32[2,256,128]{2,1,0:T(8,128)S(1)}, u32[]{:S(2)}, u32[]{:S(2)}) collective-permute-start(f32[2,256,128]{2,1,0:T(8,128)S(1)} %get-tuple-element.98), channel_id=1, source_target_pairs={{0,1},{1,0},{2,3},{3,2},{4,5},{5,4},{6,7},{7,6},{8,9},{9,8},{10,11... | collective-permute-start | bytes 786440 | tf_op jit(solution)/shard_map/ppermute | solution.py:21
  19.1 10.8 %collective-permute-start.5 = (f32[2,256,128]{2,1,0:T(8,128)S(1)}, f32[2,256,128]{2,1,0:T(8,128)S(1)}, u32[]{:S(2)}, u32[]{:S(2)}) collective-permute-start(f32[2,256,128]{2,1,0:T(8,128)S(1)} %get-tuple-element.99), channel_id=1, source_target_pairs={{0,1},{1,0},{2,3},{3,2},{4,5},{5,4},{6,7},{7,6},{8,9},{9,8},{10,11... | collective-permute-start | bytes 786440 | tf_op jit(solution)/shard_map/ppermute | solution.py:21
  24.1 10.2 %collective-permute-start.11 = (f32[512,128]{1,0:T(8,128)S(1)}, f32[512,128]{1,0:T(8,128)S(1)}, u32[]{:S(2)}, u32[]{:S(2)}) collective-permute-start(f32[512,128]{1,0:T(8,128)S(1)} %pad_maximum_fusion.3), channel_id=1, source_target_pairs={{0,16},{2,18},{4,20},{6,22},{8,24},{10,26},{12,28},{14,30},{16,0},... | collective-permute-start | bytes 786440 | tf_op jit(solution)/shard_map/ppermute | solution.py:21
  34.4 6.4 %collective-permute-start.12 = (f32[512,128]{1,0:T(8,128)S(1)}, f32[512,128]{1,0:T(8,128)S(1)}, u32[]{:S(2)}, u32[]{:S(2)}) collective-permute-start(f32[512,128]{1,0:T(8,128)S(1)} %add_multiply_fusion.1), channel_id=1, source_target_pairs={{0,4},{2,6},{4,0},{6,2},{8,12},{10,14},{12,8},{14,10},{16,20},{18,... | collective-permute-start | bytes 786440 | tf_op jit(solution)/shard_map/ppermute | solution.py:21
  40.9 1.6 %collective-permute-start.14 = (f32[512,128]{1,0:T(8,128)S(1)}, f32[512,128]{1,0:T(8,128)S(1)}, u32[]{:S(2)}, u32[]{:S(2)}) collective-permute-start(f32[512,128]{1,0:T(8,128)S(1)} %get-tuple-element.120), channel_id=1, source_target_pairs={{0,2},{2,0},{4,6},{6,4},{8,10},{10,8},{12,14},{14,12},{16,18},{18,... | collective-permute-start | bytes 786440 | tf_op jit(solution)/shard_map/ppermute | solution.py:21
  41.0 1.9 %collective-permute-start.13 = (f32[512,128]{1,0:T(8,128)S(1)}, f32[512,128]{1,0:T(8,128)S(1)}, u32[]{:S(2)}, u32[]{:S(2)}) collective-permute-start(f32[512,128]{1,0:T(8,128)S(1)} %get-tuple-element.121), channel_id=1, source_target_pairs={{0,2},{2,0},{4,6},{6,4},{8,10},{10,8},{12,14},{14,12},{16,18},{18,... | collective-permute-start | bytes 786440 | tf_op jit(solution)/shard_map/ppermute | solution.py:21
  41.6 14.1 %collective-permute-start.7 = (f32[512,128]{1,0:T(8,128)S(1)}, f32[512,128]{1,0:T(8,128)S(1)}, u32[]{:S(2)}, u32[]{:S(2)}) collective-permute-start(f32[512,128]{1,0:T(8,128)S(1)} %multiply_add_fusion.5), channel_id=1, source_target_pairs={{0,16},{2,18},{4,20},{6,22},{8,24},{10,26},{12,28},{14,30},{16,0},... | collective-permute-start | bytes 786440 | tf_op jit(solution)/shard_map/ppermute | solution.py:21
  55.9 13.1 %collective-permute-start.15 = (f32[512,128]{1,0:T(8,128)S(1)}, f32[512,128]{1,0:T(8,128)S(1)}, u32[]{:S(2)}, u32[]{:S(2)}) collective-permute-start(f32[512,128]{1,0:T(8,128)S(1)} %add_multiply_fusion), channel_id=1, source_target_pairs={{0,8},{2,10},{4,12},{6,14},{8,0},{10,2},{12,4},{14,6},{16,24},{18,... | collective-permute-start | bytes 786440 | tf_op jit(solution)/shard_map/ppermute | solution.py:21
  56.0 21.0 %collective-permute-start.18 = (f32[2,256,128]{2,1,0:T(8,128)S(1)}, f32[2,256,128]{2,1,0:T(8,128)S(1)}, u32[]{:S(2)}, u32[]{:S(2)}) collective-permute-start(f32[2,256,128]{2,1,0:T(8,128)S(1)} %pad_maximum_fusion.5), channel_id=1, source_target_pairs={{0,16},{2,18},{4,20},{6,22},{8,24},{10,26},{12,28},{14,30},{16,0},... | collective-permute-start | bytes 786440 | tf_op jit(solution)/shard_map/ppermute | solution.py:21
  69.1 9.2 %collective-permute-start.16 = (f32[512,128]{1,0:T(8,128)S(1)}, f32[512,128]{1,0:T(8,128)S(1)}, u32[]{:S(2)}, u32[]{:S(2)}) collective-permute-start(f32[512,128]{1,0:T(8,128)S(1)} %get-tuple-element.117), channel_id=1, source_target_pairs={{0,4},{2,6},{4,0},{6,2},{8,12},{10,14},{12,8},{14,10},{16,20},{18,... | collective-permute-start | bytes 786440 | tf_op jit(solution)/shard_map/ppermute | solution.py:21
  70.7 11.5 %collective-permute-start.17 = (f32[512,128]{1,0:T(8,128)S(1)}, f32[512,128]{1,0:T(8,128)S(1)}, u32[]{:S(2)}, u32[]{:S(2)}) collective-permute-start(f32[512,128]{1,0:T(8,128)S(1)} %get-tuple-element.116), channel_id=1, source_target_pairs={{0,4},{2,6},{4,0},{6,2},{8,12},{10,14},{12,8},{14,10},{16,20},{18,... | collective-permute-start | bytes 786440 | tf_op jit(solution)/shard_map/ppermute | solution.py:21
  71.2 24.8 %collective-permute-start.20 = (f32[2,256,128]{2,1,0:T(8,128)S(1)}, f32[2,256,128]{2,1,0:T(8,128)S(1)}, u32[]{:S(2)}, u32[]{:S(2)}) collective-permute-start(f32[2,256,128]{2,1,0:T(8,128)S(1)} %pad_maximum_fusion.4), channel_id=1, source_target_pairs={{0,16},{2,18},{4,20},{6,22},{8,24},{10,26},{12,28},{14,30},{16,0},... | collective-permute-start | bytes 786440 | tf_op jit(solution)/shard_map/ppermute | solution.py:21
  82.2 6.0 %collective-permute-start.22 = (f32[512,128]{1,0:T(8,128)S(1)}, f32[512,128]{1,0:T(8,128)S(1)}, u32[]{:S(2)}, u32[]{:S(2)}) collective-permute-start(f32[512,128]{1,0:T(8,128)S(1)} %get-tuple-element.109), channel_id=1, source_target_pairs={{0,2},{2,0},{4,6},{6,4},{8,10},{10,8},{12,14},{14,12},{16,18},{18,... | collective-permute-start | bytes 786440 | tf_op jit(solution)/shard_map/ppermute | solution.py:21
  82.3 9.0 %collective-permute-start.24 = (f32[512,128]{1,0:T(8,128)S(1)}, f32[512,128]{1,0:T(8,128)S(1)}, u32[]{:S(2)}, u32[]{:S(2)}) collective-permute-start(f32[512,128]{1,0:T(8,128)S(1)} %get-tuple-element.108), channel_id=1, source_target_pairs={{0,2},{2,0},{4,6},{6,4},{8,10},{10,8},{12,14},{14,12},{16,18},{18,... | collective-permute-start | bytes 786440 | tf_op jit(solution)/shard_map/ppermute | solution.py:21
  82.8 8.5 %collective-permute-start.21 = (f32[512,128]{1,0:T(8,128)S(1)}, f32[512,128]{1,0:T(8,128)S(1)}, u32[]{:S(2)}, u32[]{:S(2)}) collective-permute-start(f32[512,128]{1,0:T(8,128)S(1)} %get-tuple-element.111), channel_id=1, source_target_pairs={{0,2},{2,0},{4,6},{6,4},{8,10},{10,8},{12,14},{14,12},{16,18},{18,... | collective-permute-start | bytes 786440 | tf_op jit(solution)/shard_map/ppermute | solution.py:21
  83.0 8.4 %collective-permute-start.23 = (f32[512,128]{1,0:T(8,128)S(1)}, f32[512,128]{1,0:T(8,128)S(1)}, u32[]{:S(2)}, u32[]{:S(2)}) collective-permute-start(f32[512,128]{1,0:T(8,128)S(1)} %get-tuple-element.110), channel_id=1, source_target_pairs={{0,2},{2,0},{4,6},{6,4},{8,10},{10,8},{12,14},{14,12},{16,18},{18,... | collective-permute-start | bytes 786440 | tf_op jit(solution)/shard_map/ppermute | solution.py:21
  88.2 8.7 %collective-permute-start.19 = (f32[512,128]{1,0:T(8,128)S(1)}, f32[512,128]{1,0:T(8,128)S(1)}, u32[]{:S(2)}, u32[]{:S(2)}) collective-permute-start(f32[512,128]{1,0:T(8,128)S(1)} %bitcast.128), channel_id=1, source_target_pairs={{0,1},{2,3},{4,5},{6,7},{8,9},{10,11},{12,13},{14,15},{16,17},{18,... | collective-permute-start | bytes 786440 | tf_op jit(solution)/shard_map/ppermute | solution.py:327

commit v6 on v4

--- a/solution.py
+++ b/solution.py
@@ -108,11 +108,11 @@
         work[j, here, :] = solved[j]
 
 
-def first_kernel(*refs):
+def first_kernel(info, *refs):
     blocks = LEAD // BLK
     pieces, (work, packed, inverted) = refs[:blocks], refs[blocks:]
-    for j in range(blocks):
-        work[j] = pieces[j][...]
+    for n in range(blocks):
+        work[info[3] ^ n] = pieces[n][...]
     eliminate_block(0, work, packed, inverted)
 
 
@@ -144,11 +144,14 @@
         here = pl.ds(BLK * k, BLK)
         terms = [hdot(work[j, here, :], reduced[pl.ds(BLK * j, BLK), :]) for j in range(k + 1, blocks)]
         reduced[here, :] = reduced[here, :] - tree_sum(terms)
-    part_rows = own[0].shape[0]
-
-    def below(part, first):
-        where = pl.ds(first, SPLIT)
-        terms = [hdot(pieces[2 * j + part][where, :], reduced[pl.ds(BLK * j, BLK), :]) for j in range(blocks)]
+    runs = pieces[0].shape[0] // SPLIT
+
+    def below(part, run):
+        where = pl.ds(pl.multiple_of(run * SPLIT, SPLIT), SPLIT)
+        terms = []
+        for n in range(blocks):
+            block = pl.ds(pl.multiple_of((info[3] ^ n) * BLK, BLK), BLK)
+            terms.append(hdot(pieces[2 * n + part][where, :], reduced[block, :]))
         total = tree_sum(terms)
         return jnp.where(is_panel, total, own[part][where, :] - total)
 
@@ -156,17 +159,16 @@
         where = pl.ds(SPLIT * part, SPLIT)
         out[where, :] = jnp.where(is_top, top[where, :], below(part, 0))
 
-    def step(n, carry):
+    def step(run):
         for part in range(2):
-            first = pl.multiple_of(n * SPLIT, SPLIT)
-            out[pl.ds(pl.multiple_of(n * LEAD, LEAD) + SPLIT * part, SPLIT), :] = below(part, first)
-        return carry
-
-    if part_rows // SPLIT <= 2:
-        for n in range(1, part_rows // SPLIT):
-            step(n, 0)
+            rows = pl.ds(pl.multiple_of(run * LEAD, LEAD) + SPLIT * part, SPLIT)
+            out[rows, :] = below(part, run)
+
+    if runs <= 2:
+        for run in range(1, runs):
+            step(run)
     else:
-        lax.fori_loop(1, part_rows // SPLIT, step, 0)
+        pl.loop(1, runs)(step)
 
 
 def shards(matrix, row_diag, col_diag):
@@ -189,7 +191,7 @@
 
     rows_p, rows_q = parts_of(matrix)
     other_p = swapped(rows_p, "row", 1)
-    near_q = swapped(rows_q, "col", low)
+    far_q = swapped(rows_q, "col", high)
     other_rows = swapped(row_diag, "row", 1)
     pair = jnp.concatenate([col_diag, swapped(col_diag, "col", low)], 0)
     far_pair = swapped(pair, "col", high)
@@ -200,13 +202,17 @@
 
     none, yes = jnp.bool_(False), jnp.bool_(True)
 
-    def contribution(parts, h, l):
+    def of_half(parts, h, l):
         even, odd = parts
         sign = jnp.where(in_high & h, -0.5, 0.5)
         scale_even = sign * diag_of(h, none)[0]
         scale_odd = jnp.where(l, -sign, sign) * diag_of(h, yes)[0]
         return scale_even * even + scale_odd * odd
 
+    def of_bit(parts, h, l):
+        scale = jnp.where(in_low & l, -0.5, 0.5) * diag_of(h, in_low)[0]
+        return scale * (parts[0] + jnp.where(h, -parts[1], parts[1]))
+
     first_diag = jnp.where(is_first, row_diag, other_rows)
     own_scales = [parts_of(row_diag[level]) for level in range(2)]
     first_scales = [parts_of(first_diag[level]) for level in range(2)]
@@ -221,15 +227,15 @@
         scale1 = first_scales[1][part][0, :SPLIT, None]
         return 0.5 * scale1 * (scale0[0] * values[0][:SPLIT] + scale0[1] * values[1][:SPLIT])
 
-    even_q = jnp.where(in_low, near_q, rows_q)
-    odd_q = jnp.where(in_low, rows_q, near_q)
+    first_q = jnp.where(in_high, far_q, rows_q)
+    second_q = jnp.where(in_high, rows_q, far_q)
     lead_own = lead_mixed(0, [rows_p[i, :SPLIT] + other_p[i, :SPLIT] for i in range(2)])
     lead_own = (0.5 * diag_of(none, in_low)[0]) * lead_own
-    lead_near = lead_mixed(1, contribution((even_q[:, :SPLIT], odd_q[:, :SPLIT]), none, none))
+    lead_bit = lead_mixed(1, of_bit((first_q[:, :SPLIT], second_q[:, :SPLIT]), none, none))
     lead_p = lead_own + swapped(lead_own, "col", low)
-    lead_q = lead_near + swapped(lead_near, "row", 1)
-    lead = jnp.concatenate([lead_p, lead_q], 0)
-    lead, rows_p, other_p, even_q, odd_q = lax.optimization_barrier((lead, rows_p, other_p, even_q, odd_q))
+    lead_q = lead_bit + swapped(lead_bit, "row", 1)
+    far_lead = swapped(lead_p, "col", high)
+    near_lead = swapped(lead_q, "col", low)
 
     def spread(values):
         for bit in range(block_bits, high_bit - 1):
@@ -237,39 +243,40 @@
             values = jnp.where((col_pos & 2**bit) != 0, arrived, values)
         return values
 
-    def gather(pieces, bit):
-        return joined(pieces, [swapped(p, "col", 2**bit) for p in pieces], bit)
-
-    def joined(pieces, arrived, bit):
-        second = (col_pos & 2**bit) != 0
-        return [
-            piece
-            for a, b in zip(pieces, arrived)
-            for piece in (jnp.where(second, b, a), jnp.where(second, a, b))
-        ]
+    def gather(values):
+        pieces = {0: values}
+        for bit in range(block_bits - 1, -1, -1):
+            for n in sorted(pieces):
+                pieces[n ^ 2**bit] = swapped(pieces[n], "col", 2**bit)
+        return [pieces[n] for n in range(blocks)]
 
     lead_scale = diag_of(none, none)[1]
-    far_lead = swapped(lead, "col", high)
-    lead_pieces = [spread(lead_scale * (lead + far_lead))]
-    for bit in range(block_bits - 1, -1, -1):
-        lead_pieces = gather(lead_pieces, bit)
+    lead = lead_scale * jnp.concatenate([lead_p + far_lead, lead_q + near_lead], 0)
+    lead_pieces = gather(spread(lead))
 
     own_p = jnp.stack(own_mixed(0, rows_p, other_p))
     near_p = swapped(own_p, "col", low)
-    even_p = jnp.where(in_low, near_p, own_p)
-    odd_p = jnp.where(in_low, own_p, near_p)
-    other_even, other_odd = swapped(even_q, "row", 1), swapped(odd_q, "row", 1)
-    even_q = jnp.stack(own_mixed(1, even_q, other_even))
-    odd_q = jnp.stack(own_mixed(1, odd_q, other_odd))
-    flat = lambda values: values.reshape(2 * part_rows, width)
-    both = [(flat(even_p), flat(odd_p)), (flat(even_q), flat(odd_q))]
-
-    mine = [jnp.where(in_low, q, p) for p, q in zip(*both)]
-    panel_half = contribution(mine, none, none)
-    far_half = swapped(panel_half, "col", high)
-    received = [swapped(contribution(v, ~in_high, in_low), "col", high) for v in both]
-    kept = [contribution(v, in_high, in_low) for v in both]
-
+    other_q = swapped(first_q, "row", 1), swapped(second_q, "row", 1)
+
+    def flat(values):
+        return values.reshape(2 * part_rows, width)
+
+    parts_p = flat(jnp.where(in_low, near_p, own_p)), flat(jnp.where(in_low, own_p, near_p))
+    parts_q = [flat(jnp.stack(own_mixed(1, a, b))) for a, b in zip((first_q, second_q), other_q)]
+    panel_p = of_half(parts_p, none, none)
+    panel_q = of_bit(parts_q, none, none)
+    far_p = swapped(panel_p, "col", high)
+    near_q = swapped(panel_q, "col", low)
+
+    info = jnp.stack(
+        [
+            (col_pos < blocks).astype(jnp.int32),
+            jnp.minimum(col_pos, blocks - 1).astype(jnp.int32),
+            is_first.astype(jnp.int32),
+            (col_pos & (blocks - 1)).astype(jnp.int32),
+        ]
+    )
+    smem = pl.BlockSpec(memory_space=pltpu.SMEM)
     vmem = pl.BlockSpec(memory_space=pltpu.VMEM)
     cost = pl.CostEstimate(flops=4_000_000_000, bytes_accessed=12_000_000, transcendentals=0)
     size = 4 * width * (5 * blocks * LEAD + (blocks + 4) * (height + LEAD))
@@ -279,17 +286,19 @@
     state = pl.pallas_call(
         first_kernel,
         out_shape=state_shapes,
-        in_specs=[vmem] * blocks,
+        in_specs=[smem] + [vmem] * blocks,
         out_specs=(vmem,) * 3,
         cost_estimate=cost,
         compiler_params=params,
         name="eliminate_0",
-    )(*lead_pieces)
-    far_half, *state = lax.optimization_barrier((far_half, *state))
-    panel_half = lead_scale * (panel_half + far_half)
-    other_half = swapped(panel_half, "col", low)
-    panel_pieces = []
-    own_top = own_parts = None
+    )(info, *lead_pieces)
+    far_p, near_q, parts_p, parts_q, *state = lax.optimization_barrier((far_p, near_q, parts_p, parts_q, *state))
+    pieces_p = gather(spread(lead_scale * (panel_p + far_p)))
+    pieces_q = gather(spread(lead_scale * (panel_q + near_q)))
+    kept_p, kept_q = of_half(parts_p, in_high, in_low), of_bit(parts_q, in_high, in_low)
+    received_p = swapped(of_half(parts_p, ~in_high, in_low), "col", high)
+    received_q = swapped(of_bit(parts_q, in_high, ~in_low), "col", low)
+    scale = diag_of(in_high, in_low)[1]
 
     for k in range(1, blocks):
         state = pl.pallas_call(
@@ -301,50 +310,25 @@
             cost_estimate=cost,
             compiler_params=params,
         )(*state)
-        bit = block_bits - k + 1
-        arrived = [other_half] if k == 1 else [swapped(p, "col", 2**bit) for p in panel_pieces]
-        count = len(arrived)
         if k == blocks - 2:
-            arrived += received
-        if k == blocks - 1:
-            arrived += [far_top]
-        *arrived, state0, state1, state2 = lax.optimization_barrier((*arrived, *state))
-        state = (state0, state1, state2)
-        arrived, extra = arrived[:count], arrived[count:]
-        if k == blocks - 2:
-            scale = diag_of(in_high, in_low)[1]
-            own_parts = [scale * (a + b) for a, b in zip(kept, extra)]
-            own_top = jnp.concatenate([v[:SPLIT] for v in own_parts], 0)
+            received_p, received_q, *state = lax.optimization_barrier((received_p, received_q, *state))
+            own = scale * (kept_p + received_p), scale * (kept_q + received_q)
+            own_top = jnp.concatenate([v[:SPLIT] for v in own], 0)
             far_top = lax.ppermute(own_top, "row", [(0, 1)])
-        if k == blocks - 1:
-            own_top = jnp.where(is_first, own_top, extra[0])
-        if k == 1:
-            panel_pieces = [
-                spread(jnp.where(in_low, arrived[0], panel_half)),
-                spread(jnp.where(in_low, panel_half, arrived[0])),
-            ]
-        else:
-            first = joined(panel_pieces[0::2], arrived[0::2], bit)
-            second = joined(panel_pieces[1::2], arrived[1::2], bit)
-            panel_pieces = [v for pq in zip(first, second) for v in pq]
-
-    info = jnp.stack(
-        [
-            (col_pos < blocks).astype(jnp.int32),
-            jnp.minimum(col_pos, blocks - 1).astype(jnp.int32),
-            is_first.astype(jnp.int32),
-        ]
-    )
+    far_top, *state = lax.optimization_barrier((far_top, *state))
+    own_top = jnp.where(is_first, own_top, far_top)
+    panel_pieces = [v for pq in zip(pieces_p, pieces_q) for v in pq]
+
     return pl.pallas_call(
         last_kernel,
         out_shape=jax.ShapeDtypeStruct((height, width), jnp.float32),
-        in_specs=[pl.BlockSpec(memory_space=pltpu.SMEM)] + [vmem] * (2 * blocks + 6),
+        in_specs=[smem] + [vmem] * (2 * blocks + 6),
         out_specs=vmem,
         scratch_shapes=[pltpu.VMEM((LEAD, width), jnp.float32)] * 3,
         cost_estimate=cost,
         compiler_params=params,
         name="own_columns",
-    )(info, *state, own_top, *own_parts, *panel_pieces)
+    )(info, *state, own_top, *own, *panel_pieces)
 
 
 def solution(mesh):

time: 110 us -> 93.8 us (0.85)
  waiting for transfers between devices: 49.2 us -> 34.5 us
  starting transfers between devices: 29.6 us -> 27.2 us
    ppermute x24 -> x25, waiting for transfers between devices: 49.2 us -> 34.5 us  [swapped(): lax.ppermute(x, axis, [(i, i ^ mask) for i in range(lax.axis_size(axis))])]
    ppermute x24 -> x25, starting transfers between devices: 27 us -> 23.6 us  [swapped(): lax.ppermute(x, axis, [(i, i ^ mask) for i in range(lax.axis_size(axis))])]
  transfers between devices with their start and end apart: 25 -> 26, of which waited for: 9 -> 11; matrix products, arithmetic and copies ran while one was open for 3% -> 3% of each run, Pallas kernels for 19% -> 23%
where the time goes in v6:
time: 93.8 us; the launch traced here: 93.6 us
  waiting for transfers between devices  34.5 us (37%)
  Pallas kernels  27.7 us (30%)
  starting transfers between devices  27.2 us (29%)
  local copies, waits for them, and re-layouts  1.93 us (2%)
  other arithmetic  1.8 us (2%)
    ppermute x25, waiting for transfers between devices, swapped(): lax.ppermute(x, axis, [(i, i ^ mask) for i in range(lax.axis_size(axis))])  34.5 us
    ppermute x25, starting transfers between devices, swapped(): lax.ppermute(x, axis, [(i, i ^ mask) for i in range(lax.axis_size(axis))])  23.6 us
    pallas_call x3, Pallas kernels, shards(): pl.pallas_call(functools.partial(next_kernel, k), out_shape=state_shapes,...  15 us
    pallas_call x1, Pallas kernels, shards(): pl.pallas_call(first_kernel, out_shape=state_shapes, in_specs=[smem] + [v...  6.98 us
    pallas_call x1, Pallas kernels, shards(): pl.pallas_call(last_kernel, out_shape=jax.ShapeDtypeStruct((height, width...  5.73 us
    ppermute x1, starting transfers between devices, shards(): far_top = lax.ppermute(own_top, 'row', [(0, 1)])  3.66 us
  transfers between devices with their start and end apart: 26, of which 11 were waited for; matrix products, arithmetic and copies ran while one was open for 3% of the time, Pallas kernels for 23%

profile of v6, /device:TPU:0, one launch (start us, length us, event | category | flops | bytes accessed | tf_op | source)
XLA Modules:
  0.0 93.6 jit_solution(3396360084760015888)
XLA Ops:
  0.0 3.1 %collective-permute-start = (f32[2,128]{1,0:T(2,128)}, f32[2,128]{1,0:T(2,128)S(1)}, u32[]{:S(2)}, u32[]{:S(2)}) collective-permute-start(f32[2,128]{1,0:T(2,128)} %param.5), channel_id=1, source_target_pairs={{0,8},{2,10},{4,12},{6,14},{8,0},{10,2},{12,4},{14,6},{16,24},{18,... | collective-permute-start | bytes 3080 | tf_op jit(solution)/shard_map/ppermute | solution.py:21
  3.1 1.1 %slice_bitcast_fusion = (f32[2,256,128]{2,1,0:T(8,128)S(1)}, f32[2,256,128]{2,1,0:T(8,128)S(1)}) fusion(f32[2,1,2,256,128]{4,3,2,0,1:T(8,128)} %bitcast.123), kind=kLoop, calls=%fused_computation.2 | loop fusion | bytes 1048576 | tf_op jit(solution)/shard_map/reshape;squeeze | solution.py:190
  4.2 2.7 %collective-permute-start.5 = (f32[2,256,128]{2,1,0:T(8,128)S(1)}, f32[2,256,128]{2,1,0:T(8,128)S(1)}, u32[]{:S(2)}, u32[]{:S(2)}) collective-permute-start(f32[2,256,128]{2,1,0:T(8,128)S(1)} %get-tuple-element.73), channel_id=1, source_target_pairs={{0,16},{2,18},{4,20},{6,22},{8,24},{10,26},{12,28},{14,30},{16,0},... | collective-permute-start | bytes 786440 | tf_op jit(solution)/shard_map/ppermute | solution.py:21
  6.8 1.5 %collective-permute-start.2 = (f32[2,256,128]{2,1,0:T(8,128)S(1)}, f32[2,256,128]{2,1,0:T(8,128)S(1)}, u32[]{:S(2)}, u32[]{:S(2)}) collective-permute-start(f32[2,256,128]{2,1,0:T(8,128)S(1)} %get-tuple-element.74), channel_id=1, source_target_pairs={{0,1},{1,0},{2,3},{3,2},{4,5},{5,4},{6,7},{7,6},{8,9},{9,8},{10,11... | collective-permute-start | bytes 786440 | tf_op jit(solution)/shard_map/ppermute | solution.py:21
  8.4 0.5 collective-permute-start.9
  9.0 0.0 copy-start.2
  9.0 0.7 copy-done.2
  9.7 0.1 pad_add_fusion.info
  9.8 0.4 collective-permute-start.1
  10.2 8.3 %collective-permute-done.1 = f32[4,128]{1,0:T(4,128)S(1)} collective-permute-done((f32[4,128]{1,0:T(4,128)S(1)}, f32[4,128]{1,0:T(4,128)S(1)}, u32[]{:S(2)}, u32[]{:S(2)}) %collective-permute-start.1) | collective-permute-done | bytes 2080 | tf_op jit(solution)/shard_map/ppermute | solution.py:21
  18.6 0.0 collective-permute-done.9
  18.7 0.1 add_multiply_fusion.4
  18.9 0.1 add_multiply_fusion.8
  19.0 0.1 collective-permute-start.3
  19.1 0.2 fusion.3
  19.3 1.6 %collective-permute-start.12 = (f32[256,128]{1,0:T(8,128)S(1)}, f32[256,128]{1,0:T(8,128)S(1)}, u32[]{:S(2)}, u32[]{:S(2)}) collective-permute-start(f32[256,128]{1,0:T(8,128)S(1)} %fusion.3), channel_id=1, source_target_pairs={{0,1},{1,0},{2,3},{3,2},{4,5},{5,4},{6,7},{7,6},{8,9},{9,8},{10,11... | collective-permute-start | bytes 393224 | tf_op jit(solution)/shard_map/ppermute | solution.py:21
  20.9 0.2 fusion.9
  21.1 2.1 %collective-permute-start.10 = (f32[256,128]{1,0:T(8,128)S(1)}, f32[256,128]{1,0:T(8,128)S(1)}, u32[]{:S(2)}, u32[]{:S(2)}) collective-permute-start(f32[256,128]{1,0:T(8,128)S(1)} %fusion.9), channel_id=1, source_target_pairs={{0,8},{2,10},{4,12},{6,14},{8,0},{10,2},{12,4},{14,6},{16,24},{18,... | collective-permute-start | bytes 393224 | tf_op jit(solution)/shard_map/ppermute | solution.py:21
  23.2 1.6 %collective-permute-done.12 = f32[256,128]{1,0:T(8,128)S(1)} collective-permute-done((f32[256,128]{1,0:T(8,128)S(1)}, f32[256,128]{1,0:T(8,128)S(1)}, u32[]{:S(2)}, u32[]{:S(2)}) %collective-permute-start.12) | collective-permute-done | bytes 131104 | tf_op jit(solution)/shard_map/ppermute | solution.py:21
  24.8 0.2 fusion.14
  24.9 1.8 %collective-permute-start.13 = (f32[256,128]{1,0:T(8,128)S(1)}, f32[256,128]{1,0:T(8,128)S(1)}, u32[]{:S(2)}, u32[]{:S(2)}) collective-permute-start(f32[256,128]{1,0:T(8,128)S(1)} %fusion.14), channel_id=1, source_target_pairs={{0,8},{2,10},{4,12},{6,14},{8,0},{10,2},{12,4},{14,6},{16,24},{18,... | collective-permute-start | bytes 393224 | tf_op jit(solution)/shard_map/ppermute | solution.py:21
  26.7 4.3 %collective-permute-done.10 = f32[256,128]{1,0:T(8,128)S(1)} collective-permute-done((f32[256,128]{1,0:T(8,128)S(1)}, f32[256,128]{1,0:T(8,128)S(1)}, u32[]{:S(2)}, u32[]{:S(2)}) %collective-permute-start.10) | collective-permute-done | bytes 131104 | tf_op jit(solution)/shard_map/ppermute | solution.py:21
  31.1 1.0 %collective-permute-start.11 = (f32[256,128]{1,0:T(8,128)S(1)}, f32[256,128]{1,0:T(8,128)S(1)}, u32[]{:S(2)}, u32[]{:S(2)}) collective-permute-start(f32[256,128]{1,0:T(8,128)S(1)} %add.87), channel_id=1, source_target_pairs={{0,16},{2,18},{4,20},{6,22},{8,24},{10,26},{12,28},{14,30},{16,0},... | collective-permute-start | bytes 393224 | tf_op jit(solution)/shard_map/ppermute | solution.py:21
  32.0 1.5 %collective-permute-start.6 = (f32[2,256,128]{2,1,0:T(8,128)S(1)}, f32[2,256,128]{2,1,0:T(8,128)S(1)}, u32[]{:S(2)}, u32[]{:S(2)}) collective-permute-start(f32[2,256,128]{2,1,0:T(8,128)S(1)} %get-tuple-element.70), channel_id=1, source_target_pairs={{0,1},{1,0},{2,3},{3,2},{4,5},{5,4},{6,7},{7,6},{8,9},{9,8},{10,11... | collective-permute-start | bytes 786440 | tf_op jit(solution)/shard_map/ppermute | solution.py:21
  33.6 0.5 collective-permute-start.7
  34.1 0.0 collective-permute-done.13
  34.1 4.4 %collective-permute-done.11 = f32[256,128]{1,0:T(8,128)S(1)} collective-permute-done((f32[256,128]{1,0:T(8,128)S(1)}, f32[256,128]{1,0:T(8,128)S(1)}, u32[]{:S(2)}, u32[]{:S(2)}) %collective-permute-start.11) | collective-permute-done | bytes 131104 | tf_op jit(solution)/shard_map/ppermute | solution.py:21
  38.5 0.1 collective-permute-start.14
  38.6 1.6 %collective-permute-start.15 = (f32[512,128]{1,0:T(8,128)S(1)}, f32[512,128]{1,0:T(8,128)S(1)}, u32[]{:S(2)}, u32[]{:S(2)}) collective-permute-start(f32[512,128]{1,0:T(8,128)S(1)} %maximum_multiply_fusion.refs_0_), channel_id=1, source_target_pairs={{0,4},{2,6},{4,0},{6,2},{8,12},{10,14},{12,8},{14,10},{16,20},{18,... | collective-permute-start | bytes 786440 | tf_op jit(solution)/shard_map/ppermute | solution.py:21
  40.3 0.1 collective-permute-start.4
  40.4 0.1 collective-permute-done.6
  40.5 2.8 %collective-permute-done.7 = f32[2,256,128]{2,1,0:T(8,128)S(1)} collective-permute-done((f32[2,256,128]{2,1,0:T(8,128)S(1)}, f32[2,256,128]{2,1,0:T(8,128)S(1)}, u32[]{:S(2)}, u32[]{:S(2)}) %collective-permute-start.7) | collective-permute-done | bytes 262176 | tf_op jit(solution)/shard_map/ppermute | solution.py:21
  43.3 0.2 select_multiply_fusion.1
  43.5 0.1 add_multiply_fusion.6
  43.6 3.7 %collective-permute-done.15.refs_2_ = f32[512,128]{1,0:T(8,128)S(1)} collective-permute-done((f32[512,128]{1,0:T(8,128)S(1)}, f32[512,128]{1,0:T(8,128)S(1)}, u32[]{:S(2)}, u32[]{:S(2)}) %collective-permute-start.15) | collective-permute-done | bytes 262176 | tf_op jit(solution)/shard_map/ppermute | solution.py:21
  47.3 0.0 collective-permute-start.16
  47.4 0.1 collective-permute-start.8
  47.5 0.0 collective-permute-done.14.refs_1_
  47.5 1.4 %collective-permute-done.16.refs_3_ = f32[512,128]{1,0:T(8,128)S(1)} collective-permute-done((f32[512,128]{1,0:T(8,128)S(1)}, f32[512,128]{1,0:T(8,128)S(1)}, u32[]{:S(2)}, u32[]{:S(2)}) %collective-permute-start.16) | collective-permute-done | bytes 262176 | tf_op jit(solution)/shard_map/ppermute | solution.py:21
  48.8 7.0 %eliminate_0.1 = (f32[4,512,128]{2,1,0:T(8,128)S(1)}, f32[4,512,128]{2,1,0:T(8,128)S(1)}, f32[512,128]{1,0:T(8,128)S(1)}) custom-call(s32[4]{0:T(128)S(1)} %pad_add_fusion.info, f32[512,128]{1,0:T(8,128)S(1)} %maximum_multiply_fusion.refs_0_, f32[512,128]{1,0:T(8,128)S(1)} %collective-permute-done.14.refs_1_, ...), custom_call_target="tpu_custom_call" | custom-call | flops 4000000000 | bytes 12000000 | tf_op jit(solution)/shard_map/eliminate_0/pallas_call | solution.py:286
  55.8 0.0 collective-permute-done.4
  55.8 4.1 %collective-permute-done.8 = f32[512,128]{1,0:T(8,128)S(1)} collective-permute-done((f32[512,128]{1,0:T(8,128)S(1)}, f32[512,128]{1,0:T(8,128)S(1)}, u32[]{:S(2)}, u32[]{:S(2)}) %collective-permute-start.8) | collective-permute-done | bytes 262176 | tf_op jit(solution)/shard_map/ppermute | solution.py:21
  59.9 0.1 add_multiply_fusion
  60.0 0.1 collective-permute-start.20
  60.1 0.5 collective-permute-start.22
  60.7 0.3 collective-permute-start.17
  61.0 2.5 %collective-permute-start.18 = (f32[512,128]{1,0:T(8,128)S(1)}, f32[512,128]{1,0:T(8,128)S(1)}, u32[]{:S(2)}, u32[]{:S(2)}) collective-permute-start(f32[512,128]{1,0:T(8,128)S(1)} %broadcast_multiply_fusion), channel_id=1, source_target_pairs={{0,8},{2,10},{4,12},{6,14},{8,0},{10,2},{12,4},{14,6},{16,24},{18,... | collective-permute-start | bytes 786440 | tf_op jit(solution)/shard_map/ppermute | solution.py:21
  63.5 0.0 collective-permute-start.21
  63.5 5.8 %shard_map.37 = (f32[4,512,128]{2,1,0:T(8,128)S(1)}, f32[4,512,128]{2,1,0:T(8,128)S(1)}, f32[512,128]{1,0:T(8,128)S(1)}) custom-call(f32[4,512,128]{2,1,0:T(8,128)S(1)} %get-tuple-element.42.old_work, f32[4,512,128]{2,1,0:T(8,128)S(1)} %get-tuple-element.43.old_packed, ...), custom_call_target="tpu_custom_call", output_to_operand_aliasing={{0}: (0, {}), {1}: (1, {}), {2}: (2, {})} | custom-call | flops 4000000000 | bytes 12000000 | tf_op jit(solution)/shard_map/pallas_call | solution.py:304
  69.3 4.7 %shard_map.38 = (f32[4,512,128]{2,1,0:T(8,128)S(1)}, f32[4,512,128]{2,1,0:T(8,128)S(1)}, f32[512,128]{1,0:T(8,128)S(1)}) custom-call(f32[4,512,128]{2,1,0:T(8,128)S(1)} %get-tuple-element.45.old_work, f32[4,512,128]{2,1,0:T(8,128)S(1)} %get-tuple-element.46.old_packed, ...), custom_call_target="tpu_custom_call", output_to_operand_aliasing={{0}: (0, {}), {1}: (1, {}), {2}: (2, {})} | custom-call | flops 4000000000 | bytes 12000000 | tf_op jit(solution)/shard_map/pallas_call | solution.py:304
  74.1 1.1 %collective-permute-done.17 = f32[512,128]{1,0:T(8,128)S(1)} collective-permute-done((f32[512,128]{1,0:T(8,128)S(1)}, f32[512,128]{1,0:T(8,128)S(1)}, u32[]{:S(2)}, u32[]{:S(2)}) %collective-permute-start.17) | collective-permute-done | bytes 262176 | tf_op jit(solution)/shard_map/ppermute | solution.py:21
  75.2 1.5 %collective-permute-start.23 = (f32[512,128]{1,0:T(8,128)S(1)}, f32[512,128]{1,0:T(8,128)S(1)}, u32[]{:S(2)}, u32[]{:S(2)}) collective-permute-start(f32[512,128]{1,0:T(8,128)S(1)} %get-tuple-element.112.refs_3_), channel_id=1, source_target_pairs={{0,4},{2,6},{4,0},{6,2},{8,12},{10,14},{12,8},{14,10},{16,20},{18,... | collective-permute-start | bytes 786440 | tf_op jit(solution)/shard_map/ppermute | solution.py:21
  76.7 0.0 collective-permute-done.18
  76.7 0.1 add_multiply_fusion.3
  76.9 3.7 %collective-permute-start.19 = (f32[512,128]{1,0:T(8,128)S(1)}, f32[512,128]{1,0:T(8,128)S(1)}, u32[]{:S(2)}, u32[]{:S(2)}) collective-permute-start(f32[512,128]{1,0:T(8,128)S(1)} %pad_maximum_fusion.3), channel_id=1, source_target_pairs={{0,1},{2,3},{4,5},{6,7},{8,9},{10,11},{12,13},{14,15},{16,17},{18,... | collective-permute-start | bytes 786440 | tf_op jit(solution)/shard_map/ppermute | solution.py:317
  80.6 0.0 collective-permute-done.22.refs_6_
  80.6 0.1 collective-permute-start.24
  80.7 2.7 %collective-permute-done.23.refs_7_ = f32[512,128]{1,0:T(8,128)S(1)} collective-permute-done((f32[512,128]{1,0:T(8,128)S(1)}, f32[512,128]{1,0:T(8,128)S(1)}, u32[]{:S(2)}, u32[]{:S(2)}) %collective-permute-start.23) | collective-permute-done | bytes 262176 | tf_op jit(solution)/shard_map/ppermute | solution.py:21
  83.4 0.0 collective-permute-start.25
  83.4 4.4 %shard_map.39 = (f32[4,512,128]{2,1,0:T(8,128)S(1)}, f32[4,512,128]{2,1,0:T(8,128)S(1)}, f32[512,128]{1,0:T(8,128)S(1)}) custom-call(f32[4,512,128]{2,1,0:T(8,128)S(1)} %get-tuple-element.53.old_work, f32[4,512,128]{2,1,0:T(8,128)S(1)} %get-tuple-element.54.old_packed, ...), custom_call_target="tpu_custom_call", output_to_operand_aliasing={{0}: (0, {}), {1}: (1, {}), {2}: (2, {})} | custom-call | flops 4000000000 | bytes 12000000 | tf_op jit(solution)/shard_map/pallas_call | solution.py:304
  87.8 0.0 collective-permute-done.19
  87.9 0.0 collective-permute-done.21.refs_5_
  87.9 0.0 collective-permute-done.24.refs_8_
  87.9 5.7 %own_columns.1 = f32[1024,128]{1,0:T(8,128)} custom-call(s32[4]{0:T(128)S(1)} %pad_add_fusion.info, f32[4,512,128]{2,1,0:T(8,128)S(1)} %get-tuple-element.59.work, f32[4,512,128]{2,1,0:T(8,128)S(1)} %get-tuple-element.60.packed, f32[512,128]{1,0:T(8,128)S(1)} %get-tuple-element.61.inverted, f32[512,128]{1,0:T(8,128)S(1)} %broadcast_select_fusion.own_top, ...), custom_call_target="tpu_custom_call" | custom-call | flops 4000000000 | bytes 12000000 | tf_op jit(solution)/shard_map/own_columns/pallas_call | solution.py:322
  (51 shorter events, 0.6 us)
Async XLA Ops:
  0.0 9.7 %collective-permute-start = (f32[2,128]{1,0:T(2,128)}, f32[2,128]{1,0:T(2,128)S(1)}, u32[]{:S(2)}, u32[]{:S(2)}) collective-permute-start(f32[2,128]{1,0:T(2,128)} %param.5), channel_id=1, source_target_pairs={{0,8},{2,10},{4,12},{6,14},{8,0},{10,2},{12,4},{14,6},{16,24},{18,... | collective-permute-start | bytes 3080 | tf_op jit(solution)/shard_map/ppermute | solution.py:21
  3.1 5.3 %copy-start.1 = (f32[2,1024]{1,0:T(2,128)S(1)}, f32[2,1024]{1,0:T(2,128)}, u32[]{:S(2)}) copy-start(f32[2,1024]{1,0:T(2,128)} %param.4) | copy-start | bytes 24580
  3.1 15.6 %copy-start = (f32[1024,128]{1,0:T(8,128)S(1)}, f32[1024,128]{1,0:T(8,128)}, u32[]{:S(2)}) copy-start(f32[1024,128]{1,0:T(8,128)} %param.3) | copy-start | bytes 1572868
  4.2 14.5 %collective-permute-start.5 = (f32[2,256,128]{2,1,0:T(8,128)S(1)}, f32[2,256,128]{2,1,0:T(8,128)S(1)}, u32[]{:S(2)}, u32[]{:S(2)}) collective-permute-start(f32[2,256,128]{2,1,0:T(8,128)S(1)} %get-tuple-element.73), channel_id=1, source_target_pairs={{0,16},{2,18},{4,20},{6,22},{8,24},{10,26},{12,28},{14,30},{16,0},... | collective-permute-start | bytes 786440 | tf_op jit(solution)/shard_map/ppermute | solution.py:21
  6.8 11.8 %collective-permute-start.2 = (f32[2,256,128]{2,1,0:T(8,128)S(1)}, f32[2,256,128]{2,1,0:T(8,128)S(1)}, u32[]{:S(2)}, u32[]{:S(2)}) collective-permute-start(f32[2,256,128]{2,1,0:T(8,128)S(1)} %get-tuple-element.74), channel_id=1, source_target_pairs={{0,1},{1,0},{2,3},{3,2},{4,5},{5,4},{6,7},{7,6},{8,9},{9,8},{10,11... | collective-permute-start | bytes 786440 | tf_op jit(solution)/shard_map/ppermute | solution.py:21
  8.4 10.2 %collective-permute-start.9 = (f32[2,1024]{1,0:T(2,128)S(1)}, f32[2,1024]{1,0:T(2,128)S(1)}, u32[]{:S(2)}, u32[]{:S(2)}) collective-permute-start(f32[2,1024]{1,0:T(2,128)S(1)} %copy-done.1), channel_id=1, source_target_pairs={{0,1},{1,0},{2,3},{3,2},{4,5},{5,4},{6,7},{7,6},{8,9},{9,8},{10,11... | collective-permute-start | bytes 24584 | tf_op jit(solution)/shard_map/ppermute | solution.py:21
  9.0 0.7 copy-start.2
  9.8 8.7 %collective-permute-start.1 = (f32[4,128]{1,0:T(4,128)S(1)}, f32[4,128]{1,0:T(4,128)S(1)}, u32[]{:S(2)}, u32[]{:S(2)}) collective-permute-start(f32[4,128]{1,0:T(4,128)S(1)} %pad_maximum_fusion.4), channel_id=1, source_target_pairs={{0,16},{2,18},{4,20},{6,22},{8,24},{10,26},{12,28},{14,30},{16,0},... | collective-permute-start | bytes 6152 | tf_op jit(solution)/shard_map/ppermute | solution.py:21
  19.0 21.2 %collective-permute-start.3 = (f32[2,256,128]{2,1,0:T(8,128)S(1)}, f32[2,256,128]{2,1,0:T(8,128)S(1)}, u32[]{:S(2)}, u32[]{:S(2)}) collective-permute-start(f32[2,256,128]{2,1,0:T(8,128)S(1)} %pad_maximum_fusion), channel_id=1, source_target_pairs={{0,8},{2,10},{4,12},{6,14},{8,0},{10,2},{12,4},{14,6},{16,24},{18,... | collective-permute-start | bytes 786440 | tf_op jit(solution)/shard_map/ppermute | solution.py:21
  19.3 5.5 %collective-permute-start.12 = (f32[256,128]{1,0:T(8,128)S(1)}, f32[256,128]{1,0:T(8,128)S(1)}, u32[]{:S(2)}, u32[]{:S(2)}) collective-permute-start(f32[256,128]{1,0:T(8,128)S(1)} %fusion.3), channel_id=1, source_target_pairs={{0,1},{1,0},{2,3},{3,2},{4,5},{5,4},{6,7},{7,6},{8,9},{9,8},{10,11... | collective-permute-start | bytes 393224 | tf_op jit(solution)/shard_map/ppermute | solution.py:21
  21.1 10.0 %collective-permute-start.10 = (f32[256,128]{1,0:T(8,128)S(1)}, f32[256,128]{1,0:T(8,128)S(1)}, u32[]{:S(2)}, u32[]{:S(2)}) collective-permute-start(f32[256,128]{1,0:T(8,128)S(1)} %fusion.9), channel_id=1, source_target_pairs={{0,8},{2,10},{4,12},{6,14},{8,0},{10,2},{12,4},{14,6},{16,24},{18,... | collective-permute-start | bytes 393224 | tf_op jit(solution)/shard_map/ppermute | solution.py:21
  24.9 9.1 %collective-permute-start.13 = (f32[256,128]{1,0:T(8,128)S(1)}, f32[256,128]{1,0:T(8,128)S(1)}, u32[]{:S(2)}, u32[]{:S(2)}) collective-permute-start(f32[256,128]{1,0:T(8,128)S(1)} %fusion.14), channel_id=1, source_target_pairs={{0,8},{2,10},{4,12},{6,14},{8,0},{10,2},{12,4},{14,6},{16,24},{18,... | collective-permute-start | bytes 393224 | tf_op jit(solution)/shard_map/ppermute | solution.py:21
  31.1 7.4 %collective-permute-start.11 = (f32[256,128]{1,0:T(8,128)S(1)}, f32[256,128]{1,0:T(8,128)S(1)}, u32[]{:S(2)}, u32[]{:S(2)}) collective-permute-start(f32[256,128]{1,0:T(8,128)S(1)} %add.87), channel_id=1, source_target_pairs={{0,16},{2,18},{4,20},{6,22},{8,24},{10,26},{12,28},{14,30},{16,0},... | collective-permute-start | bytes 393224 | tf_op jit(solution)/shard_map/ppermute | solution.py:21
  32.0 8.4 %collective-permute-start.6 = (f32[2,256,128]{2,1,0:T(8,128)S(1)}, f32[2,256,128]{2,1,0:T(8,128)S(1)}, u32[]{:S(2)}, u32[]{:S(2)}) collective-permute-start(f32[2,256,128]{2,1,0:T(8,128)S(1)} %get-tuple-element.70), channel_id=1, source_target_pairs={{0,1},{1,0},{2,3},{3,2},{4,5},{5,4},{6,7},{7,6},{8,9},{9,8},{10,11... | collective-permute-start | bytes 786440 | tf_op jit(solution)/shard_map/ppermute | solution.py:21
  33.6 9.7 %collective-permute-start.7 = (f32[2,256,128]{2,1,0:T(8,128)S(1)}, f32[2,256,128]{2,1,0:T(8,128)S(1)}, u32[]{:S(2)}, u32[]{:S(2)}) collective-permute-start(f32[2,256,128]{2,1,0:T(8,128)S(1)} %get-tuple-element.71), channel_id=1, source_target_pairs={{0,1},{1,0},{2,3},{3,2},{4,5},{5,4},{6,7},{7,6},{8,9},{9,8},{10,11... | collective-permute-start | bytes 786440 | tf_op jit(solution)/shard_map/ppermute | solution.py:21
  38.5 9.0 %collective-permute-start.14 = (f32[512,128]{1,0:T(8,128)S(1)}, f32[512,128]{1,0:T(8,128)S(1)}, u32[]{:S(2)}, u32[]{:S(2)}) collective-permute-start(f32[512,128]{1,0:T(8,128)S(1)} %maximum_multiply_fusion.refs_0_), channel_id=1, source_target_pairs={{0,2},{2,0},{4,6},{6,4},{8,10},{10,8},{12,14},{14,12},{16,18},{18,... | collective-permute-start | bytes 786440 | tf_op jit(solution)/shard_map/ppermute | solution.py:21
  38.6 8.7 %collective-permute-start.15 = (f32[512,128]{1,0:T(8,128)S(1)}, f32[512,128]{1,0:T(8,128)S(1)}, u32[]{:S(2)}, u32[]{:S(2)}) collective-permute-start(f32[512,128]{1,0:T(8,128)S(1)} %maximum_multiply_fusion.refs_0_), channel_id=1, source_target_pairs={{0,4},{2,6},{4,0},{6,2},{8,12},{10,14},{12,8},{14,10},{16,20},{18,... | collective-permute-start | bytes 786440 | tf_op jit(solution)/shard_map/ppermute | solution.py:21
  40.3 15.5 %collective-permute-start.4 = (f32[512,128]{1,0:T(8,128)S(1)}, f32[512,128]{1,0:T(8,128)S(1)}, u32[]{:S(2)}, u32[]{:S(2)}) collective-permute-start(f32[512,128]{1,0:T(8,128)S(1)} %multiply_add_fusion.1), channel_id=1, source_target_pairs={{0,16},{2,18},{4,20},{6,22},{8,24},{10,26},{12,28},{14,30},{16,0},... | collective-permute-start | bytes 786440 | tf_op jit(solution)/shard_map/ppermute | solution.py:21
  47.3 1.5 %collective-permute-start.16 = (f32[512,128]{1,0:T(8,128)S(1)}, f32[512,128]{1,0:T(8,128)S(1)}, u32[]{:S(2)}, u32[]{:S(2)}) collective-permute-start(f32[512,128]{1,0:T(8,128)S(1)} %collective-permute-done.15.refs_2_), channel_id=1, source_target_pairs={{0,2},{2,0},{4,6},{6,4},{8,10},{10,8},{12,14},{14,12},{16,18},{18,... | collective-permute-start | bytes 786440 | tf_op jit(solution)/shard_map/ppermute | solution.py:21
  47.4 12.5 %collective-permute-start.8 = (f32[512,128]{1,0:T(8,128)S(1)}, f32[512,128]{1,0:T(8,128)S(1)}, u32[]{:S(2)}, u32[]{:S(2)}) collective-permute-start(f32[512,128]{1,0:T(8,128)S(1)} %add_multiply_fusion.5), channel_id=1, source_target_pairs={{0,8},{2,10},{4,12},{6,14},{8,0},{10,2},{12,4},{14,6},{16,24},{18,... | collective-permute-start | bytes 786440 | tf_op jit(solution)/shard_map/ppermute | solution.py:21
  60.0 27.9 %collective-permute-start.20 = (f32[512,128]{1,0:T(8,128)S(1)}, f32[512,128]{1,0:T(8,128)S(1)}, u32[]{:S(2)}, u32[]{:S(2)}) collective-permute-start(f32[512,128]{1,0:T(8,128)S(1)} %get-tuple-element.113.refs_2_), channel_id=1, source_target_pairs={{0,2},{2,0},{4,6},{6,4},{8,10},{10,8},{12,14},{14,12},{16,18},{18,... | collective-permute-start | bytes 786440 | tf_op jit(solution)/shard_map/ppermute | solution.py:21
  60.1 20.5 %collective-permute-start.22 = (f32[512,128]{1,0:T(8,128)S(1)}, f32[512,128]{1,0:T(8,128)S(1)}, u32[]{:S(2)}, u32[]{:S(2)}) collective-permute-start(f32[512,128]{1,0:T(8,128)S(1)} %get-tuple-element.113.refs_2_), channel_id=1, source_target_pairs={{0,4},{2,6},{4,0},{6,2},{8,12},{10,14},{12,8},{14,10},{16,20},{18,... | collective-permute-start | bytes 786440 | tf_op jit(solution)/shard_map/ppermute | solution.py:21
  60.7 14.5 %collective-permute-start.17 = (f32[512,128]{1,0:T(8,128)S(1)}, f32[512,128]{1,0:T(8,128)S(1)}, u32[]{:S(2)}, u32[]{:S(2)}) collective-permute-start(f32[512,128]{1,0:T(8,128)S(1)} %multiply_add_fusion), channel_id=1, source_target_pairs={{0,16},{2,18},{4,20},{6,22},{8,24},{10,26},{12,28},{14,30},{16,0},... | collective-permute-start | bytes 786440 | tf_op jit(solution)/shard_map/ppermute | solution.py:21
  61.0 15.7 %collective-permute-start.18 = (f32[512,128]{1,0:T(8,128)S(1)}, f32[512,128]{1,0:T(8,128)S(1)}, u32[]{:S(2)}, u32[]{:S(2)}) collective-permute-start(f32[512,128]{1,0:T(8,128)S(1)} %broadcast_multiply_fusion), channel_id=1, source_target_pairs={{0,8},{2,10},{4,12},{6,14},{8,0},{10,2},{12,4},{14,6},{16,24},{18,... | collective-permute-start | bytes 786440 | tf_op jit(solution)/shard_map/ppermute | solution.py:21
  63.5 24.4 %collective-permute-start.21 = (f32[512,128]{1,0:T(8,128)S(1)}, f32[512,128]{1,0:T(8,128)S(1)}, u32[]{:S(2)}, u32[]{:S(2)}) collective-permute-start(f32[512,128]{1,0:T(8,128)S(1)} %get-tuple-element.112.refs_3_), channel_id=1, source_target_pairs={{0,2},{2,0},{4,6},{6,4},{8,10},{10,8},{12,14},{14,12},{16,18},{18,... | collective-permute-start | bytes 786440 | tf_op jit(solution)/shard_map/ppermute | solution.py:21
  75.2 8.2 %collective-permute-start.23 = (f32[512,128]{1,0:T(8,128)S(1)}, f32[512,128]{1,0:T(8,128)S(1)}, u32[]{:S(2)}, u32[]{:S(2)}) collective-permute-start(f32[512,128]{1,0:T(8,128)S(1)} %get-tuple-element.112.refs_3_), channel_id=1, source_target_pairs={{0,4},{2,6},{4,0},{6,2},{8,12},{10,14},{12,8},{14,10},{16,20},{18,... | collective-permute-start | bytes 786440 | tf_op jit(solution)/shard_map/ppermute | solution.py:21
  76.9 10.9 %collective-permute-start.19 = (f32[512,128]{1,0:T(8,128)S(1)}, f32[512,128]{1,0:T(8,128)S(1)}, u32[]{:S(2)}, u32[]{:S(2)}) collective-permute-start(f32[512,128]{1,0:T(8,128)S(1)} %pad_maximum_fusion.3), channel_id=1, source_target_pairs={{0,1},{2,3},{4,5},{6,7},{8,9},{10,11},{12,13},{14,15},{16,17},{18,... | collective-permute-start | bytes 786440 | tf_op jit(solution)/shard_map/ppermute | solution.py:317
  80.6 7.3 %collective-permute-start.24 = (f32[512,128]{1,0:T(8,128)S(1)}, f32[512,128]{1,0:T(8,128)S(1)}, u32[]{:S(2)}, u32[]{:S(2)}) collective-permute-start(f32[512,128]{1,0:T(8,128)S(1)} %collective-permute-done.22.refs_6_), channel_id=1, source_target_pairs={{0,2},{2,0},{4,6},{6,4},{8,10},{10,8},{12,14},{14,12},{16,18},{18,... | collective-permute-start | bytes 786440 | tf_op jit(solution)/shard_map/ppermute | solution.py:21
  83.4 4.5 %collective-permute-start.25 = (f32[512,128]{1,0:T(8,128)S(1)}, f32[512,128]{1,0:T(8,128)S(1)}, u32[]{:S(2)}, u32[]{:S(2)}) collective-permute-start(f32[512,128]{1,0:T(8,128)S(1)} %collective-permute-done.23.refs_7_), channel_id=1, source_target_pairs={{0,2},{2,0},{4,6},{6,4},{8,10},{10,8},{12,14},{14,12},{16,18},{18,... | collective-permute-start | bytes 786440 | tf_op jit(solution)/shard_map/ppermute | solution.py:21

commit v7 on v6

--- a/solution.py
+++ b/solution.py
@@ -261,11 +261,8 @@
     def flat(values):
         return values.reshape(2 * part_rows, width)
 
-    parts_p = flat(jnp.where(in_low, near_p, own_p)), flat(jnp.where(in_low, own_p, near_p))
     parts_q = [flat(jnp.stack(own_mixed(1, a, b))) for a, b in zip((first_q, second_q), other_q)]
-    panel_p = of_half(parts_p, none, none)
     panel_q = of_bit(parts_q, none, none)
-    far_p = swapped(panel_p, "col", high)
     near_q = swapped(panel_q, "col", low)
 
     info = jnp.stack(
@@ -292,9 +289,12 @@
         compiler_params=params,
         name="eliminate_0",
     )(info, *lead_pieces)
-    far_p, near_q, parts_p, parts_q, *state = lax.optimization_barrier((far_p, near_q, parts_p, parts_q, *state))
-    pieces_p = gather(spread(lead_scale * (panel_p + far_p)))
-    pieces_q = gather(spread(lead_scale * (panel_q + near_q)))
+    near_q, near_p, parts_q, *state = lax.optimization_barrier((near_q, near_p, parts_q, *state))
+    parts_p = flat(jnp.where(in_low, near_p, own_p)), flat(jnp.where(in_low, own_p, near_p))
+    panel_p = of_half(parts_p, none, none)
+    far_p = swapped(panel_p, "col", high)
+    panel_q = spread(lead_scale * (panel_q + near_q))
+    pieces_q = gather(panel_q)
     kept_p, kept_q = of_half(parts_p, in_high, in_low), of_bit(parts_q, in_high, in_low)
     received_p = swapped(of_half(parts_p, ~in_high, in_low), "col", high)
     received_q = swapped(of_bit(parts_q, in_high, ~in_low), "col", low)
@@ -310,6 +310,9 @@
             cost_estimate=cost,
             compiler_params=params,
         )(*state)
+        if k == 1:
+            far_p, _, *state = lax.optimization_barrier((far_p, panel_q, *state))
+            pieces_p = gather(spread(lead_scale * (panel_p + far_p)))
         if k == blocks - 2:
             received_p, received_q, *state = lax.optimization_barrier((received_p, received_q, *state))
             own = scale * (kept_p + received_p), scale * (kept_q + received_q)

time: 93.8 us -> 114 us (1.22)
  waiting for transfers between devices: 34.5 us -> 55.1 us
    ppermute x25, waiting for transfers between devices: 34.5 us -> 55.1 us  [swapped(): lax.ppermute(x, axis, [(i, i ^ mask) for i in range(lax.axis_size(axis))])]
  transfers between devices with their start and end apart: 26 -> 26, of which waited for: 11 -> 8; matrix products, arithmetic and copies ran while one was open for 3% -> 3% of each run, Pallas kernels for 23% -> 19%
where the time goes in v7:
time: 114 us
  waiting for transfers between devices  55.1 us (48%)
  Pallas kernels  27.7 us (24%)
  starting transfers between devices  26.9 us (24%)
  local copies, waits for them, and re-layouts  1.93 us (2%)
  other arithmetic  1.81 us (2%)
    ppermute x25, waiting for transfers between devices, swapped(): lax.ppermute(x, axis, [(i, i ^ mask) for i in range(lax.axis_size(axis))])  55.1 us
    ppermute x25, starting transfers between devices, swapped(): lax.ppermute(x, axis, [(i, i ^ mask) for i in range(lax.axis_size(axis))])  23.2 us
    pallas_call x3, Pallas kernels, shards(): pl.pallas_call(functools.partial(next_kernel, k), out_shape=state_shapes,...  15 us
    pallas_call x1, Pallas kernels, shards(): pl.pallas_call(first_kernel, out_shape=state_shapes, in_specs=[smem] + [v...  6.98 us
    pallas_call x1, Pallas kernels, shards(): pl.pallas_call(last_kernel, out_shape=jax.ShapeDtypeStruct((height, width...  5.74 us
    ppermute x1, starting transfers between devices, shards(): far_top = lax.ppermute(own_top, 'row', [(0, 1)])  3.71 us
  transfers between devices with their start and end apart: 26, of which 8 were waited for; matrix products, arithmetic and copies ran while one was open for 3% of the time, Pallas kernels for 19%

profile of v7, /device:TPU:0, one launch (start us, length us, event | category | flops | bytes accessed | tf_op | source)
XLA Modules:
  0.0 114.0 jit_solution(7754601910992132985)
XLA Ops:
  0.0 3.1 %collective-permute-start = (f32[2,128]{1,0:T(2,128)}, f32[2,128]{1,0:T(2,128)S(1)}, u32[]{:S(2)}, u32[]{:S(2)}) collective-permute-start(f32[2,128]{1,0:T(2,128)} %param.5), channel_id=1, source_target_pairs={{0,8},{2,10},{4,12},{6,14},{8,0},{10,2},{12,4},{14,6},{16,24},{18,... | collective-permute-start | bytes 3080 | tf_op jit(solution)/shard_map/ppermute | solution.py:21
  3.1 1.1 slice_bitcast_fusion
  4.2 2.7 %collective-permute-start.2 = (f32[2,256,128]{2,1,0:T(8,128)S(1)}, f32[2,256,128]{2,1,0:T(8,128)S(1)}, u32[]{:S(2)}, u32[]{:S(2)}) collective-permute-start(f32[2,256,128]{2,1,0:T(8,128)S(1)} %get-tuple-element.82), channel_id=1, source_target_pairs={{0,16},{2,18},{4,20},{6,22},{8,24},{10,26},{12,28},{14,30},{16,0},... | collective-permute-start | bytes 786440 | tf_op jit(solution)/shard_map/ppermute | solution.py:21
  6.8 1.5 %collective-permute-start.6 = (f32[2,256,128]{2,1,0:T(8,128)S(1)}, f32[2,256,128]{2,1,0:T(8,128)S(1)}, u32[]{:S(2)}, u32[]{:S(2)}) collective-permute-start(f32[2,256,128]{2,1,0:T(8,128)S(1)} %get-tuple-element.81), channel_id=1, source_target_pairs={{0,1},{1,0},{2,3},{3,2},{4,5},{5,4},{6,7},{7,6},{8,9},{9,8},{10,11... | collective-permute-start | bytes 786440 | tf_op jit(solution)/shard_map/ppermute | solution.py:21
  8.4 0.5 collective-permute-start.8
  9.0 0.0 copy-start.2
  9.0 0.7 copy-done.2
  9.7 0.1 pad_add_fusion.info
  9.8 0.0 collective-permute-done
  9.8 0.4 collective-permute-start.1
  10.2 8.3 %collective-permute-done.1 = f32[4,128]{1,0:T(4,128)S(1)} collective-permute-done((f32[4,128]{1,0:T(4,128)S(1)}, f32[4,128]{1,0:T(4,128)S(1)}, u32[]{:S(2)}, u32[]{:S(2)}) %collective-permute-start.1) | collective-permute-done | bytes 2080 | tf_op jit(solution)/shard_map/ppermute | solution.py:21
  18.6 0.0 collective-permute-done.8
  18.7 0.0 collective-permute-done.2
  18.7 0.1 add_multiply_fusion.3
  18.9 1.6 %collective-permute-start.3 = (f32[2,256,128]{2,1,0:T(8,128)S(1)}, f32[2,256,128]{2,1,0:T(8,128)S(1)}, u32[]{:S(2)}, u32[]{:S(2)}) collective-permute-start(f32[2,256,128]{2,1,0:T(8,128)S(1)} %get-tuple-element.74), channel_id=1, source_target_pairs={{0,1},{1,0},{2,3},{3,2},{4,5},{5,4},{6,7},{7,6},{8,9},{9,8},{10,11... | collective-permute-start | bytes 786440 | tf_op jit(solution)/shard_map/ppermute | solution.py:21
  20.5 0.5 collective-permute-start.4
  20.9 0.2 fusion.8
  21.1 1.6 %collective-permute-start.11 = (f32[256,128]{1,0:T(8,128)S(1)}, f32[256,128]{1,0:T(8,128)S(1)}, u32[]{:S(2)}, u32[]{:S(2)}) collective-permute-start(f32[256,128]{1,0:T(8,128)S(1)} %fusion.8), channel_id=1, source_target_pairs={{0,1},{1,0},{2,3},{3,2},{4,5},{5,4},{6,7},{7,6},{8,9},{9,8},{10,11... | collective-permute-start | bytes 393224 | tf_op jit(solution)/shard_map/ppermute | solution.py:21
  22.8 0.2 fusion.14
  22.9 0.1 collective-permute-start.9
  23.0 12.6 %collective-permute-done.11 = f32[256,128]{1,0:T(8,128)S(1)} collective-permute-done((f32[256,128]{1,0:T(8,128)S(1)}, f32[256,128]{1,0:T(8,128)S(1)}, u32[]{:S(2)}, u32[]{:S(2)}) %collective-permute-start.11) | collective-permute-done | bytes 131104 | tf_op jit(solution)/shard_map/ppermute | solution.py:21
  35.6 0.2 fusion.19
  35.8 0.1 collective-permute-start.12
  35.9 2.2 %collective-permute-start.10 = (f32[256,128]{1,0:T(8,128)S(1)}, f32[256,128]{1,0:T(8,128)S(1)}, u32[]{:S(2)}, u32[]{:S(2)}) collective-permute-start(f32[256,128]{1,0:T(8,128)S(1)} %add.86), channel_id=1, source_target_pairs={{0,16},{2,18},{4,20},{6,22},{8,24},{10,26},{12,28},{14,30},{16,0},... | collective-permute-start | bytes 393224 | tf_op jit(solution)/shard_map/ppermute | solution.py:21
  38.1 0.1 add_multiply_fusion.5
  38.2 0.1 collective-permute-start.7
  38.3 6.0 %collective-permute-done.12 = f32[256,128]{1,0:T(8,128)S(1)} collective-permute-done((f32[256,128]{1,0:T(8,128)S(1)}, f32[256,128]{1,0:T(8,128)S(1)}, u32[]{:S(2)}, u32[]{:S(2)}) %collective-permute-start.12) | collective-permute-done | bytes 131104 | tf_op jit(solution)/shard_map/ppermute | solution.py:21
  44.3 0.0 collective-permute-done.10
  44.4 0.1 collective-permute-start.13
  44.5 1.6 %collective-permute-start.14 = (f32[512,128]{1,0:T(8,128)S(1)}, f32[512,128]{1,0:T(8,128)S(1)}, u32[]{:S(2)}, u32[]{:S(2)}) collective-permute-start(f32[512,128]{1,0:T(8,128)S(1)} %maximum_multiply_fusion.refs_0_), channel_id=1, source_target_pairs={{0,4},{2,6},{4,0},{6,2},{8,12},{10,14},{12,8},{14,10},{16,20},{18,... | collective-permute-start | bytes 786440 | tf_op jit(solution)/shard_map/ppermute | solution.py:21
  46.1 0.0 collective-permute-done.4
  46.1 0.2 select_multiply_fusion.2
  46.2 0.1 add_multiply_fusion.6
  46.4 6.8 %collective-permute-done.14.refs_2_ = f32[512,128]{1,0:T(8,128)S(1)} collective-permute-done((f32[512,128]{1,0:T(8,128)S(1)}, f32[512,128]{1,0:T(8,128)S(1)}, u32[]{:S(2)}, u32[]{:S(2)}) %collective-permute-start.14) | collective-permute-done | bytes 262176 | tf_op jit(solution)/shard_map/ppermute | solution.py:21
  53.2 0.0 collective-permute-start.15
  53.3 0.9 collective-permute-start.5
  54.2 0.5 collective-permute-done.15.refs_3_
  54.7 7.0 %eliminate_0.1 = (f32[4,512,128]{2,1,0:T(8,128)S(1)}, f32[4,512,128]{2,1,0:T(8,128)S(1)}, f32[512,128]{1,0:T(8,128)S(1)}) custom-call(s32[4]{0:T(128)S(1)} %pad_add_fusion.info, f32[512,128]{1,0:T(8,128)S(1)} %maximum_multiply_fusion.refs_0_, f32[512,128]{1,0:T(8,128)S(1)} %collective-permute-done.13.refs_1_, ...), custom_call_target="tpu_custom_call" | custom-call | flops 4000000000 | bytes 12000000 | tf_op jit(solution)/shard_map/eliminate_0/pallas_call | solution.py:283
  61.7 0.3 collective-permute-done.5
  62.1 0.1 collective-permute-start.21
  62.2 1.6 %collective-permute-start.23 = (f32[512,128]{1,0:T(8,128)S(1)}, f32[512,128]{1,0:T(8,128)S(1)}, u32[]{:S(2)}, u32[]{:S(2)}) collective-permute-start(f32[512,128]{1,0:T(8,128)S(1)} %add_multiply_fusion.2.refs_3_), channel_id=1, source_target_pairs={{0,4},{2,6},{4,0},{6,2},{8,12},{10,14},{12,8},{14,10},{16,20},{18,... | collective-permute-start | bytes 786440 | tf_op jit(solution)/shard_map/ppermute | solution.py:21
  63.8 0.1 fusion.5
  63.9 1.6 %collective-permute-start.16 = (f32[512,128]{1,0:T(8,128)S(1)}, f32[512,128]{1,0:T(8,128)S(1)}, u32[]{:S(2)}, u32[]{:S(2)}) collective-permute-start(f32[512,128]{1,0:T(8,128)S(1)} %get-tuple-element.77), channel_id=1, source_target_pairs={{0,16},{2,18},{4,20},{6,22},{8,24},{10,26},{12,28},{14,30},{16,0},... | collective-permute-start | bytes 786440 | tf_op jit(solution)/shard_map/ppermute | solution.py:21
  65.5 0.5 collective-permute-start.17
  66.1 1.7 %collective-permute-start.18 = (f32[512,128]{1,0:T(8,128)S(1)}, f32[512,128]{1,0:T(8,128)S(1)}, u32[]{:S(2)}, u32[]{:S(2)}) collective-permute-start(f32[512,128]{1,0:T(8,128)S(1)} %get-tuple-element.76), channel_id=1, source_target_pairs={{0,16},{2,18},{4,20},{6,22},{8,24},{10,26},{12,28},{14,30},{16,0},... | collective-permute-start | bytes 786440 | tf_op jit(solution)/shard_map/ppermute | solution.py:21
  67.8 5.8 %shard_map.37 = (f32[4,512,128]{2,1,0:T(8,128)S(1)}, f32[4,512,128]{2,1,0:T(8,128)S(1)}, f32[512,128]{1,0:T(8,128)S(1)}) custom-call(f32[4,512,128]{2,1,0:T(8,128)S(1)} %get-tuple-element.44.old_work, f32[4,512,128]{2,1,0:T(8,128)S(1)} %get-tuple-element.45.old_packed, ...), custom_call_target="tpu_custom_call", output_to_operand_aliasing={{0}: (0, {}), {1}: (1, {}), {2}: (2, {})} | custom-call | flops 4000000000 | bytes 12000000 | tf_op jit(solution)/shard_map/pallas_call | solution.py:304
  73.7 16.4 %collective-permute-done.18 = f32[512,128]{1,0:T(8,128)S(1)} collective-permute-done((f32[512,128]{1,0:T(8,128)S(1)}, f32[512,128]{1,0:T(8,128)S(1)}, u32[]{:S(2)}, u32[]{:S(2)}) %collective-permute-start.18) | collective-permute-done | bytes 262176 | tf_op jit(solution)/shard_map/ppermute | solution.py:21
  90.1 0.1 collective-permute-start.20
  90.2 4.7 %shard_map.38 = (f32[4,512,128]{2,1,0:T(8,128)S(1)}, f32[4,512,128]{2,1,0:T(8,128)S(1)}, f32[512,128]{1,0:T(8,128)S(1)}) custom-call(f32[4,512,128]{2,1,0:T(8,128)S(1)} %get-tuple-element.50.old_work, f32[4,512,128]{2,1,0:T(8,128)S(1)} %get-tuple-element.51.old_packed, ...), custom_call_target="tpu_custom_call", output_to_operand_aliasing={{0}: (0, {}), {1}: (1, {}), {2}: (2, {})} | custom-call | flops 4000000000 | bytes 12000000 | tf_op jit(solution)/shard_map/pallas_call | solution.py:304
  94.9 0.0 collective-permute-done.16
  94.9 0.5 collective-permute-start.22
  95.5 0.0 collective-permute-done.17
  95.5 0.1 fusion.3
  95.7 3.7 %collective-permute-start.19 = (f32[512,128]{1,0:T(8,128)S(1)}, f32[512,128]{1,0:T(8,128)S(1)}, u32[]{:S(2)}, u32[]{:S(2)}) collective-permute-start(f32[512,128]{1,0:T(8,128)S(1)} %pad_maximum_fusion.3), channel_id=1, source_target_pairs={{0,1},{2,3},{4,5},{6,7},{8,9},{10,11},{12,13},{14,15},{16,17},{18,... | collective-permute-start | bytes 786440 | tf_op jit(solution)/shard_map/ppermute | solution.py:320
  99.4 0.0 collective-permute-done.23.refs_7_
  99.4 0.1 collective-permute-start.25
  99.5 4.2 %collective-permute-done.22.refs_6_ = f32[512,128]{1,0:T(8,128)S(1)} collective-permute-done((f32[512,128]{1,0:T(8,128)S(1)}, f32[512,128]{1,0:T(8,128)S(1)}, u32[]{:S(2)}, u32[]{:S(2)}) %collective-permute-start.22) | collective-permute-done | bytes 262176 | tf_op jit(solution)/shard_map/ppermute | solution.py:21
  103.7 0.0 collective-permute-start.24
  103.7 4.4 %shard_map.39 = (f32[4,512,128]{2,1,0:T(8,128)S(1)}, f32[4,512,128]{2,1,0:T(8,128)S(1)}, f32[512,128]{1,0:T(8,128)S(1)}) custom-call(f32[4,512,128]{2,1,0:T(8,128)S(1)} %get-tuple-element.58.old_work, f32[4,512,128]{2,1,0:T(8,128)S(1)} %get-tuple-element.59.old_packed, ...), custom_call_target="tpu_custom_call", output_to_operand_aliasing={{0}: (0, {}), {1}: (1, {}), {2}: (2, {})} | custom-call | flops 4000000000 | bytes 12000000 | tf_op jit(solution)/shard_map/pallas_call | solution.py:304
  108.1 0.0 collective-permute-done.19
  108.2 0.0 collective-permute-done.21.refs_5_
  108.2 0.0 collective-permute-done.20.refs_4_
  108.2 0.0 collective-permute-done.24.refs_8_
  108.2 5.7 %own_columns.1 = f32[1024,128]{1,0:T(8,128)} custom-call(s32[4]{0:T(128)S(1)} %pad_add_fusion.info, f32[4,512,128]{2,1,0:T(8,128)S(1)} %get-tuple-element.64.work, f32[4,512,128]{2,1,0:T(8,128)S(1)} %get-tuple-element.65.packed, f32[512,128]{1,0:T(8,128)S(1)} %get-tuple-element.66.inverted, f32[512,128]{1,0:T(8,128)S(1)} %broadcast_select_fusion.own_top, ...), custom_call_target="tpu_custom_call" | custom-call | flops 4000000000 | bytes 12000000 | tf_op jit(solution)/shard_map/own_columns/pallas_call | solution.py:325
  (49 shorter events, 0.6 us)
Async XLA Ops:
  0.0 9.8 %collective-permute-start = (f32[2,128]{1,0:T(2,128)}, f32[2,128]{1,0:T(2,128)S(1)}, u32[]{:S(2)}, u32[]{:S(2)}) collective-permute-start(f32[2,128]{1,0:T(2,128)} %param.5), channel_id=1, source_target_pairs={{0,8},{2,10},{4,12},{6,14},{8,0},{10,2},{12,4},{14,6},{16,24},{18,... | collective-permute-start | bytes 3080 | tf_op jit(solution)/shard_map/ppermute | solution.py:21
  3.1 5.3 %copy-start.1 = (f32[2,1024]{1,0:T(2,128)S(1)}, f32[2,1024]{1,0:T(2,128)}, u32[]{:S(2)}) copy-start(f32[2,1024]{1,0:T(2,128)} %param.4) | copy-start | bytes 24580
  3.1 15.6 %copy-start = (f32[1024,128]{1,0:T(8,128)S(1)}, f32[1024,128]{1,0:T(8,128)}, u32[]{:S(2)}) copy-start(f32[1024,128]{1,0:T(8,128)} %param.3) | copy-start | bytes 1572868
  4.2 14.5 %collective-permute-start.2 = (f32[2,256,128]{2,1,0:T(8,128)S(1)}, f32[2,256,128]{2,1,0:T(8,128)S(1)}, u32[]{:S(2)}, u32[]{:S(2)}) collective-permute-start(f32[2,256,128]{2,1,0:T(8,128)S(1)} %get-tuple-element.82), channel_id=1, source_target_pairs={{0,16},{2,18},{4,20},{6,22},{8,24},{10,26},{12,28},{14,30},{16,0},... | collective-permute-start | bytes 786440 | tf_op jit(solution)/shard_map/ppermute | solution.py:21
  6.8 11.8 %collective-permute-start.6 = (f32[2,256,128]{2,1,0:T(8,128)S(1)}, f32[2,256,128]{2,1,0:T(8,128)S(1)}, u32[]{:S(2)}, u32[]{:S(2)}) collective-permute-start(f32[2,256,128]{2,1,0:T(8,128)S(1)} %get-tuple-element.81), channel_id=1, source_target_pairs={{0,1},{1,0},{2,3},{3,2},{4,5},{5,4},{6,7},{7,6},{8,9},{9,8},{10,11... | collective-permute-start | bytes 786440 | tf_op jit(solution)/shard_map/ppermute | solution.py:21
  8.4 10.2 %collective-permute-start.8 = (f32[2,1024]{1,0:T(2,128)S(1)}, f32[2,1024]{1,0:T(2,128)S(1)}, u32[]{:S(2)}, u32[]{:S(2)}) collective-permute-start(f32[2,1024]{1,0:T(2,128)S(1)} %copy-done.1), channel_id=1, source_target_pairs={{0,1},{1,0},{2,3},{3,2},{4,5},{5,4},{6,7},{7,6},{8,9},{9,8},{10,11... | collective-permute-start | bytes 24584 | tf_op jit(solution)/shard_map/ppermute | solution.py:21
  9.0 0.7 copy-start.2
  9.8 8.7 %collective-permute-start.1 = (f32[4,128]{1,0:T(4,128)S(1)}, f32[4,128]{1,0:T(4,128)S(1)}, u32[]{:S(2)}, u32[]{:S(2)}) collective-permute-start(f32[4,128]{1,0:T(4,128)S(1)} %pad_maximum_fusion.4), channel_id=1, source_target_pairs={{0,16},{2,18},{4,20},{6,22},{8,24},{10,26},{12,28},{14,30},{16,0},... | collective-permute-start | bytes 6152 | tf_op jit(solution)/shard_map/ppermute | solution.py:21
  18.9 27.2 %collective-permute-start.3 = (f32[2,256,128]{2,1,0:T(8,128)S(1)}, f32[2,256,128]{2,1,0:T(8,128)S(1)}, u32[]{:S(2)}, u32[]{:S(2)}) collective-permute-start(f32[2,256,128]{2,1,0:T(8,128)S(1)} %get-tuple-element.74), channel_id=1, source_target_pairs={{0,1},{1,0},{2,3},{3,2},{4,5},{5,4},{6,7},{7,6},{8,9},{9,8},{10,11... | collective-permute-start | bytes 786440 | tf_op jit(solution)/shard_map/ppermute | solution.py:21
  20.5 25.6 %collective-permute-start.4 = (f32[2,256,128]{2,1,0:T(8,128)S(1)}, f32[2,256,128]{2,1,0:T(8,128)S(1)}, u32[]{:S(2)}, u32[]{:S(2)}) collective-permute-start(f32[2,256,128]{2,1,0:T(8,128)S(1)} %get-tuple-element.75), channel_id=1, source_target_pairs={{0,1},{1,0},{2,3},{3,2},{4,5},{5,4},{6,7},{7,6},{8,9},{9,8},{10,11... | collective-permute-start | bytes 786440 | tf_op jit(solution)/shard_map/ppermute | solution.py:21
  21.1 14.5 %collective-permute-start.11 = (f32[256,128]{1,0:T(8,128)S(1)}, f32[256,128]{1,0:T(8,128)S(1)}, u32[]{:S(2)}, u32[]{:S(2)}) collective-permute-start(f32[256,128]{1,0:T(8,128)S(1)} %fusion.8), channel_id=1, source_target_pairs={{0,1},{1,0},{2,3},{3,2},{4,5},{5,4},{6,7},{7,6},{8,9},{9,8},{10,11... | collective-permute-start | bytes 393224 | tf_op jit(solution)/shard_map/ppermute | solution.py:21
  22.9 12.9 %collective-permute-start.9 = (f32[256,128]{1,0:T(8,128)S(1)}, f32[256,128]{1,0:T(8,128)S(1)}, u32[]{:S(2)}, u32[]{:S(2)}) collective-permute-start(f32[256,128]{1,0:T(8,128)S(1)} %fusion.14), channel_id=1, source_target_pairs={{0,8},{2,10},{4,12},{6,14},{8,0},{10,2},{12,4},{14,6},{16,24},{18,... | collective-permute-start | bytes 393224 | tf_op jit(solution)/shard_map/ppermute | solution.py:21
  35.8 8.5 %collective-permute-start.12 = (f32[256,128]{1,0:T(8,128)S(1)}, f32[256,128]{1,0:T(8,128)S(1)}, u32[]{:S(2)}, u32[]{:S(2)}) collective-permute-start(f32[256,128]{1,0:T(8,128)S(1)} %fusion.19), channel_id=1, source_target_pairs={{0,8},{2,10},{4,12},{6,14},{8,0},{10,2},{12,4},{14,6},{16,24},{18,... | collective-permute-start | bytes 393224 | tf_op jit(solution)/shard_map/ppermute | solution.py:21
  35.9 8.5 %collective-permute-start.10 = (f32[256,128]{1,0:T(8,128)S(1)}, f32[256,128]{1,0:T(8,128)S(1)}, u32[]{:S(2)}, u32[]{:S(2)}) collective-permute-start(f32[256,128]{1,0:T(8,128)S(1)} %add.86), channel_id=1, source_target_pairs={{0,16},{2,18},{4,20},{6,22},{8,24},{10,26},{12,28},{14,30},{16,0},... | collective-permute-start | bytes 393224 | tf_op jit(solution)/shard_map/ppermute | solution.py:21
  38.2 23.4 %collective-permute-start.7 = (f32[2,256,128]{2,1,0:T(8,128)S(1)}, f32[2,256,128]{2,1,0:T(8,128)S(1)}, u32[]{:S(2)}, u32[]{:S(2)}) collective-permute-start(f32[2,256,128]{2,1,0:T(8,128)S(1)} %pad_maximum_fusion.2), channel_id=1, source_target_pairs={{0,8},{2,10},{4,12},{6,14},{8,0},{10,2},{12,4},{14,6},{16,24},{18,... | collective-permute-start | bytes 786440 | tf_op jit(solution)/shard_map/ppermute | solution.py:21
  44.4 9.8 %collective-permute-start.13 = (f32[512,128]{1,0:T(8,128)S(1)}, f32[512,128]{1,0:T(8,128)S(1)}, u32[]{:S(2)}, u32[]{:S(2)}) collective-permute-start(f32[512,128]{1,0:T(8,128)S(1)} %maximum_multiply_fusion.refs_0_), channel_id=1, source_target_pairs={{0,2},{2,0},{4,6},{6,4},{8,10},{10,8},{12,14},{14,12},{16,18},{18,... | collective-permute-start | bytes 786440 | tf_op jit(solution)/shard_map/ppermute | solution.py:21
  44.5 8.7 %collective-permute-start.14 = (f32[512,128]{1,0:T(8,128)S(1)}, f32[512,128]{1,0:T(8,128)S(1)}, u32[]{:S(2)}, u32[]{:S(2)}) collective-permute-start(f32[512,128]{1,0:T(8,128)S(1)} %maximum_multiply_fusion.refs_0_), channel_id=1, source_target_pairs={{0,4},{2,6},{4,0},{6,2},{8,12},{10,14},{12,8},{14,10},{16,20},{18,... | collective-permute-start | bytes 786440 | tf_op jit(solution)/shard_map/ppermute | solution.py:21
  53.2 1.5 %collective-permute-start.15 = (f32[512,128]{1,0:T(8,128)S(1)}, f32[512,128]{1,0:T(8,128)S(1)}, u32[]{:S(2)}, u32[]{:S(2)}) collective-permute-start(f32[512,128]{1,0:T(8,128)S(1)} %collective-permute-done.14.refs_2_), channel_id=1, source_target_pairs={{0,2},{2,0},{4,6},{6,4},{8,10},{10,8},{12,14},{14,12},{16,18},{18,... | collective-permute-start | bytes 786440 | tf_op jit(solution)/shard_map/ppermute | solution.py:21
  53.3 8.8 %collective-permute-start.5 = (f32[512,128]{1,0:T(8,128)S(1)}, f32[512,128]{1,0:T(8,128)S(1)}, u32[]{:S(2)}, u32[]{:S(2)}) collective-permute-start(f32[512,128]{1,0:T(8,128)S(1)} %add_multiply_fusion.4), channel_id=1, source_target_pairs={{0,8},{2,10},{4,12},{6,14},{8,0},{10,2},{12,4},{14,6},{16,24},{18,... | collective-permute-start | bytes 786440 | tf_op jit(solution)/shard_map/ppermute | solution.py:21
  62.1 46.1 %collective-permute-start.21 = (f32[512,128]{1,0:T(8,128)S(1)}, f32[512,128]{1,0:T(8,128)S(1)}, u32[]{:S(2)}, u32[]{:S(2)}) collective-permute-start(f32[512,128]{1,0:T(8,128)S(1)} %add_multiply_fusion.2.refs_3_), channel_id=1, source_target_pairs={{0,2},{2,0},{4,6},{6,4},{8,10},{10,8},{12,14},{14,12},{16,18},{18,... | collective-permute-start | bytes 786440 | tf_op jit(solution)/shard_map/ppermute | solution.py:21
  62.2 37.3 %collective-permute-start.23 = (f32[512,128]{1,0:T(8,128)S(1)}, f32[512,128]{1,0:T(8,128)S(1)}, u32[]{:S(2)}, u32[]{:S(2)}) collective-permute-start(f32[512,128]{1,0:T(8,128)S(1)} %add_multiply_fusion.2.refs_3_), channel_id=1, source_target_pairs={{0,4},{2,6},{4,0},{6,2},{8,12},{10,14},{12,8},{14,10},{16,20},{18,... | collective-permute-start | bytes 786440 | tf_op jit(solution)/shard_map/ppermute | solution.py:21
  63.9 31.1 %collective-permute-start.16 = (f32[512,128]{1,0:T(8,128)S(1)}, f32[512,128]{1,0:T(8,128)S(1)}, u32[]{:S(2)}, u32[]{:S(2)}) collective-permute-start(f32[512,128]{1,0:T(8,128)S(1)} %get-tuple-element.77), channel_id=1, source_target_pairs={{0,16},{2,18},{4,20},{6,22},{8,24},{10,26},{12,28},{14,30},{16,0},... | collective-permute-start | bytes 786440 | tf_op jit(solution)/shard_map/ppermute | solution.py:21
  65.5 29.9 %collective-permute-start.17 = (f32[512,128]{1,0:T(8,128)S(1)}, f32[512,128]{1,0:T(8,128)S(1)}, u32[]{:S(2)}, u32[]{:S(2)}) collective-permute-start(f32[512,128]{1,0:T(8,128)S(1)} %broadcast_multiply_fusion), channel_id=1, source_target_pairs={{0,8},{2,10},{4,12},{6,14},{8,0},{10,2},{12,4},{14,6},{16,24},{18,... | collective-permute-start | bytes 786440 | tf_op jit(solution)/shard_map/ppermute | solution.py:21
  66.1 24.0 %collective-permute-start.18 = (f32[512,128]{1,0:T(8,128)S(1)}, f32[512,128]{1,0:T(8,128)S(1)}, u32[]{:S(2)}, u32[]{:S(2)}) collective-permute-start(f32[512,128]{1,0:T(8,128)S(1)} %get-tuple-element.76), channel_id=1, source_target_pairs={{0,16},{2,18},{4,20},{6,22},{8,24},{10,26},{12,28},{14,30},{16,0},... | collective-permute-start | bytes 786440 | tf_op jit(solution)/shard_map/ppermute | solution.py:21
  90.1 18.1 %collective-permute-start.20 = (f32[512,128]{1,0:T(8,128)S(1)}, f32[512,128]{1,0:T(8,128)S(1)}, u32[]{:S(2)}, u32[]{:S(2)}) collective-permute-start(f32[512,128]{1,0:T(8,128)S(1)} %add_multiply_fusion.refs_2_), channel_id=1, source_target_pairs={{0,2},{2,0},{4,6},{6,4},{8,10},{10,8},{12,14},{14,12},{16,18},{18,... | collective-permute-start | bytes 786440 | tf_op jit(solution)/shard_map/ppermute | solution.py:21
  94.9 8.8 %collective-permute-start.22 = (f32[512,128]{1,0:T(8,128)S(1)}, f32[512,128]{1,0:T(8,128)S(1)}, u32[]{:S(2)}, u32[]{:S(2)}) collective-permute-start(f32[512,128]{1,0:T(8,128)S(1)} %add_multiply_fusion.refs_2_), channel_id=1, source_target_pairs={{0,4},{2,6},{4,0},{6,2},{8,12},{10,14},{12,8},{14,10},{16,20},{18,... | collective-permute-start | bytes 786440 | tf_op jit(solution)/shard_map/ppermute | solution.py:21
  95.7 12.5 %collective-permute-start.19 = (f32[512,128]{1,0:T(8,128)S(1)}, f32[512,128]{1,0:T(8,128)S(1)}, u32[]{:S(2)}, u32[]{:S(2)}) collective-permute-start(f32[512,128]{1,0:T(8,128)S(1)} %pad_maximum_fusion.3), channel_id=1, source_target_pairs={{0,1},{2,3},{4,5},{6,7},{8,9},{10,11},{12,13},{14,15},{16,17},{18,... | collective-permute-start | bytes 786440 | tf_op jit(solution)/shard_map/ppermute | solution.py:320
  99.4 8.8 %collective-permute-start.25 = (f32[512,128]{1,0:T(8,128)S(1)}, f32[512,128]{1,0:T(8,128)S(1)}, u32[]{:S(2)}, u32[]{:S(2)}) collective-permute-start(f32[512,128]{1,0:T(8,128)S(1)} %collective-permute-done.23.refs_7_), channel_id=1, source_target_pairs={{0,2},{2,0},{4,6},{6,4},{8,10},{10,8},{12,14},{14,12},{16,18},{18,... | collective-permute-start | bytes 786440 | tf_op jit(solution)/shard_map/ppermute | solution.py:21
  103.7 4.5 %collective-permute-start.24 = (f32[512,128]{1,0:T(8,128)S(1)}, f32[512,128]{1,0:T(8,128)S(1)}, u32[]{:S(2)}, u32[]{:S(2)}) collective-permute-start(f32[512,128]{1,0:T(8,128)S(1)} %collective-permute-done.22.refs_6_), channel_id=1, source_target_pairs={{0,2},{2,0},{4,6},{6,4},{8,10},{10,8},{12,14},{14,12},{16,18},{18,... | collective-permute-start | bytes 786440 | tf_op jit(solution)/shard_map/ppermute | solution.py:21

commit v8 on v7

--- a/solution.py
+++ b/solution.py
@@ -265,6 +265,11 @@
     panel_q = of_bit(parts_q, none, none)
     near_q = swapped(panel_q, "col", low)
 
+    parts_p = flat(jnp.where(in_low, near_p, own_p)), flat(jnp.where(in_low, own_p, near_p))
+    panel_p = of_half(parts_p, none, none)
+    far_p = swapped(panel_p, "col", high)
+    received_p = swapped(of_half(parts_p, ~in_high, in_low), "col", high)
+
     info = jnp.stack(
         [
             (col_pos < blocks).astype(jnp.int32),
@@ -289,14 +294,10 @@
         compiler_params=params,
         name="eliminate_0",
     )(info, *lead_pieces)
-    near_q, near_p, parts_q, *state = lax.optimization_barrier((near_q, near_p, parts_q, *state))
-    parts_p = flat(jnp.where(in_low, near_p, own_p)), flat(jnp.where(in_low, own_p, near_p))
-    panel_p = of_half(parts_p, none, none)
-    far_p = swapped(panel_p, "col", high)
+    near_q, parts_q, *state = lax.optimization_barrier((near_q, parts_q, *state))
     panel_q = spread(lead_scale * (panel_q + near_q))
     pieces_q = gather(panel_q)
     kept_p, kept_q = of_half(parts_p, in_high, in_low), of_bit(parts_q, in_high, in_low)
-    received_p = swapped(of_half(parts_p, ~in_high, in_low), "col", high)
     received_q = swapped(of_bit(parts_q, in_high, ~in_low), "col", low)
     scale = diag_of(in_high, in_low)[1]
 
@@ -311,10 +312,10 @@
             compiler_params=params,
         )(*state)
         if k == 1:
-            far_p, _, *state = lax.optimization_barrier((far_p, panel_q, *state))
+            far_p, received_p, received_q, _, *state = lax.optimization_barrier(
+                (far_p, received_p, received_q, panel_q, *state)
+            )
             pieces_p = gather(spread(lead_scale * (panel_p + far_p)))
-        if k == blocks - 2:
-            received_p, received_q, *state = lax.optimization_barrier((received_p, received_q, *state))
             own = scale * (kept_p + received_p), scale * (kept_q + received_q)
             own_top = jnp.concatenate([v[:SPLIT] for v in own], 0)
             far_top = lax.ppermute(own_top, "row", [(0, 1)])

time: 114 us -> 97.7 us (0.86)
  waiting for transfers between devices: 55.1 us -> 37.7 us
    ppermute x25, waiting for transfers between devices: 55.1 us -> 37.7 us  [swapped(): lax.ppermute(x, axis, [(i, i ^ mask) for i in range(lax.axis_size(axis))])]
    ppermute x25, starting transfers between devices: 23.2 us -> 24.4 us  [swapped(): lax.ppermute(x, axis, [(i, i ^ mask) for i in range(lax.axis_size(axis))])]
  transfers between devices with their start and end apart: 26 -> 26, of which waited for: 8 -> 9; matrix products, arithmetic and copies ran while one was open for 3% -> 3% of each run, Pallas kernels for 19% -> 23%
where the time goes in v8:
time: 97.7 us; the launch traced here: 97.5 us
  waiting for transfers between devices  37.7 us (39%)
  starting transfers between devices  27.8 us (28%)
  Pallas kernels  27.7 us (28%)
  local copies, waits for them, and re-layouts  1.93 us (2%)
  other arithmetic  1.81 us (2%)
    ppermute x25, waiting for transfers between devices, swapped(): lax.ppermute(x, axis, [(i, i ^ mask) for i in range(lax.axis_size(axis))])  37.7 us
    ppermute x25, starting transfers between devices, swapped(): lax.ppermute(x, axis, [(i, i ^ mask) for i in range(lax.axis_size(axis))])  24.4 us
    pallas_call x3, Pallas kernels, shards(): pl.pallas_call(functools.partial(next_kernel, k), out_shape=state_shapes,...  15 us
    pallas_call x1, Pallas kernels, shards(): pl.pallas_call(first_kernel, out_shape=state_shapes, in_specs=[smem] + [v...  6.98 us
    pallas_call x1, Pallas kernels, shards(): pl.pallas_call(last_kernel, out_shape=jax.ShapeDtypeStruct((height, width...  5.72 us
    ppermute x1, starting transfers between devices, shards(): far_top = lax.ppermute(own_top, 'row', [(0, 1)])  3.49 us
  transfers between devices with their start and end apart: 26, of which 9 were waited for; matrix products, arithmetic and copies ran while one was open for 3% of the time, Pallas kernels for 23%

profile of v8, /device:TPU:0, one launch (start us, length us, event | category | flops | bytes accessed | tf_op | source)
XLA Modules:
  0.0 97.5 jit_solution(18129591566000292029)
XLA Ops:
  0.0 3.1 %collective-permute-start = (f32[2,128]{1,0:T(2,128)}, f32[2,128]{1,0:T(2,128)S(1)}, u32[]{:S(2)}, u32[]{:S(2)}) collective-permute-start(f32[2,128]{1,0:T(2,128)} %param.5), channel_id=1, source_target_pairs={{0,8},{2,10},{4,12},{6,14},{8,0},{10,2},{12,4},{14,6},{16,24},{18,... | collective-permute-start | bytes 3080 | tf_op jit(solution)/shard_map/ppermute | solution.py:21
  3.1 1.1 %slice_bitcast_fusion = (f32[2,256,128]{2,1,0:T(8,128)S(1)}, f32[2,256,128]{2,1,0:T(8,128)S(1)}) fusion(f32[2,1,2,256,128]{4,3,2,0,1:T(8,128)} %bitcast.139), kind=kLoop, calls=%fused_computation.2 | loop fusion | bytes 1048576 | tf_op jit(solution)/shard_map/reshape;squeeze | solution.py:190
  4.2 2.7 %collective-permute-start.6 = (f32[2,256,128]{2,1,0:T(8,128)S(1)}, f32[2,256,128]{2,1,0:T(8,128)S(1)}, u32[]{:S(2)}, u32[]{:S(2)}) collective-permute-start(f32[2,256,128]{2,1,0:T(8,128)S(1)} %get-tuple-element.69), channel_id=1, source_target_pairs={{0,16},{2,18},{4,20},{6,22},{8,24},{10,26},{12,28},{14,30},{16,0},... | collective-permute-start | bytes 786440 | tf_op jit(solution)/shard_map/ppermute | solution.py:21
  6.8 1.5 %collective-permute-start.1 = (f32[2,256,128]{2,1,0:T(8,128)S(1)}, f32[2,256,128]{2,1,0:T(8,128)S(1)}, u32[]{:S(2)}, u32[]{:S(2)}) collective-permute-start(f32[2,256,128]{2,1,0:T(8,128)S(1)} %get-tuple-element.70), channel_id=1, source_target_pairs={{0,1},{1,0},{2,3},{3,2},{4,5},{5,4},{6,7},{7,6},{8,9},{9,8},{10,11... | collective-permute-start | bytes 786440 | tf_op jit(solution)/shard_map/ppermute | solution.py:21
  8.4 0.5 collective-permute-start.10
  9.0 0.0 copy-start.2
  9.0 0.7 copy-done.2
  9.7 0.1 pad_add_fusion.info
  9.8 0.0 collective-permute-done
  9.8 0.4 collective-permute-start.3
  10.2 8.3 %collective-permute-done.3 = f32[4,128]{1,0:T(4,128)S(1)} collective-permute-done((f32[4,128]{1,0:T(4,128)S(1)}, f32[4,128]{1,0:T(4,128)S(1)}, u32[]{:S(2)}, u32[]{:S(2)}) %collective-permute-start.3) | collective-permute-done | bytes 2080 | tf_op jit(solution)/shard_map/ppermute | solution.py:21
  18.5 0.0 collective-permute-done.10
  18.7 0.0 collective-permute-done.1
  18.7 0.1 add_multiply_fusion.3
  18.8 0.1 add_multiply_fusion.7
  19.0 0.1 collective-permute-start.2
  19.1 0.2 fusion.8
  19.3 1.6 %collective-permute-start.13 = (f32[256,128]{1,0:T(8,128)S(1)}, f32[256,128]{1,0:T(8,128)S(1)}, u32[]{:S(2)}, u32[]{:S(2)}) collective-permute-start(f32[256,128]{1,0:T(8,128)S(1)} %fusion.8), channel_id=1, source_target_pairs={{0,1},{1,0},{2,3},{3,2},{4,5},{5,4},{6,7},{7,6},{8,9},{9,8},{10,11... | collective-permute-start | bytes 393224 | tf_op jit(solution)/shard_map/ppermute | solution.py:21
  20.9 0.2 fusion.14
  21.1 2.1 %collective-permute-start.11 = (f32[256,128]{1,0:T(8,128)S(1)}, f32[256,128]{1,0:T(8,128)S(1)}, u32[]{:S(2)}, u32[]{:S(2)}) collective-permute-start(f32[256,128]{1,0:T(8,128)S(1)} %fusion.14), channel_id=1, source_target_pairs={{0,8},{2,10},{4,12},{6,14},{8,0},{10,2},{12,4},{14,6},{16,24},{18,... | collective-permute-start | bytes 393224 | tf_op jit(solution)/shard_map/ppermute | solution.py:21
  23.1 1.6 %collective-permute-done.13 = f32[256,128]{1,0:T(8,128)S(1)} collective-permute-done((f32[256,128]{1,0:T(8,128)S(1)}, f32[256,128]{1,0:T(8,128)S(1)}, u32[]{:S(2)}, u32[]{:S(2)}) %collective-permute-start.13) | collective-permute-done | bytes 131104 | tf_op jit(solution)/shard_map/ppermute | solution.py:21
  24.7 0.2 fusion.19
  24.9 1.8 %collective-permute-start.14 = (f32[256,128]{1,0:T(8,128)S(1)}, f32[256,128]{1,0:T(8,128)S(1)}, u32[]{:S(2)}, u32[]{:S(2)}) collective-permute-start(f32[256,128]{1,0:T(8,128)S(1)} %fusion.19), channel_id=1, source_target_pairs={{0,8},{2,10},{4,12},{6,14},{8,0},{10,2},{12,4},{14,6},{16,24},{18,... | collective-permute-start | bytes 393224 | tf_op jit(solution)/shard_map/ppermute | solution.py:21
  26.7 4.3 %collective-permute-done.11 = f32[256,128]{1,0:T(8,128)S(1)} collective-permute-done((f32[256,128]{1,0:T(8,128)S(1)}, f32[256,128]{1,0:T(8,128)S(1)}, u32[]{:S(2)}, u32[]{:S(2)}) %collective-permute-start.11) | collective-permute-done | bytes 131104 | tf_op jit(solution)/shard_map/ppermute | solution.py:21
  31.1 1.0 collective-permute-start.12
  32.0 1.5 %collective-permute-start.7 = (f32[2,256,128]{2,1,0:T(8,128)S(1)}, f32[2,256,128]{2,1,0:T(8,128)S(1)}, u32[]{:S(2)}, u32[]{:S(2)}) collective-permute-start(f32[2,256,128]{2,1,0:T(8,128)S(1)} %get-tuple-element.66), channel_id=1, source_target_pairs={{0,1},{1,0},{2,3},{3,2},{4,5},{5,4},{6,7},{7,6},{8,9},{9,8},{10,11... | collective-permute-start | bytes 786440 | tf_op jit(solution)/shard_map/ppermute | solution.py:21
  33.6 0.5 collective-permute-start.8
  34.1 4.4 %collective-permute-done.12 = f32[256,128]{1,0:T(8,128)S(1)} collective-permute-done((f32[256,128]{1,0:T(8,128)S(1)}, f32[256,128]{1,0:T(8,128)S(1)}, u32[]{:S(2)}, u32[]{:S(2)}) %collective-permute-start.12) | collective-permute-done | bytes 131104 | tf_op jit(solution)/shard_map/ppermute | solution.py:21
  38.5 0.1 collective-permute-start.15
  38.6 1.6 %collective-permute-start.16 = (f32[512,128]{1,0:T(8,128)S(1)}, f32[512,128]{1,0:T(8,128)S(1)}, u32[]{:S(2)}, u32[]{:S(2)}) collective-permute-start(f32[512,128]{1,0:T(8,128)S(1)} %maximum_multiply_fusion.refs_0_), channel_id=1, source_target_pairs={{0,4},{2,6},{4,0},{6,2},{8,12},{10,14},{12,8},{14,10},{16,20},{18,... | collective-permute-start | bytes 786440 | tf_op jit(solution)/shard_map/ppermute | solution.py:21
  40.2 0.0 collective-permute-done.2
  40.2 0.1 fusion.5
  40.3 0.1 collective-permute-start.4
  40.4 0.1 collective-permute-done.7
  40.5 2.8 %collective-permute-start.5 = (f32[512,128]{1,0:T(8,128)S(1)}, f32[512,128]{1,0:T(8,128)S(1)}, u32[]{:S(2)}, u32[]{:S(2)}) collective-permute-start(f32[512,128]{1,0:T(8,128)S(1)} %get-tuple-element.71), channel_id=1, source_target_pairs={{0,16},{2,18},{4,20},{6,22},{8,24},{10,26},{12,28},{14,30},{16,0},... | collective-permute-start | bytes 786440 | tf_op jit(solution)/shard_map/ppermute | solution.py:21
  43.3 0.2 select_multiply_fusion.1
  43.5 0.1 add_multiply_fusion.5
  43.6 3.7 %collective-permute-done.16.refs_2_ = f32[512,128]{1,0:T(8,128)S(1)} collective-permute-done((f32[512,128]{1,0:T(8,128)S(1)}, f32[512,128]{1,0:T(8,128)S(1)}, u32[]{:S(2)}, u32[]{:S(2)}) %collective-permute-start.16) | collective-permute-done | bytes 262176 | tf_op jit(solution)/shard_map/ppermute | solution.py:21
  47.3 0.0 collective-permute-start.17
  47.3 0.1 pad_maximum_fusion.1
  47.4 0.1 collective-permute-start.9
  47.5 0.0 collective-permute-done.15.refs_1_
  47.5 1.3 %collective-permute-done.17.refs_3_ = f32[512,128]{1,0:T(8,128)S(1)} collective-permute-done((f32[512,128]{1,0:T(8,128)S(1)}, f32[512,128]{1,0:T(8,128)S(1)}, u32[]{:S(2)}, u32[]{:S(2)}) %collective-permute-start.17) | collective-permute-done | bytes 262176 | tf_op jit(solution)/shard_map/ppermute | solution.py:21
  48.8 7.0 %eliminate_0.1 = (f32[4,512,128]{2,1,0:T(8,128)S(1)}, f32[4,512,128]{2,1,0:T(8,128)S(1)}, f32[512,128]{1,0:T(8,128)S(1)}) custom-call(s32[4]{0:T(128)S(1)} %pad_add_fusion.info, f32[512,128]{1,0:T(8,128)S(1)} %maximum_multiply_fusion.refs_0_, f32[512,128]{1,0:T(8,128)S(1)} %collective-permute-done.15.refs_1_, ...), custom_call_target="tpu_custom_call" | custom-call | flops 4000000000 | bytes 12000000 | tf_op jit(solution)/shard_map/eliminate_0/pallas_call | solution.py:288
  55.8 11.5 %collective-permute-done.9 = f32[512,128]{1,0:T(8,128)S(1)} collective-permute-done((f32[512,128]{1,0:T(8,128)S(1)}, f32[512,128]{1,0:T(8,128)S(1)}, u32[]{:S(2)}, u32[]{:S(2)}) %collective-permute-start.9) | collective-permute-done | bytes 262176 | tf_op jit(solution)/shard_map/ppermute | solution.py:21
  67.4 0.1 collective-permute-start.21
  67.4 1.6 %collective-permute-start.23 = (f32[512,128]{1,0:T(8,128)S(1)}, f32[512,128]{1,0:T(8,128)S(1)}, u32[]{:S(2)}, u32[]{:S(2)}) collective-permute-start(f32[512,128]{1,0:T(8,128)S(1)} %add_multiply_fusion.2.refs_3_), channel_id=1, source_target_pairs={{0,4},{2,6},{4,0},{6,2},{8,12},{10,14},{12,8},{14,10},{16,20},{18,... | collective-permute-start | bytes 786440 | tf_op jit(solution)/shard_map/ppermute | solution.py:21
  69.1 0.1 collective-permute-start.18
  69.2 5.8 %shard_map.37 = (f32[4,512,128]{2,1,0:T(8,128)S(1)}, f32[4,512,128]{2,1,0:T(8,128)S(1)}, f32[512,128]{1,0:T(8,128)S(1)}) custom-call(f32[4,512,128]{2,1,0:T(8,128)S(1)} %get-tuple-element.39.old_work, f32[4,512,128]{2,1,0:T(8,128)S(1)} %get-tuple-element.40.old_packed, ...), custom_call_target="tpu_custom_call", output_to_operand_aliasing={{0}: (0, {}), {1}: (1, {}), {2}: (2, {})} | custom-call | flops 4000000000 | bytes 12000000 | tf_op jit(solution)/shard_map/pallas_call | solution.py:305
  75.0 0.0 collective-permute-done.4
  75.0 0.0 collective-permute-done.5
  75.0 2.5 %collective-permute-done.18 = f32[512,128]{1,0:T(8,128)S(1)} collective-permute-done((f32[512,128]{1,0:T(8,128)S(1)}, f32[512,128]{1,0:T(8,128)S(1)}, u32[]{:S(2)}, u32[]{:S(2)}) %collective-permute-start.18) | collective-permute-done | bytes 262176 | tf_op jit(solution)/shard_map/ppermute | solution.py:21
  77.5 0.1 collective-permute-start.20
  77.6 0.6 collective-permute-start.22
  78.2 0.1 fusion.3
  78.4 3.5 %collective-permute-start.19 = (f32[512,128]{1,0:T(8,128)S(1)}, f32[512,128]{1,0:T(8,128)S(1)}, u32[]{:S(2)}, u32[]{:S(2)}) collective-permute-start(f32[512,128]{1,0:T(8,128)S(1)} %pad_maximum_fusion.3), channel_id=1, source_target_pairs={{0,1},{2,3},{4,5},{6,7},{8,9},{10,11},{12,13},{14,15},{16,17},{18,... | collective-permute-start | bytes 786440 | tf_op jit(solution)/shard_map/ppermute | solution.py:321
  81.9 0.1 collective-permute-start.25
  82.0 4.7 %shard_map.38 = (f32[4,512,128]{2,1,0:T(8,128)S(1)}, f32[4,512,128]{2,1,0:T(8,128)S(1)}, f32[512,128]{1,0:T(8,128)S(1)}) custom-call(f32[4,512,128]{2,1,0:T(8,128)S(1)} %get-tuple-element.47.old_work, f32[4,512,128]{2,1,0:T(8,128)S(1)} %get-tuple-element.48.old_packed, ...), custom_call_target="tpu_custom_call", output_to_operand_aliasing={{0}: (0, {}), {1}: (1, {}), {2}: (2, {})} | custom-call | flops 4000000000 | bytes 12000000 | tf_op jit(solution)/shard_map/pallas_call | solution.py:305
  86.7 0.6 collective-permute-start.24
  87.3 4.4 %shard_map.39 = (f32[4,512,128]{2,1,0:T(8,128)S(1)}, f32[4,512,128]{2,1,0:T(8,128)S(1)}, f32[512,128]{1,0:T(8,128)S(1)}) custom-call(f32[4,512,128]{2,1,0:T(8,128)S(1)} %get-tuple-element.50.old_work, f32[4,512,128]{2,1,0:T(8,128)S(1)} %get-tuple-element.51.old_packed, ...), custom_call_target="tpu_custom_call", output_to_operand_aliasing={{0}: (0, {}), {1}: (1, {}), {2}: (2, {})} | custom-call | flops 4000000000 | bytes 12000000 | tf_op jit(solution)/shard_map/pallas_call | solution.py:305
  91.7 0.0 collective-permute-done.19
  91.8 0.0 collective-permute-done.20.refs_4_
  91.8 0.0 collective-permute-done.25.refs_9_
  91.8 5.7 %own_columns.1 = f32[1024,128]{1,0:T(8,128)} custom-call(s32[4]{0:T(128)S(1)} %pad_add_fusion.info, f32[4,512,128]{2,1,0:T(8,128)S(1)} %get-tuple-element.56.work, f32[4,512,128]{2,1,0:T(8,128)S(1)} %get-tuple-element.57.packed, f32[512,128]{1,0:T(8,128)S(1)} %get-tuple-element.58.inverted, f32[512,128]{1,0:T(8,128)S(1)} %broadcast_select_fusion.own_top, ...), custom_call_target="tpu_custom_call" | custom-call | flops 4000000000 | bytes 12000000 | tf_op jit(solution)/shard_map/own_columns/pallas_call | solution.py:326
  (49 shorter events, 0.5 us)
Async XLA Ops:
  0.0 9.8 %collective-permute-start = (f32[2,128]{1,0:T(2,128)}, f32[2,128]{1,0:T(2,128)S(1)}, u32[]{:S(2)}, u32[]{:S(2)}) collective-permute-start(f32[2,128]{1,0:T(2,128)} %param.5), channel_id=1, source_target_pairs={{0,8},{2,10},{4,12},{6,14},{8,0},{10,2},{12,4},{14,6},{16,24},{18,... | collective-permute-start | bytes 3080 | tf_op jit(solution)/shard_map/ppermute | solution.py:21
  3.1 5.3 %copy-start.1 = (f32[2,1024]{1,0:T(2,128)S(1)}, f32[2,1024]{1,0:T(2,128)}, u32[]{:S(2)}) copy-start(f32[2,1024]{1,0:T(2,128)} %param.4) | copy-start | bytes 24580
  3.1 15.6 %copy-start = (f32[1024,128]{1,0:T(8,128)S(1)}, f32[1024,128]{1,0:T(8,128)}, u32[]{:S(2)}) copy-start(f32[1024,128]{1,0:T(8,128)} %param.3) | copy-start | bytes 1572868
  4.2 14.5 %collective-permute-start.6 = (f32[2,256,128]{2,1,0:T(8,128)S(1)}, f32[2,256,128]{2,1,0:T(8,128)S(1)}, u32[]{:S(2)}, u32[]{:S(2)}) collective-permute-start(f32[2,256,128]{2,1,0:T(8,128)S(1)} %get-tuple-element.69), channel_id=1, source_target_pairs={{0,16},{2,18},{4,20},{6,22},{8,24},{10,26},{12,28},{14,30},{16,0},... | collective-permute-start | bytes 786440 | tf_op jit(solution)/shard_map/ppermute | solution.py:21
  6.8 11.8 %collective-permute-start.1 = (f32[2,256,128]{2,1,0:T(8,128)S(1)}, f32[2,256,128]{2,1,0:T(8,128)S(1)}, u32[]{:S(2)}, u32[]{:S(2)}) collective-permute-start(f32[2,256,128]{2,1,0:T(8,128)S(1)} %get-tuple-element.70), channel_id=1, source_target_pairs={{0,1},{1,0},{2,3},{3,2},{4,5},{5,4},{6,7},{7,6},{8,9},{9,8},{10,11... | collective-permute-start | bytes 786440 | tf_op jit(solution)/shard_map/ppermute | solution.py:21
  8.4 10.2 %collective-permute-start.10 = (f32[2,1024]{1,0:T(2,128)S(1)}, f32[2,1024]{1,0:T(2,128)S(1)}, u32[]{:S(2)}, u32[]{:S(2)}) collective-permute-start(f32[2,1024]{1,0:T(2,128)S(1)} %copy-done.1), channel_id=1, source_target_pairs={{0,1},{1,0},{2,3},{3,2},{4,5},{5,4},{6,7},{7,6},{8,9},{9,8},{10,11... | collective-permute-start | bytes 24584 | tf_op jit(solution)/shard_map/ppermute | solution.py:21
  9.0 0.7 copy-start.2
  9.8 8.7 %collective-permute-start.3 = (f32[4,128]{1,0:T(4,128)S(1)}, f32[4,128]{1,0:T(4,128)S(1)}, u32[]{:S(2)}, u32[]{:S(2)}) collective-permute-start(f32[4,128]{1,0:T(4,128)S(1)} %pad_maximum_fusion.4), channel_id=1, source_target_pairs={{0,16},{2,18},{4,20},{6,22},{8,24},{10,26},{12,28},{14,30},{16,0},... | collective-permute-start | bytes 6152 | tf_op jit(solution)/shard_map/ppermute | solution.py:21
  19.0 21.2 %collective-permute-start.2 = (f32[2,256,128]{2,1,0:T(8,128)S(1)}, f32[2,256,128]{2,1,0:T(8,128)S(1)}, u32[]{:S(2)}, u32[]{:S(2)}) collective-permute-start(f32[2,256,128]{2,1,0:T(8,128)S(1)} %pad_maximum_fusion), channel_id=1, source_target_pairs={{0,8},{2,10},{4,12},{6,14},{8,0},{10,2},{12,4},{14,6},{16,24},{18,... | collective-permute-start | bytes 786440 | tf_op jit(solution)/shard_map/ppermute | solution.py:21
  19.3 5.5 %collective-permute-start.13 = (f32[256,128]{1,0:T(8,128)S(1)}, f32[256,128]{1,0:T(8,128)S(1)}, u32[]{:S(2)}, u32[]{:S(2)}) collective-permute-start(f32[256,128]{1,0:T(8,128)S(1)} %fusion.8), channel_id=1, source_target_pairs={{0,1},{1,0},{2,3},{3,2},{4,5},{5,4},{6,7},{7,6},{8,9},{9,8},{10,11... | collective-permute-start | bytes 393224 | tf_op jit(solution)/shard_map/ppermute | solution.py:21
  21.1 10.0 %collective-permute-start.11 = (f32[256,128]{1,0:T(8,128)S(1)}, f32[256,128]{1,0:T(8,128)S(1)}, u32[]{:S(2)}, u32[]{:S(2)}) collective-permute-start(f32[256,128]{1,0:T(8,128)S(1)} %fusion.14), channel_id=1, source_target_pairs={{0,8},{2,10},{4,12},{6,14},{8,0},{10,2},{12,4},{14,6},{16,24},{18,... | collective-permute-start | bytes 393224 | tf_op jit(solution)/shard_map/ppermute | solution.py:21
  24.9 9.1 %collective-permute-start.14 = (f32[256,128]{1,0:T(8,128)S(1)}, f32[256,128]{1,0:T(8,128)S(1)}, u32[]{:S(2)}, u32[]{:S(2)}) collective-permute-start(f32[256,128]{1,0:T(8,128)S(1)} %fusion.19), channel_id=1, source_target_pairs={{0,8},{2,10},{4,12},{6,14},{8,0},{10,2},{12,4},{14,6},{16,24},{18,... | collective-permute-start | bytes 393224 | tf_op jit(solution)/shard_map/ppermute | solution.py:21
  31.1 7.4 %collective-permute-start.12 = (f32[256,128]{1,0:T(8,128)S(1)}, f32[256,128]{1,0:T(8,128)S(1)}, u32[]{:S(2)}, u32[]{:S(2)}) collective-permute-start(f32[256,128]{1,0:T(8,128)S(1)} %add.89), channel_id=1, source_target_pairs={{0,16},{2,18},{4,20},{6,22},{8,24},{10,26},{12,28},{14,30},{16,0},... | collective-permute-start | bytes 393224 | tf_op jit(solution)/shard_map/ppermute | solution.py:21
  32.0 8.4 %collective-permute-start.7 = (f32[2,256,128]{2,1,0:T(8,128)S(1)}, f32[2,256,128]{2,1,0:T(8,128)S(1)}, u32[]{:S(2)}, u32[]{:S(2)}) collective-permute-start(f32[2,256,128]{2,1,0:T(8,128)S(1)} %get-tuple-element.66), channel_id=1, source_target_pairs={{0,1},{1,0},{2,3},{3,2},{4,5},{5,4},{6,7},{7,6},{8,9},{9,8},{10,11... | collective-permute-start | bytes 786440 | tf_op jit(solution)/shard_map/ppermute | solution.py:21
  33.6 9.7 %collective-permute-start.8 = (f32[2,256,128]{2,1,0:T(8,128)S(1)}, f32[2,256,128]{2,1,0:T(8,128)S(1)}, u32[]{:S(2)}, u32[]{:S(2)}) collective-permute-start(f32[2,256,128]{2,1,0:T(8,128)S(1)} %get-tuple-element.67), channel_id=1, source_target_pairs={{0,1},{1,0},{2,3},{3,2},{4,5},{5,4},{6,7},{7,6},{8,9},{9,8},{10,11... | collective-permute-start | bytes 786440 | tf_op jit(solution)/shard_map/ppermute | solution.py:21
  38.5 9.0 %collective-permute-start.15 = (f32[512,128]{1,0:T(8,128)S(1)}, f32[512,128]{1,0:T(8,128)S(1)}, u32[]{:S(2)}, u32[]{:S(2)}) collective-permute-start(f32[512,128]{1,0:T(8,128)S(1)} %maximum_multiply_fusion.refs_0_), channel_id=1, source_target_pairs={{0,2},{2,0},{4,6},{6,4},{8,10},{10,8},{12,14},{14,12},{16,18},{18,... | collective-permute-start | bytes 786440 | tf_op jit(solution)/shard_map/ppermute | solution.py:21
  38.6 8.7 %collective-permute-start.16 = (f32[512,128]{1,0:T(8,128)S(1)}, f32[512,128]{1,0:T(8,128)S(1)}, u32[]{:S(2)}, u32[]{:S(2)}) collective-permute-start(f32[512,128]{1,0:T(8,128)S(1)} %maximum_multiply_fusion.refs_0_), channel_id=1, source_target_pairs={{0,4},{2,6},{4,0},{6,2},{8,12},{10,14},{12,8},{14,10},{16,20},{18,... | collective-permute-start | bytes 786440 | tf_op jit(solution)/shard_map/ppermute | solution.py:21
  40.3 34.7 %collective-permute-start.4 = (f32[512,128]{1,0:T(8,128)S(1)}, f32[512,128]{1,0:T(8,128)S(1)}, u32[]{:S(2)}, u32[]{:S(2)}) collective-permute-start(f32[512,128]{1,0:T(8,128)S(1)} %get-tuple-element.72), channel_id=1, source_target_pairs={{0,16},{2,18},{4,20},{6,22},{8,24},{10,26},{12,28},{14,30},{16,0},... | collective-permute-start | bytes 786440 | tf_op jit(solution)/shard_map/ppermute | solution.py:21
  40.5 34.5 %collective-permute-start.5 = (f32[512,128]{1,0:T(8,128)S(1)}, f32[512,128]{1,0:T(8,128)S(1)}, u32[]{:S(2)}, u32[]{:S(2)}) collective-permute-start(f32[512,128]{1,0:T(8,128)S(1)} %get-tuple-element.71), channel_id=1, source_target_pairs={{0,16},{2,18},{4,20},{6,22},{8,24},{10,26},{12,28},{14,30},{16,0},... | collective-permute-start | bytes 786440 | tf_op jit(solution)/shard_map/ppermute | solution.py:21
  47.3 1.5 %collective-permute-start.17 = (f32[512,128]{1,0:T(8,128)S(1)}, f32[512,128]{1,0:T(8,128)S(1)}, u32[]{:S(2)}, u32[]{:S(2)}) collective-permute-start(f32[512,128]{1,0:T(8,128)S(1)} %collective-permute-done.16.refs_2_), channel_id=1, source_target_pairs={{0,2},{2,0},{4,6},{6,4},{8,10},{10,8},{12,14},{14,12},{16,18},{18,... | collective-permute-start | bytes 786440 | tf_op jit(solution)/shard_map/ppermute | solution.py:21
  47.4 19.9 %collective-permute-start.9 = (f32[512,128]{1,0:T(8,128)S(1)}, f32[512,128]{1,0:T(8,128)S(1)}, u32[]{:S(2)}, u32[]{:S(2)}) collective-permute-start(f32[512,128]{1,0:T(8,128)S(1)} %add_multiply_fusion.4), channel_id=1, source_target_pairs={{0,8},{2,10},{4,12},{6,14},{8,0},{10,2},{12,4},{14,6},{16,24},{18,... | collective-permute-start | bytes 786440 | tf_op jit(solution)/shard_map/ppermute | solution.py:21
  67.4 24.4 %collective-permute-start.21 = (f32[512,128]{1,0:T(8,128)S(1)}, f32[512,128]{1,0:T(8,128)S(1)}, u32[]{:S(2)}, u32[]{:S(2)}) collective-permute-start(f32[512,128]{1,0:T(8,128)S(1)} %add_multiply_fusion.2.refs_3_), channel_id=1, source_target_pairs={{0,2},{2,0},{4,6},{6,4},{8,10},{10,8},{12,14},{14,12},{16,18},{18,... | collective-permute-start | bytes 786440 | tf_op jit(solution)/shard_map/ppermute | solution.py:21
  67.4 14.4 %collective-permute-start.23 = (f32[512,128]{1,0:T(8,128)S(1)}, f32[512,128]{1,0:T(8,128)S(1)}, u32[]{:S(2)}, u32[]{:S(2)}) collective-permute-start(f32[512,128]{1,0:T(8,128)S(1)} %add_multiply_fusion.2.refs_3_), channel_id=1, source_target_pairs={{0,4},{2,6},{4,0},{6,2},{8,12},{10,14},{12,8},{14,10},{16,20},{18,... | collective-permute-start | bytes 786440 | tf_op jit(solution)/shard_map/ppermute | solution.py:21
  69.1 8.4 %collective-permute-start.18 = (f32[512,128]{1,0:T(8,128)S(1)}, f32[512,128]{1,0:T(8,128)S(1)}, u32[]{:S(2)}, u32[]{:S(2)}) collective-permute-start(f32[512,128]{1,0:T(8,128)S(1)} %broadcast_multiply_fusion), channel_id=1, source_target_pairs={{0,8},{2,10},{4,12},{6,14},{8,0},{10,2},{12,4},{14,6},{16,24},{18,... | collective-permute-start | bytes 786440 | tf_op jit(solution)/shard_map/ppermute | solution.py:21
  77.5 14.2 %collective-permute-start.20 = (f32[512,128]{1,0:T(8,128)S(1)}, f32[512,128]{1,0:T(8,128)S(1)}, u32[]{:S(2)}, u32[]{:S(2)}) collective-permute-start(f32[512,128]{1,0:T(8,128)S(1)} %add_multiply_fusion.refs_2_), channel_id=1, source_target_pairs={{0,2},{2,0},{4,6},{6,4},{8,10},{10,8},{12,14},{14,12},{16,18},{18,... | collective-permute-start | bytes 786440 | tf_op jit(solution)/shard_map/ppermute | solution.py:21
  77.6 9.1 %collective-permute-start.22 = (f32[512,128]{1,0:T(8,128)S(1)}, f32[512,128]{1,0:T(8,128)S(1)}, u32[]{:S(2)}, u32[]{:S(2)}) collective-permute-start(f32[512,128]{1,0:T(8,128)S(1)} %add_multiply_fusion.refs_2_), channel_id=1, source_target_pairs={{0,4},{2,6},{4,0},{6,2},{8,12},{10,14},{12,8},{14,10},{16,20},{18,... | collective-permute-start | bytes 786440 | tf_op jit(solution)/shard_map/ppermute | solution.py:21
  78.4 13.3 %collective-permute-start.19 = (f32[512,128]{1,0:T(8,128)S(1)}, f32[512,128]{1,0:T(8,128)S(1)}, u32[]{:S(2)}, u32[]{:S(2)}) collective-permute-start(f32[512,128]{1,0:T(8,128)S(1)} %pad_maximum_fusion.3), channel_id=1, source_target_pairs={{0,1},{2,3},{4,5},{6,7},{8,9},{10,11},{12,13},{14,15},{16,17},{18,... | collective-permute-start | bytes 786440 | tf_op jit(solution)/shard_map/ppermute | solution.py:321
  81.9 9.9 %collective-permute-start.25 = (f32[512,128]{1,0:T(8,128)S(1)}, f32[512,128]{1,0:T(8,128)S(1)}, u32[]{:S(2)}, u32[]{:S(2)}) collective-permute-start(f32[512,128]{1,0:T(8,128)S(1)} %collective-permute-done.23.refs_7_), channel_id=1, source_target_pairs={{0,2},{2,0},{4,6},{6,4},{8,10},{10,8},{12,14},{14,12},{16,18},{18,... | collective-permute-start | bytes 786440 | tf_op jit(solution)/shard_map/ppermute | solution.py:21
  86.7 5.1 %collective-permute-start.24 = (f32[512,128]{1,0:T(8,128)S(1)}, f32[512,128]{1,0:T(8,128)S(1)}, u32[]{:S(2)}, u32[]{:S(2)}) collective-permute-start(f32[512,128]{1,0:T(8,128)S(1)} %collective-permute-done.22.refs_6_), channel_id=1, source_target_pairs={{0,2},{2,0},{4,6},{6,4},{8,10},{10,8},{12,14},{14,12},{16,18},{18,... | collective-permute-start | bytes 786440 | tf_op jit(solution)/shard_map/ppermute | solution.py:21

commit v9 on v6

--- a/solution.py
+++ b/solution.py
@@ -191,7 +191,7 @@
 
     rows_p, rows_q = parts_of(matrix)
     other_p = swapped(rows_p, "row", 1)
-    far_q = swapped(rows_q, "col", high)
+    near_q = swapped(rows_q, "col", low)
     other_rows = swapped(row_diag, "row", 1)
     pair = jnp.concatenate([col_diag, swapped(col_diag, "col", low)], 0)
     far_pair = swapped(pair, "col", high)
@@ -227,15 +227,15 @@
         scale1 = first_scales[1][part][0, :SPLIT, None]
         return 0.5 * scale1 * (scale0[0] * values[0][:SPLIT] + scale0[1] * values[1][:SPLIT])
 
-    first_q = jnp.where(in_high, far_q, rows_q)
-    second_q = jnp.where(in_high, rows_q, far_q)
+    even_q = jnp.where(in_low, near_q, rows_q)
+    odd_q = jnp.where(in_low, rows_q, near_q)
     lead_own = lead_mixed(0, [rows_p[i, :SPLIT] + other_p[i, :SPLIT] for i in range(2)])
     lead_own = (0.5 * diag_of(none, in_low)[0]) * lead_own
-    lead_bit = lead_mixed(1, of_bit((first_q[:, :SPLIT], second_q[:, :SPLIT]), none, none))
-    lead_p = lead_own + swapped(lead_own, "col", low)
-    lead_q = lead_bit + swapped(lead_bit, "row", 1)
-    far_lead = swapped(lead_p, "col", high)
-    near_lead = swapped(lead_q, "col", low)
+    lead_half = lead_mixed(1, of_half((even_q[:, :SPLIT], odd_q[:, :SPLIT]), none, none))
+    lead_p = lead_own + swapped(lead_own, "col", high)
+    lead_q = lead_half + swapped(lead_half, "row", 1)
+    near_lead = swapped(lead_p, "col", low)
+    far_lead = swapped(lead_q, "col", high)
 
     def spread(values):
         for bit in range(block_bits, high_bit - 1):
@@ -251,22 +251,18 @@
         return [pieces[n] for n in range(blocks)]
 
     lead_scale = diag_of(none, none)[1]
-    lead = lead_scale * jnp.concatenate([lead_p + far_lead, lead_q + near_lead], 0)
+    lead = lead_scale * jnp.concatenate([lead_p + near_lead, lead_q + far_lead], 0)
     lead_pieces = gather(spread(lead))
-
-    own_p = jnp.stack(own_mixed(0, rows_p, other_p))
-    near_p = swapped(own_p, "col", low)
-    other_q = swapped(first_q, "row", 1), swapped(second_q, "row", 1)
 
     def flat(values):
         return values.reshape(2 * part_rows, width)
 
-    parts_p = flat(jnp.where(in_low, near_p, own_p)), flat(jnp.where(in_low, own_p, near_p))
-    parts_q = [flat(jnp.stack(own_mixed(1, a, b))) for a, b in zip((first_q, second_q), other_q)]
-    panel_p = of_half(parts_p, none, none)
-    panel_q = of_bit(parts_q, none, none)
-    far_p = swapped(panel_p, "col", high)
-    near_q = swapped(panel_q, "col", low)
+    own_p = jnp.stack(own_mixed(0, rows_p, other_p))
+    far_own = swapped(own_p, "col", high)
+    other_q = swapped(even_q, "row", 1), swapped(odd_q, "row", 1)
+    parts_p = flat(jnp.where(in_high, far_own, own_p)), flat(jnp.where(in_high, own_p, far_own))
+    panel_p = of_bit(parts_p, none, none)
+    near_p = swapped(panel_p, "col", low)
 
     info = jnp.stack(
         [
@@ -292,12 +288,17 @@
         compiler_params=params,
         name="eliminate_0",
     )(info, *lead_pieces)
-    far_p, near_q, parts_p, parts_q, *state = lax.optimization_barrier((far_p, near_q, parts_p, parts_q, *state))
-    pieces_p = gather(spread(lead_scale * (panel_p + far_p)))
-    pieces_q = gather(spread(lead_scale * (panel_q + near_q)))
-    kept_p, kept_q = of_half(parts_p, in_high, in_low), of_bit(parts_q, in_high, in_low)
-    received_p = swapped(of_half(parts_p, ~in_high, in_low), "col", high)
-    received_q = swapped(of_bit(parts_q, in_high, ~in_low), "col", low)
+    near_p, parts_p, even_q, odd_q, other_q, *state = lax.optimization_barrier(
+        (near_p, parts_p, even_q, odd_q, other_q, *state)
+    )
+    parts_q = [flat(jnp.stack(own_mixed(1, a, b))) for a, b in zip((even_q, odd_q), other_q)]
+    panel_q = of_half(parts_q, none, none)
+    far_q = swapped(panel_q, "col", high)
+    received_q = swapped(of_half(parts_q, ~in_high, in_low), "col", high)
+    panel_p = spread(lead_scale * (panel_p + near_p))
+    pieces_p = gather(panel_p)
+    kept_p, kept_q = of_bit(parts_p, in_high, in_low), of_half(parts_q, in_high, in_low)
+    received_p = swapped(of_bit(parts_p, in_high, ~in_low), "col", low)
     scale = diag_of(in_high, in_low)[1]
 
     for k in range(1, blocks):
@@ -311,7 +312,10 @@
             compiler_params=params,
         )(*state)
         if k == blocks - 2:
-            received_p, received_q, *state = lax.optimization_barrier((received_p, received_q, *state))
+            far_q, received_p, received_q, _, *state = lax.optimization_barrier(
+                (far_q, received_p, received_q, panel_p, *state)
+            )
+            pieces_q = gather(spread(lead_scale * (panel_q + far_q)))
             own = scale * (kept_p + received_p), scale * (kept_q + received_q)
             own_top = jnp.concatenate([v[:SPLIT] for v in own], 0)
             far_top = lax.ppermute(own_top, "row", [(0, 1)])

time: 93.8 us -> 97 us (1.034)
  starting transfers between devices: 27.2 us -> 34.5 us
  waiting for transfers between devices: 34.5 us -> 29.8 us
    ppermute x25, starting transfers between devices: 23.6 us -> 29.5 us  [swapped(): lax.ppermute(x, axis, [(i, i ^ mask) for i in range(lax.axis_size(axis))])]
    ppermute x25, waiting for transfers between devices: 34.5 us -> 29.8 us  [swapped(): lax.ppermute(x, axis, [(i, i ^ mask) for i in range(lax.axis_size(axis))])]
    ppermute x1, starting transfers between devices: 3.66 us -> 5.04 us  [shards(): far_top = lax.ppermute(own_top, 'row', [(0, 1)])]
  transfers between devices with their start and end apart: 26 -> 26, of which waited for: 11 -> 12; matrix products, arithmetic and copies ran while one was open for 3% -> 3% of each run, Pallas kernels for 23% -> 23%
where the time goes in v9:
time: 97 us; the launch traced here: 96.2 us
  starting transfers between devices  34.5 us (36%)
  waiting for transfers between devices  29.8 us (31%)
  Pallas kernels  27.7 us (29%)
  local copies, waits for them, and re-layouts  1.93 us (2%)
  other arithmetic  1.78 us (2%)
    ppermute x25, waiting for transfers between devices, swapped(): lax.ppermute(x, axis, [(i, i ^ mask) for i in range(lax.axis_size(axis))])  29.8 us
    ppermute x25, starting transfers between devices, swapped(): lax.ppermute(x, axis, [(i, i ^ mask) for i in range(lax.axis_size(axis))])  29.5 us
    pallas_call x3, Pallas kernels, shards(): pl.pallas_call(functools.partial(next_kernel, k), out_shape=state_shapes,...  15 us
    pallas_call x1, Pallas kernels, shards(): pl.pallas_call(first_kernel, out_shape=state_shapes, in_specs=[smem] + [v...  6.98 us
    pallas_call x1, Pallas kernels, shards(): pl.pallas_call(last_kernel, out_shape=jax.ShapeDtypeStruct((height, width...  5.73 us
    ppermute x1, starting transfers between devices, shards(): far_top = lax.ppermute(own_top, 'row', [(0, 1)])  5.04 us
  transfers between devices with their start and end apart: 26, of which 12 were waited for; matrix products, arithmetic and copies ran while one was open for 3% of the time, Pallas kernels for 23%

profile of v9, /device:TPU:0, one launch (start us, length us, event | category | flops | bytes accessed | tf_op | source)
XLA Modules:
  0.0 96.2 jit_solution(8694741238081619602)
XLA Ops:
  0.0 3.1 %collective-permute-start = (f32[2,128]{1,0:T(2,128)}, f32[2,128]{1,0:T(2,128)S(1)}, u32[]{:S(2)}, u32[]{:S(2)}) collective-permute-start(f32[2,128]{1,0:T(2,128)} %param.5), channel_id=1, source_target_pairs={{0,8},{2,10},{4,12},{6,14},{8,0},{10,2},{12,4},{14,6},{16,24},{18,... | collective-permute-start | bytes 3080 | tf_op jit(solution)/shard_map/ppermute | solution.py:21
  3.1 1.1 %slice_bitcast_fusion = (f32[2,256,128]{2,1,0:T(8,128)S(1)}, f32[2,256,128]{2,1,0:T(8,128)S(1)}) fusion(f32[2,1,2,256,128]{4,3,2,0,1:T(8,128)} %bitcast.139), kind=kLoop, calls=%fused_computation.2 | loop fusion | bytes 1048576 | tf_op jit(solution)/shard_map/reshape;squeeze | solution.py:190
  4.2 0.1 collective-permute-start.5
  4.3 2.0 %collective-permute-start.2 = (f32[2,256,128]{2,1,0:T(8,128)S(1)}, f32[2,256,128]{2,1,0:T(8,128)S(1)}, u32[]{:S(2)}, u32[]{:S(2)}) collective-permute-start(f32[2,256,128]{2,1,0:T(8,128)S(1)} %get-tuple-element.80), channel_id=1, source_target_pairs={{0,1},{1,0},{2,3},{3,2},{4,5},{5,4},{6,7},{7,6},{8,9},{9,8},{10,11... | collective-permute-start | bytes 786440 | tf_op jit(solution)/shard_map/ppermute | solution.py:21
  6.2 0.1 collective-permute-start.8
  6.5 0.0 copy-start.2
  6.5 0.7 copy-done.2
  7.2 0.1 pad_add_fusion.info
  7.3 3.0 %collective-permute-start.1 = (f32[4,128]{1,0:T(4,128)S(1)}, f32[4,128]{1,0:T(4,128)S(1)}, u32[]{:S(2)}, u32[]{:S(2)}) collective-permute-start(f32[4,128]{1,0:T(4,128)S(1)} %pad_maximum_fusion.4), channel_id=1, source_target_pairs={{0,16},{2,18},{4,20},{6,22},{8,24},{10,26},{12,28},{14,30},{16,0},... | collective-permute-start | bytes 6152 | tf_op jit(solution)/shard_map/ppermute | solution.py:21
  10.3 1.7 %collective-permute-done.1 = f32[4,128]{1,0:T(4,128)S(1)} collective-permute-done((f32[4,128]{1,0:T(4,128)S(1)}, f32[4,128]{1,0:T(4,128)S(1)}, u32[]{:S(2)}, u32[]{:S(2)}) %collective-permute-start.1) | collective-permute-done | bytes 2080 | tf_op jit(solution)/shard_map/ppermute | solution.py:21
  12.0 0.2 collective-permute-done.8
  12.4 0.0 collective-permute-done.5
  12.4 0.0 collective-permute-done.2
  12.4 0.1 multiply_add_fusion
  12.5 0.2 fusion.8
  12.7 1.7 %collective-permute-start.11 = (f32[256,128]{1,0:T(8,128)S(1)}, f32[256,128]{1,0:T(8,128)S(1)}, u32[]{:S(2)}, u32[]{:S(2)}) collective-permute-start(f32[256,128]{1,0:T(8,128)S(1)} %fusion.8), channel_id=1, source_target_pairs={{0,1},{1,0},{2,3},{3,2},{4,5},{5,4},{6,7},{7,6},{8,9},{9,8},{10,11... | collective-permute-start | bytes 393224 | tf_op jit(solution)/shard_map/ppermute | solution.py:21
  14.4 0.2 fusion.14
  14.6 2.7 %collective-permute-start.9 = (f32[256,128]{1,0:T(8,128)S(1)}, f32[256,128]{1,0:T(8,128)S(1)}, u32[]{:S(2)}, u32[]{:S(2)}) collective-permute-start(f32[256,128]{1,0:T(8,128)S(1)} %fusion.14), channel_id=1, source_target_pairs={{0,16},{2,18},{4,20},{6,22},{8,24},{10,26},{12,28},{14,30},{16,0},... | collective-permute-start | bytes 393224 | tf_op jit(solution)/shard_map/ppermute | solution.py:21
  17.2 0.5 collective-permute-done.11
  17.8 0.2 fusion.19
  17.9 2.7 %collective-permute-start.12 = (f32[256,128]{1,0:T(8,128)S(1)}, f32[256,128]{1,0:T(8,128)S(1)}, u32[]{:S(2)}, u32[]{:S(2)}) collective-permute-start(f32[256,128]{1,0:T(8,128)S(1)} %fusion.19), channel_id=1, source_target_pairs={{0,16},{2,18},{4,20},{6,22},{8,24},{10,26},{12,28},{14,30},{16,0},... | collective-permute-start | bytes 393224 | tf_op jit(solution)/shard_map/ppermute | solution.py:21
  20.7 5.8 %collective-permute-done.9 = f32[256,128]{1,0:T(8,128)S(1)} collective-permute-done((f32[256,128]{1,0:T(8,128)S(1)}, f32[256,128]{1,0:T(8,128)S(1)}, u32[]{:S(2)}, u32[]{:S(2)}) %collective-permute-start.9) | collective-permute-done | bytes 131104 | tf_op jit(solution)/shard_map/ppermute | solution.py:21
  26.5 0.2 collective-permute-start.10
  26.7 0.1 add_multiply_fusion.6
  26.9 3.5 %collective-permute-start.3 = (f32[2,256,128]{2,1,0:T(8,128)S(1)}, f32[2,256,128]{2,1,0:T(8,128)S(1)}, u32[]{:S(2)}, u32[]{:S(2)}) collective-permute-start(f32[2,256,128]{2,1,0:T(8,128)S(1)} %pad_maximum_fusion), channel_id=1, source_target_pairs={{0,16},{2,18},{4,20},{6,22},{8,24},{10,26},{12,28},{14,30},{16,0},... | collective-permute-start | bytes 786440 | tf_op jit(solution)/shard_map/ppermute | solution.py:21
  30.4 1.2 %collective-permute-done.12 = f32[256,128]{1,0:T(8,128)S(1)} collective-permute-done((f32[256,128]{1,0:T(8,128)S(1)}, f32[256,128]{1,0:T(8,128)S(1)}, u32[]{:S(2)}, u32[]{:S(2)}) %collective-permute-start.12) | collective-permute-done | bytes 131104 | tf_op jit(solution)/shard_map/ppermute | solution.py:21
  31.7 1.8 %collective-permute-done.10 = f32[256,128]{1,0:T(8,128)S(1)} collective-permute-done((f32[256,128]{1,0:T(8,128)S(1)}, f32[256,128]{1,0:T(8,128)S(1)}, u32[]{:S(2)}, u32[]{:S(2)}) %collective-permute-start.10) | collective-permute-done | bytes 131104 | tf_op jit(solution)/shard_map/ppermute | solution.py:21
  33.5 1.6 %collective-permute-start.14 = (f32[512,128]{1,0:T(8,128)S(1)}, f32[512,128]{1,0:T(8,128)S(1)}, u32[]{:S(2)}, u32[]{:S(2)}) collective-permute-start(f32[512,128]{1,0:T(8,128)S(1)} %maximum_multiply_fusion.refs_0_), channel_id=1, source_target_pairs={{0,4},{2,6},{4,0},{6,2},{8,12},{10,14},{12,8},{14,10},{16,20},{18,... | collective-permute-start | bytes 786440 | tf_op jit(solution)/shard_map/ppermute | solution.py:21
  35.1 2.7 %collective-permute-start.6 = (f32[2,256,128]{2,1,0:T(8,128)S(1)}, f32[2,256,128]{2,1,0:T(8,128)S(1)}, u32[]{:S(2)}, u32[]{:S(2)}) collective-permute-start(f32[2,256,128]{2,1,0:T(8,128)S(1)} %get-tuple-element.42), channel_id=1, source_target_pairs={{0,1},{1,0},{2,3},{3,2},{4,5},{5,4},{6,7},{7,6},{8,9},{9,8},{10,11... | collective-permute-start | bytes 786440 | tf_op jit(solution)/shard_map/ppermute | solution.py:21
  37.8 0.1 collective-permute-start.7
  37.8 2.1 %collective-permute-done.14.refs_2_ = f32[512,128]{1,0:T(8,128)S(1)} collective-permute-done((f32[512,128]{1,0:T(8,128)S(1)}, f32[512,128]{1,0:T(8,128)S(1)}, u32[]{:S(2)}, u32[]{:S(2)}) %collective-permute-start.14) | collective-permute-done | bytes 262176 | tf_op jit(solution)/shard_map/ppermute | solution.py:21
  40.0 0.0 collective-permute-done.3
  40.1 0.1 collective-permute-start.4
  40.1 0.0 collective-permute-done.13.refs_1_
  40.2 1.3 %collective-permute-done.15.refs_3_ = f32[512,128]{1,0:T(8,128)S(1)} collective-permute-done((f32[512,128]{1,0:T(8,128)S(1)}, f32[512,128]{1,0:T(8,128)S(1)}, u32[]{:S(2)}, u32[]{:S(2)}) %collective-permute-start.15) | collective-permute-done | bytes 262176 | tf_op jit(solution)/shard_map/ppermute | solution.py:21
  41.5 7.0 %eliminate_0.1 = (f32[4,512,128]{2,1,0:T(8,128)S(1)}, f32[4,512,128]{2,1,0:T(8,128)S(1)}, f32[512,128]{1,0:T(8,128)S(1)}) custom-call(s32[4]{0:T(128)S(1)} %pad_add_fusion.info, f32[512,128]{1,0:T(8,128)S(1)} %maximum_multiply_fusion.refs_0_, f32[512,128]{1,0:T(8,128)S(1)} %collective-permute-done.13.refs_1_, ...), custom_call_target="tpu_custom_call" | custom-call | flops 4000000000 | bytes 12000000 | tf_op jit(solution)/shard_map/eliminate_0/pallas_call | solution.py:282
  48.5 0.0 collective-permute-done.6
  48.5 0.0 collective-permute-done.7
  48.5 0.3 collective-permute-done.4
  48.9 0.1 collective-permute-start.20
  49.0 1.6 %collective-permute-start.22 = (f32[512,128]{1,0:T(8,128)S(1)}, f32[512,128]{1,0:T(8,128)S(1)}, u32[]{:S(2)}, u32[]{:S(2)}) collective-permute-start(f32[512,128]{1,0:T(8,128)S(1)} %add_multiply_fusion.2.refs_2_), channel_id=1, source_target_pairs={{0,4},{2,6},{4,0},{6,2},{8,12},{10,14},{12,8},{14,10},{16,20},{18,... | collective-permute-start | bytes 786440 | tf_op jit(solution)/shard_map/ppermute | solution.py:21
  50.5 0.2 select_multiply_fusion.1
  50.7 0.1 add_multiply_fusion.4
  50.9 0.1 fusion.2
  50.9 2.1 %collective-permute-start.16 = (f32[512,128]{1,0:T(8,128)S(1)}, f32[512,128]{1,0:T(8,128)S(1)}, u32[]{:S(2)}, u32[]{:S(2)}) collective-permute-start(f32[512,128]{1,0:T(8,128)S(1)} %get-tuple-element.77), channel_id=1, source_target_pairs={{0,16},{2,18},{4,20},{6,22},{8,24},{10,26},{12,28},{14,30},{16,0},... | collective-permute-start | bytes 786440 | tf_op jit(solution)/shard_map/ppermute | solution.py:21
  53.1 1.6 %collective-permute-start.17 = (f32[512,128]{1,0:T(8,128)S(1)}, f32[512,128]{1,0:T(8,128)S(1)}, u32[]{:S(2)}, u32[]{:S(2)}) collective-permute-start(f32[512,128]{1,0:T(8,128)S(1)} %broadcast_multiply_fusion), channel_id=1, source_target_pairs={{0,8},{2,10},{4,12},{6,14},{8,0},{10,2},{12,4},{14,6},{16,24},{18,... | collective-permute-start | bytes 786440 | tf_op jit(solution)/shard_map/ppermute | solution.py:21
  54.7 0.0 collective-permute-start.18
  54.7 5.8 %shard_map.37 = (f32[4,512,128]{2,1,0:T(8,128)S(1)}, f32[4,512,128]{2,1,0:T(8,128)S(1)}, f32[512,128]{1,0:T(8,128)S(1)}) custom-call(f32[4,512,128]{2,1,0:T(8,128)S(1)} %get-tuple-element.47.old_work, f32[4,512,128]{2,1,0:T(8,128)S(1)} %get-tuple-element.48.old_packed, ...), custom_call_target="tpu_custom_call", output_to_operand_aliasing={{0}: (0, {}), {1}: (1, {}), {2}: (2, {})} | custom-call | flops 4000000000 | bytes 12000000 | tf_op jit(solution)/shard_map/pallas_call | solution.py:305
  60.5 4.7 %shard_map.38 = (f32[4,512,128]{2,1,0:T(8,128)S(1)}, f32[4,512,128]{2,1,0:T(8,128)S(1)}, f32[512,128]{1,0:T(8,128)S(1)}) custom-call(f32[4,512,128]{2,1,0:T(8,128)S(1)} %get-tuple-element.50.old_work, f32[4,512,128]{2,1,0:T(8,128)S(1)} %get-tuple-element.51.old_packed, ...), custom_call_target="tpu_custom_call", output_to_operand_aliasing={{0}: (0, {}), {1}: (1, {}), {2}: (2, {})} | custom-call | flops 4000000000 | bytes 12000000 | tf_op jit(solution)/shard_map/pallas_call | solution.py:305
  65.3 1.7 %collective-permute-done.16 = f32[512,128]{1,0:T(8,128)S(1)} collective-permute-done((f32[512,128]{1,0:T(8,128)S(1)}, f32[512,128]{1,0:T(8,128)S(1)}, u32[]{:S(2)}, u32[]{:S(2)}) %collective-permute-start.16) | collective-permute-done | bytes 262176 | tf_op jit(solution)/shard_map/ppermute | solution.py:21
  66.9 0.0 collective-permute-done.17
  66.9 10.2 %collective-permute-done.18 = f32[512,128]{1,0:T(8,128)S(1)} collective-permute-done((f32[512,128]{1,0:T(8,128)S(1)}, f32[512,128]{1,0:T(8,128)S(1)}, u32[]{:S(2)}, u32[]{:S(2)}) %collective-permute-start.18) | collective-permute-done | bytes 262176 | tf_op jit(solution)/shard_map/ppermute | solution.py:21
  77.2 0.1 collective-permute-start.21
  77.3 0.6 collective-permute-start.23
  77.9 0.1 add_multiply_fusion.1
  78.1 5.0 %collective-permute-start.19 = (f32[512,128]{1,0:T(8,128)S(1)}, f32[512,128]{1,0:T(8,128)S(1)}, u32[]{:S(2)}, u32[]{:S(2)}) collective-permute-start(f32[512,128]{1,0:T(8,128)S(1)} %pad_maximum_fusion.3), channel_id=1, source_target_pairs={{0,1},{2,3},{4,5},{6,7},{8,9},{10,11},{12,13},{14,15},{16,17},{18,... | collective-permute-start | bytes 786440 | tf_op jit(solution)/shard_map/ppermute | solution.py:321
  83.1 0.0 collective-permute-done.22.refs_6_
  83.1 0.1 collective-permute-start.24
  83.2 2.8 %collective-permute-done.23.refs_7_ = f32[512,128]{1,0:T(8,128)S(1)} collective-permute-done((f32[512,128]{1,0:T(8,128)S(1)}, f32[512,128]{1,0:T(8,128)S(1)}, u32[]{:S(2)}, u32[]{:S(2)}) %collective-permute-start.23) | collective-permute-done | bytes 262176 | tf_op jit(solution)/shard_map/ppermute | solution.py:21
  86.0 0.0 collective-permute-start.25
  86.0 4.4 %shard_map.39 = (f32[4,512,128]{2,1,0:T(8,128)S(1)}, f32[4,512,128]{2,1,0:T(8,128)S(1)}, f32[512,128]{1,0:T(8,128)S(1)}) custom-call(f32[4,512,128]{2,1,0:T(8,128)S(1)} %get-tuple-element.58.old_work, f32[4,512,128]{2,1,0:T(8,128)S(1)} %get-tuple-element.59.old_packed, ...), custom_call_target="tpu_custom_call", output_to_operand_aliasing={{0}: (0, {}), {1}: (1, {}), {2}: (2, {})} | custom-call | flops 4000000000 | bytes 12000000 | tf_op jit(solution)/shard_map/pallas_call | solution.py:305
  90.4 0.0 collective-permute-done.19
  90.5 0.0 collective-permute-done.20.refs_4_
  90.5 5.7 %own_columns.1 = f32[1024,128]{1,0:T(8,128)} custom-call(s32[4]{0:T(128)S(1)} %pad_add_fusion.info, f32[4,512,128]{2,1,0:T(8,128)S(1)} %get-tuple-element.64.work, f32[4,512,128]{2,1,0:T(8,128)S(1)} %get-tuple-element.65.packed, f32[512,128]{1,0:T(8,128)S(1)} %get-tuple-element.66.inverted, f32[512,128]{1,0:T(8,128)S(1)} %broadcast_select_fusion.own_top, ...), custom_call_target="tpu_custom_call" | custom-call | flops 4000000000 | bytes 12000000 | tf_op jit(solution)/shard_map/own_columns/pallas_call | solution.py:326
  (51 shorter events, 0.6 us)
Async XLA Ops:
  0.0 7.2 %collective-permute-start = (f32[2,128]{1,0:T(2,128)}, f32[2,128]{1,0:T(2,128)S(1)}, u32[]{:S(2)}, u32[]{:S(2)}) collective-permute-start(f32[2,128]{1,0:T(2,128)} %param.5), channel_id=1, source_target_pairs={{0,8},{2,10},{4,12},{6,14},{8,0},{10,2},{12,4},{14,6},{16,24},{18,... | collective-permute-start | bytes 3080 | tf_op jit(solution)/shard_map/ppermute | solution.py:21
  3.1 3.2 %copy-start.1 = (f32[2,1024]{1,0:T(2,128)S(1)}, f32[2,1024]{1,0:T(2,128)}, u32[]{:S(2)}) copy-start(f32[2,1024]{1,0:T(2,128)} %param.4) | copy-start | bytes 24580
  3.1 9.3 %copy-start = (f32[1024,128]{1,0:T(8,128)S(1)}, f32[1024,128]{1,0:T(8,128)}, u32[]{:S(2)}) copy-start(f32[1024,128]{1,0:T(8,128)} %param.3) | copy-start | bytes 1572868
  4.2 8.2 %collective-permute-start.5 = (f32[2,256,128]{2,1,0:T(8,128)S(1)}, f32[2,256,128]{2,1,0:T(8,128)S(1)}, u32[]{:S(2)}, u32[]{:S(2)}) collective-permute-start(f32[2,256,128]{2,1,0:T(8,128)S(1)} %get-tuple-element.79), channel_id=1, source_target_pairs={{0,8},{2,10},{4,12},{6,14},{8,0},{10,2},{12,4},{14,6},{16,24},{18,... | collective-permute-start | bytes 786440 | tf_op jit(solution)/shard_map/ppermute | solution.py:21
  4.3 8.1 %collective-permute-start.2 = (f32[2,256,128]{2,1,0:T(8,128)S(1)}, f32[2,256,128]{2,1,0:T(8,128)S(1)}, u32[]{:S(2)}, u32[]{:S(2)}) collective-permute-start(f32[2,256,128]{2,1,0:T(8,128)S(1)} %get-tuple-element.80), channel_id=1, source_target_pairs={{0,1},{1,0},{2,3},{3,2},{4,5},{5,4},{6,7},{7,6},{8,9},{9,8},{10,11... | collective-permute-start | bytes 786440 | tf_op jit(solution)/shard_map/ppermute | solution.py:21
  6.2 6.0 %collective-permute-start.8 = (f32[2,1024]{1,0:T(2,128)S(1)}, f32[2,1024]{1,0:T(2,128)S(1)}, u32[]{:S(2)}, u32[]{:S(2)}) collective-permute-start(f32[2,1024]{1,0:T(2,128)S(1)} %copy-done.1), channel_id=1, source_target_pairs={{0,1},{1,0},{2,3},{3,2},{4,5},{5,4},{6,7},{7,6},{8,9},{9,8},{10,11... | collective-permute-start | bytes 24584 | tf_op jit(solution)/shard_map/ppermute | solution.py:21
  6.5 0.7 copy-start.2
  7.3 4.7 %collective-permute-start.1 = (f32[4,128]{1,0:T(4,128)S(1)}, f32[4,128]{1,0:T(4,128)S(1)}, u32[]{:S(2)}, u32[]{:S(2)}) collective-permute-start(f32[4,128]{1,0:T(4,128)S(1)} %pad_maximum_fusion.4), channel_id=1, source_target_pairs={{0,16},{2,18},{4,20},{6,22},{8,24},{10,26},{12,28},{14,30},{16,0},... | collective-permute-start | bytes 6152 | tf_op jit(solution)/shard_map/ppermute | solution.py:21
  12.7 5.0 %collective-permute-start.11 = (f32[256,128]{1,0:T(8,128)S(1)}, f32[256,128]{1,0:T(8,128)S(1)}, u32[]{:S(2)}, u32[]{:S(2)}) collective-permute-start(f32[256,128]{1,0:T(8,128)S(1)} %fusion.8), channel_id=1, source_target_pairs={{0,1},{1,0},{2,3},{3,2},{4,5},{5,4},{6,7},{7,6},{8,9},{9,8},{10,11... | collective-permute-start | bytes 393224 | tf_op jit(solution)/shard_map/ppermute | solution.py:21
  14.6 11.9 %collective-permute-start.9 = (f32[256,128]{1,0:T(8,128)S(1)}, f32[256,128]{1,0:T(8,128)S(1)}, u32[]{:S(2)}, u32[]{:S(2)}) collective-permute-start(f32[256,128]{1,0:T(8,128)S(1)} %fusion.14), channel_id=1, source_target_pairs={{0,16},{2,18},{4,20},{6,22},{8,24},{10,26},{12,28},{14,30},{16,0},... | collective-permute-start | bytes 393224 | tf_op jit(solution)/shard_map/ppermute | solution.py:21
  17.9 13.7 %collective-permute-start.12 = (f32[256,128]{1,0:T(8,128)S(1)}, f32[256,128]{1,0:T(8,128)S(1)}, u32[]{:S(2)}, u32[]{:S(2)}) collective-permute-start(f32[256,128]{1,0:T(8,128)S(1)} %fusion.19), channel_id=1, source_target_pairs={{0,16},{2,18},{4,20},{6,22},{8,24},{10,26},{12,28},{14,30},{16,0},... | collective-permute-start | bytes 393224 | tf_op jit(solution)/shard_map/ppermute | solution.py:21
  26.5 7.0 %collective-permute-start.10 = (f32[256,128]{1,0:T(8,128)S(1)}, f32[256,128]{1,0:T(8,128)S(1)}, u32[]{:S(2)}, u32[]{:S(2)}) collective-permute-start(f32[256,128]{1,0:T(8,128)S(1)} %add.82), channel_id=1, source_target_pairs={{0,8},{2,10},{4,12},{6,14},{8,0},{10,2},{12,4},{14,6},{16,24},{18,... | collective-permute-start | bytes 393224 | tf_op jit(solution)/shard_map/ppermute | solution.py:21
  26.9 13.1 %collective-permute-start.3 = (f32[2,256,128]{2,1,0:T(8,128)S(1)}, f32[2,256,128]{2,1,0:T(8,128)S(1)}, u32[]{:S(2)}, u32[]{:S(2)}) collective-permute-start(f32[2,256,128]{2,1,0:T(8,128)S(1)} %pad_maximum_fusion), channel_id=1, source_target_pairs={{0,16},{2,18},{4,20},{6,22},{8,24},{10,26},{12,28},{14,30},{16,0},... | collective-permute-start | bytes 786440 | tf_op jit(solution)/shard_map/ppermute | solution.py:21
  33.5 6.4 %collective-permute-start.14 = (f32[512,128]{1,0:T(8,128)S(1)}, f32[512,128]{1,0:T(8,128)S(1)}, u32[]{:S(2)}, u32[]{:S(2)}) collective-permute-start(f32[512,128]{1,0:T(8,128)S(1)} %maximum_multiply_fusion.refs_0_), channel_id=1, source_target_pairs={{0,4},{2,6},{4,0},{6,2},{8,12},{10,14},{12,8},{14,10},{16,20},{18,... | collective-permute-start | bytes 786440 | tf_op jit(solution)/shard_map/ppermute | solution.py:21
  35.1 13.4 %collective-permute-start.6 = (f32[2,256,128]{2,1,0:T(8,128)S(1)}, f32[2,256,128]{2,1,0:T(8,128)S(1)}, u32[]{:S(2)}, u32[]{:S(2)}) collective-permute-start(f32[2,256,128]{2,1,0:T(8,128)S(1)} %get-tuple-element.42), channel_id=1, source_target_pairs={{0,1},{1,0},{2,3},{3,2},{4,5},{5,4},{6,7},{7,6},{8,9},{9,8},{10,11... | collective-permute-start | bytes 786440 | tf_op jit(solution)/shard_map/ppermute | solution.py:21
  37.8 10.7 %collective-permute-start.7 = (f32[2,256,128]{2,1,0:T(8,128)S(1)}, f32[2,256,128]{2,1,0:T(8,128)S(1)}, u32[]{:S(2)}, u32[]{:S(2)}) collective-permute-start(f32[2,256,128]{2,1,0:T(8,128)S(1)} %get-tuple-element.44), channel_id=1, source_target_pairs={{0,1},{1,0},{2,3},{3,2},{4,5},{5,4},{6,7},{7,6},{8,9},{9,8},{10,11... | collective-permute-start | bytes 786440 | tf_op jit(solution)/shard_map/ppermute | solution.py:21
  37.8 2.3 %collective-permute-start.13 = (f32[512,128]{1,0:T(8,128)S(1)}, f32[512,128]{1,0:T(8,128)S(1)}, u32[]{:S(2)}, u32[]{:S(2)}) collective-permute-start(f32[512,128]{1,0:T(8,128)S(1)} %maximum_multiply_fusion.refs_0_), channel_id=1, source_target_pairs={{0,2},{2,0},{4,6},{6,4},{8,10},{10,8},{12,14},{14,12},{16,18},{18,... | collective-permute-start | bytes 786440 | tf_op jit(solution)/shard_map/ppermute | solution.py:21
  40.0 1.5 %collective-permute-start.15 = (f32[512,128]{1,0:T(8,128)S(1)}, f32[512,128]{1,0:T(8,128)S(1)}, u32[]{:S(2)}, u32[]{:S(2)}) collective-permute-start(f32[512,128]{1,0:T(8,128)S(1)} %collective-permute-done.14.refs_2_), channel_id=1, source_target_pairs={{0,2},{2,0},{4,6},{6,4},{8,10},{10,8},{12,14},{14,12},{16,18},{18,... | collective-permute-start | bytes 786440 | tf_op jit(solution)/shard_map/ppermute | solution.py:21
  40.1 8.8 %collective-permute-start.4 = (f32[512,128]{1,0:T(8,128)S(1)}, f32[512,128]{1,0:T(8,128)S(1)}, u32[]{:S(2)}, u32[]{:S(2)}) collective-permute-start(f32[512,128]{1,0:T(8,128)S(1)} %add_multiply_fusion.3), channel_id=1, source_target_pairs={{0,8},{2,10},{4,12},{6,14},{8,0},{10,2},{12,4},{14,6},{16,24},{18,... | collective-permute-start | bytes 786440 | tf_op jit(solution)/shard_map/ppermute | solution.py:21
  48.9 41.6 %collective-permute-start.20 = (f32[512,128]{1,0:T(8,128)S(1)}, f32[512,128]{1,0:T(8,128)S(1)}, u32[]{:S(2)}, u32[]{:S(2)}) collective-permute-start(f32[512,128]{1,0:T(8,128)S(1)} %add_multiply_fusion.2.refs_2_), channel_id=1, source_target_pairs={{0,2},{2,0},{4,6},{6,4},{8,10},{10,8},{12,14},{14,12},{16,18},{18,... | collective-permute-start | bytes 786440 | tf_op jit(solution)/shard_map/ppermute | solution.py:21
  49.0 34.2 %collective-permute-start.22 = (f32[512,128]{1,0:T(8,128)S(1)}, f32[512,128]{1,0:T(8,128)S(1)}, u32[]{:S(2)}, u32[]{:S(2)}) collective-permute-start(f32[512,128]{1,0:T(8,128)S(1)} %add_multiply_fusion.2.refs_2_), channel_id=1, source_target_pairs={{0,4},{2,6},{4,0},{6,2},{8,12},{10,14},{12,8},{14,10},{16,20},{18,... | collective-permute-start | bytes 786440 | tf_op jit(solution)/shard_map/ppermute | solution.py:21
  50.9 16.0 %collective-permute-start.16 = (f32[512,128]{1,0:T(8,128)S(1)}, f32[512,128]{1,0:T(8,128)S(1)}, u32[]{:S(2)}, u32[]{:S(2)}) collective-permute-start(f32[512,128]{1,0:T(8,128)S(1)} %get-tuple-element.77), channel_id=1, source_target_pairs={{0,16},{2,18},{4,20},{6,22},{8,24},{10,26},{12,28},{14,30},{16,0},... | collective-permute-start | bytes 786440 | tf_op jit(solution)/shard_map/ppermute | solution.py:21
  53.1 13.9 %collective-permute-start.17 = (f32[512,128]{1,0:T(8,128)S(1)}, f32[512,128]{1,0:T(8,128)S(1)}, u32[]{:S(2)}, u32[]{:S(2)}) collective-permute-start(f32[512,128]{1,0:T(8,128)S(1)} %broadcast_multiply_fusion), channel_id=1, source_target_pairs={{0,8},{2,10},{4,12},{6,14},{8,0},{10,2},{12,4},{14,6},{16,24},{18,... | collective-permute-start | bytes 786440 | tf_op jit(solution)/shard_map/ppermute | solution.py:21
  54.7 22.5 %collective-permute-start.18 = (f32[512,128]{1,0:T(8,128)S(1)}, f32[512,128]{1,0:T(8,128)S(1)}, u32[]{:S(2)}, u32[]{:S(2)}) collective-permute-start(f32[512,128]{1,0:T(8,128)S(1)} %get-tuple-element.76), channel_id=1, source_target_pairs={{0,16},{2,18},{4,20},{6,22},{8,24},{10,26},{12,28},{14,30},{16,0},... | collective-permute-start | bytes 786440 | tf_op jit(solution)/shard_map/ppermute | solution.py:21
  77.2 13.3 %collective-permute-start.21 = (f32[512,128]{1,0:T(8,128)S(1)}, f32[512,128]{1,0:T(8,128)S(1)}, u32[]{:S(2)}, u32[]{:S(2)}) collective-permute-start(f32[512,128]{1,0:T(8,128)S(1)} %add_multiply_fusion.refs_3_), channel_id=1, source_target_pairs={{0,2},{2,0},{4,6},{6,4},{8,10},{10,8},{12,14},{14,12},{16,18},{18,... | collective-permute-start | bytes 786440 | tf_op jit(solution)/shard_map/ppermute | solution.py:21
  77.3 8.7 %collective-permute-start.23 = (f32[512,128]{1,0:T(8,128)S(1)}, f32[512,128]{1,0:T(8,128)S(1)}, u32[]{:S(2)}, u32[]{:S(2)}) collective-permute-start(f32[512,128]{1,0:T(8,128)S(1)} %add_multiply_fusion.refs_3_), channel_id=1, source_target_pairs={{0,4},{2,6},{4,0},{6,2},{8,12},{10,14},{12,8},{14,10},{16,20},{18,... | collective-permute-start | bytes 786440 | tf_op jit(solution)/shard_map/ppermute | solution.py:21
  78.1 12.4 %collective-permute-start.19 = (f32[512,128]{1,0:T(8,128)S(1)}, f32[512,128]{1,0:T(8,128)S(1)}, u32[]{:S(2)}, u32[]{:S(2)}) collective-permute-start(f32[512,128]{1,0:T(8,128)S(1)} %pad_maximum_fusion.3), channel_id=1, source_target_pairs={{0,1},{2,3},{4,5},{6,7},{8,9},{10,11},{12,13},{14,15},{16,17},{18,... | collective-permute-start | bytes 786440 | tf_op jit(solution)/shard_map/ppermute | solution.py:321
  83.1 7.4 %collective-permute-start.24 = (f32[512,128]{1,0:T(8,128)S(1)}, f32[512,128]{1,0:T(8,128)S(1)}, u32[]{:S(2)}, u32[]{:S(2)}) collective-permute-start(f32[512,128]{1,0:T(8,128)S(1)} %collective-permute-done.22.refs_6_), channel_id=1, source_target_pairs={{0,2},{2,0},{4,6},{6,4},{8,10},{10,8},{12,14},{14,12},{16,18},{18,... | collective-permute-start | bytes 786440 | tf_op jit(solution)/shard_map/ppermute | solution.py:21
  86.0 4.5 %collective-permute-start.25 = (f32[512,128]{1,0:T(8,128)S(1)}, f32[512,128]{1,0:T(8,128)S(1)}, u32[]{:S(2)}, u32[]{:S(2)}) collective-permute-start(f32[512,128]{1,0:T(8,128)S(1)} %collective-permute-done.23.refs_7_), channel_id=1, source_target_pairs={{0,2},{2,0},{4,6},{6,4},{8,10},{10,8},{12,14},{14,12},{16,18},{18,... | collective-permute-start | bytes 786440 | tf_op jit(solution)/shard_map/ppermute | solution.py:21

commit v10 on v9

--- a/solution.py
+++ b/solution.py
@@ -260,9 +260,14 @@
     own_p = jnp.stack(own_mixed(0, rows_p, other_p))
     far_own = swapped(own_p, "col", high)
     other_q = swapped(even_q, "row", 1), swapped(odd_q, "row", 1)
+    parts_q = [flat(jnp.stack(own_mixed(1, a, b))) for a, b in zip((even_q, odd_q), other_q)]
+    panel_q = of_half(parts_q, none, none)
+    far_q = swapped(panel_q, "col", high)
+    received_q = swapped(of_half(parts_q, ~in_high, in_low), "col", high)
     parts_p = flat(jnp.where(in_high, far_own, own_p)), flat(jnp.where(in_high, own_p, far_own))
     panel_p = of_bit(parts_p, none, none)
     near_p = swapped(panel_p, "col", low)
+    received_p = swapped(of_bit(parts_p, in_high, ~in_low), "col", low)
 
     info = jnp.stack(
         [
@@ -288,17 +293,10 @@
         compiler_params=params,
         name="eliminate_0",
     )(info, *lead_pieces)
-    near_p, parts_p, even_q, odd_q, other_q, *state = lax.optimization_barrier(
-        (near_p, parts_p, even_q, odd_q, other_q, *state)
-    )
-    parts_q = [flat(jnp.stack(own_mixed(1, a, b))) for a, b in zip((even_q, odd_q), other_q)]
-    panel_q = of_half(parts_q, none, none)
-    far_q = swapped(panel_q, "col", high)
-    received_q = swapped(of_half(parts_q, ~in_high, in_low), "col", high)
+    near_p, *state = lax.optimization_barrier((near_p, *state))
     panel_p = spread(lead_scale * (panel_p + near_p))
     pieces_p = gather(panel_p)
     kept_p, kept_q = of_bit(parts_p, in_high, in_low), of_half(parts_q, in_high, in_low)
-    received_p = swapped(of_bit(parts_p, in_high, ~in_low), "col", low)
     scale = diag_of(in_high, in_low)[1]
 
     for k in range(1, blocks):
@@ -311,7 +309,7 @@
             cost_estimate=cost,
             compiler_params=params,
         )(*state)
-        if k == blocks - 2:
+        if k == 1:
             far_q, received_p, received_q, _, *state = lax.optimization_barrier(
                 (far_q, received_p, received_q, panel_p, *state)
             )

time: 97 us -> 102 us (1.052)
  starting transfers between devices: 34.5 us -> 38 us
  waiting for transfers between devices: 29.8 us -> 31.6 us
    ppermute x25, starting transfers between devices: 29.5 us -> 34.6 us  [swapped(): lax.ppermute(x, axis, [(i, i ^ mask) for i in range(lax.axis_size(axis))])]
    ppermute x25, waiting for transfers between devices: 29.8 us -> 31.6 us  [swapped(): lax.ppermute(x, axis, [(i, i ^ mask) for i in range(lax.axis_size(axis))])]
    ppermute x1, starting transfers between devices: 5.04 us -> 3.44 us  [shards(): far_top = lax.ppermute(own_top, 'row', [(0, 1)])]
  transfers between devices with their start and end apart: 26 -> 26, of which waited for: 12 -> 6; matrix products, arithmetic and copies ran while one was open for 3% -> 3% of each run, Pallas kernels for 23% -> 22%
where the time goes in v10:
time: 102 us; the launch traced here: 101 us
  starting transfers between devices  38 us (37%)
  waiting for transfers between devices  31.6 us (31%)
  Pallas kernels  27.7 us (27%)
  local copies, waits for them, and re-layouts  1.93 us (2%)
  other arithmetic  1.77 us (2%)
    ppermute x25, starting transfers between devices, swapped(): lax.ppermute(x, axis, [(i, i ^ mask) for i in range(lax.axis_size(axis))])  34.6 us
    ppermute x25, waiting for transfers between devices, swapped(): lax.ppermute(x, axis, [(i, i ^ mask) for i in range(lax.axis_size(axis))])  31.6 us
    pallas_call x3, Pallas kernels, shards(): pl.pallas_call(functools.partial(next_kernel, k), out_shape=state_shapes,...  15 us
    pallas_call x1, Pallas kernels, shards(): pl.pallas_call(first_kernel, out_shape=state_shapes, in_specs=[smem] + [v...  6.98 us
    pallas_call x1, Pallas kernels, shards(): pl.pallas_call(last_kernel, out_shape=jax.ShapeDtypeStruct((height, width...  5.73 us
    ppermute x1, starting transfers between devices, shards(): far_top = lax.ppermute(own_top, 'row', [(0, 1)])  3.44 us
  transfers between devices with their start and end apart: 26, of which 6 were waited for; matrix products, arithmetic and copies ran while one was open for 3% of the time, Pallas kernels for 22%

profile of v10, /device:TPU:0, one launch (start us, length us, event | category | flops | bytes accessed | tf_op | source)
XLA Modules:
  0.0 101.5 jit_solution(8077480558086108781)
XLA Ops:
  0.0 3.1 %collective-permute-start.2 = (f32[2,128]{1,0:T(2,128)}, f32[2,128]{1,0:T(2,128)S(1)}, u32[]{:S(2)}, u32[]{:S(2)}) collective-permute-start(f32[2,128]{1,0:T(2,128)} %param.5), channel_id=1, source_target_pairs={{0,8},{2,10},{4,12},{6,14},{8,0},{10,2},{12,4},{14,6},{16,24},{18,... | collective-permute-start | bytes 3080 | tf_op jit(solution)/shard_map/ppermute | solution.py:21
  3.1 1.1 %slice_bitcast_fusion.1 = (f32[2,256,128]{2,1,0:T(8,128)S(1)}, f32[2,256,128]{2,1,0:T(8,128)S(1)}) fusion(f32[2,1,2,256,128]{4,3,2,0,1:T(8,128)} %bitcast.147), kind=kLoop, calls=%fused_computation.3 | loop fusion | bytes 1048576 | tf_op jit(solution)/shard_map/reshape;squeeze | solution.py:190
  4.2 0.1 collective-permute-start.4
  4.3 2.0 %collective-permute-start = (f32[2,256,128]{2,1,0:T(8,128)S(1)}, f32[2,256,128]{2,1,0:T(8,128)S(1)}, u32[]{:S(2)}, u32[]{:S(2)}) collective-permute-start(f32[2,256,128]{2,1,0:T(8,128)S(1)} %get-tuple-element.71), channel_id=1, source_target_pairs={{0,1},{1,0},{2,3},{3,2},{4,5},{5,4},{6,7},{7,6},{8,9},{9,8},{10,11... | collective-permute-start | bytes 786440 | tf_op jit(solution)/shard_map/ppermute | solution.py:21
  6.2 0.1 collective-permute-start.11
  6.5 0.0 copy-start.2
  6.5 0.7 copy-done.2
  7.2 0.1 pad_add_fusion.info
  7.3 3.0 %collective-permute-start.3 = (f32[4,128]{1,0:T(4,128)S(1)}, f32[4,128]{1,0:T(4,128)S(1)}, u32[]{:S(2)}, u32[]{:S(2)}) collective-permute-start(f32[4,128]{1,0:T(4,128)S(1)} %pad_maximum_fusion.4), channel_id=1, source_target_pairs={{0,16},{2,18},{4,20},{6,22},{8,24},{10,26},{12,28},{14,30},{16,0},... | collective-permute-start | bytes 6152 | tf_op jit(solution)/shard_map/ppermute | solution.py:21
  10.3 1.7 %collective-permute-done.3 = f32[4,128]{1,0:T(4,128)S(1)} collective-permute-done((f32[4,128]{1,0:T(4,128)S(1)}, f32[4,128]{1,0:T(4,128)S(1)}, u32[]{:S(2)}, u32[]{:S(2)}) %collective-permute-start.3) | collective-permute-done | bytes 2080 | tf_op jit(solution)/shard_map/ppermute | solution.py:21
  12.0 0.2 collective-permute-done.11
  12.4 0.0 collective-permute-done.4
  12.4 0.0 collective-permute-done
  12.4 0.1 multiply_add_fusion
  12.5 1.7 %collective-permute-start.5 = (f32[2,256,128]{2,1,0:T(8,128)S(1)}, f32[2,256,128]{2,1,0:T(8,128)S(1)}, u32[]{:S(2)}, u32[]{:S(2)}) collective-permute-start(f32[2,256,128]{2,1,0:T(8,128)S(1)} %get-tuple-element.62), channel_id=1, source_target_pairs={{0,1},{1,0},{2,3},{3,2},{4,5},{5,4},{6,7},{7,6},{8,9},{9,8},{10,11... | collective-permute-start | bytes 786440 | tf_op jit(solution)/shard_map/ppermute | solution.py:21
  14.2 0.4 collective-permute-start.6
  14.6 0.2 fusion.9
  14.8 1.7 %collective-permute-start.14 = (f32[256,128]{1,0:T(8,128)S(1)}, f32[256,128]{1,0:T(8,128)S(1)}, u32[]{:S(2)}, u32[]{:S(2)}) collective-permute-start(f32[256,128]{1,0:T(8,128)S(1)} %fusion.9), channel_id=1, source_target_pairs={{0,1},{1,0},{2,3},{3,2},{4,5},{5,4},{6,7},{7,6},{8,9},{9,8},{10,11... | collective-permute-start | bytes 393224 | tf_op jit(solution)/shard_map/ppermute | solution.py:21
  16.5 0.2 fusion.15
  16.7 2.7 %collective-permute-start.12 = (f32[256,128]{1,0:T(8,128)S(1)}, f32[256,128]{1,0:T(8,128)S(1)}, u32[]{:S(2)}, u32[]{:S(2)}) collective-permute-start(f32[256,128]{1,0:T(8,128)S(1)} %fusion.15), channel_id=1, source_target_pairs={{0,16},{2,18},{4,20},{6,22},{8,24},{10,26},{12,28},{14,30},{16,0},... | collective-permute-start | bytes 393224 | tf_op jit(solution)/shard_map/ppermute | solution.py:21
  19.3 8.6 %collective-permute-done.14 = f32[256,128]{1,0:T(8,128)S(1)} collective-permute-done((f32[256,128]{1,0:T(8,128)S(1)}, f32[256,128]{1,0:T(8,128)S(1)}, u32[]{:S(2)}, u32[]{:S(2)}) %collective-permute-start.14) | collective-permute-done | bytes 131104 | tf_op jit(solution)/shard_map/ppermute | solution.py:21
  27.9 0.2 fusion.20
  28.1 2.5 %collective-permute-start.15 = (f32[256,128]{1,0:T(8,128)S(1)}, f32[256,128]{1,0:T(8,128)S(1)}, u32[]{:S(2)}, u32[]{:S(2)}) collective-permute-start(f32[256,128]{1,0:T(8,128)S(1)} %fusion.20), channel_id=1, source_target_pairs={{0,16},{2,18},{4,20},{6,22},{8,24},{10,26},{12,28},{14,30},{16,0},... | collective-permute-start | bytes 393224 | tf_op jit(solution)/shard_map/ppermute | solution.py:21
  30.6 0.0 collective-permute-done.12
  30.6 1.6 %collective-permute-start.13 = (f32[256,128]{1,0:T(8,128)S(1)}, f32[256,128]{1,0:T(8,128)S(1)}, u32[]{:S(2)}, u32[]{:S(2)}) collective-permute-start(f32[256,128]{1,0:T(8,128)S(1)} %add.89), channel_id=1, source_target_pairs={{0,8},{2,10},{4,12},{6,14},{8,0},{10,2},{12,4},{14,6},{16,24},{18,... | collective-permute-start | bytes 393224 | tf_op jit(solution)/shard_map/ppermute | solution.py:21
  32.2 0.1 add_multiply_fusion.5
  32.4 1.2 %collective-permute-start.1 = (f32[2,256,128]{2,1,0:T(8,128)S(1)}, f32[2,256,128]{2,1,0:T(8,128)S(1)}, u32[]{:S(2)}, u32[]{:S(2)}) collective-permute-start(f32[2,256,128]{2,1,0:T(8,128)S(1)} %pad_maximum_fusion), channel_id=1, source_target_pairs={{0,16},{2,18},{4,20},{6,22},{8,24},{10,26},{12,28},{14,30},{16,0},... | collective-permute-start | bytes 786440 | tf_op jit(solution)/shard_map/ppermute | solution.py:21
  33.6 5.7 %collective-permute-done.15 = f32[256,128]{1,0:T(8,128)S(1)} collective-permute-done((f32[256,128]{1,0:T(8,128)S(1)}, f32[256,128]{1,0:T(8,128)S(1)}, u32[]{:S(2)}, u32[]{:S(2)}) %collective-permute-start.15) | collective-permute-done | bytes 131104 | tf_op jit(solution)/shard_map/ppermute | solution.py:21
  39.4 0.0 collective-permute-done.13
  39.5 0.1 collective-permute-start.16
  39.5 1.2 %collective-permute-start.17 = (f32[512,128]{1,0:T(8,128)S(1)}, f32[512,128]{1,0:T(8,128)S(1)}, u32[]{:S(2)}, u32[]{:S(2)}) collective-permute-start(f32[512,128]{1,0:T(8,128)S(1)} %maximum_multiply_fusion.refs_0_), channel_id=1, source_target_pairs={{0,4},{2,6},{4,0},{6,2},{8,12},{10,14},{12,8},{14,10},{16,20},{18,... | collective-permute-start | bytes 786440 | tf_op jit(solution)/shard_map/ppermute | solution.py:21
  40.7 0.0 collective-permute-done.5
  40.7 0.0 collective-permute-done.6
  40.7 0.2 select_multiply_fusion.1
  40.9 0.1 add_multiply_fusion.3
  41.0 0.1 fusion.2
  41.1 1.0 collective-permute-start.7
  42.1 6.2 %collective-permute-done.17.refs_2_ = f32[512,128]{1,0:T(8,128)S(1)} collective-permute-done((f32[512,128]{1,0:T(8,128)S(1)}, f32[512,128]{1,0:T(8,128)S(1)}, u32[]{:S(2)}, u32[]{:S(2)}) %collective-permute-start.17) | collective-permute-done | bytes 262176 | tf_op jit(solution)/shard_map/ppermute | solution.py:21
  48.2 0.0 collective-permute-start.18
  48.2 0.0 collective-permute-done.1
  48.3 0.1 fusion.6
  48.4 5.5 %collective-permute-start.8 = (f32[512,128]{1,0:T(8,128)S(1)}, f32[512,128]{1,0:T(8,128)S(1)}, u32[]{:S(2)}, u32[]{:S(2)}) collective-permute-start(f32[512,128]{1,0:T(8,128)S(1)} %get-tuple-element.65), channel_id=1, source_target_pairs={{0,8},{2,10},{4,12},{6,14},{8,0},{10,2},{12,4},{14,6},{16,24},{18,... | collective-permute-start | bytes 786440 | tf_op jit(solution)/shard_map/ppermute | solution.py:21
  53.9 3.4 %collective-permute-start.9 = (f32[512,128]{1,0:T(8,128)S(1)}, f32[512,128]{1,0:T(8,128)S(1)}, u32[]{:S(2)}, u32[]{:S(2)}) collective-permute-start(f32[512,128]{1,0:T(8,128)S(1)} %get-tuple-element.66), channel_id=1, source_target_pairs={{0,16},{2,18},{4,20},{6,22},{8,24},{10,26},{12,28},{14,30},{16,0},... | collective-permute-start | bytes 786440 | tf_op jit(solution)/shard_map/ppermute | solution.py:21
  57.3 0.0 collective-permute-done.16.refs_1_
  57.3 0.1 collective-permute-start.10
  57.3 0.0 collective-permute-done.18.refs_3_
  57.3 7.0 %eliminate_0.1 = (f32[4,512,128]{2,1,0:T(8,128)S(1)}, f32[4,512,128]{2,1,0:T(8,128)S(1)}, f32[512,128]{1,0:T(8,128)S(1)}) custom-call(s32[4]{0:T(128)S(1)} %pad_add_fusion.info, f32[512,128]{1,0:T(8,128)S(1)} %maximum_multiply_fusion.refs_0_, f32[512,128]{1,0:T(8,128)S(1)} %collective-permute-done.16.refs_1_, ...), custom_call_target="tpu_custom_call" | custom-call | flops 4000000000 | bytes 12000000 | tf_op jit(solution)/shard_map/eliminate_0/pallas_call | solution.py:287
  64.3 9.1 %collective-permute-done.10 = f32[512,128]{1,0:T(8,128)S(1)} collective-permute-done((f32[512,128]{1,0:T(8,128)S(1)}, f32[512,128]{1,0:T(8,128)S(1)}, u32[]{:S(2)}, u32[]{:S(2)}) %collective-permute-start.10) | collective-permute-done | bytes 262176 | tf_op jit(solution)/shard_map/ppermute | solution.py:21
  73.5 0.1 collective-permute-start.20
  73.6 2.3 %collective-permute-start.22 = (f32[512,128]{1,0:T(8,128)S(1)}, f32[512,128]{1,0:T(8,128)S(1)}, u32[]{:S(2)}, u32[]{:S(2)}) collective-permute-start(f32[512,128]{1,0:T(8,128)S(1)} %add_multiply_fusion.2.refs_2_), channel_id=1, source_target_pairs={{0,4},{2,6},{4,0},{6,2},{8,12},{10,14},{12,8},{14,10},{16,20},{18,... | collective-permute-start | bytes 786440 | tf_op jit(solution)/shard_map/ppermute | solution.py:21
  75.9 5.8 %shard_map.37 = (f32[4,512,128]{2,1,0:T(8,128)S(1)}, f32[4,512,128]{2,1,0:T(8,128)S(1)}, f32[512,128]{1,0:T(8,128)S(1)}) custom-call(f32[4,512,128]{2,1,0:T(8,128)S(1)} %get-tuple-element.35.old_work, f32[4,512,128]{2,1,0:T(8,128)S(1)} %get-tuple-element.36.old_packed, ...), custom_call_target="tpu_custom_call", output_to_operand_aliasing={{0}: (0, {}), {1}: (1, {}), {2}: (2, {})} | custom-call | flops 4000000000 | bytes 12000000 | tf_op jit(solution)/shard_map/pallas_call | solution.py:303
  81.7 0.0 collective-permute-done.7
  81.7 0.0 collective-permute-done.8
  81.8 0.2 collective-permute-start.21
  82.0 0.3 collective-permute-start.23
  82.3 0.1 add_multiply_fusion.1
  82.5 3.4 %collective-permute-start.19 = (f32[512,128]{1,0:T(8,128)S(1)}, f32[512,128]{1,0:T(8,128)S(1)}, u32[]{:S(2)}, u32[]{:S(2)}) collective-permute-start(f32[512,128]{1,0:T(8,128)S(1)} %pad_maximum_fusion.3), channel_id=1, source_target_pairs={{0,1},{2,3},{4,5},{6,7},{8,9},{10,11},{12,13},{14,15},{16,17},{18,... | collective-permute-start | bytes 786440 | tf_op jit(solution)/shard_map/ppermute | solution.py:319
  85.9 4.7 %shard_map.38 = (f32[4,512,128]{2,1,0:T(8,128)S(1)}, f32[4,512,128]{2,1,0:T(8,128)S(1)}, f32[512,128]{1,0:T(8,128)S(1)}) custom-call(f32[4,512,128]{2,1,0:T(8,128)S(1)} %get-tuple-element.43.old_work, f32[4,512,128]{2,1,0:T(8,128)S(1)} %get-tuple-element.44.old_packed, ...), custom_call_target="tpu_custom_call", output_to_operand_aliasing={{0}: (0, {}), {1}: (1, {}), {2}: (2, {})} | custom-call | flops 4000000000 | bytes 12000000 | tf_op jit(solution)/shard_map/pallas_call | solution.py:303
  90.6 0.0 collective-permute-done.22.refs_6_
  90.7 0.1 collective-permute-start.24
  90.7 0.0 collective-permute-done.23.refs_7_
  90.7 0.5 collective-permute-start.25
  91.2 4.4 %shard_map.39 = (f32[4,512,128]{2,1,0:T(8,128)S(1)}, f32[4,512,128]{2,1,0:T(8,128)S(1)}, f32[512,128]{1,0:T(8,128)S(1)}) custom-call(f32[4,512,128]{2,1,0:T(8,128)S(1)} %get-tuple-element.46.old_work, f32[4,512,128]{2,1,0:T(8,128)S(1)} %get-tuple-element.47.old_packed, ...), custom_call_target="tpu_custom_call", output_to_operand_aliasing={{0}: (0, {}), {1}: (1, {}), {2}: (2, {})} | custom-call | flops 4000000000 | bytes 12000000 | tf_op jit(solution)/shard_map/pallas_call | solution.py:303
  95.8 5.7 %own_columns.1 = f32[1024,128]{1,0:T(8,128)} custom-call(s32[4]{0:T(128)S(1)} %pad_add_fusion.info, f32[4,512,128]{2,1,0:T(8,128)S(1)} %get-tuple-element.52.work, f32[4,512,128]{2,1,0:T(8,128)S(1)} %get-tuple-element.53.packed, f32[512,128]{1,0:T(8,128)S(1)} %get-tuple-element.54.inverted, f32[512,128]{1,0:T(8,128)S(1)} %broadcast_select_fusion.own_top, ...), custom_call_target="tpu_custom_call" | custom-call | flops 4000000000 | bytes 12000000 | tf_op jit(solution)/shard_map/own_columns/pallas_call | solution.py:324
  (50 shorter events, 0.5 us)
Async XLA Ops:
  0.0 7.2 %collective-permute-start.2 = (f32[2,128]{1,0:T(2,128)}, f32[2,128]{1,0:T(2,128)S(1)}, u32[]{:S(2)}, u32[]{:S(2)}) collective-permute-start(f32[2,128]{1,0:T(2,128)} %param.5), channel_id=1, source_target_pairs={{0,8},{2,10},{4,12},{6,14},{8,0},{10,2},{12,4},{14,6},{16,24},{18,... | collective-permute-start | bytes 3080 | tf_op jit(solution)/shard_map/ppermute | solution.py:21
  3.1 3.2 %copy-start.1 = (f32[2,1024]{1,0:T(2,128)S(1)}, f32[2,1024]{1,0:T(2,128)}, u32[]{:S(2)}) copy-start(f32[2,1024]{1,0:T(2,128)} %param.4) | copy-start | bytes 24580
  3.1 9.3 %copy-start = (f32[1024,128]{1,0:T(8,128)S(1)}, f32[1024,128]{1,0:T(8,128)}, u32[]{:S(2)}) copy-start(f32[1024,128]{1,0:T(8,128)} %param.3) | copy-start | bytes 1572868
  4.2 8.2 %collective-permute-start.4 = (f32[2,256,128]{2,1,0:T(8,128)S(1)}, f32[2,256,128]{2,1,0:T(8,128)S(1)}, u32[]{:S(2)}, u32[]{:S(2)}) collective-permute-start(f32[2,256,128]{2,1,0:T(8,128)S(1)} %get-tuple-element.72), channel_id=1, source_target_pairs={{0,8},{2,10},{4,12},{6,14},{8,0},{10,2},{12,4},{14,6},{16,24},{18,... | collective-permute-start | bytes 786440 | tf_op jit(solution)/shard_map/ppermute | solution.py:21
  4.3 8.1 %collective-permute-start = (f32[2,256,128]{2,1,0:T(8,128)S(1)}, f32[2,256,128]{2,1,0:T(8,128)S(1)}, u32[]{:S(2)}, u32[]{:S(2)}) collective-permute-start(f32[2,256,128]{2,1,0:T(8,128)S(1)} %get-tuple-element.71), channel_id=1, source_target_pairs={{0,1},{1,0},{2,3},{3,2},{4,5},{5,4},{6,7},{7,6},{8,9},{9,8},{10,11... | collective-permute-start | bytes 786440 | tf_op jit(solution)/shard_map/ppermute | solution.py:21
  6.2 6.0 %collective-permute-start.11 = (f32[2,1024]{1,0:T(2,128)S(1)}, f32[2,1024]{1,0:T(2,128)S(1)}, u32[]{:S(2)}, u32[]{:S(2)}) collective-permute-start(f32[2,1024]{1,0:T(2,128)S(1)} %copy-done.1), channel_id=1, source_target_pairs={{0,1},{1,0},{2,3},{3,2},{4,5},{5,4},{6,7},{7,6},{8,9},{9,8},{10,11... | collective-permute-start | bytes 24584 | tf_op jit(solution)/shard_map/ppermute | solution.py:21
  6.5 0.7 copy-start.2
  7.3 4.7 %collective-permute-start.3 = (f32[4,128]{1,0:T(4,128)S(1)}, f32[4,128]{1,0:T(4,128)S(1)}, u32[]{:S(2)}, u32[]{:S(2)}) collective-permute-start(f32[4,128]{1,0:T(4,128)S(1)} %pad_maximum_fusion.4), channel_id=1, source_target_pairs={{0,16},{2,18},{4,20},{6,22},{8,24},{10,26},{12,28},{14,30},{16,0},... | collective-permute-start | bytes 6152 | tf_op jit(solution)/shard_map/ppermute | solution.py:21
  12.5 28.2 %collective-permute-start.5 = (f32[2,256,128]{2,1,0:T(8,128)S(1)}, f32[2,256,128]{2,1,0:T(8,128)S(1)}, u32[]{:S(2)}, u32[]{:S(2)}) collective-permute-start(f32[2,256,128]{2,1,0:T(8,128)S(1)} %get-tuple-element.62), channel_id=1, source_target_pairs={{0,1},{1,0},{2,3},{3,2},{4,5},{5,4},{6,7},{7,6},{8,9},{9,8},{10,11... | collective-permute-start | bytes 786440 | tf_op jit(solution)/shard_map/ppermute | solution.py:21
  14.2 26.5 %collective-permute-start.6 = (f32[2,256,128]{2,1,0:T(8,128)S(1)}, f32[2,256,128]{2,1,0:T(8,128)S(1)}, u32[]{:S(2)}, u32[]{:S(2)}) collective-permute-start(f32[2,256,128]{2,1,0:T(8,128)S(1)} %get-tuple-element.63), channel_id=1, source_target_pairs={{0,1},{1,0},{2,3},{3,2},{4,5},{5,4},{6,7},{7,6},{8,9},{9,8},{10,11... | collective-permute-start | bytes 786440 | tf_op jit(solution)/shard_map/ppermute | solution.py:21
  14.8 13.1 %collective-permute-start.14 = (f32[256,128]{1,0:T(8,128)S(1)}, f32[256,128]{1,0:T(8,128)S(1)}, u32[]{:S(2)}, u32[]{:S(2)}) collective-permute-start(f32[256,128]{1,0:T(8,128)S(1)} %fusion.9), channel_id=1, source_target_pairs={{0,1},{1,0},{2,3},{3,2},{4,5},{5,4},{6,7},{7,6},{8,9},{9,8},{10,11... | collective-permute-start | bytes 393224 | tf_op jit(solution)/shard_map/ppermute | solution.py:21
  16.7 13.9 %collective-permute-start.12 = (f32[256,128]{1,0:T(8,128)S(1)}, f32[256,128]{1,0:T(8,128)S(1)}, u32[]{:S(2)}, u32[]{:S(2)}) collective-permute-start(f32[256,128]{1,0:T(8,128)S(1)} %fusion.15), channel_id=1, source_target_pairs={{0,16},{2,18},{4,20},{6,22},{8,24},{10,26},{12,28},{14,30},{16,0},... | collective-permute-start | bytes 393224 | tf_op jit(solution)/shard_map/ppermute | solution.py:21
  28.1 11.2 %collective-permute-start.15 = (f32[256,128]{1,0:T(8,128)S(1)}, f32[256,128]{1,0:T(8,128)S(1)}, u32[]{:S(2)}, u32[]{:S(2)}) collective-permute-start(f32[256,128]{1,0:T(8,128)S(1)} %fusion.20), channel_id=1, source_target_pairs={{0,16},{2,18},{4,20},{6,22},{8,24},{10,26},{12,28},{14,30},{16,0},... | collective-permute-start | bytes 393224 | tf_op jit(solution)/shard_map/ppermute | solution.py:21
  30.6 8.8 %collective-permute-start.13 = (f32[256,128]{1,0:T(8,128)S(1)}, f32[256,128]{1,0:T(8,128)S(1)}, u32[]{:S(2)}, u32[]{:S(2)}) collective-permute-start(f32[256,128]{1,0:T(8,128)S(1)} %add.89), channel_id=1, source_target_pairs={{0,8},{2,10},{4,12},{6,14},{8,0},{10,2},{12,4},{14,6},{16,24},{18,... | collective-permute-start | bytes 393224 | tf_op jit(solution)/shard_map/ppermute | solution.py:21
  32.4 15.8 %collective-permute-start.1 = (f32[2,256,128]{2,1,0:T(8,128)S(1)}, f32[2,256,128]{2,1,0:T(8,128)S(1)}, u32[]{:S(2)}, u32[]{:S(2)}) collective-permute-start(f32[2,256,128]{2,1,0:T(8,128)S(1)} %pad_maximum_fusion), channel_id=1, source_target_pairs={{0,16},{2,18},{4,20},{6,22},{8,24},{10,26},{12,28},{14,30},{16,0},... | collective-permute-start | bytes 786440 | tf_op jit(solution)/shard_map/ppermute | solution.py:21
  39.5 17.8 %collective-permute-start.16 = (f32[512,128]{1,0:T(8,128)S(1)}, f32[512,128]{1,0:T(8,128)S(1)}, u32[]{:S(2)}, u32[]{:S(2)}) collective-permute-start(f32[512,128]{1,0:T(8,128)S(1)} %maximum_multiply_fusion.refs_0_), channel_id=1, source_target_pairs={{0,2},{2,0},{4,6},{6,4},{8,10},{10,8},{12,14},{14,12},{16,18},{18,... | collective-permute-start | bytes 786440 | tf_op jit(solution)/shard_map/ppermute | solution.py:21
  39.5 8.7 %collective-permute-start.17 = (f32[512,128]{1,0:T(8,128)S(1)}, f32[512,128]{1,0:T(8,128)S(1)}, u32[]{:S(2)}, u32[]{:S(2)}) collective-permute-start(f32[512,128]{1,0:T(8,128)S(1)} %maximum_multiply_fusion.refs_0_), channel_id=1, source_target_pairs={{0,4},{2,6},{4,0},{6,2},{8,12},{10,14},{12,8},{14,10},{16,20},{18,... | collective-permute-start | bytes 786440 | tf_op jit(solution)/shard_map/ppermute | solution.py:21
  41.1 40.6 %collective-permute-start.7 = (f32[512,128]{1,0:T(8,128)S(1)}, f32[512,128]{1,0:T(8,128)S(1)}, u32[]{:S(2)}, u32[]{:S(2)}) collective-permute-start(f32[512,128]{1,0:T(8,128)S(1)} %get-tuple-element.67), channel_id=1, source_target_pairs={{0,16},{2,18},{4,20},{6,22},{8,24},{10,26},{12,28},{14,30},{16,0},... | collective-permute-start | bytes 786440 | tf_op jit(solution)/shard_map/ppermute | solution.py:21
  48.2 9.1 %collective-permute-start.18 = (f32[512,128]{1,0:T(8,128)S(1)}, f32[512,128]{1,0:T(8,128)S(1)}, u32[]{:S(2)}, u32[]{:S(2)}) collective-permute-start(f32[512,128]{1,0:T(8,128)S(1)} %collective-permute-done.17.refs_2_), channel_id=1, source_target_pairs={{0,2},{2,0},{4,6},{6,4},{8,10},{10,8},{12,14},{14,12},{16,18},{18,... | collective-permute-start | bytes 786440 | tf_op jit(solution)/shard_map/ppermute | solution.py:21
  48.4 33.4 %collective-permute-start.8 = (f32[512,128]{1,0:T(8,128)S(1)}, f32[512,128]{1,0:T(8,128)S(1)}, u32[]{:S(2)}, u32[]{:S(2)}) collective-permute-start(f32[512,128]{1,0:T(8,128)S(1)} %get-tuple-element.65), channel_id=1, source_target_pairs={{0,8},{2,10},{4,12},{6,14},{8,0},{10,2},{12,4},{14,6},{16,24},{18,... | collective-permute-start | bytes 786440 | tf_op jit(solution)/shard_map/ppermute | solution.py:21
  53.9 27.9 %collective-permute-start.9 = (f32[512,128]{1,0:T(8,128)S(1)}, f32[512,128]{1,0:T(8,128)S(1)}, u32[]{:S(2)}, u32[]{:S(2)}) collective-permute-start(f32[512,128]{1,0:T(8,128)S(1)} %get-tuple-element.66), channel_id=1, source_target_pairs={{0,16},{2,18},{4,20},{6,22},{8,24},{10,26},{12,28},{14,30},{16,0},... | collective-permute-start | bytes 786440 | tf_op jit(solution)/shard_map/ppermute | solution.py:21
  57.3 16.2 %collective-permute-start.10 = (f32[512,128]{1,0:T(8,128)S(1)}, f32[512,128]{1,0:T(8,128)S(1)}, u32[]{:S(2)}, u32[]{:S(2)}) collective-permute-start(f32[512,128]{1,0:T(8,128)S(1)} %get-tuple-element.64), channel_id=1, source_target_pairs={{0,8},{2,10},{4,12},{6,14},{8,0},{10,2},{12,4},{14,6},{16,24},{18,... | collective-permute-start | bytes 786440 | tf_op jit(solution)/shard_map/ppermute | solution.py:21
  73.5 22.2 %collective-permute-start.20 = (f32[512,128]{1,0:T(8,128)S(1)}, f32[512,128]{1,0:T(8,128)S(1)}, u32[]{:S(2)}, u32[]{:S(2)}) collective-permute-start(f32[512,128]{1,0:T(8,128)S(1)} %add_multiply_fusion.2.refs_2_), channel_id=1, source_target_pairs={{0,2},{2,0},{4,6},{6,4},{8,10},{10,8},{12,14},{14,12},{16,18},{18,... | collective-permute-start | bytes 786440 | tf_op jit(solution)/shard_map/ppermute | solution.py:21
  73.6 17.1 %collective-permute-start.22 = (f32[512,128]{1,0:T(8,128)S(1)}, f32[512,128]{1,0:T(8,128)S(1)}, u32[]{:S(2)}, u32[]{:S(2)}) collective-permute-start(f32[512,128]{1,0:T(8,128)S(1)} %add_multiply_fusion.2.refs_2_), channel_id=1, source_target_pairs={{0,4},{2,6},{4,0},{6,2},{8,12},{10,14},{12,8},{14,10},{16,20},{18,... | collective-permute-start | bytes 786440 | tf_op jit(solution)/shard_map/ppermute | solution.py:21
  81.8 13.9 %collective-permute-start.21 = (f32[512,128]{1,0:T(8,128)S(1)}, f32[512,128]{1,0:T(8,128)S(1)}, u32[]{:S(2)}, u32[]{:S(2)}) collective-permute-start(f32[512,128]{1,0:T(8,128)S(1)} %add_multiply_fusion.refs_3_), channel_id=1, source_target_pairs={{0,2},{2,0},{4,6},{6,4},{8,10},{10,8},{12,14},{14,12},{16,18},{18,... | collective-permute-start | bytes 786440 | tf_op jit(solution)/shard_map/ppermute | solution.py:21
  82.0 8.7 %collective-permute-start.23 = (f32[512,128]{1,0:T(8,128)S(1)}, f32[512,128]{1,0:T(8,128)S(1)}, u32[]{:S(2)}, u32[]{:S(2)}) collective-permute-start(f32[512,128]{1,0:T(8,128)S(1)} %add_multiply_fusion.refs_3_), channel_id=1, source_target_pairs={{0,4},{2,6},{4,0},{6,2},{8,12},{10,14},{12,8},{14,10},{16,20},{18,... | collective-permute-start | bytes 786440 | tf_op jit(solution)/shard_map/ppermute | solution.py:21
  82.5 13.2 %collective-permute-start.19 = (f32[512,128]{1,0:T(8,128)S(1)}, f32[512,128]{1,0:T(8,128)S(1)}, u32[]{:S(2)}, u32[]{:S(2)}) collective-permute-start(f32[512,128]{1,0:T(8,128)S(1)} %pad_maximum_fusion.3), channel_id=1, source_target_pairs={{0,1},{2,3},{4,5},{6,7},{8,9},{10,11},{12,13},{14,15},{16,17},{18,... | collective-permute-start | bytes 786440 | tf_op jit(solution)/shard_map/ppermute | solution.py:319
  90.7 5.1 %collective-permute-start.24 = (f32[512,128]{1,0:T(8,128)S(1)}, f32[512,128]{1,0:T(8,128)S(1)}, u32[]{:S(2)}, u32[]{:S(2)}) collective-permute-start(f32[512,128]{1,0:T(8,128)S(1)} %collective-permute-done.22.refs_6_), channel_id=1, source_target_pairs={{0,2},{2,0},{4,6},{6,4},{8,10},{10,8},{12,14},{14,12},{16,18},{18,... | collective-permute-start | bytes 786440 | tf_op jit(solution)/shard_map/ppermute | solution.py:21
  90.7 5.0 %collective-permute-start.25 = (f32[512,128]{1,0:T(8,128)S(1)}, f32[512,128]{1,0:T(8,128)S(1)}, u32[]{:S(2)}, u32[]{:S(2)}) collective-permute-start(f32[512,128]{1,0:T(8,128)S(1)} %collective-permute-done.23.refs_7_), channel_id=1, source_target_pairs={{0,2},{2,0},{4,6},{6,4},{8,10},{10,8},{12,14},{14,12},{16,18},{18,... | collective-permute-start | bytes 786440 | tf_op jit(solution)/shard_map/ppermute | solution.py:21

commit v11 on v10

--- a/solution.py
+++ b/solution.py
@@ -293,9 +293,6 @@
         compiler_params=params,
         name="eliminate_0",
     )(info, *lead_pieces)
-    near_p, *state = lax.optimization_barrier((near_p, *state))
-    panel_p = spread(lead_scale * (panel_p + near_p))
-    pieces_p = gather(panel_p)
     kept_p, kept_q = of_bit(parts_p, in_high, in_low), of_half(parts_q, in_high, in_low)
     scale = diag_of(in_high, in_low)[1]
 
@@ -310,9 +307,12 @@
             compiler_params=params,
         )(*state)
         if k == 1:
-            far_q, received_p, received_q, _, *state = lax.optimization_barrier(
-                (far_q, received_p, received_q, panel_p, *state)
+            near_p, far_q, received_p, received_q, *state = lax.optimization_barrier(
+                (near_p, far_q, received_p, received_q, *state)
             )
+            panel_p = spread(lead_scale * (panel_p + near_p))
+            pieces_p = gather(panel_p)
+            panel_q, _ = lax.optimization_barrier((panel_q, panel_p))
             pieces_q = gather(spread(lead_scale * (panel_q + far_q)))
             own = scale * (kept_p + received_p), scale * (kept_q + received_q)
             own_top = jnp.concatenate([v[:SPLIT] for v in own], 0)

time: 102 us -> 101 us (level)
  starting transfers between devices: 38 us -> 26 us
  waiting for transfers between devices: 31.6 us -> 43.3 us
    ppermute x25, starting transfers between devices: 34.6 us -> 22.6 us  [swapped(): lax.ppermute(x, axis, [(i, i ^ mask) for i in range(lax.axis_size(axis))])]
    ppermute x25, waiting for transfers between devices: 31.6 us -> 43.3 us  [swapped(): lax.ppermute(x, axis, [(i, i ^ mask) for i in range(lax.axis_size(axis))])]
  transfers between devices with their start and end apart: 26 -> 26, of which waited for: 6 -> 11; matrix products, arithmetic and copies ran while one was open for 3% -> 3% of each run, Pallas kernels for 22% -> 22%
where the time goes in v11:
time: 101 us
  waiting for transfers between devices  43.3 us (43%)
  Pallas kernels  27.7 us (27%)
  starting transfers between devices  26 us (26%)
  local copies, waits for them, and re-layouts  1.91 us (2%)
  other arithmetic  1.79 us (2%)
    ppermute x25, waiting for transfers between devices, swapped(): lax.ppermute(x, axis, [(i, i ^ mask) for i in range(lax.axis_size(axis))])  43.3 us
    ppermute x25, starting transfers between devices, swapped(): lax.ppermute(x, axis, [(i, i ^ mask) for i in range(lax.axis_size(axis))])  22.6 us
    pallas_call x3, Pallas kernels, shards(): pl.pallas_call(functools.partial(next_kernel, k), out_shape=state_shapes,...  15 us
    pallas_call x1, Pallas kernels, shards(): pl.pallas_call(first_kernel, out_shape=state_shapes, in_specs=[smem] + [v...  6.98 us
    pallas_call x1, Pallas kernels, shards(): pl.pallas_call(last_kernel, out_shape=jax.ShapeDtypeStruct((height, width...  5.74 us
    ppermute x1, starting transfers between devices, shards(): far_top = lax.ppermute(own_top, 'row', [(0, 1)])  3.44 us
  transfers between devices with their start and end apart: 26, of which 11 were waited for; matrix products, arithmetic and copies ran while one was open for 3% of the time, Pallas kernels for 22%

profile of v11, /device:TPU:0, one launch (start us, length us, event | category | flops | bytes accessed | tf_op | source)
XLA Modules:
  0.0 101.1 jit_solution(5881747144893911914)
XLA Ops:
  0.0 3.1 %collective-permute-start.2 = (f32[2,128]{1,0:T(2,128)}, f32[2,128]{1,0:T(2,128)S(1)}, u32[]{:S(2)}, u32[]{:S(2)}) collective-permute-start(f32[2,128]{1,0:T(2,128)} %param.5), channel_id=1, source_target_pairs={{0,8},{2,10},{4,12},{6,14},{8,0},{10,2},{12,4},{14,6},{16,24},{18,... | collective-permute-start | bytes 3080 | tf_op jit(solution)/shard_map/ppermute | solution.py:21
  3.1 1.1 %slice_bitcast_fusion = (f32[2,256,128]{2,1,0:T(8,128)S(1)}, f32[2,256,128]{2,1,0:T(8,128)S(1)}) fusion(f32[2,1,2,256,128]{4,3,2,0,1:T(8,128)} %bitcast.147), kind=kLoop, calls=%fused_computation.2 | loop fusion | bytes 1048576 | tf_op jit(solution)/shard_map/reshape;squeeze | solution.py:190
  4.2 0.1 collective-permute-start.5
  4.3 2.0 %collective-permute-start = (f32[2,256,128]{2,1,0:T(8,128)S(1)}, f32[2,256,128]{2,1,0:T(8,128)S(1)}, u32[]{:S(2)}, u32[]{:S(2)}) collective-permute-start(f32[2,256,128]{2,1,0:T(8,128)S(1)} %get-tuple-element.66), channel_id=1, source_target_pairs={{0,1},{1,0},{2,3},{3,2},{4,5},{5,4},{6,7},{7,6},{8,9},{9,8},{10,11... | collective-permute-start | bytes 786440 | tf_op jit(solution)/shard_map/ppermute | solution.py:21
  6.2 0.1 collective-permute-start.11
  6.4 0.0 copy-start.2
  6.5 0.7 copy-done.2
  7.1 0.1 pad_add_fusion.info
  7.2 0.0 collective-permute-done.2
  7.2 3.0 %collective-permute-start.3 = (f32[4,128]{1,0:T(4,128)S(1)}, f32[4,128]{1,0:T(4,128)S(1)}, u32[]{:S(2)}, u32[]{:S(2)}) collective-permute-start(f32[4,128]{1,0:T(4,128)S(1)} %pad_maximum_fusion.4), channel_id=1, source_target_pairs={{0,16},{2,18},{4,20},{6,22},{8,24},{10,26},{12,28},{14,30},{16,0},... | collective-permute-start | bytes 6152 | tf_op jit(solution)/shard_map/ppermute | solution.py:21
  10.3 1.7 %collective-permute-done.3 = f32[4,128]{1,0:T(4,128)S(1)} collective-permute-done((f32[4,128]{1,0:T(4,128)S(1)}, f32[4,128]{1,0:T(4,128)S(1)}, u32[]{:S(2)}, u32[]{:S(2)}) %collective-permute-start.3) | collective-permute-done | bytes 2080 | tf_op jit(solution)/shard_map/ppermute | solution.py:21
  12.0 0.3 collective-permute-done.11
  12.4 0.0 collective-permute-done.5
  12.4 0.0 collective-permute-done
  12.4 0.1 multiply_add_fusion
  12.5 0.1 add_multiply_fusion.5
  12.7 2.7 %collective-permute-start.1 = (f32[2,256,128]{2,1,0:T(8,128)S(1)}, f32[2,256,128]{2,1,0:T(8,128)S(1)}, u32[]{:S(2)}, u32[]{:S(2)}) collective-permute-start(f32[2,256,128]{2,1,0:T(8,128)S(1)} %pad_maximum_fusion), channel_id=1, source_target_pairs={{0,16},{2,18},{4,20},{6,22},{8,24},{10,26},{12,28},{14,30},{16,0},... | collective-permute-start | bytes 786440 | tf_op jit(solution)/shard_map/ppermute | solution.py:21
  15.5 0.2 fusion.9
  15.6 1.6 %collective-permute-start.14 = (f32[256,128]{1,0:T(8,128)S(1)}, f32[256,128]{1,0:T(8,128)S(1)}, u32[]{:S(2)}, u32[]{:S(2)}) collective-permute-start(f32[256,128]{1,0:T(8,128)S(1)} %fusion.9), channel_id=1, source_target_pairs={{0,1},{1,0},{2,3},{3,2},{4,5},{5,4},{6,7},{7,6},{8,9},{9,8},{10,11... | collective-permute-start | bytes 393224 | tf_op jit(solution)/shard_map/ppermute | solution.py:21
  17.2 0.2 fusion.15
  17.4 0.4 collective-permute-start.12
  17.8 2.9 %collective-permute-done.14 = f32[256,128]{1,0:T(8,128)S(1)} collective-permute-done((f32[256,128]{1,0:T(8,128)S(1)}, f32[256,128]{1,0:T(8,128)S(1)}, u32[]{:S(2)}, u32[]{:S(2)}) %collective-permute-start.14) | collective-permute-done | bytes 131104 | tf_op jit(solution)/shard_map/ppermute | solution.py:21
  20.7 0.2 fusion.20
  20.8 0.3 collective-permute-start.15
  21.1 14.9 %collective-permute-done.12 = f32[256,128]{1,0:T(8,128)S(1)} collective-permute-done((f32[256,128]{1,0:T(8,128)S(1)}, f32[256,128]{1,0:T(8,128)S(1)}, u32[]{:S(2)}, u32[]{:S(2)}) %collective-permute-start.12) | collective-permute-done | bytes 131104 | tf_op jit(solution)/shard_map/ppermute | solution.py:21
  36.0 0.1 collective-permute-start.13
  36.1 1.4 %collective-permute-start.6 = (f32[2,256,128]{2,1,0:T(8,128)S(1)}, f32[2,256,128]{2,1,0:T(8,128)S(1)}, u32[]{:S(2)}, u32[]{:S(2)}) collective-permute-start(f32[2,256,128]{2,1,0:T(8,128)S(1)} %get-tuple-element.58), channel_id=1, source_target_pairs={{0,1},{1,0},{2,3},{3,2},{4,5},{5,4},{6,7},{7,6},{8,9},{9,8},{10,11... | collective-permute-start | bytes 786440 | tf_op jit(solution)/shard_map/ppermute | solution.py:21
  37.5 0.7 collective-permute-start.7
  38.3 2.8 %collective-permute-done.13 = f32[256,128]{1,0:T(8,128)S(1)} collective-permute-done((f32[256,128]{1,0:T(8,128)S(1)}, f32[256,128]{1,0:T(8,128)S(1)}, u32[]{:S(2)}, u32[]{:S(2)}) %collective-permute-start.13) | collective-permute-done | bytes 131104 | tf_op jit(solution)/shard_map/ppermute | solution.py:21
  41.1 0.1 collective-permute-start.16
  41.2 1.4 %collective-permute-start.17 = (f32[512,128]{1,0:T(8,128)S(1)}, f32[512,128]{1,0:T(8,128)S(1)}, u32[]{:S(2)}, u32[]{:S(2)}) collective-permute-start(f32[512,128]{1,0:T(8,128)S(1)} %maximum_multiply_fusion.refs_0_), channel_id=1, source_target_pairs={{0,4},{2,6},{4,0},{6,2},{8,12},{10,14},{12,8},{14,10},{16,20},{18,... | collective-permute-start | bytes 786440 | tf_op jit(solution)/shard_map/ppermute | solution.py:21
  42.6 0.1 broadcast_multiply_fusion
  42.7 0.1 collective-permute-start.4
  42.8 2.6 %collective-permute-done.6 = f32[2,256,128]{2,1,0:T(8,128)S(1)} collective-permute-done((f32[2,256,128]{2,1,0:T(8,128)S(1)}, f32[2,256,128]{2,1,0:T(8,128)S(1)}, u32[]{:S(2)}, u32[]{:S(2)}) %collective-permute-start.6) | collective-permute-done | bytes 262176 | tf_op jit(solution)/shard_map/ppermute | solution.py:21
  45.4 3.4 %collective-permute-done.7 = f32[2,256,128]{2,1,0:T(8,128)S(1)} collective-permute-done((f32[2,256,128]{2,1,0:T(8,128)S(1)}, f32[2,256,128]{2,1,0:T(8,128)S(1)}, u32[]{:S(2)}, u32[]{:S(2)}) %collective-permute-start.7) | collective-permute-done | bytes 262176 | tf_op jit(solution)/shard_map/ppermute | solution.py:21
  48.8 0.2 select_multiply_fusion.1
  48.9 0.1 add_multiply_fusion.3
  49.1 0.8 collective-permute-done.17.refs_2_
  49.9 0.0 collective-permute-start.18
  49.9 0.1 pad_maximum_fusion.1
  50.0 0.1 fusion.2
  50.0 2.7 %collective-permute-start.8 = (f32[512,128]{1,0:T(8,128)S(1)}, f32[512,128]{1,0:T(8,128)S(1)}, u32[]{:S(2)}, u32[]{:S(2)}) collective-permute-start(f32[512,128]{1,0:T(8,128)S(1)} %get-tuple-element.51), channel_id=1, source_target_pairs={{0,16},{2,18},{4,20},{6,22},{8,24},{10,26},{12,28},{14,30},{16,0},... | collective-permute-start | bytes 786440 | tf_op jit(solution)/shard_map/ppermute | solution.py:21
  52.7 0.4 collective-permute-start.9
  53.1 0.0 collective-permute-done.16.refs_1_
  53.1 0.1 collective-permute-start.10
  53.2 7.0 %eliminate_0.1 = (f32[4,512,128]{2,1,0:T(8,128)S(1)}, f32[4,512,128]{2,1,0:T(8,128)S(1)}, f32[512,128]{1,0:T(8,128)S(1)}) custom-call(s32[4]{0:T(128)S(1)} %pad_add_fusion.info, f32[512,128]{1,0:T(8,128)S(1)} %maximum_multiply_fusion.refs_0_, f32[512,128]{1,0:T(8,128)S(1)} %collective-permute-done.16.refs_1_, ...), custom_call_target="tpu_custom_call" | custom-call | flops 4000000000 | bytes 12000000 | tf_op jit(solution)/shard_map/eliminate_0/pallas_call | solution.py:287
  60.2 5.8 %shard_map.37 = (f32[4,512,128]{2,1,0:T(8,128)S(1)}, f32[4,512,128]{2,1,0:T(8,128)S(1)}, f32[512,128]{1,0:T(8,128)S(1)}) custom-call(f32[4,512,128]{2,1,0:T(8,128)S(1)} %get-tuple-element.29.old_work, f32[4,512,128]{2,1,0:T(8,128)S(1)} %get-tuple-element.30.old_packed, ...), custom_call_target="tpu_custom_call", output_to_operand_aliasing={{0}: (0, {}), {1}: (1, {}), {2}: (2, {})} | custom-call | flops 4000000000 | bytes 12000000 | tf_op jit(solution)/shard_map/pallas_call | solution.py:300
  66.0 0.7 collective-permute-done.9
  66.8 9.7 %collective-permute-done.10 = f32[512,128]{1,0:T(8,128)S(1)} collective-permute-done((f32[512,128]{1,0:T(8,128)S(1)}, f32[512,128]{1,0:T(8,128)S(1)}, u32[]{:S(2)}, u32[]{:S(2)}) %collective-permute-start.10) | collective-permute-done | bytes 262176 | tf_op jit(solution)/shard_map/ppermute | solution.py:21
  76.5 0.1 collective-permute-start.20
  76.6 1.5 %collective-permute-start.22 = (f32[512,128]{1,0:T(8,128)S(1)}, f32[512,128]{1,0:T(8,128)S(1)}, u32[]{:S(2)}, u32[]{:S(2)}) collective-permute-start(f32[512,128]{1,0:T(8,128)S(1)} %add_multiply_fusion.1.refs_2_), channel_id=1, source_target_pairs={{0,4},{2,6},{4,0},{6,2},{8,12},{10,14},{12,8},{14,10},{16,20},{18,... | collective-permute-start | bytes 786440 | tf_op jit(solution)/shard_map/ppermute | solution.py:21
  78.2 0.2 collective-permute-start.21
  78.4 0.5 collective-permute-start.23
  78.9 0.1 add_multiply_fusion.2
  79.1 3.4 %collective-permute-start.19 = (f32[512,128]{1,0:T(8,128)S(1)}, f32[512,128]{1,0:T(8,128)S(1)}, u32[]{:S(2)}, u32[]{:S(2)}) collective-permute-start(f32[512,128]{1,0:T(8,128)S(1)} %pad_maximum_fusion.3), channel_id=1, source_target_pairs={{0,1},{2,3},{4,5},{6,7},{8,9},{10,11},{12,13},{14,15},{16,17},{18,... | collective-permute-start | bytes 786440 | tf_op jit(solution)/shard_map/ppermute | solution.py:319
  82.5 4.7 %shard_map.38 = (f32[4,512,128]{2,1,0:T(8,128)S(1)}, f32[4,512,128]{2,1,0:T(8,128)S(1)}, f32[512,128]{1,0:T(8,128)S(1)}) custom-call(f32[4,512,128]{2,1,0:T(8,128)S(1)} %get-tuple-element.37.old_work, f32[4,512,128]{2,1,0:T(8,128)S(1)} %get-tuple-element.38.old_packed, ...), custom_call_target="tpu_custom_call", output_to_operand_aliasing={{0}: (0, {}), {1}: (1, {}), {2}: (2, {})} | custom-call | flops 4000000000 | bytes 12000000 | tf_op jit(solution)/shard_map/pallas_call | solution.py:300
  87.2 0.0 collective-permute-done.22.refs_6_
  87.3 0.1 collective-permute-start.24
  87.3 3.5 %collective-permute-done.23.refs_7_ = f32[512,128]{1,0:T(8,128)S(1)} collective-permute-done((f32[512,128]{1,0:T(8,128)S(1)}, f32[512,128]{1,0:T(8,128)S(1)}, u32[]{:S(2)}, u32[]{:S(2)}) %collective-permute-start.23) | collective-permute-done | bytes 262176 | tf_op jit(solution)/shard_map/ppermute | solution.py:21
  90.9 4.4 %shard_map.39 = (f32[4,512,128]{2,1,0:T(8,128)S(1)}, f32[4,512,128]{2,1,0:T(8,128)S(1)}, f32[512,128]{1,0:T(8,128)S(1)}) custom-call(f32[4,512,128]{2,1,0:T(8,128)S(1)} %get-tuple-element.40.old_work, f32[4,512,128]{2,1,0:T(8,128)S(1)} %get-tuple-element.41.old_packed, ...), custom_call_target="tpu_custom_call", output_to_operand_aliasing={{0}: (0, {}), {1}: (1, {}), {2}: (2, {})} | custom-call | flops 4000000000 | bytes 12000000 | tf_op jit(solution)/shard_map/pallas_call | solution.py:300
  95.4 0.0 collective-permute-done.20.refs_4_
  95.4 0.0 collective-permute-done.24.refs_8_
  95.4 0.0 collective-permute-done.25.refs_9_
  95.4 5.7 %own_columns.1 = f32[1024,128]{1,0:T(8,128)} custom-call(s32[4]{0:T(128)S(1)} %pad_add_fusion.info, f32[4,512,128]{2,1,0:T(8,128)S(1)} %get-tuple-element.46.work, f32[4,512,128]{2,1,0:T(8,128)S(1)} %get-tuple-element.47.packed, f32[512,128]{1,0:T(8,128)S(1)} %get-tuple-element.48.inverted, f32[512,128]{1,0:T(8,128)S(1)} %broadcast_select_fusion.own_top, ...), custom_call_target="tpu_custom_call" | custom-call | flops 4000000000 | bytes 12000000 | tf_op jit(solution)/shard_map/own_columns/pallas_call | solution.py:324
  (50 shorter events, 0.5 us)
Async XLA Ops:
  0.0 7.2 %collective-permute-start.2 = (f32[2,128]{1,0:T(2,128)}, f32[2,128]{1,0:T(2,128)S(1)}, u32[]{:S(2)}, u32[]{:S(2)}) collective-permute-start(f32[2,128]{1,0:T(2,128)} %param.5), channel_id=1, source_target_pairs={{0,8},{2,10},{4,12},{6,14},{8,0},{10,2},{12,4},{14,6},{16,24},{18,... | collective-permute-start | bytes 3080 | tf_op jit(solution)/shard_map/ppermute | solution.py:21
  3.1 3.2 %copy-start.1 = (f32[2,1024]{1,0:T(2,128)S(1)}, f32[2,1024]{1,0:T(2,128)}, u32[]{:S(2)}) copy-start(f32[2,1024]{1,0:T(2,128)} %param.4) | copy-start | bytes 24580
  3.1 9.3 %copy-start = (f32[1024,128]{1,0:T(8,128)S(1)}, f32[1024,128]{1,0:T(8,128)}, u32[]{:S(2)}) copy-start(f32[1024,128]{1,0:T(8,128)} %param.3) | copy-start | bytes 1572868
  4.2 8.2 %collective-permute-start.5 = (f32[2,256,128]{2,1,0:T(8,128)S(1)}, f32[2,256,128]{2,1,0:T(8,128)S(1)}, u32[]{:S(2)}, u32[]{:S(2)}) collective-permute-start(f32[2,256,128]{2,1,0:T(8,128)S(1)} %get-tuple-element.65), channel_id=1, source_target_pairs={{0,8},{2,10},{4,12},{6,14},{8,0},{10,2},{12,4},{14,6},{16,24},{18,... | collective-permute-start | bytes 786440 | tf_op jit(solution)/shard_map/ppermute | solution.py:21
  4.3 8.1 %collective-permute-start = (f32[2,256,128]{2,1,0:T(8,128)S(1)}, f32[2,256,128]{2,1,0:T(8,128)S(1)}, u32[]{:S(2)}, u32[]{:S(2)}) collective-permute-start(f32[2,256,128]{2,1,0:T(8,128)S(1)} %get-tuple-element.66), channel_id=1, source_target_pairs={{0,1},{1,0},{2,3},{3,2},{4,5},{5,4},{6,7},{7,6},{8,9},{9,8},{10,11... | collective-permute-start | bytes 786440 | tf_op jit(solution)/shard_map/ppermute | solution.py:21
  6.2 6.0 %collective-permute-start.11 = (f32[2,1024]{1,0:T(2,128)S(1)}, f32[2,1024]{1,0:T(2,128)S(1)}, u32[]{:S(2)}, u32[]{:S(2)}) collective-permute-start(f32[2,1024]{1,0:T(2,128)S(1)} %copy-done.1), channel_id=1, source_target_pairs={{0,1},{1,0},{2,3},{3,2},{4,5},{5,4},{6,7},{7,6},{8,9},{9,8},{10,11... | collective-permute-start | bytes 24584 | tf_op jit(solution)/shard_map/ppermute | solution.py:21
  6.4 0.7 copy-start.2
  7.2 4.7 %collective-permute-start.3 = (f32[4,128]{1,0:T(4,128)S(1)}, f32[4,128]{1,0:T(4,128)S(1)}, u32[]{:S(2)}, u32[]{:S(2)}) collective-permute-start(f32[4,128]{1,0:T(4,128)S(1)} %pad_maximum_fusion.4), channel_id=1, source_target_pairs={{0,16},{2,18},{4,20},{6,22},{8,24},{10,26},{12,28},{14,30},{16,0},... | collective-permute-start | bytes 6152 | tf_op jit(solution)/shard_map/ppermute | solution.py:21
  12.7 29.9 %collective-permute-start.1 = (f32[2,256,128]{2,1,0:T(8,128)S(1)}, f32[2,256,128]{2,1,0:T(8,128)S(1)}, u32[]{:S(2)}, u32[]{:S(2)}) collective-permute-start(f32[2,256,128]{2,1,0:T(8,128)S(1)} %pad_maximum_fusion), channel_id=1, source_target_pairs={{0,16},{2,18},{4,20},{6,22},{8,24},{10,26},{12,28},{14,30},{16,0},... | collective-permute-start | bytes 786440 | tf_op jit(solution)/shard_map/ppermute | solution.py:21
  15.6 5.0 %collective-permute-start.14 = (f32[256,128]{1,0:T(8,128)S(1)}, f32[256,128]{1,0:T(8,128)S(1)}, u32[]{:S(2)}, u32[]{:S(2)}) collective-permute-start(f32[256,128]{1,0:T(8,128)S(1)} %fusion.9), channel_id=1, source_target_pairs={{0,1},{1,0},{2,3},{3,2},{4,5},{5,4},{6,7},{7,6},{8,9},{9,8},{10,11... | collective-permute-start | bytes 393224 | tf_op jit(solution)/shard_map/ppermute | solution.py:21
  17.4 18.6 %collective-permute-start.12 = (f32[256,128]{1,0:T(8,128)S(1)}, f32[256,128]{1,0:T(8,128)S(1)}, u32[]{:S(2)}, u32[]{:S(2)}) collective-permute-start(f32[256,128]{1,0:T(8,128)S(1)} %fusion.15), channel_id=1, source_target_pairs={{0,16},{2,18},{4,20},{6,22},{8,24},{10,26},{12,28},{14,30},{16,0},... | collective-permute-start | bytes 393224 | tf_op jit(solution)/shard_map/ppermute | solution.py:21
  20.8 17.4 %collective-permute-start.15 = (f32[256,128]{1,0:T(8,128)S(1)}, f32[256,128]{1,0:T(8,128)S(1)}, u32[]{:S(2)}, u32[]{:S(2)}) collective-permute-start(f32[256,128]{1,0:T(8,128)S(1)} %fusion.20), channel_id=1, source_target_pairs={{0,16},{2,18},{4,20},{6,22},{8,24},{10,26},{12,28},{14,30},{16,0},... | collective-permute-start | bytes 393224 | tf_op jit(solution)/shard_map/ppermute | solution.py:21
  36.0 5.0 %collective-permute-start.13 = (f32[256,128]{1,0:T(8,128)S(1)}, f32[256,128]{1,0:T(8,128)S(1)}, u32[]{:S(2)}, u32[]{:S(2)}) collective-permute-start(f32[256,128]{1,0:T(8,128)S(1)} %add.89), channel_id=1, source_target_pairs={{0,8},{2,10},{4,12},{6,14},{8,0},{10,2},{12,4},{14,6},{16,24},{18,... | collective-permute-start | bytes 393224 | tf_op jit(solution)/shard_map/ppermute | solution.py:21
  36.1 9.2 %collective-permute-start.6 = (f32[2,256,128]{2,1,0:T(8,128)S(1)}, f32[2,256,128]{2,1,0:T(8,128)S(1)}, u32[]{:S(2)}, u32[]{:S(2)}) collective-permute-start(f32[2,256,128]{2,1,0:T(8,128)S(1)} %get-tuple-element.58), channel_id=1, source_target_pairs={{0,1},{1,0},{2,3},{3,2},{4,5},{5,4},{6,7},{7,6},{8,9},{9,8},{10,11... | collective-permute-start | bytes 786440 | tf_op jit(solution)/shard_map/ppermute | solution.py:21
  37.5 11.2 %collective-permute-start.7 = (f32[2,256,128]{2,1,0:T(8,128)S(1)}, f32[2,256,128]{2,1,0:T(8,128)S(1)}, u32[]{:S(2)}, u32[]{:S(2)}) collective-permute-start(f32[2,256,128]{2,1,0:T(8,128)S(1)} %get-tuple-element.59), channel_id=1, source_target_pairs={{0,1},{1,0},{2,3},{3,2},{4,5},{5,4},{6,7},{7,6},{8,9},{9,8},{10,11... | collective-permute-start | bytes 786440 | tf_op jit(solution)/shard_map/ppermute | solution.py:21
  41.1 12.0 %collective-permute-start.16 = (f32[512,128]{1,0:T(8,128)S(1)}, f32[512,128]{1,0:T(8,128)S(1)}, u32[]{:S(2)}, u32[]{:S(2)}) collective-permute-start(f32[512,128]{1,0:T(8,128)S(1)} %maximum_multiply_fusion.refs_0_), channel_id=1, source_target_pairs={{0,2},{2,0},{4,6},{6,4},{8,10},{10,8},{12,14},{14,12},{16,18},{18,... | collective-permute-start | bytes 786440 | tf_op jit(solution)/shard_map/ppermute | solution.py:21
  41.2 8.7 %collective-permute-start.17 = (f32[512,128]{1,0:T(8,128)S(1)}, f32[512,128]{1,0:T(8,128)S(1)}, u32[]{:S(2)}, u32[]{:S(2)}) collective-permute-start(f32[512,128]{1,0:T(8,128)S(1)} %maximum_multiply_fusion.refs_0_), channel_id=1, source_target_pairs={{0,4},{2,6},{4,0},{6,2},{8,12},{10,14},{12,8},{14,10},{16,20},{18,... | collective-permute-start | bytes 786440 | tf_op jit(solution)/shard_map/ppermute | solution.py:21
  42.7 23.3 %collective-permute-start.4 = (f32[512,128]{1,0:T(8,128)S(1)}, f32[512,128]{1,0:T(8,128)S(1)}, u32[]{:S(2)}, u32[]{:S(2)}) collective-permute-start(f32[512,128]{1,0:T(8,128)S(1)} %get-tuple-element.63), channel_id=1, source_target_pairs={{0,8},{2,10},{4,12},{6,14},{8,0},{10,2},{12,4},{14,6},{16,24},{18,... | collective-permute-start | bytes 786440 | tf_op jit(solution)/shard_map/ppermute | solution.py:21
  49.9 3.3 %collective-permute-start.18 = (f32[512,128]{1,0:T(8,128)S(1)}, f32[512,128]{1,0:T(8,128)S(1)}, u32[]{:S(2)}, u32[]{:S(2)}) collective-permute-start(f32[512,128]{1,0:T(8,128)S(1)} %collective-permute-done.17.refs_2_), channel_id=1, source_target_pairs={{0,2},{2,0},{4,6},{6,4},{8,10},{10,8},{12,14},{14,12},{16,18},{18,... | collective-permute-start | bytes 786440 | tf_op jit(solution)/shard_map/ppermute | solution.py:21
  50.0 16.0 %collective-permute-start.8 = (f32[512,128]{1,0:T(8,128)S(1)}, f32[512,128]{1,0:T(8,128)S(1)}, u32[]{:S(2)}, u32[]{:S(2)}) collective-permute-start(f32[512,128]{1,0:T(8,128)S(1)} %get-tuple-element.51), channel_id=1, source_target_pairs={{0,16},{2,18},{4,20},{6,22},{8,24},{10,26},{12,28},{14,30},{16,0},... | collective-permute-start | bytes 786440 | tf_op jit(solution)/shard_map/ppermute | solution.py:21
  52.7 14.0 %collective-permute-start.9 = (f32[512,128]{1,0:T(8,128)S(1)}, f32[512,128]{1,0:T(8,128)S(1)}, u32[]{:S(2)}, u32[]{:S(2)}) collective-permute-start(f32[512,128]{1,0:T(8,128)S(1)} %get-tuple-element.62), channel_id=1, source_target_pairs={{0,8},{2,10},{4,12},{6,14},{8,0},{10,2},{12,4},{14,6},{16,24},{18,... | collective-permute-start | bytes 786440 | tf_op jit(solution)/shard_map/ppermute | solution.py:21
  53.1 23.3 %collective-permute-start.10 = (f32[512,128]{1,0:T(8,128)S(1)}, f32[512,128]{1,0:T(8,128)S(1)}, u32[]{:S(2)}, u32[]{:S(2)}) collective-permute-start(f32[512,128]{1,0:T(8,128)S(1)} %get-tuple-element.60), channel_id=1, source_target_pairs={{0,16},{2,18},{4,20},{6,22},{8,24},{10,26},{12,28},{14,30},{16,0},... | collective-permute-start | bytes 786440 | tf_op jit(solution)/shard_map/ppermute | solution.py:21
  76.5 18.9 %collective-permute-start.20 = (f32[512,128]{1,0:T(8,128)S(1)}, f32[512,128]{1,0:T(8,128)S(1)}, u32[]{:S(2)}, u32[]{:S(2)}) collective-permute-start(f32[512,128]{1,0:T(8,128)S(1)} %add_multiply_fusion.1.refs_2_), channel_id=1, source_target_pairs={{0,2},{2,0},{4,6},{6,4},{8,10},{10,8},{12,14},{14,12},{16,18},{18,... | collective-permute-start | bytes 786440 | tf_op jit(solution)/shard_map/ppermute | solution.py:21
  76.6 10.6 %collective-permute-start.22 = (f32[512,128]{1,0:T(8,128)S(1)}, f32[512,128]{1,0:T(8,128)S(1)}, u32[]{:S(2)}, u32[]{:S(2)}) collective-permute-start(f32[512,128]{1,0:T(8,128)S(1)} %add_multiply_fusion.1.refs_2_), channel_id=1, source_target_pairs={{0,4},{2,6},{4,0},{6,2},{8,12},{10,14},{12,8},{14,10},{16,20},{18,... | collective-permute-start | bytes 786440 | tf_op jit(solution)/shard_map/ppermute | solution.py:21
  78.2 17.2 %collective-permute-start.21 = (f32[512,128]{1,0:T(8,128)S(1)}, f32[512,128]{1,0:T(8,128)S(1)}, u32[]{:S(2)}, u32[]{:S(2)}) collective-permute-start(f32[512,128]{1,0:T(8,128)S(1)} %add_multiply_fusion.refs_3_), channel_id=1, source_target_pairs={{0,2},{2,0},{4,6},{6,4},{8,10},{10,8},{12,14},{14,12},{16,18},{18,... | collective-permute-start | bytes 786440 | tf_op jit(solution)/shard_map/ppermute | solution.py:21
  78.4 12.5 %collective-permute-start.23 = (f32[512,128]{1,0:T(8,128)S(1)}, f32[512,128]{1,0:T(8,128)S(1)}, u32[]{:S(2)}, u32[]{:S(2)}) collective-permute-start(f32[512,128]{1,0:T(8,128)S(1)} %add_multiply_fusion.refs_3_), channel_id=1, source_target_pairs={{0,4},{2,6},{4,0},{6,2},{8,12},{10,14},{12,8},{14,10},{16,20},{18,... | collective-permute-start | bytes 786440 | tf_op jit(solution)/shard_map/ppermute | solution.py:21
  79.1 16.3 %collective-permute-start.19 = (f32[512,128]{1,0:T(8,128)S(1)}, f32[512,128]{1,0:T(8,128)S(1)}, u32[]{:S(2)}, u32[]{:S(2)}) collective-permute-start(f32[512,128]{1,0:T(8,128)S(1)} %pad_maximum_fusion.3), channel_id=1, source_target_pairs={{0,1},{2,3},{4,5},{6,7},{8,9},{10,11},{12,13},{14,15},{16,17},{18,... | collective-permute-start | bytes 786440 | tf_op jit(solution)/shard_map/ppermute | solution.py:319
  87.3 8.1 %collective-permute-start.24 = (f32[512,128]{1,0:T(8,128)S(1)}, f32[512,128]{1,0:T(8,128)S(1)}, u32[]{:S(2)}, u32[]{:S(2)}) collective-permute-start(f32[512,128]{1,0:T(8,128)S(1)} %collective-permute-done.22.refs_6_), channel_id=1, source_target_pairs={{0,2},{2,0},{4,6},{6,4},{8,10},{10,8},{12,14},{14,12},{16,18},{18,... | collective-permute-start | bytes 786440 | tf_op jit(solution)/shard_map/ppermute | solution.py:21
  90.9 4.5 %collective-permute-start.25 = (f32[512,128]{1,0:T(8,128)S(1)}, f32[512,128]{1,0:T(8,128)S(1)}, u32[]{:S(2)}, u32[]{:S(2)}) collective-permute-start(f32[512,128]{1,0:T(8,128)S(1)} %collective-permute-done.23.refs_7_), channel_id=1, source_target_pairs={{0,2},{2,0},{4,6},{6,4},{8,10},{10,8},{12,14},{14,12},{16,18},{18,... | collective-permute-start | bytes 786440 | tf_op jit(solution)/shard_map/ppermute | solution.py:21

commit v12 on v11

--- a/solution.py
+++ b/solution.py
@@ -263,12 +263,6 @@
     parts_q = [flat(jnp.stack(own_mixed(1, a, b))) for a, b in zip((even_q, odd_q), other_q)]
     panel_q = of_half(parts_q, none, none)
     far_q = swapped(panel_q, "col", high)
-    received_q = swapped(of_half(parts_q, ~in_high, in_low), "col", high)
-    parts_p = flat(jnp.where(in_high, far_own, own_p)), flat(jnp.where(in_high, own_p, far_own))
-    panel_p = of_bit(parts_p, none, none)
-    near_p = swapped(panel_p, "col", low)
-    received_p = swapped(of_bit(parts_p, in_high, ~in_low), "col", low)
-
     info = jnp.stack(
         [
             (col_pos < blocks).astype(jnp.int32),
@@ -293,6 +287,12 @@
         compiler_params=params,
         name="eliminate_0",
     )(info, *lead_pieces)
+    far_own, parts_q, *state = lax.optimization_barrier((far_own, parts_q, *state))
+    parts_p = flat(jnp.where(in_high, far_own, own_p)), flat(jnp.where(in_high, own_p, far_own))
+    panel_p = of_bit(parts_p, none, none)
+    near_p = swapped(panel_p, "col", low)
+    received_q = swapped(of_half(parts_q, ~in_high, in_low), "col", high)
+    received_p = swapped(of_bit(parts_p, in_high, ~in_low), "col", low)
     kept_p, kept_q = of_bit(parts_p, in_high, in_low), of_half(parts_q, in_high, in_low)
     scale = diag_of(in_high, in_low)[1]
 
@@ -307,13 +307,13 @@
             compiler_params=params,
         )(*state)
         if k == 1:
-            near_p, far_q, received_p, received_q, *state = lax.optimization_barrier(
-                (near_p, far_q, received_p, received_q, *state)
-            )
+            near_p, far_q, *state = lax.optimization_barrier((near_p, far_q, *state))
             panel_p = spread(lead_scale * (panel_p + near_p))
             pieces_p = gather(panel_p)
             panel_q, _ = lax.optimization_barrier((panel_q, panel_p))
             pieces_q = gather(spread(lead_scale * (panel_q + far_q)))
+        if k == blocks - 2:
+            received_p, received_q, *state = lax.optimization_barrier((received_p, received_q, *state))
             own = scale * (kept_p + received_p), scale * (kept_q + received_q)
             own_top = jnp.concatenate([v[:SPLIT] for v in own], 0)
             far_top = lax.ppermute(own_top, "row", [(0, 1)])

time: 101 us -> 106 us (1.050)
  starting transfers between devices: 26 us -> 34.2 us
  waiting for transfers between devices: 43.3 us -> 39.6 us
    ppermute x25, starting transfers between devices: 22.6 us -> 30.9 us  [swapped(): lax.ppermute(x, axis, [(i, i ^ mask) for i in range(lax.axis_size(axis))])]
    ppermute x25, waiting for transfers between devices: 43.3 us -> 39.6 us  [swapped(): lax.ppermute(x, axis, [(i, i ^ mask) for i in range(lax.axis_size(axis))])]
  transfers between devices with their start and end apart: 26 -> 26, of which waited for: 11 -> 8; matrix products, arithmetic and copies ran while one was open for 3% -> 3% of each run, Pallas kernels for 22% -> 21%
where the time goes in v12:
time: 106 us
  waiting for transfers between devices  39.6 us (37%)
  starting transfers between devices  34.2 us (32%)
  Pallas kernels  27.7 us (26%)
  local copies, waits for them, and re-layouts  1.93 us (2%)
  other arithmetic  1.77 us (2%)
    ppermute x25, waiting for transfers between devices, swapped(): lax.ppermute(x, axis, [(i, i ^ mask) for i in range(lax.axis_size(axis))])  39.6 us
    ppermute x25, starting transfers between devices, swapped(): lax.ppermute(x, axis, [(i, i ^ mask) for i in range(lax.axis_size(axis))])  30.9 us
    pallas_call x3, Pallas kernels, shards(): pl.pallas_call(functools.partial(next_kernel, k), out_shape=state_shapes,...  15 us
    pallas_call x1, Pallas kernels, shards(): pl.pallas_call(first_kernel, out_shape=state_shapes, in_specs=[smem] + [v...  6.98 us
    pallas_call x1, Pallas kernels, shards(): pl.pallas_call(last_kernel, out_shape=jax.ShapeDtypeStruct((height, width...  5.72 us
    ppermute x1, starting transfers between devices, shards(): far_top = lax.ppermute(own_top, 'row', [(0, 1)])  3.26 us
  transfers between devices with their start and end apart: 26, of which 8 were waited for; matrix products, arithmetic and copies ran while one was open for 3% of the time, Pallas kernels for 21%

profile of v12, /device:TPU:0, one launch (start us, length us, event | category | flops | bytes accessed | tf_op | source)
XLA Modules:
  0.0 105.6 jit_solution(14930030623768548097)
XLA Ops:
  0.0 3.1 %collective-permute-start.5 = (f32[2,128]{1,0:T(2,128)}, f32[2,128]{1,0:T(2,128)S(1)}, u32[]{:S(2)}, u32[]{:S(2)}) collective-permute-start(f32[2,128]{1,0:T(2,128)} %param.5), channel_id=1, source_target_pairs={{0,8},{2,10},{4,12},{6,14},{8,0},{10,2},{12,4},{14,6},{16,24},{18,... | collective-permute-start | bytes 3080 | tf_op jit(solution)/shard_map/ppermute | solution.py:21
  3.1 1.1 %slice_bitcast_fusion = (f32[2,256,128]{2,1,0:T(8,128)S(1)}, f32[2,256,128]{2,1,0:T(8,128)S(1)}) fusion(f32[2,1,2,256,128]{4,3,2,0,1:T(8,128)} %bitcast.131), kind=kLoop, calls=%fused_computation.2 | loop fusion | bytes 1048576 | tf_op jit(solution)/shard_map/reshape;squeeze | solution.py:190
  4.2 0.1 collective-permute-start.2
  4.3 2.0 %collective-permute-start = (f32[2,256,128]{2,1,0:T(8,128)S(1)}, f32[2,256,128]{2,1,0:T(8,128)S(1)}, u32[]{:S(2)}, u32[]{:S(2)}) collective-permute-start(f32[2,256,128]{2,1,0:T(8,128)S(1)} %get-tuple-element.84), channel_id=1, source_target_pairs={{0,1},{1,0},{2,3},{3,2},{4,5},{5,4},{6,7},{7,6},{8,9},{9,8},{10,11... | collective-permute-start | bytes 786440 | tf_op jit(solution)/shard_map/ppermute | solution.py:21
  6.2 0.1 collective-permute-start.7
  6.5 0.0 copy-start.2
  6.5 0.7 copy-done.2
  7.2 0.1 pad_add_fusion.info
  7.2 0.0 collective-permute-done.5
  7.3 3.0 %collective-permute-start.6 = (f32[4,128]{1,0:T(4,128)S(1)}, f32[4,128]{1,0:T(4,128)S(1)}, u32[]{:S(2)}, u32[]{:S(2)}) collective-permute-start(f32[4,128]{1,0:T(4,128)S(1)} %pad_maximum_fusion.4), channel_id=1, source_target_pairs={{0,16},{2,18},{4,20},{6,22},{8,24},{10,26},{12,28},{14,30},{16,0},... | collective-permute-start | bytes 6152 | tf_op jit(solution)/shard_map/ppermute | solution.py:21
  10.3 1.7 %collective-permute-done.6 = f32[4,128]{1,0:T(4,128)S(1)} collective-permute-done((f32[4,128]{1,0:T(4,128)S(1)}, f32[4,128]{1,0:T(4,128)S(1)}, u32[]{:S(2)}, u32[]{:S(2)}) %collective-permute-start.6) | collective-permute-done | bytes 2080 | tf_op jit(solution)/shard_map/ppermute | solution.py:21
  12.0 0.2 collective-permute-done.7
  12.4 0.0 collective-permute-done.2
  12.4 0.0 collective-permute-done
  12.4 0.1 multiply_add_fusion.2
  12.5 1.7 %collective-permute-start.4 = (f32[2,256,128]{2,1,0:T(8,128)S(1)}, f32[2,256,128]{2,1,0:T(8,128)S(1)}, u32[]{:S(2)}, u32[]{:S(2)}) collective-permute-start(f32[2,256,128]{2,1,0:T(8,128)S(1)} %get-tuple-element.76), channel_id=1, source_target_pairs={{0,1},{1,0},{2,3},{3,2},{4,5},{5,4},{6,7},{7,6},{8,9},{9,8},{10,11... | collective-permute-start | bytes 786440 | tf_op jit(solution)/shard_map/ppermute | solution.py:21
  14.2 0.4 collective-permute-start.3
  14.6 0.2 fusion.4
  14.8 1.7 %collective-permute-start.10 = (f32[256,128]{1,0:T(8,128)S(1)}, f32[256,128]{1,0:T(8,128)S(1)}, u32[]{:S(2)}, u32[]{:S(2)}) collective-permute-start(f32[256,128]{1,0:T(8,128)S(1)} %fusion.4), channel_id=1, source_target_pairs={{0,1},{1,0},{2,3},{3,2},{4,5},{5,4},{6,7},{7,6},{8,9},{9,8},{10,11... | collective-permute-start | bytes 393224 | tf_op jit(solution)/shard_map/ppermute | solution.py:21
  16.5 0.2 fusion.10
  16.7 2.7 %collective-permute-start.8 = (f32[256,128]{1,0:T(8,128)S(1)}, f32[256,128]{1,0:T(8,128)S(1)}, u32[]{:S(2)}, u32[]{:S(2)}) collective-permute-start(f32[256,128]{1,0:T(8,128)S(1)} %fusion.10), channel_id=1, source_target_pairs={{0,16},{2,18},{4,20},{6,22},{8,24},{10,26},{12,28},{14,30},{16,0},... | collective-permute-start | bytes 393224 | tf_op jit(solution)/shard_map/ppermute | solution.py:21
  19.3 8.6 %collective-permute-done.10 = f32[256,128]{1,0:T(8,128)S(1)} collective-permute-done((f32[256,128]{1,0:T(8,128)S(1)}, f32[256,128]{1,0:T(8,128)S(1)}, u32[]{:S(2)}, u32[]{:S(2)}) %collective-permute-start.10) | collective-permute-done | bytes 131104 | tf_op jit(solution)/shard_map/ppermute | solution.py:21
  27.9 0.2 fusion.15
  28.1 2.5 %collective-permute-start.11 = (f32[256,128]{1,0:T(8,128)S(1)}, f32[256,128]{1,0:T(8,128)S(1)}, u32[]{:S(2)}, u32[]{:S(2)}) collective-permute-start(f32[256,128]{1,0:T(8,128)S(1)} %fusion.15), channel_id=1, source_target_pairs={{0,16},{2,18},{4,20},{6,22},{8,24},{10,26},{12,28},{14,30},{16,0},... | collective-permute-start | bytes 393224 | tf_op jit(solution)/shard_map/ppermute | solution.py:21
  30.6 0.0 collective-permute-done.8
  30.6 1.6 %collective-permute-start.9 = (f32[256,128]{1,0:T(8,128)S(1)}, f32[256,128]{1,0:T(8,128)S(1)}, u32[]{:S(2)}, u32[]{:S(2)}) collective-permute-start(f32[256,128]{1,0:T(8,128)S(1)} %add.85), channel_id=1, source_target_pairs={{0,8},{2,10},{4,12},{6,14},{8,0},{10,2},{12,4},{14,6},{16,24},{18,... | collective-permute-start | bytes 393224 | tf_op jit(solution)/shard_map/ppermute | solution.py:21
  32.2 0.1 add_multiply_fusion.6
  32.4 1.2 %collective-permute-start.1 = (f32[2,256,128]{2,1,0:T(8,128)S(1)}, f32[2,256,128]{2,1,0:T(8,128)S(1)}, u32[]{:S(2)}, u32[]{:S(2)}) collective-permute-start(f32[2,256,128]{2,1,0:T(8,128)S(1)} %pad_maximum_fusion), channel_id=1, source_target_pairs={{0,16},{2,18},{4,20},{6,22},{8,24},{10,26},{12,28},{14,30},{16,0},... | collective-permute-start | bytes 786440 | tf_op jit(solution)/shard_map/ppermute | solution.py:21
  33.6 5.7 %collective-permute-done.11 = f32[256,128]{1,0:T(8,128)S(1)} collective-permute-done((f32[256,128]{1,0:T(8,128)S(1)}, f32[256,128]{1,0:T(8,128)S(1)}, u32[]{:S(2)}, u32[]{:S(2)}) %collective-permute-start.11) | collective-permute-done | bytes 131104 | tf_op jit(solution)/shard_map/ppermute | solution.py:21
  39.4 0.0 collective-permute-done.9
  39.4 0.1 collective-permute-start.12
  39.5 1.2 %collective-permute-start.13 = (f32[512,128]{1,0:T(8,128)S(1)}, f32[512,128]{1,0:T(8,128)S(1)}, u32[]{:S(2)}, u32[]{:S(2)}) collective-permute-start(f32[512,128]{1,0:T(8,128)S(1)} %maximum_multiply_fusion.refs_0_), channel_id=1, source_target_pairs={{0,4},{2,6},{4,0},{6,2},{8,12},{10,14},{12,8},{14,10},{16,20},{18,... | collective-permute-start | bytes 786440 | tf_op jit(solution)/shard_map/ppermute | solution.py:21
  40.7 0.0 collective-permute-done.4
  40.7 0.0 collective-permute-done.3
  40.7 0.2 select_multiply_fusion
  40.9 0.1 add_multiply_fusion.5
  41.0 7.2 %collective-permute-done.13.refs_2_ = f32[512,128]{1,0:T(8,128)S(1)} collective-permute-done((f32[512,128]{1,0:T(8,128)S(1)}, f32[512,128]{1,0:T(8,128)S(1)}, u32[]{:S(2)}, u32[]{:S(2)}) %collective-permute-start.13) | collective-permute-done | bytes 262176 | tf_op jit(solution)/shard_map/ppermute | solution.py:21
  48.2 0.0 collective-permute-start.14
  48.3 0.6 collective-permute-start.18
  48.9 0.0 collective-permute-done.12.refs_1_
  48.9 0.9 collective-permute-done.14.refs_3_
  49.8 7.0 %eliminate_0.1 = (f32[4,512,128]{2,1,0:T(8,128)S(1)}, f32[4,512,128]{2,1,0:T(8,128)S(1)}, f32[512,128]{1,0:T(8,128)S(1)}) custom-call(s32[4]{0:T(128)S(1)} %pad_add_fusion.info, f32[512,128]{1,0:T(8,128)S(1)} %maximum_multiply_fusion.refs_0_, f32[512,128]{1,0:T(8,128)S(1)} %collective-permute-done.12.refs_1_, ...), custom_call_target="tpu_custom_call" | custom-call | flops 4000000000 | bytes 12000000 | tf_op jit(solution)/shard_map/eliminate_0/pallas_call | solution.py:281
  56.8 0.1 fusion.1
  56.9 5.2 %collective-permute-start.15 = (f32[512,128]{1,0:T(8,128)S(1)}, f32[512,128]{1,0:T(8,128)S(1)}, u32[]{:S(2)}, u32[]{:S(2)}) collective-permute-start(f32[512,128]{1,0:T(8,128)S(1)} %get-tuple-element.79), channel_id=1, source_target_pairs={{0,8},{2,10},{4,12},{6,14},{8,0},{10,2},{12,4},{14,6},{16,24},{18,... | collective-permute-start | bytes 786440 | tf_op jit(solution)/shard_map/ppermute | solution.py:21
  62.1 1.4 %collective-permute-start.16 = (f32[512,128]{1,0:T(8,128)S(1)}, f32[512,128]{1,0:T(8,128)S(1)}, u32[]{:S(2)}, u32[]{:S(2)}) collective-permute-start(f32[512,128]{1,0:T(8,128)S(1)} %multiply_add_fusion.1), channel_id=1, source_target_pairs={{0,16},{2,18},{4,20},{6,22},{8,24},{10,26},{12,28},{14,30},{16,0},... | collective-permute-start | bytes 786440 | tf_op jit(solution)/shard_map/ppermute | solution.py:21
  63.5 0.0 collective-permute-start.17
  63.5 5.8 %shard_map.37 = (f32[4,512,128]{2,1,0:T(8,128)S(1)}, f32[4,512,128]{2,1,0:T(8,128)S(1)}, f32[512,128]{1,0:T(8,128)S(1)}) custom-call(f32[4,512,128]{2,1,0:T(8,128)S(1)} %get-tuple-element.44.old_work, f32[4,512,128]{2,1,0:T(8,128)S(1)} %get-tuple-element.45.old_packed, ...), custom_call_target="tpu_custom_call", output_to_operand_aliasing={{0}: (0, {}), {1}: (1, {}), {2}: (2, {})} | custom-call | flops 4000000000 | bytes 12000000 | tf_op jit(solution)/shard_map/pallas_call | solution.py:300
  69.4 11.1 %collective-permute-done.17 = f32[512,128]{1,0:T(8,128)S(1)} collective-permute-done((f32[512,128]{1,0:T(8,128)S(1)}, f32[512,128]{1,0:T(8,128)S(1)}, u32[]{:S(2)}, u32[]{:S(2)}) %collective-permute-start.17) | collective-permute-done | bytes 262176 | tf_op jit(solution)/shard_map/ppermute | solution.py:21
  80.5 0.1 collective-permute-start.20
  80.6 1.1 %collective-permute-start.22 = (f32[512,128]{1,0:T(8,128)S(1)}, f32[512,128]{1,0:T(8,128)S(1)}, u32[]{:S(2)}, u32[]{:S(2)}) collective-permute-start(f32[512,128]{1,0:T(8,128)S(1)} %add_multiply_fusion.1.refs_2_), channel_id=1, source_target_pairs={{0,4},{2,6},{4,0},{6,2},{8,12},{10,14},{12,8},{14,10},{16,20},{18,... | collective-permute-start | bytes 786440 | tf_op jit(solution)/shard_map/ppermute | solution.py:21
  81.8 0.2 collective-permute-start.21
  82.0 4.7 %shard_map.38 = (f32[4,512,128]{2,1,0:T(8,128)S(1)}, f32[4,512,128]{2,1,0:T(8,128)S(1)}, f32[512,128]{1,0:T(8,128)S(1)}) custom-call(f32[4,512,128]{2,1,0:T(8,128)S(1)} %get-tuple-element.50.old_work, f32[4,512,128]{2,1,0:T(8,128)S(1)} %get-tuple-element.51.old_packed, ...), custom_call_target="tpu_custom_call", output_to_operand_aliasing={{0}: (0, {}), {1}: (1, {}), {2}: (2, {})} | custom-call | flops 4000000000 | bytes 12000000 | tf_op jit(solution)/shard_map/pallas_call | solution.py:300
  86.7 1.0 collective-permute-start.23
  87.7 0.0 collective-permute-done.16
  87.7 0.1 add_multiply_fusion.3
  87.9 3.3 %collective-permute-start.19 = (f32[512,128]{1,0:T(8,128)S(1)}, f32[512,128]{1,0:T(8,128)S(1)}, u32[]{:S(2)}, u32[]{:S(2)}) collective-permute-start(f32[512,128]{1,0:T(8,128)S(1)} %pad_maximum_fusion.3), channel_id=1, source_target_pairs={{0,1},{2,3},{4,5},{6,7},{8,9},{10,11},{12,13},{14,15},{16,17},{18,... | collective-permute-start | bytes 786440 | tf_op jit(solution)/shard_map/ppermute | solution.py:319
  91.2 0.0 collective-permute-done.22.refs_6_
  91.2 0.1 collective-permute-start.24
  91.3 4.1 %collective-permute-done.23.refs_7_ = f32[512,128]{1,0:T(8,128)S(1)} collective-permute-done((f32[512,128]{1,0:T(8,128)S(1)}, f32[512,128]{1,0:T(8,128)S(1)}, u32[]{:S(2)}, u32[]{:S(2)}) %collective-permute-start.23) | collective-permute-done | bytes 262176 | tf_op jit(solution)/shard_map/ppermute | solution.py:21
  95.4 0.0 collective-permute-start.25
  95.4 4.4 %shard_map.39 = (f32[4,512,128]{2,1,0:T(8,128)S(1)}, f32[4,512,128]{2,1,0:T(8,128)S(1)}, f32[512,128]{1,0:T(8,128)S(1)}) custom-call(f32[4,512,128]{2,1,0:T(8,128)S(1)} %get-tuple-element.58.old_work, f32[4,512,128]{2,1,0:T(8,128)S(1)} %get-tuple-element.59.old_packed, ...), custom_call_target="tpu_custom_call", output_to_operand_aliasing={{0}: (0, {}), {1}: (1, {}), {2}: (2, {})} | custom-call | flops 4000000000 | bytes 12000000 | tf_op jit(solution)/shard_map/pallas_call | solution.py:300
  99.8 0.0 collective-permute-done.19
  99.9 0.0 collective-permute-done.21.refs_5_
  99.9 5.7 %own_columns.1 = f32[1024,128]{1,0:T(8,128)} custom-call(s32[4]{0:T(128)S(1)} %pad_add_fusion.info, f32[4,512,128]{2,1,0:T(8,128)S(1)} %get-tuple-element.64.work, f32[4,512,128]{2,1,0:T(8,128)S(1)} %get-tuple-element.65.packed, f32[512,128]{1,0:T(8,128)S(1)} %get-tuple-element.66.inverted, f32[512,128]{1,0:T(8,128)S(1)} %broadcast_select_fusion.own_top, ...), custom_call_target="tpu_custom_call" | custom-call | flops 4000000000 | bytes 12000000 | tf_op jit(solution)/shard_map/own_columns/pallas_call | solution.py:324
  (51 shorter events, 0.6 us)
Async XLA Ops:
  0.0 7.2 %collective-permute-start.5 = (f32[2,128]{1,0:T(2,128)}, f32[2,128]{1,0:T(2,128)S(1)}, u32[]{:S(2)}, u32[]{:S(2)}) collective-permute-start(f32[2,128]{1,0:T(2,128)} %param.5), channel_id=1, source_target_pairs={{0,8},{2,10},{4,12},{6,14},{8,0},{10,2},{12,4},{14,6},{16,24},{18,... | collective-permute-start | bytes 3080 | tf_op jit(solution)/shard_map/ppermute | solution.py:21
  3.1 3.2 %copy-start.1 = (f32[2,1024]{1,0:T(2,128)S(1)}, f32[2,1024]{1,0:T(2,128)}, u32[]{:S(2)}) copy-start(f32[2,1024]{1,0:T(2,128)} %param.4) | copy-start | bytes 24580
  3.1 9.3 %copy-start = (f32[1024,128]{1,0:T(8,128)S(1)}, f32[1024,128]{1,0:T(8,128)}, u32[]{:S(2)}) copy-start(f32[1024,128]{1,0:T(8,128)} %param.3) | copy-start | bytes 1572868
  4.2 8.2 %collective-permute-start.2 = (f32[2,256,128]{2,1,0:T(8,128)S(1)}, f32[2,256,128]{2,1,0:T(8,128)S(1)}, u32[]{:S(2)}, u32[]{:S(2)}) collective-permute-start(f32[2,256,128]{2,1,0:T(8,128)S(1)} %get-tuple-element.83), channel_id=1, source_target_pairs={{0,8},{2,10},{4,12},{6,14},{8,0},{10,2},{12,4},{14,6},{16,24},{18,... | collective-permute-start | bytes 786440 | tf_op jit(solution)/shard_map/ppermute | solution.py:21
  4.3 8.1 %collective-permute-start = (f32[2,256,128]{2,1,0:T(8,128)S(1)}, f32[2,256,128]{2,1,0:T(8,128)S(1)}, u32[]{:S(2)}, u32[]{:S(2)}) collective-permute-start(f32[2,256,128]{2,1,0:T(8,128)S(1)} %get-tuple-element.84), channel_id=1, source_target_pairs={{0,1},{1,0},{2,3},{3,2},{4,5},{5,4},{6,7},{7,6},{8,9},{9,8},{10,11... | collective-permute-start | bytes 786440 | tf_op jit(solution)/shard_map/ppermute | solution.py:21
  6.2 6.0 %collective-permute-start.7 = (f32[2,1024]{1,0:T(2,128)S(1)}, f32[2,1024]{1,0:T(2,128)S(1)}, u32[]{:S(2)}, u32[]{:S(2)}) collective-permute-start(f32[2,1024]{1,0:T(2,128)S(1)} %copy-done.1), channel_id=1, source_target_pairs={{0,1},{1,0},{2,3},{3,2},{4,5},{5,4},{6,7},{7,6},{8,9},{9,8},{10,11... | collective-permute-start | bytes 24584 | tf_op jit(solution)/shard_map/ppermute | solution.py:21
  6.5 0.7 copy-start.2
  7.3 4.7 %collective-permute-start.6 = (f32[4,128]{1,0:T(4,128)S(1)}, f32[4,128]{1,0:T(4,128)S(1)}, u32[]{:S(2)}, u32[]{:S(2)}) collective-permute-start(f32[4,128]{1,0:T(4,128)S(1)} %pad_maximum_fusion.4), channel_id=1, source_target_pairs={{0,16},{2,18},{4,20},{6,22},{8,24},{10,26},{12,28},{14,30},{16,0},... | collective-permute-start | bytes 6152 | tf_op jit(solution)/shard_map/ppermute | solution.py:21
  12.5 28.1 %collective-permute-start.4 = (f32[2,256,128]{2,1,0:T(8,128)S(1)}, f32[2,256,128]{2,1,0:T(8,128)S(1)}, u32[]{:S(2)}, u32[]{:S(2)}) collective-permute-start(f32[2,256,128]{2,1,0:T(8,128)S(1)} %get-tuple-element.76), channel_id=1, source_target_pairs={{0,1},{1,0},{2,3},{3,2},{4,5},{5,4},{6,7},{7,6},{8,9},{9,8},{10,11... | collective-permute-start | bytes 786440 | tf_op jit(solution)/shard_map/ppermute | solution.py:21
  14.2 26.5 %collective-permute-start.3 = (f32[2,256,128]{2,1,0:T(8,128)S(1)}, f32[2,256,128]{2,1,0:T(8,128)S(1)}, u32[]{:S(2)}, u32[]{:S(2)}) collective-permute-start(f32[2,256,128]{2,1,0:T(8,128)S(1)} %get-tuple-element.77), channel_id=1, source_target_pairs={{0,1},{1,0},{2,3},{3,2},{4,5},{5,4},{6,7},{7,6},{8,9},{9,8},{10,11... | collective-permute-start | bytes 786440 | tf_op jit(solution)/shard_map/ppermute | solution.py:21
  14.8 13.1 %collective-permute-start.10 = (f32[256,128]{1,0:T(8,128)S(1)}, f32[256,128]{1,0:T(8,128)S(1)}, u32[]{:S(2)}, u32[]{:S(2)}) collective-permute-start(f32[256,128]{1,0:T(8,128)S(1)} %fusion.4), channel_id=1, source_target_pairs={{0,1},{1,0},{2,3},{3,2},{4,5},{5,4},{6,7},{7,6},{8,9},{9,8},{10,11... | collective-permute-start | bytes 393224 | tf_op jit(solution)/shard_map/ppermute | solution.py:21
  16.7 13.9 %collective-permute-start.8 = (f32[256,128]{1,0:T(8,128)S(1)}, f32[256,128]{1,0:T(8,128)S(1)}, u32[]{:S(2)}, u32[]{:S(2)}) collective-permute-start(f32[256,128]{1,0:T(8,128)S(1)} %fusion.10), channel_id=1, source_target_pairs={{0,16},{2,18},{4,20},{6,22},{8,24},{10,26},{12,28},{14,30},{16,0},... | collective-permute-start | bytes 393224 | tf_op jit(solution)/shard_map/ppermute | solution.py:21
  28.1 11.2 %collective-permute-start.11 = (f32[256,128]{1,0:T(8,128)S(1)}, f32[256,128]{1,0:T(8,128)S(1)}, u32[]{:S(2)}, u32[]{:S(2)}) collective-permute-start(f32[256,128]{1,0:T(8,128)S(1)} %fusion.15), channel_id=1, source_target_pairs={{0,16},{2,18},{4,20},{6,22},{8,24},{10,26},{12,28},{14,30},{16,0},... | collective-permute-start | bytes 393224 | tf_op jit(solution)/shard_map/ppermute | solution.py:21
  30.6 8.8 %collective-permute-start.9 = (f32[256,128]{1,0:T(8,128)S(1)}, f32[256,128]{1,0:T(8,128)S(1)}, u32[]{:S(2)}, u32[]{:S(2)}) collective-permute-start(f32[256,128]{1,0:T(8,128)S(1)} %add.85), channel_id=1, source_target_pairs={{0,8},{2,10},{4,12},{6,14},{8,0},{10,2},{12,4},{14,6},{16,24},{18,... | collective-permute-start | bytes 393224 | tf_op jit(solution)/shard_map/ppermute | solution.py:21
  32.4 24.4 %collective-permute-start.1 = (f32[2,256,128]{2,1,0:T(8,128)S(1)}, f32[2,256,128]{2,1,0:T(8,128)S(1)}, u32[]{:S(2)}, u32[]{:S(2)}) collective-permute-start(f32[2,256,128]{2,1,0:T(8,128)S(1)} %pad_maximum_fusion), channel_id=1, source_target_pairs={{0,16},{2,18},{4,20},{6,22},{8,24},{10,26},{12,28},{14,30},{16,0},... | collective-permute-start | bytes 786440 | tf_op jit(solution)/shard_map/ppermute | solution.py:21
  39.4 9.4 %collective-permute-start.12 = (f32[512,128]{1,0:T(8,128)S(1)}, f32[512,128]{1,0:T(8,128)S(1)}, u32[]{:S(2)}, u32[]{:S(2)}) collective-permute-start(f32[512,128]{1,0:T(8,128)S(1)} %maximum_multiply_fusion.refs_0_), channel_id=1, source_target_pairs={{0,2},{2,0},{4,6},{6,4},{8,10},{10,8},{12,14},{14,12},{16,18},{18,... | collective-permute-start | bytes 786440 | tf_op jit(solution)/shard_map/ppermute | solution.py:21
  39.5 8.7 %collective-permute-start.13 = (f32[512,128]{1,0:T(8,128)S(1)}, f32[512,128]{1,0:T(8,128)S(1)}, u32[]{:S(2)}, u32[]{:S(2)}) collective-permute-start(f32[512,128]{1,0:T(8,128)S(1)} %maximum_multiply_fusion.refs_0_), channel_id=1, source_target_pairs={{0,4},{2,6},{4,0},{6,2},{8,12},{10,14},{12,8},{14,10},{16,20},{18,... | collective-permute-start | bytes 786440 | tf_op jit(solution)/shard_map/ppermute | solution.py:21
  48.2 1.5 %collective-permute-start.14 = (f32[512,128]{1,0:T(8,128)S(1)}, f32[512,128]{1,0:T(8,128)S(1)}, u32[]{:S(2)}, u32[]{:S(2)}) collective-permute-start(f32[512,128]{1,0:T(8,128)S(1)} %collective-permute-done.13.refs_2_), channel_id=1, source_target_pairs={{0,2},{2,0},{4,6},{6,4},{8,10},{10,8},{12,14},{14,12},{16,18},{18,... | collective-permute-start | bytes 786440 | tf_op jit(solution)/shard_map/ppermute | solution.py:21
  48.3 21.1 %collective-permute-start.18 = (f32[512,128]{1,0:T(8,128)S(1)}, f32[512,128]{1,0:T(8,128)S(1)}, u32[]{:S(2)}, u32[]{:S(2)}) collective-permute-start(f32[512,128]{1,0:T(8,128)S(1)} %multiply_add_fusion), channel_id=1, source_target_pairs={{0,16},{2,18},{4,20},{6,22},{8,24},{10,26},{12,28},{14,30},{16,0},... | collective-permute-start | bytes 786440 | tf_op jit(solution)/shard_map/ppermute | solution.py:21
  56.9 29.8 %collective-permute-start.15 = (f32[512,128]{1,0:T(8,128)S(1)}, f32[512,128]{1,0:T(8,128)S(1)}, u32[]{:S(2)}, u32[]{:S(2)}) collective-permute-start(f32[512,128]{1,0:T(8,128)S(1)} %get-tuple-element.79), channel_id=1, source_target_pairs={{0,8},{2,10},{4,12},{6,14},{8,0},{10,2},{12,4},{14,6},{16,24},{18,... | collective-permute-start | bytes 786440 | tf_op jit(solution)/shard_map/ppermute | solution.py:21
  62.1 25.7 %collective-permute-start.16 = (f32[512,128]{1,0:T(8,128)S(1)}, f32[512,128]{1,0:T(8,128)S(1)}, u32[]{:S(2)}, u32[]{:S(2)}) collective-permute-start(f32[512,128]{1,0:T(8,128)S(1)} %multiply_add_fusion.1), channel_id=1, source_target_pairs={{0,16},{2,18},{4,20},{6,22},{8,24},{10,26},{12,28},{14,30},{16,0},... | collective-permute-start | bytes 786440 | tf_op jit(solution)/shard_map/ppermute | solution.py:21
  63.5 16.9 %collective-permute-start.17 = (f32[512,128]{1,0:T(8,128)S(1)}, f32[512,128]{1,0:T(8,128)S(1)}, u32[]{:S(2)}, u32[]{:S(2)}) collective-permute-start(f32[512,128]{1,0:T(8,128)S(1)} %get-tuple-element.78), channel_id=1, source_target_pairs={{0,8},{2,10},{4,12},{6,14},{8,0},{10,2},{12,4},{14,6},{16,24},{18,... | collective-permute-start | bytes 786440 | tf_op jit(solution)/shard_map/ppermute | solution.py:21
  80.5 19.4 %collective-permute-start.20 = (f32[512,128]{1,0:T(8,128)S(1)}, f32[512,128]{1,0:T(8,128)S(1)}, u32[]{:S(2)}, u32[]{:S(2)}) collective-permute-start(f32[512,128]{1,0:T(8,128)S(1)} %add_multiply_fusion.1.refs_2_), channel_id=1, source_target_pairs={{0,2},{2,0},{4,6},{6,4},{8,10},{10,8},{12,14},{14,12},{16,18},{18,... | collective-permute-start | bytes 786440 | tf_op jit(solution)/shard_map/ppermute | solution.py:21
  80.6 10.5 %collective-permute-start.22 = (f32[512,128]{1,0:T(8,128)S(1)}, f32[512,128]{1,0:T(8,128)S(1)}, u32[]{:S(2)}, u32[]{:S(2)}) collective-permute-start(f32[512,128]{1,0:T(8,128)S(1)} %add_multiply_fusion.1.refs_2_), channel_id=1, source_target_pairs={{0,4},{2,6},{4,0},{6,2},{8,12},{10,14},{12,8},{14,10},{16,20},{18,... | collective-permute-start | bytes 786440 | tf_op jit(solution)/shard_map/ppermute | solution.py:21
  81.8 18.1 %collective-permute-start.21 = (f32[512,128]{1,0:T(8,128)S(1)}, f32[512,128]{1,0:T(8,128)S(1)}, u32[]{:S(2)}, u32[]{:S(2)}) collective-permute-start(f32[512,128]{1,0:T(8,128)S(1)} %add_multiply_fusion.refs_3_), channel_id=1, source_target_pairs={{0,2},{2,0},{4,6},{6,4},{8,10},{10,8},{12,14},{14,12},{16,18},{18,... | collective-permute-start | bytes 786440 | tf_op jit(solution)/shard_map/ppermute | solution.py:21
  86.7 8.6 %collective-permute-start.23 = (f32[512,128]{1,0:T(8,128)S(1)}, f32[512,128]{1,0:T(8,128)S(1)}, u32[]{:S(2)}, u32[]{:S(2)}) collective-permute-start(f32[512,128]{1,0:T(8,128)S(1)} %add_multiply_fusion.refs_3_), channel_id=1, source_target_pairs={{0,4},{2,6},{4,0},{6,2},{8,12},{10,14},{12,8},{14,10},{16,20},{18,... | collective-permute-start | bytes 786440 | tf_op jit(solution)/shard_map/ppermute | solution.py:21
  87.9 11.9 %collective-permute-start.19 = (f32[512,128]{1,0:T(8,128)S(1)}, f32[512,128]{1,0:T(8,128)S(1)}, u32[]{:S(2)}, u32[]{:S(2)}) collective-permute-start(f32[512,128]{1,0:T(8,128)S(1)} %pad_maximum_fusion.3), channel_id=1, source_target_pairs={{0,1},{2,3},{4,5},{6,7},{8,9},{10,11},{12,13},{14,15},{16,17},{18,... | collective-permute-start | bytes 786440 | tf_op jit(solution)/shard_map/ppermute | solution.py:319
  91.2 8.7 %collective-permute-start.24 = (f32[512,128]{1,0:T(8,128)S(1)}, f32[512,128]{1,0:T(8,128)S(1)}, u32[]{:S(2)}, u32[]{:S(2)}) collective-permute-start(f32[512,128]{1,0:T(8,128)S(1)} %collective-permute-done.22.refs_6_), channel_id=1, source_target_pairs={{0,2},{2,0},{4,6},{6,4},{8,10},{10,8},{12,14},{14,12},{16,18},{18,... | collective-permute-start | bytes 786440 | tf_op jit(solution)/shard_map/ppermute | solution.py:21
  95.4 4.5 %collective-permute-start.25 = (f32[512,128]{1,0:T(8,128)S(1)}, f32[512,128]{1,0:T(8,128)S(1)}, u32[]{:S(2)}, u32[]{:S(2)}) collective-permute-start(f32[512,128]{1,0:T(8,128)S(1)} %collective-permute-done.23.refs_7_), channel_id=1, source_target_pairs={{0,2},{2,0},{4,6},{6,4},{8,10},{10,8},{12,14},{14,12},{16,18},{18,... | collective-permute-start | bytes 786440 | tf_op jit(solution)/shard_map/ppermute | solution.py:21

commit v13 on v12

--- a/solution.py
+++ b/solution.py
@@ -292,7 +292,7 @@
     panel_p = of_bit(parts_p, none, none)
     near_p = swapped(panel_p, "col", low)
     received_q = swapped(of_half(parts_q, ~in_high, in_low), "col", high)
-    received_p = swapped(of_bit(parts_p, in_high, ~in_low), "col", low)
+    rest_p = of_bit(parts_p, in_high, ~in_low)
     kept_p, kept_q = of_bit(parts_p, in_high, in_low), of_half(parts_q, in_high, in_low)
     scale = diag_of(in_high, in_low)[1]
 
@@ -307,7 +307,8 @@
             compiler_params=params,
         )(*state)
         if k == 1:
-            near_p, far_q, *state = lax.optimization_barrier((near_p, far_q, *state))
+            near_p, far_q, rest_p, *state = lax.optimization_barrier((near_p, far_q, rest_p, *state))
+            received_p = swapped(rest_p, "col", low)
             panel_p = spread(lead_scale * (panel_p + near_p))
             pieces_p = gather(panel_p)
             panel_q, _ = lax.optimization_barrier((panel_q, panel_p))

time: 106 us -> 99.7 us (0.941)
  waiting for transfers between devices: 39.6 us -> 31.9 us
    ppermute x25, waiting for transfers between devices: 39.6 us -> 31.9 us  [swapped(): lax.ppermute(x, axis, [(i, i ^ mask) for i in range(lax.axis_size(axis))])]
  transfers between devices with their start and end apart: 26 -> 26, of which waited for: 8 -> 9; matrix products, arithmetic and copies ran while one was open for 3% -> 3% of each run, Pallas kernels for 21% -> 22%
where the time goes in v13:
time: 99.7 us; the launch traced here: 98.3 us
  starting transfers between devices  34.6 us (35%)
  waiting for transfers between devices  31.9 us (32%)
  Pallas kernels  27.7 us (28%)
  local copies, waits for them, and re-layouts  1.91 us (2%)
  other arithmetic  1.77 us (2%)
    ppermute x25, waiting for transfers between devices, swapped(): lax.ppermute(x, axis, [(i, i ^ mask) for i in range(lax.axis_size(axis))])  31.9 us
    ppermute x25, starting transfers between devices, swapped(): lax.ppermute(x, axis, [(i, i ^ mask) for i in range(lax.axis_size(axis))])  30.9 us
    pallas_call x3, Pallas kernels, shards(): pl.pallas_call(functools.partial(next_kernel, k), out_shape=state_shapes,...  15 us
    pallas_call x1, Pallas kernels, shards(): pl.pallas_call(first_kernel, out_shape=state_shapes, in_specs=[smem] + [v...  6.98 us
    pallas_call x1, Pallas kernels, shards(): pl.pallas_call(last_kernel, out_shape=jax.ShapeDtypeStruct((height, width...  5.74 us
    ppermute x1, starting transfers between devices, shards(): far_top = lax.ppermute(own_top, 'row', [(0, 1)])  3.66 us
  transfers between devices with their start and end apart: 26, of which 9 were waited for; matrix products, arithmetic and copies ran while one was open for 3% of the time, Pallas kernels for 22%

profile of v13, /device:TPU:0, one launch (start us, length us, event | category | flops | bytes accessed | tf_op | source)
XLA Modules:
  0.0 98.3 jit_solution(13952270682651271263)
XLA Ops:
  0.0 3.1 %collective-permute-start.5 = (f32[2,128]{1,0:T(2,128)}, f32[2,128]{1,0:T(2,128)S(1)}, u32[]{:S(2)}, u32[]{:S(2)}) collective-permute-start(f32[2,128]{1,0:T(2,128)} %param.5), channel_id=1, source_target_pairs={{0,8},{2,10},{4,12},{6,14},{8,0},{10,2},{12,4},{14,6},{16,24},{18,... | collective-permute-start | bytes 3080 | tf_op jit(solution)/shard_map/ppermute | solution.py:21
  3.1 1.1 %slice_bitcast_fusion = (f32[2,256,128]{2,1,0:T(8,128)S(1)}, f32[2,256,128]{2,1,0:T(8,128)S(1)}) fusion(f32[2,1,2,256,128]{4,3,2,0,1:T(8,128)} %bitcast.131), kind=kLoop, calls=%fused_computation.2 | loop fusion | bytes 1048576 | tf_op jit(solution)/shard_map/reshape;squeeze | solution.py:190
  4.2 0.1 collective-permute-start.2
  4.3 2.0 %collective-permute-start = (f32[2,256,128]{2,1,0:T(8,128)S(1)}, f32[2,256,128]{2,1,0:T(8,128)S(1)}, u32[]{:S(2)}, u32[]{:S(2)}) collective-permute-start(f32[2,256,128]{2,1,0:T(8,128)S(1)} %get-tuple-element.86), channel_id=1, source_target_pairs={{0,1},{1,0},{2,3},{3,2},{4,5},{5,4},{6,7},{7,6},{8,9},{9,8},{10,11... | collective-permute-start | bytes 786440 | tf_op jit(solution)/shard_map/ppermute | solution.py:21
  6.2 0.1 collective-permute-start.7
  6.4 0.0 copy-start.2
  6.5 0.7 copy-done.2
  7.1 0.1 pad_add_fusion.info
  7.2 0.0 collective-permute-done.5
  7.2 3.0 %collective-permute-start.6 = (f32[4,128]{1,0:T(4,128)S(1)}, f32[4,128]{1,0:T(4,128)S(1)}, u32[]{:S(2)}, u32[]{:S(2)}) collective-permute-start(f32[4,128]{1,0:T(4,128)S(1)} %pad_maximum_fusion.4), channel_id=1, source_target_pairs={{0,16},{2,18},{4,20},{6,22},{8,24},{10,26},{12,28},{14,30},{16,0},... | collective-permute-start | bytes 6152 | tf_op jit(solution)/shard_map/ppermute | solution.py:21
  10.3 1.7 %collective-permute-done.6 = f32[4,128]{1,0:T(4,128)S(1)} collective-permute-done((f32[4,128]{1,0:T(4,128)S(1)}, f32[4,128]{1,0:T(4,128)S(1)}, u32[]{:S(2)}, u32[]{:S(2)}) %collective-permute-start.6) | collective-permute-done | bytes 2080 | tf_op jit(solution)/shard_map/ppermute | solution.py:21
  12.0 0.2 collective-permute-done.7
  12.4 0.0 collective-permute-done.2
  12.4 0.0 collective-permute-done
  12.4 0.1 multiply_add_fusion.2
  12.5 1.7 %collective-permute-start.4 = (f32[2,256,128]{2,1,0:T(8,128)S(1)}, f32[2,256,128]{2,1,0:T(8,128)S(1)}, u32[]{:S(2)}, u32[]{:S(2)}) collective-permute-start(f32[2,256,128]{2,1,0:T(8,128)S(1)} %get-tuple-element.78), channel_id=1, source_target_pairs={{0,1},{1,0},{2,3},{3,2},{4,5},{5,4},{6,7},{7,6},{8,9},{9,8},{10,11... | collective-permute-start | bytes 786440 | tf_op jit(solution)/shard_map/ppermute | solution.py:21
  14.2 0.4 collective-permute-start.3
  14.6 0.2 fusion.4
  14.8 1.7 %collective-permute-start.10 = (f32[256,128]{1,0:T(8,128)S(1)}, f32[256,128]{1,0:T(8,128)S(1)}, u32[]{:S(2)}, u32[]{:S(2)}) collective-permute-start(f32[256,128]{1,0:T(8,128)S(1)} %fusion.4), channel_id=1, source_target_pairs={{0,1},{1,0},{2,3},{3,2},{4,5},{5,4},{6,7},{7,6},{8,9},{9,8},{10,11... | collective-permute-start | bytes 393224 | tf_op jit(solution)/shard_map/ppermute | solution.py:21
  16.5 0.2 fusion.10
  16.7 2.7 %collective-permute-start.8 = (f32[256,128]{1,0:T(8,128)S(1)}, f32[256,128]{1,0:T(8,128)S(1)}, u32[]{:S(2)}, u32[]{:S(2)}) collective-permute-start(f32[256,128]{1,0:T(8,128)S(1)} %fusion.10), channel_id=1, source_target_pairs={{0,16},{2,18},{4,20},{6,22},{8,24},{10,26},{12,28},{14,30},{16,0},... | collective-permute-start | bytes 393224 | tf_op jit(solution)/shard_map/ppermute | solution.py:21
  19.3 8.6 %collective-permute-done.10 = f32[256,128]{1,0:T(8,128)S(1)} collective-permute-done((f32[256,128]{1,0:T(8,128)S(1)}, f32[256,128]{1,0:T(8,128)S(1)}, u32[]{:S(2)}, u32[]{:S(2)}) %collective-permute-start.10) | collective-permute-done | bytes 131104 | tf_op jit(solution)/shard_map/ppermute | solution.py:21
  27.9 0.2 fusion.15
  28.1 2.5 %collective-permute-start.11 = (f32[256,128]{1,0:T(8,128)S(1)}, f32[256,128]{1,0:T(8,128)S(1)}, u32[]{:S(2)}, u32[]{:S(2)}) collective-permute-start(f32[256,128]{1,0:T(8,128)S(1)} %fusion.15), channel_id=1, source_target_pairs={{0,16},{2,18},{4,20},{6,22},{8,24},{10,26},{12,28},{14,30},{16,0},... | collective-permute-start | bytes 393224 | tf_op jit(solution)/shard_map/ppermute | solution.py:21
  30.6 0.0 collective-permute-done.8
  30.6 1.6 %collective-permute-start.9 = (f32[256,128]{1,0:T(8,128)S(1)}, f32[256,128]{1,0:T(8,128)S(1)}, u32[]{:S(2)}, u32[]{:S(2)}) collective-permute-start(f32[256,128]{1,0:T(8,128)S(1)} %add.85), channel_id=1, source_target_pairs={{0,8},{2,10},{4,12},{6,14},{8,0},{10,2},{12,4},{14,6},{16,24},{18,... | collective-permute-start | bytes 393224 | tf_op jit(solution)/shard_map/ppermute | solution.py:21
  32.2 0.1 add_multiply_fusion.6
  32.4 1.2 %collective-permute-start.1 = (f32[2,256,128]{2,1,0:T(8,128)S(1)}, f32[2,256,128]{2,1,0:T(8,128)S(1)}, u32[]{:S(2)}, u32[]{:S(2)}) collective-permute-start(f32[2,256,128]{2,1,0:T(8,128)S(1)} %pad_maximum_fusion), channel_id=1, source_target_pairs={{0,16},{2,18},{4,20},{6,22},{8,24},{10,26},{12,28},{14,30},{16,0},... | collective-permute-start | bytes 786440 | tf_op jit(solution)/shard_map/ppermute | solution.py:21
  33.6 5.7 %collective-permute-done.11 = f32[256,128]{1,0:T(8,128)S(1)} collective-permute-done((f32[256,128]{1,0:T(8,128)S(1)}, f32[256,128]{1,0:T(8,128)S(1)}, u32[]{:S(2)}, u32[]{:S(2)}) %collective-permute-start.11) | collective-permute-done | bytes 131104 | tf_op jit(solution)/shard_map/ppermute | solution.py:21
  39.4 0.0 collective-permute-done.9
  39.4 0.1 collective-permute-start.12
  39.5 1.2 %collective-permute-start.13 = (f32[512,128]{1,0:T(8,128)S(1)}, f32[512,128]{1,0:T(8,128)S(1)}, u32[]{:S(2)}, u32[]{:S(2)}) collective-permute-start(f32[512,128]{1,0:T(8,128)S(1)} %maximum_multiply_fusion.refs_0_), channel_id=1, source_target_pairs={{0,4},{2,6},{4,0},{6,2},{8,12},{10,14},{12,8},{14,10},{16,20},{18,... | collective-permute-start | bytes 786440 | tf_op jit(solution)/shard_map/ppermute | solution.py:21
  40.7 0.0 collective-permute-done.4
  40.7 0.0 collective-permute-done.3
  40.7 0.2 select_multiply_fusion
  40.9 0.1 add_multiply_fusion.5
  41.0 7.2 %collective-permute-done.13.refs_2_ = f32[512,128]{1,0:T(8,128)S(1)} collective-permute-done((f32[512,128]{1,0:T(8,128)S(1)}, f32[512,128]{1,0:T(8,128)S(1)}, u32[]{:S(2)}, u32[]{:S(2)}) %collective-permute-start.13) | collective-permute-done | bytes 262176 | tf_op jit(solution)/shard_map/ppermute | solution.py:21
  48.3 0.6 collective-permute-start.16
  48.9 0.0 collective-permute-done.12.refs_1_
  48.9 0.9 collective-permute-done.14.refs_3_
  49.8 7.0 %eliminate_0.1 = (f32[4,512,128]{2,1,0:T(8,128)S(1)}, f32[4,512,128]{2,1,0:T(8,128)S(1)}, f32[512,128]{1,0:T(8,128)S(1)}) custom-call(s32[4]{0:T(128)S(1)} %pad_add_fusion.info, f32[512,128]{1,0:T(8,128)S(1)} %maximum_multiply_fusion.refs_0_, f32[512,128]{1,0:T(8,128)S(1)} %collective-permute-done.12.refs_1_, ...), custom_call_target="tpu_custom_call" | custom-call | flops 4000000000 | bytes 12000000 | tf_op jit(solution)/shard_map/eliminate_0/pallas_call | solution.py:281
  56.8 0.1 broadcast_multiply_fusion
  56.9 5.2 %collective-permute-start.15 = (f32[512,128]{1,0:T(8,128)S(1)}, f32[512,128]{1,0:T(8,128)S(1)}, u32[]{:S(2)}, u32[]{:S(2)}) collective-permute-start(f32[512,128]{1,0:T(8,128)S(1)} %get-tuple-element.81), channel_id=1, source_target_pairs={{0,8},{2,10},{4,12},{6,14},{8,0},{10,2},{12,4},{14,6},{16,24},{18,... | collective-permute-start | bytes 786440 | tf_op jit(solution)/shard_map/ppermute | solution.py:21
  62.1 1.4 %collective-permute-start.18 = (f32[512,128]{1,0:T(8,128)S(1)}, f32[512,128]{1,0:T(8,128)S(1)}, u32[]{:S(2)}, u32[]{:S(2)}) collective-permute-start(f32[512,128]{1,0:T(8,128)S(1)} %multiply_add_fusion), channel_id=1, source_target_pairs={{0,16},{2,18},{4,20},{6,22},{8,24},{10,26},{12,28},{14,30},{16,0},... | collective-permute-start | bytes 786440 | tf_op jit(solution)/shard_map/ppermute | solution.py:21
  63.5 5.8 %shard_map.37 = (f32[4,512,128]{2,1,0:T(8,128)S(1)}, f32[4,512,128]{2,1,0:T(8,128)S(1)}, f32[512,128]{1,0:T(8,128)S(1)}) custom-call(f32[4,512,128]{2,1,0:T(8,128)S(1)} %get-tuple-element.43.old_work, f32[4,512,128]{2,1,0:T(8,128)S(1)} %get-tuple-element.44.old_packed, ...), custom_call_target="tpu_custom_call", output_to_operand_aliasing={{0}: (0, {}), {1}: (1, {}), {2}: (2, {})} | custom-call | flops 4000000000 | bytes 12000000 | tf_op jit(solution)/shard_map/pallas_call | solution.py:300
  69.4 3.8 %collective-permute-done.15 = f32[512,128]{1,0:T(8,128)S(1)} collective-permute-done((f32[512,128]{1,0:T(8,128)S(1)}, f32[512,128]{1,0:T(8,128)S(1)}, u32[]{:S(2)}, u32[]{:S(2)}) %collective-permute-start.15) | collective-permute-done | bytes 262176 | tf_op jit(solution)/shard_map/ppermute | solution.py:21
  73.2 0.1 collective-permute-start.20
  73.3 1.1 %collective-permute-start.22 = (f32[512,128]{1,0:T(8,128)S(1)}, f32[512,128]{1,0:T(8,128)S(1)}, u32[]{:S(2)}, u32[]{:S(2)}) collective-permute-start(f32[512,128]{1,0:T(8,128)S(1)} %add_multiply_fusion.1.refs_2_), channel_id=1, source_target_pairs={{0,4},{2,6},{4,0},{6,2},{8,12},{10,14},{12,8},{14,10},{16,20},{18,... | collective-permute-start | bytes 786440 | tf_op jit(solution)/shard_map/ppermute | solution.py:21
  74.5 0.2 collective-permute-start.21
  74.7 4.7 %shard_map.38 = (f32[4,512,128]{2,1,0:T(8,128)S(1)}, f32[4,512,128]{2,1,0:T(8,128)S(1)}, f32[512,128]{1,0:T(8,128)S(1)}) custom-call(f32[4,512,128]{2,1,0:T(8,128)S(1)} %get-tuple-element.52.old_work, f32[4,512,128]{2,1,0:T(8,128)S(1)} %get-tuple-element.53.old_packed, ...), custom_call_target="tpu_custom_call", output_to_operand_aliasing={{0}: (0, {}), {1}: (1, {}), {2}: (2, {})} | custom-call | flops 4000000000 | bytes 12000000 | tf_op jit(solution)/shard_map/pallas_call | solution.py:300
  79.4 1.0 %collective-permute-start.23 = (f32[512,128]{1,0:T(8,128)S(1)}, f32[512,128]{1,0:T(8,128)S(1)}, u32[]{:S(2)}, u32[]{:S(2)}) collective-permute-start(f32[512,128]{1,0:T(8,128)S(1)} %add_multiply_fusion.refs_3_), channel_id=1, source_target_pairs={{0,4},{2,6},{4,0},{6,2},{8,12},{10,14},{12,8},{14,10},{16,20},{18,... | collective-permute-start | bytes 786440 | tf_op jit(solution)/shard_map/ppermute | solution.py:21
  80.4 2.4 %collective-permute-done.17 = f32[512,128]{1,0:T(8,128)S(1)} collective-permute-done((f32[512,128]{1,0:T(8,128)S(1)}, f32[512,128]{1,0:T(8,128)S(1)}, u32[]{:S(2)}, u32[]{:S(2)}) %collective-permute-start.17) | collective-permute-done | bytes 262176 | tf_op jit(solution)/shard_map/ppermute | solution.py:21
  82.8 0.1 add_multiply_fusion.3
  83.0 3.7 %collective-permute-start.19 = (f32[512,128]{1,0:T(8,128)S(1)}, f32[512,128]{1,0:T(8,128)S(1)}, u32[]{:S(2)}, u32[]{:S(2)}) collective-permute-start(f32[512,128]{1,0:T(8,128)S(1)} %pad_maximum_fusion.3), channel_id=1, source_target_pairs={{0,1},{2,3},{4,5},{6,7},{8,9},{10,11},{12,13},{14,15},{16,17},{18,... | collective-permute-start | bytes 786440 | tf_op jit(solution)/shard_map/ppermute | solution.py:320
  86.7 0.0 collective-permute-done.22.refs_6_
  86.7 0.1 collective-permute-start.24
  86.7 1.3 %collective-permute-done.23.refs_7_ = f32[512,128]{1,0:T(8,128)S(1)} collective-permute-done((f32[512,128]{1,0:T(8,128)S(1)}, f32[512,128]{1,0:T(8,128)S(1)}, u32[]{:S(2)}, u32[]{:S(2)}) %collective-permute-start.23) | collective-permute-done | bytes 262176 | tf_op jit(solution)/shard_map/ppermute | solution.py:21
  88.1 0.0 collective-permute-start.25
  88.1 4.4 %shard_map.39 = (f32[4,512,128]{2,1,0:T(8,128)S(1)}, f32[4,512,128]{2,1,0:T(8,128)S(1)}, f32[512,128]{1,0:T(8,128)S(1)}) custom-call(f32[4,512,128]{2,1,0:T(8,128)S(1)} %get-tuple-element.60.old_work, f32[4,512,128]{2,1,0:T(8,128)S(1)} %get-tuple-element.61.old_packed, ...), custom_call_target="tpu_custom_call", output_to_operand_aliasing={{0}: (0, {}), {1}: (1, {}), {2}: (2, {})} | custom-call | flops 4000000000 | bytes 12000000 | tf_op jit(solution)/shard_map/pallas_call | solution.py:300
  92.5 0.0 collective-permute-done.19
  92.6 0.0 collective-permute-done.20.refs_4_
  92.6 0.0 collective-permute-done.21.refs_5_
  92.6 0.0 collective-permute-done.25.refs_9_
  92.6 5.7 %own_columns.1 = f32[1024,128]{1,0:T(8,128)} custom-call(s32[4]{0:T(128)S(1)} %pad_add_fusion.info, f32[4,512,128]{2,1,0:T(8,128)S(1)} %get-tuple-element.66.work, f32[4,512,128]{2,1,0:T(8,128)S(1)} %get-tuple-element.67.packed, f32[512,128]{1,0:T(8,128)S(1)} %get-tuple-element.68.inverted, f32[512,128]{1,0:T(8,128)S(1)} %broadcast_select_fusion.own_top, ...), custom_call_target="tpu_custom_call" | custom-call | flops 4000000000 | bytes 12000000 | tf_op jit(solution)/shard_map/own_columns/pallas_call | solution.py:325
  (51 shorter events, 0.6 us)
Async XLA Ops:
  0.0 7.2 %collective-permute-start.5 = (f32[2,128]{1,0:T(2,128)}, f32[2,128]{1,0:T(2,128)S(1)}, u32[]{:S(2)}, u32[]{:S(2)}) collective-permute-start(f32[2,128]{1,0:T(2,128)} %param.5), channel_id=1, source_target_pairs={{0,8},{2,10},{4,12},{6,14},{8,0},{10,2},{12,4},{14,6},{16,24},{18,... | collective-permute-start | bytes 3080 | tf_op jit(solution)/shard_map/ppermute | solution.py:21
  3.1 3.2 %copy-start.1 = (f32[2,1024]{1,0:T(2,128)S(1)}, f32[2,1024]{1,0:T(2,128)}, u32[]{:S(2)}) copy-start(f32[2,1024]{1,0:T(2,128)} %param.4) | copy-start | bytes 24580
  3.1 9.3 %copy-start = (f32[1024,128]{1,0:T(8,128)S(1)}, f32[1024,128]{1,0:T(8,128)}, u32[]{:S(2)}) copy-start(f32[1024,128]{1,0:T(8,128)} %param.3) | copy-start | bytes 1572868
  4.2 8.2 %collective-permute-start.2 = (f32[2,256,128]{2,1,0:T(8,128)S(1)}, f32[2,256,128]{2,1,0:T(8,128)S(1)}, u32[]{:S(2)}, u32[]{:S(2)}) collective-permute-start(f32[2,256,128]{2,1,0:T(8,128)S(1)} %get-tuple-element.85), channel_id=1, source_target_pairs={{0,8},{2,10},{4,12},{6,14},{8,0},{10,2},{12,4},{14,6},{16,24},{18,... | collective-permute-start | bytes 786440 | tf_op jit(solution)/shard_map/ppermute | solution.py:21
  4.3 8.1 %collective-permute-start = (f32[2,256,128]{2,1,0:T(8,128)S(1)}, f32[2,256,128]{2,1,0:T(8,128)S(1)}, u32[]{:S(2)}, u32[]{:S(2)}) collective-permute-start(f32[2,256,128]{2,1,0:T(8,128)S(1)} %get-tuple-element.86), channel_id=1, source_target_pairs={{0,1},{1,0},{2,3},{3,2},{4,5},{5,4},{6,7},{7,6},{8,9},{9,8},{10,11... | collective-permute-start | bytes 786440 | tf_op jit(solution)/shard_map/ppermute | solution.py:21
  6.2 6.0 %collective-permute-start.7 = (f32[2,1024]{1,0:T(2,128)S(1)}, f32[2,1024]{1,0:T(2,128)S(1)}, u32[]{:S(2)}, u32[]{:S(2)}) collective-permute-start(f32[2,1024]{1,0:T(2,128)S(1)} %copy-done.1), channel_id=1, source_target_pairs={{0,1},{1,0},{2,3},{3,2},{4,5},{5,4},{6,7},{7,6},{8,9},{9,8},{10,11... | collective-permute-start | bytes 24584 | tf_op jit(solution)/shard_map/ppermute | solution.py:21
  6.4 0.7 copy-start.2
  7.2 4.7 %collective-permute-start.6 = (f32[4,128]{1,0:T(4,128)S(1)}, f32[4,128]{1,0:T(4,128)S(1)}, u32[]{:S(2)}, u32[]{:S(2)}) collective-permute-start(f32[4,128]{1,0:T(4,128)S(1)} %pad_maximum_fusion.4), channel_id=1, source_target_pairs={{0,16},{2,18},{4,20},{6,22},{8,24},{10,26},{12,28},{14,30},{16,0},... | collective-permute-start | bytes 6152 | tf_op jit(solution)/shard_map/ppermute | solution.py:21
  12.5 28.1 %collective-permute-start.4 = (f32[2,256,128]{2,1,0:T(8,128)S(1)}, f32[2,256,128]{2,1,0:T(8,128)S(1)}, u32[]{:S(2)}, u32[]{:S(2)}) collective-permute-start(f32[2,256,128]{2,1,0:T(8,128)S(1)} %get-tuple-element.78), channel_id=1, source_target_pairs={{0,1},{1,0},{2,3},{3,2},{4,5},{5,4},{6,7},{7,6},{8,9},{9,8},{10,11... | collective-permute-start | bytes 786440 | tf_op jit(solution)/shard_map/ppermute | solution.py:21
  14.2 26.5 %collective-permute-start.3 = (f32[2,256,128]{2,1,0:T(8,128)S(1)}, f32[2,256,128]{2,1,0:T(8,128)S(1)}, u32[]{:S(2)}, u32[]{:S(2)}) collective-permute-start(f32[2,256,128]{2,1,0:T(8,128)S(1)} %get-tuple-element.79), channel_id=1, source_target_pairs={{0,1},{1,0},{2,3},{3,2},{4,5},{5,4},{6,7},{7,6},{8,9},{9,8},{10,11... | collective-permute-start | bytes 786440 | tf_op jit(solution)/shard_map/ppermute | solution.py:21
  14.8 13.1 %collective-permute-start.10 = (f32[256,128]{1,0:T(8,128)S(1)}, f32[256,128]{1,0:T(8,128)S(1)}, u32[]{:S(2)}, u32[]{:S(2)}) collective-permute-start(f32[256,128]{1,0:T(8,128)S(1)} %fusion.4), channel_id=1, source_target_pairs={{0,1},{1,0},{2,3},{3,2},{4,5},{5,4},{6,7},{7,6},{8,9},{9,8},{10,11... | collective-permute-start | bytes 393224 | tf_op jit(solution)/shard_map/ppermute | solution.py:21
  16.7 13.9 %collective-permute-start.8 = (f32[256,128]{1,0:T(8,128)S(1)}, f32[256,128]{1,0:T(8,128)S(1)}, u32[]{:S(2)}, u32[]{:S(2)}) collective-permute-start(f32[256,128]{1,0:T(8,128)S(1)} %fusion.10), channel_id=1, source_target_pairs={{0,16},{2,18},{4,20},{6,22},{8,24},{10,26},{12,28},{14,30},{16,0},... | collective-permute-start | bytes 393224 | tf_op jit(solution)/shard_map/ppermute | solution.py:21
  28.1 11.2 %collective-permute-start.11 = (f32[256,128]{1,0:T(8,128)S(1)}, f32[256,128]{1,0:T(8,128)S(1)}, u32[]{:S(2)}, u32[]{:S(2)}) collective-permute-start(f32[256,128]{1,0:T(8,128)S(1)} %fusion.15), channel_id=1, source_target_pairs={{0,16},{2,18},{4,20},{6,22},{8,24},{10,26},{12,28},{14,30},{16,0},... | collective-permute-start | bytes 393224 | tf_op jit(solution)/shard_map/ppermute | solution.py:21
  30.6 8.8 %collective-permute-start.9 = (f32[256,128]{1,0:T(8,128)S(1)}, f32[256,128]{1,0:T(8,128)S(1)}, u32[]{:S(2)}, u32[]{:S(2)}) collective-permute-start(f32[256,128]{1,0:T(8,128)S(1)} %add.85), channel_id=1, source_target_pairs={{0,8},{2,10},{4,12},{6,14},{8,0},{10,2},{12,4},{14,6},{16,24},{18,... | collective-permute-start | bytes 393224 | tf_op jit(solution)/shard_map/ppermute | solution.py:21
  32.4 24.4 %collective-permute-start.1 = (f32[2,256,128]{2,1,0:T(8,128)S(1)}, f32[2,256,128]{2,1,0:T(8,128)S(1)}, u32[]{:S(2)}, u32[]{:S(2)}) collective-permute-start(f32[2,256,128]{2,1,0:T(8,128)S(1)} %pad_maximum_fusion), channel_id=1, source_target_pairs={{0,16},{2,18},{4,20},{6,22},{8,24},{10,26},{12,28},{14,30},{16,0},... | collective-permute-start | bytes 786440 | tf_op jit(solution)/shard_map/ppermute | solution.py:21
  39.4 9.4 %collective-permute-start.12 = (f32[512,128]{1,0:T(8,128)S(1)}, f32[512,128]{1,0:T(8,128)S(1)}, u32[]{:S(2)}, u32[]{:S(2)}) collective-permute-start(f32[512,128]{1,0:T(8,128)S(1)} %maximum_multiply_fusion.refs_0_), channel_id=1, source_target_pairs={{0,2},{2,0},{4,6},{6,4},{8,10},{10,8},{12,14},{14,12},{16,18},{18,... | collective-permute-start | bytes 786440 | tf_op jit(solution)/shard_map/ppermute | solution.py:21
  39.5 8.7 %collective-permute-start.13 = (f32[512,128]{1,0:T(8,128)S(1)}, f32[512,128]{1,0:T(8,128)S(1)}, u32[]{:S(2)}, u32[]{:S(2)}) collective-permute-start(f32[512,128]{1,0:T(8,128)S(1)} %maximum_multiply_fusion.refs_0_), channel_id=1, source_target_pairs={{0,4},{2,6},{4,0},{6,2},{8,12},{10,14},{12,8},{14,10},{16,20},{18,... | collective-permute-start | bytes 786440 | tf_op jit(solution)/shard_map/ppermute | solution.py:21
  48.2 1.5 %collective-permute-start.14 = (f32[512,128]{1,0:T(8,128)S(1)}, f32[512,128]{1,0:T(8,128)S(1)}, u32[]{:S(2)}, u32[]{:S(2)}) collective-permute-start(f32[512,128]{1,0:T(8,128)S(1)} %collective-permute-done.13.refs_2_), channel_id=1, source_target_pairs={{0,2},{2,0},{4,6},{6,4},{8,10},{10,8},{12,14},{14,12},{16,18},{18,... | collective-permute-start | bytes 786440 | tf_op jit(solution)/shard_map/ppermute | solution.py:21
  48.3 21.0 %collective-permute-start.16 = (f32[512,128]{1,0:T(8,128)S(1)}, f32[512,128]{1,0:T(8,128)S(1)}, u32[]{:S(2)}, u32[]{:S(2)}) collective-permute-start(f32[512,128]{1,0:T(8,128)S(1)} %multiply_add_fusion.1), channel_id=1, source_target_pairs={{0,16},{2,18},{4,20},{6,22},{8,24},{10,26},{12,28},{14,30},{16,0},... | collective-permute-start | bytes 786440 | tf_op jit(solution)/shard_map/ppermute | solution.py:21
  56.9 16.3 %collective-permute-start.15 = (f32[512,128]{1,0:T(8,128)S(1)}, f32[512,128]{1,0:T(8,128)S(1)}, u32[]{:S(2)}, u32[]{:S(2)}) collective-permute-start(f32[512,128]{1,0:T(8,128)S(1)} %get-tuple-element.81), channel_id=1, source_target_pairs={{0,8},{2,10},{4,12},{6,14},{8,0},{10,2},{12,4},{14,6},{16,24},{18,... | collective-permute-start | bytes 786440 | tf_op jit(solution)/shard_map/ppermute | solution.py:21
  62.1 17.4 %collective-permute-start.18 = (f32[512,128]{1,0:T(8,128)S(1)}, f32[512,128]{1,0:T(8,128)S(1)}, u32[]{:S(2)}, u32[]{:S(2)}) collective-permute-start(f32[512,128]{1,0:T(8,128)S(1)} %multiply_add_fusion), channel_id=1, source_target_pairs={{0,16},{2,18},{4,20},{6,22},{8,24},{10,26},{12,28},{14,30},{16,0},... | collective-permute-start | bytes 786440 | tf_op jit(solution)/shard_map/ppermute | solution.py:21
  73.2 19.4 %collective-permute-start.20 = (f32[512,128]{1,0:T(8,128)S(1)}, f32[512,128]{1,0:T(8,128)S(1)}, u32[]{:S(2)}, u32[]{:S(2)}) collective-permute-start(f32[512,128]{1,0:T(8,128)S(1)} %add_multiply_fusion.1.refs_2_), channel_id=1, source_target_pairs={{0,2},{2,0},{4,6},{6,4},{8,10},{10,8},{12,14},{14,12},{16,18},{18,... | collective-permute-start | bytes 786440 | tf_op jit(solution)/shard_map/ppermute | solution.py:21
  73.3 13.3 %collective-permute-start.22 = (f32[512,128]{1,0:T(8,128)S(1)}, f32[512,128]{1,0:T(8,128)S(1)}, u32[]{:S(2)}, u32[]{:S(2)}) collective-permute-start(f32[512,128]{1,0:T(8,128)S(1)} %add_multiply_fusion.1.refs_2_), channel_id=1, source_target_pairs={{0,4},{2,6},{4,0},{6,2},{8,12},{10,14},{12,8},{14,10},{16,20},{18,... | collective-permute-start | bytes 786440 | tf_op jit(solution)/shard_map/ppermute | solution.py:21
  74.4 8.4 %collective-permute-start.17 = (f32[512,128]{1,0:T(8,128)S(1)}, f32[512,128]{1,0:T(8,128)S(1)}, u32[]{:S(2)}, u32[]{:S(2)}) collective-permute-start(f32[512,128]{1,0:T(8,128)S(1)} %get-tuple-element.49), channel_id=1, source_target_pairs={{0,8},{2,10},{4,12},{6,14},{8,0},{10,2},{12,4},{14,6},{16,24},{18,... | collective-permute-start | bytes 786440 | tf_op jit(solution)/shard_map/ppermute | solution.py:21
  74.5 18.1 %collective-permute-start.21 = (f32[512,128]{1,0:T(8,128)S(1)}, f32[512,128]{1,0:T(8,128)S(1)}, u32[]{:S(2)}, u32[]{:S(2)}) collective-permute-start(f32[512,128]{1,0:T(8,128)S(1)} %add_multiply_fusion.refs_3_), channel_id=1, source_target_pairs={{0,2},{2,0},{4,6},{6,4},{8,10},{10,8},{12,14},{14,12},{16,18},{18,... | collective-permute-start | bytes 786440 | tf_op jit(solution)/shard_map/ppermute | solution.py:21
  79.4 8.6 %collective-permute-start.23 = (f32[512,128]{1,0:T(8,128)S(1)}, f32[512,128]{1,0:T(8,128)S(1)}, u32[]{:S(2)}, u32[]{:S(2)}) collective-permute-start(f32[512,128]{1,0:T(8,128)S(1)} %add_multiply_fusion.refs_3_), channel_id=1, source_target_pairs={{0,4},{2,6},{4,0},{6,2},{8,12},{10,14},{12,8},{14,10},{16,20},{18,... | collective-permute-start | bytes 786440 | tf_op jit(solution)/shard_map/ppermute | solution.py:21
  83.0 9.5 %collective-permute-start.19 = (f32[512,128]{1,0:T(8,128)S(1)}, f32[512,128]{1,0:T(8,128)S(1)}, u32[]{:S(2)}, u32[]{:S(2)}) collective-permute-start(f32[512,128]{1,0:T(8,128)S(1)} %pad_maximum_fusion.3), channel_id=1, source_target_pairs={{0,1},{2,3},{4,5},{6,7},{8,9},{10,11},{12,13},{14,15},{16,17},{18,... | collective-permute-start | bytes 786440 | tf_op jit(solution)/shard_map/ppermute | solution.py:320
  86.7 5.9 %collective-permute-start.24 = (f32[512,128]{1,0:T(8,128)S(1)}, f32[512,128]{1,0:T(8,128)S(1)}, u32[]{:S(2)}, u32[]{:S(2)}) collective-permute-start(f32[512,128]{1,0:T(8,128)S(1)} %collective-permute-done.22.refs_6_), channel_id=1, source_target_pairs={{0,2},{2,0},{4,6},{6,4},{8,10},{10,8},{12,14},{14,12},{16,18},{18,... | collective-permute-start | bytes 786440 | tf_op jit(solution)/shard_map/ppermute | solution.py:21
  88.1 4.5 %collective-permute-start.25 = (f32[512,128]{1,0:T(8,128)S(1)}, f32[512,128]{1,0:T(8,128)S(1)}, u32[]{:S(2)}, u32[]{:S(2)}) collective-permute-start(f32[512,128]{1,0:T(8,128)S(1)} %collective-permute-done.23.refs_7_), channel_id=1, source_target_pairs={{0,2},{2,0},{4,6},{6,4},{8,10},{10,8},{12,14},{14,12},{16,18},{18,... | collective-permute-start | bytes 786440 | tf_op jit(solution)/shard_map/ppermute | solution.py:21

commit v14 on v12

--- a/solution.py
+++ b/solution.py
@@ -103,6 +103,7 @@
         for j in later:
             work[j, rest, :] = work[j, rest, :] - hdot(left, solved[j])
         packed[k, rest, :] = hdot(left, upper_inverse)
+        work[k, rest, :] = hdot(left, inverse)
     for j in later:
         packed[j, here, :] = hdot(upper, solved[j])
         work[j, here, :] = solved[j]
@@ -135,7 +136,7 @@
         solved = hdot(work[k, here, :], rhs[here, :])
         for i in range(k + 1, blocks):
             there = pl.ds(BLK * i, BLK)
-            rhs[there, :] = rhs[there, :] - hdot(work[k, there, :], solved)
+            rhs[there, :] = rhs[there, :] - hdot(work[k, there, :], rhs[here, :])
         upper = jnp.where(above, packed[k, here, :], 0.0)
         top[here, :] = jnp.where(is_panel, packed[slot, here, :], hdot(upper, solved))
         mine = jnp.where(slot == k, inverted[here, :], 0.0)
@@ -263,6 +264,10 @@
     parts_q = [flat(jnp.stack(own_mixed(1, a, b))) for a, b in zip((even_q, odd_q), other_q)]
     panel_q = of_half(parts_q, none, none)
     far_q = swapped(panel_q, "col", high)
+    parts_p = flat(jnp.where(in_high, far_own, own_p)), flat(jnp.where(in_high, own_p, far_own))
+    panel_p = of_bit(parts_p, none, none)
+    near_p = swapped(panel_p, "col", low)
+
     info = jnp.stack(
         [
             (col_pos < blocks).astype(jnp.int32),
@@ -287,10 +292,7 @@
         compiler_params=params,
         name="eliminate_0",
     )(info, *lead_pieces)
-    far_own, parts_q, *state = lax.optimization_barrier((far_own, parts_q, *state))
-    parts_p = flat(jnp.where(in_high, far_own, own_p)), flat(jnp.where(in_high, own_p, far_own))
-    panel_p = of_bit(parts_p, none, none)
-    near_p = swapped(panel_p, "col", low)
+    parts_p, parts_q, *state = lax.optimization_barrier((parts_p, parts_q, *state))
     received_q = swapped(of_half(parts_q, ~in_high, in_low), "col", high)
     received_p = swapped(of_bit(parts_p, in_high, ~in_low), "col", low)
     kept_p, kept_q = of_bit(parts_p, in_high, in_low), of_half(parts_q, in_high, in_low)

time: 106 us -> 98.7 us (0.931)
  starting transfers between devices: 34.2 us -> 28.1 us
  waiting for transfers between devices: 39.6 us -> 38.5 us
    ppermute x25, starting transfers between devices: 30.9 us -> 24.5 us  [swapped(): lax.ppermute(x, axis, [(i, i ^ mask) for i in range(lax.axis_size(axis))])]
    ppermute x25, waiting for transfers between devices: 39.6 us -> 38.5 us  [swapped(): lax.ppermute(x, axis, [(i, i ^ mask) for i in range(lax.axis_size(axis))])]
  transfers between devices with their start and end apart: 26 -> 26, of which waited for: 8 -> 11; matrix products, arithmetic and copies ran while one was open for 3% -> 3% of each run, Pallas kernels for 21% -> 23%
where the time goes in v14:
time: 98.7 us; the launch traced here: 98.5 us
  waiting for transfers between devices  38.5 us (39%)
  starting transfers between devices  28.1 us (28%)
  Pallas kernels  27.7 us (28%)
  local copies, waits for them, and re-layouts  1.91 us (2%)
  other arithmetic  1.78 us (2%)
    ppermute x25, waiting for transfers between devices, swapped(): lax.ppermute(x, axis, [(i, i ^ mask) for i in range(lax.axis_size(axis))])  38.5 us
    ppermute x25, starting transfers between devices, swapped(): lax.ppermute(x, axis, [(i, i ^ mask) for i in range(lax.axis_size(axis))])  24.5 us
    pallas_call x3, Pallas kernels, shards(): pl.pallas_call(functools.partial(next_kernel, k), out_shape=state_shapes,...  15.2 us
    pallas_call x1, Pallas kernels, shards(): pl.pallas_call(first_kernel, out_shape=state_shapes, in_specs=[smem] + [v...  7.3 us
    pallas_call x1, Pallas kernels, shards(): pl.pallas_call(last_kernel, out_shape=jax.ShapeDtypeStruct((height, width...  5.17 us
    ppermute x1, starting transfers between devices, shards(): far_top = lax.ppermute(own_top, 'row', [(0, 1)])  3.66 us
  transfers between devices with their start and end apart: 26, of which 11 were waited for; matrix products, arithmetic and copies ran while one was open for 3% of the time, Pallas kernels for 23%

profile of v14, /device:TPU:0, one launch (start us, length us, event | category | flops | bytes accessed | tf_op | source)
XLA Modules:
  0.0 98.5 jit_solution(17008519179857002931)
XLA Ops:
  0.0 3.1 %collective-permute-start.5 = (f32[2,128]{1,0:T(2,128)}, f32[2,128]{1,0:T(2,128)S(1)}, u32[]{:S(2)}, u32[]{:S(2)}) collective-permute-start(f32[2,128]{1,0:T(2,128)} %param.5), channel_id=1, source_target_pairs={{0,8},{2,10},{4,12},{6,14},{8,0},{10,2},{12,4},{14,6},{16,24},{18,... | collective-permute-start | bytes 3080 | tf_op jit(solution)/shard_map/ppermute | solution.py:21
  3.1 1.1 %slice_bitcast_fusion = (f32[2,256,128]{2,1,0:T(8,128)S(1)}, f32[2,256,128]{2,1,0:T(8,128)S(1)}) fusion(f32[2,1,2,256,128]{4,3,2,0,1:T(8,128)} %bitcast.123), kind=kLoop, calls=%fused_computation.2 | loop fusion | bytes 1048576 | tf_op jit(solution)/shard_map/reshape;squeeze | solution.py:191
  4.2 0.1 collective-permute-start.2
  4.3 2.0 %collective-permute-start = (f32[2,256,128]{2,1,0:T(8,128)S(1)}, f32[2,256,128]{2,1,0:T(8,128)S(1)}, u32[]{:S(2)}, u32[]{:S(2)}) collective-permute-start(f32[2,256,128]{2,1,0:T(8,128)S(1)} %get-tuple-element.82), channel_id=1, source_target_pairs={{0,1},{1,0},{2,3},{3,2},{4,5},{5,4},{6,7},{7,6},{8,9},{9,8},{10,11... | collective-permute-start | bytes 786440 | tf_op jit(solution)/shard_map/ppermute | solution.py:21
  6.2 0.1 collective-permute-start.7
  6.4 0.0 copy-start.2
  6.5 0.7 copy-done.2
  7.1 0.1 pad_add_fusion.info
  7.2 0.0 collective-permute-done.5
  7.2 3.0 %collective-permute-start.6 = (f32[4,128]{1,0:T(4,128)S(1)}, f32[4,128]{1,0:T(4,128)S(1)}, u32[]{:S(2)}, u32[]{:S(2)}) collective-permute-start(f32[4,128]{1,0:T(4,128)S(1)} %pad_maximum_fusion.4), channel_id=1, source_target_pairs={{0,16},{2,18},{4,20},{6,22},{8,24},{10,26},{12,28},{14,30},{16,0},... | collective-permute-start | bytes 6152 | tf_op jit(solution)/shard_map/ppermute | solution.py:21
  10.3 1.7 %collective-permute-done.6 = f32[4,128]{1,0:T(4,128)S(1)} collective-permute-done((f32[4,128]{1,0:T(4,128)S(1)}, f32[4,128]{1,0:T(4,128)S(1)}, u32[]{:S(2)}, u32[]{:S(2)}) %collective-permute-start.6) | collective-permute-done | bytes 2080 | tf_op jit(solution)/shard_map/ppermute | solution.py:21
  12.0 0.3 collective-permute-done.7
  12.4 0.0 collective-permute-done.2
  12.4 0.0 collective-permute-done
  12.4 0.1 multiply_add_fusion.2
  12.5 0.1 add_multiply_fusion.7
  12.7 2.7 %collective-permute-start.1 = (f32[2,256,128]{2,1,0:T(8,128)S(1)}, f32[2,256,128]{2,1,0:T(8,128)S(1)}, u32[]{:S(2)}, u32[]{:S(2)}) collective-permute-start(f32[2,256,128]{2,1,0:T(8,128)S(1)} %pad_maximum_fusion), channel_id=1, source_target_pairs={{0,16},{2,18},{4,20},{6,22},{8,24},{10,26},{12,28},{14,30},{16,0},... | collective-permute-start | bytes 786440 | tf_op jit(solution)/shard_map/ppermute | solution.py:21
  15.5 0.2 fusion.3
  15.6 1.6 %collective-permute-start.10 = (f32[256,128]{1,0:T(8,128)S(1)}, f32[256,128]{1,0:T(8,128)S(1)}, u32[]{:S(2)}, u32[]{:S(2)}) collective-permute-start(f32[256,128]{1,0:T(8,128)S(1)} %fusion.3), channel_id=1, source_target_pairs={{0,1},{1,0},{2,3},{3,2},{4,5},{5,4},{6,7},{7,6},{8,9},{9,8},{10,11... | collective-permute-start | bytes 393224 | tf_op jit(solution)/shard_map/ppermute | solution.py:21
  17.2 0.2 fusion.9
  17.4 0.4 collective-permute-start.8
  17.8 2.9 %collective-permute-done.10 = f32[256,128]{1,0:T(8,128)S(1)} collective-permute-done((f32[256,128]{1,0:T(8,128)S(1)}, f32[256,128]{1,0:T(8,128)S(1)}, u32[]{:S(2)}, u32[]{:S(2)}) %collective-permute-start.10) | collective-permute-done | bytes 131104 | tf_op jit(solution)/shard_map/ppermute | solution.py:21
  20.7 0.2 fusion.14
  20.8 0.3 collective-permute-start.11
  21.1 14.9 %collective-permute-done.8 = f32[256,128]{1,0:T(8,128)S(1)} collective-permute-done((f32[256,128]{1,0:T(8,128)S(1)}, f32[256,128]{1,0:T(8,128)S(1)}, u32[]{:S(2)}, u32[]{:S(2)}) %collective-permute-start.8) | collective-permute-done | bytes 131104 | tf_op jit(solution)/shard_map/ppermute | solution.py:21
  36.1 0.1 collective-permute-start.9
  36.1 1.4 %collective-permute-start.4 = (f32[2,256,128]{2,1,0:T(8,128)S(1)}, f32[2,256,128]{2,1,0:T(8,128)S(1)}, u32[]{:S(2)}, u32[]{:S(2)}) collective-permute-start(f32[2,256,128]{2,1,0:T(8,128)S(1)} %get-tuple-element.78), channel_id=1, source_target_pairs={{0,1},{1,0},{2,3},{3,2},{4,5},{5,4},{6,7},{7,6},{8,9},{9,8},{10,11... | collective-permute-start | bytes 786440 | tf_op jit(solution)/shard_map/ppermute | solution.py:21
  37.5 0.7 collective-permute-start.3
  38.2 0.0 collective-permute-done.11
  38.3 2.8 %collective-permute-done.9 = f32[256,128]{1,0:T(8,128)S(1)} collective-permute-done((f32[256,128]{1,0:T(8,128)S(1)}, f32[256,128]{1,0:T(8,128)S(1)}, u32[]{:S(2)}, u32[]{:S(2)}) %collective-permute-start.9) | collective-permute-done | bytes 131104 | tf_op jit(solution)/shard_map/ppermute | solution.py:21
  41.1 0.1 collective-permute-start.12
  41.2 1.4 %collective-permute-start.13 = (f32[512,128]{1,0:T(8,128)S(1)}, f32[512,128]{1,0:T(8,128)S(1)}, u32[]{:S(2)}, u32[]{:S(2)}) collective-permute-start(f32[512,128]{1,0:T(8,128)S(1)} %maximum_multiply_fusion.refs_0_), channel_id=1, source_target_pairs={{0,4},{2,6},{4,0},{6,2},{8,12},{10,14},{12,8},{14,10},{16,20},{18,... | collective-permute-start | bytes 786440 | tf_op jit(solution)/shard_map/ppermute | solution.py:21
  42.6 0.0 collective-permute-done.1
  42.7 0.1 collective-permute-start.17
  42.7 2.6 %collective-permute-done.4 = f32[2,256,128]{2,1,0:T(8,128)S(1)} collective-permute-done((f32[2,256,128]{2,1,0:T(8,128)S(1)}, f32[2,256,128]{2,1,0:T(8,128)S(1)}, u32[]{:S(2)}, u32[]{:S(2)}) %collective-permute-start.4) | collective-permute-done | bytes 262176 | tf_op jit(solution)/shard_map/ppermute | solution.py:21
  45.4 3.4 %collective-permute-done.3 = f32[2,256,128]{2,1,0:T(8,128)S(1)} collective-permute-done((f32[2,256,128]{2,1,0:T(8,128)S(1)}, f32[2,256,128]{2,1,0:T(8,128)S(1)}, u32[]{:S(2)}, u32[]{:S(2)}) %collective-permute-start.3) | collective-permute-done | bytes 262176 | tf_op jit(solution)/shard_map/ppermute | solution.py:21
  48.8 0.2 select_multiply_fusion
  48.9 0.1 add_multiply_fusion.6
  49.1 0.8 collective-permute-done.13.refs_2_
  49.9 0.0 collective-permute-start.14
  50.0 2.7 %collective-permute-start.18 = (f32[512,128]{1,0:T(8,128)S(1)}, f32[512,128]{1,0:T(8,128)S(1)}, u32[]{:S(2)}, u32[]{:S(2)}) collective-permute-start(f32[512,128]{1,0:T(8,128)S(1)} %multiply_add_fusion), channel_id=1, source_target_pairs={{0,16},{2,18},{4,20},{6,22},{8,24},{10,26},{12,28},{14,30},{16,0},... | collective-permute-start | bytes 786440 | tf_op jit(solution)/shard_map/ppermute | solution.py:21
  52.7 7.3 %eliminate_0.1 = (f32[4,512,128]{2,1,0:T(8,128)S(1)}, f32[4,512,128]{2,1,0:T(8,128)S(1)}, f32[512,128]{1,0:T(8,128)S(1)}) custom-call(s32[4]{0:T(128)S(1)} %pad_add_fusion.info, f32[512,128]{1,0:T(8,128)S(1)} %maximum_multiply_fusion.refs_0_, f32[512,128]{1,0:T(8,128)S(1)} %collective-permute-done.12.refs_1_, ...), custom_call_target="tpu_custom_call" | custom-call | flops 4000000000 | bytes 12000000 | tf_op jit(solution)/shard_map/eliminate_0/pallas_call | solution.py:286
  60.0 5.9 %shard_map.37 = (f32[4,512,128]{2,1,0:T(8,128)S(1)}, f32[4,512,128]{2,1,0:T(8,128)S(1)}, f32[512,128]{1,0:T(8,128)S(1)}) custom-call(f32[4,512,128]{2,1,0:T(8,128)S(1)} %get-tuple-element.46.old_work, f32[4,512,128]{2,1,0:T(8,128)S(1)} %get-tuple-element.47.old_packed, ...), custom_call_target="tpu_custom_call", output_to_operand_aliasing={{0}: (0, {}), {1}: (1, {}), {2}: (2, {})} | custom-call | flops 4000000000 | bytes 12000000 | tf_op jit(solution)/shard_map/pallas_call | solution.py:302
  65.9 0.0 collective-permute-done.17
  66.0 0.3 collective-permute-start.20
  66.3 1.5 %collective-permute-start.22 = (f32[512,128]{1,0:T(8,128)S(1)}, f32[512,128]{1,0:T(8,128)S(1)}, u32[]{:S(2)}, u32[]{:S(2)}) collective-permute-start(f32[512,128]{1,0:T(8,128)S(1)} %add_multiply_fusion.1.refs_2_), channel_id=1, source_target_pairs={{0,4},{2,6},{4,0},{6,2},{8,12},{10,14},{12,8},{14,10},{16,20},{18,... | collective-permute-start | bytes 786440 | tf_op jit(solution)/shard_map/ppermute | solution.py:21
  67.8 0.5 collective-permute-start.15
  68.3 1.9 %collective-permute-start.16 = (f32[512,128]{1,0:T(8,128)S(1)}, f32[512,128]{1,0:T(8,128)S(1)}, u32[]{:S(2)}, u32[]{:S(2)}) collective-permute-start(f32[512,128]{1,0:T(8,128)S(1)} %multiply_add_fusion.1), channel_id=1, source_target_pairs={{0,16},{2,18},{4,20},{6,22},{8,24},{10,26},{12,28},{14,30},{16,0},... | collective-permute-start | bytes 786440 | tf_op jit(solution)/shard_map/ppermute | solution.py:21
  70.2 0.1 collective-permute-start.21
  70.3 4.9 %shard_map.38 = (f32[4,512,128]{2,1,0:T(8,128)S(1)}, f32[4,512,128]{2,1,0:T(8,128)S(1)}, f32[512,128]{1,0:T(8,128)S(1)}) custom-call(f32[4,512,128]{2,1,0:T(8,128)S(1)} %get-tuple-element.52.old_work, f32[4,512,128]{2,1,0:T(8,128)S(1)} %get-tuple-element.53.old_packed, ...), custom_call_target="tpu_custom_call", output_to_operand_aliasing={{0}: (0, {}), {1}: (1, {}), {2}: (2, {})} | custom-call | flops 4000000000 | bytes 12000000 | tf_op jit(solution)/shard_map/pallas_call | solution.py:302
  75.2 6.2 %collective-permute-done.15 = f32[512,128]{1,0:T(8,128)S(1)} collective-permute-done((f32[512,128]{1,0:T(8,128)S(1)}, f32[512,128]{1,0:T(8,128)S(1)}, u32[]{:S(2)}, u32[]{:S(2)}) %collective-permute-start.15) | collective-permute-done | bytes 262176 | tf_op jit(solution)/shard_map/ppermute | solution.py:21
  81.4 0.5 collective-permute-start.23
  82.0 0.9 collective-permute-done.16
  82.9 0.1 add_multiply_fusion.3
  83.0 3.7 %collective-permute-start.19 = (f32[512,128]{1,0:T(8,128)S(1)}, f32[512,128]{1,0:T(8,128)S(1)}, u32[]{:S(2)}, u32[]{:S(2)}) collective-permute-start(f32[512,128]{1,0:T(8,128)S(1)} %pad_maximum_fusion.3), channel_id=1, source_target_pairs={{0,1},{2,3},{4,5},{6,7},{8,9},{10,11},{12,13},{14,15},{16,17},{18,... | collective-permute-start | bytes 786440 | tf_op jit(solution)/shard_map/ppermute | solution.py:321
  86.7 0.1 collective-permute-start.24
  86.8 2.0 %collective-permute-done.23.refs_7_ = f32[512,128]{1,0:T(8,128)S(1)} collective-permute-done((f32[512,128]{1,0:T(8,128)S(1)}, f32[512,128]{1,0:T(8,128)S(1)}, u32[]{:S(2)}, u32[]{:S(2)}) %collective-permute-start.23) | collective-permute-done | bytes 262176 | tf_op jit(solution)/shard_map/ppermute | solution.py:21
  88.8 0.0 collective-permute-start.25
  88.8 4.4 %shard_map.39 = (f32[4,512,128]{2,1,0:T(8,128)S(1)}, f32[4,512,128]{2,1,0:T(8,128)S(1)}, f32[512,128]{1,0:T(8,128)S(1)}) custom-call(f32[4,512,128]{2,1,0:T(8,128)S(1)} %get-tuple-element.60.old_work, f32[4,512,128]{2,1,0:T(8,128)S(1)} %get-tuple-element.61.old_packed, ...), custom_call_target="tpu_custom_call", output_to_operand_aliasing={{0}: (0, {}), {1}: (1, {}), {2}: (2, {})} | custom-call | flops 4000000000 | bytes 12000000 | tf_op jit(solution)/shard_map/pallas_call | solution.py:302
  93.3 0.0 collective-permute-done.19
  93.3 0.0 collective-permute-done.20.refs_4_
  93.3 0.0 collective-permute-done.21.refs_5_
  93.3 0.0 collective-permute-done.25.refs_9_
  93.3 5.2 %own_columns.1 = f32[1024,128]{1,0:T(8,128)} custom-call(s32[4]{0:T(128)S(1)} %pad_add_fusion.info, f32[4,512,128]{2,1,0:T(8,128)S(1)} %get-tuple-element.66.work, f32[4,512,128]{2,1,0:T(8,128)S(1)} %get-tuple-element.67.packed, f32[512,128]{1,0:T(8,128)S(1)} %get-tuple-element.68.inverted, f32[512,128]{1,0:T(8,128)S(1)} %broadcast_select_fusion.own_top, ...), custom_call_target="tpu_custom_call" | custom-call | flops 4000000000 | bytes 12000000 | tf_op jit(solution)/shard_map/own_columns/pallas_call | solution.py:326
  (52 shorter events, 0.6 us)
Async XLA Ops:
  0.0 7.2 %collective-permute-start.5 = (f32[2,128]{1,0:T(2,128)}, f32[2,128]{1,0:T(2,128)S(1)}, u32[]{:S(2)}, u32[]{:S(2)}) collective-permute-start(f32[2,128]{1,0:T(2,128)} %param.5), channel_id=1, source_target_pairs={{0,8},{2,10},{4,12},{6,14},{8,0},{10,2},{12,4},{14,6},{16,24},{18,... | collective-permute-start | bytes 3080 | tf_op jit(solution)/shard_map/ppermute | solution.py:21
  3.1 3.2 %copy-start.1 = (f32[2,1024]{1,0:T(2,128)S(1)}, f32[2,1024]{1,0:T(2,128)}, u32[]{:S(2)}) copy-start(f32[2,1024]{1,0:T(2,128)} %param.4) | copy-start | bytes 24580
  3.1 9.3 %copy-start = (f32[1024,128]{1,0:T(8,128)S(1)}, f32[1024,128]{1,0:T(8,128)}, u32[]{:S(2)}) copy-start(f32[1024,128]{1,0:T(8,128)} %param.3) | copy-start | bytes 1572868
  4.2 8.2 %collective-permute-start.2 = (f32[2,256,128]{2,1,0:T(8,128)S(1)}, f32[2,256,128]{2,1,0:T(8,128)S(1)}, u32[]{:S(2)}, u32[]{:S(2)}) collective-permute-start(f32[2,256,128]{2,1,0:T(8,128)S(1)} %get-tuple-element.81), channel_id=1, source_target_pairs={{0,8},{2,10},{4,12},{6,14},{8,0},{10,2},{12,4},{14,6},{16,24},{18,... | collective-permute-start | bytes 786440 | tf_op jit(solution)/shard_map/ppermute | solution.py:21
  4.3 8.1 %collective-permute-start = (f32[2,256,128]{2,1,0:T(8,128)S(1)}, f32[2,256,128]{2,1,0:T(8,128)S(1)}, u32[]{:S(2)}, u32[]{:S(2)}) collective-permute-start(f32[2,256,128]{2,1,0:T(8,128)S(1)} %get-tuple-element.82), channel_id=1, source_target_pairs={{0,1},{1,0},{2,3},{3,2},{4,5},{5,4},{6,7},{7,6},{8,9},{9,8},{10,11... | collective-permute-start | bytes 786440 | tf_op jit(solution)/shard_map/ppermute | solution.py:21
  6.2 6.0 %collective-permute-start.7 = (f32[2,1024]{1,0:T(2,128)S(1)}, f32[2,1024]{1,0:T(2,128)S(1)}, u32[]{:S(2)}, u32[]{:S(2)}) collective-permute-start(f32[2,1024]{1,0:T(2,128)S(1)} %copy-done.1), channel_id=1, source_target_pairs={{0,1},{1,0},{2,3},{3,2},{4,5},{5,4},{6,7},{7,6},{8,9},{9,8},{10,11... | collective-permute-start | bytes 24584 | tf_op jit(solution)/shard_map/ppermute | solution.py:21
  6.4 0.7 copy-start.2
  7.2 4.7 %collective-permute-start.6 = (f32[4,128]{1,0:T(4,128)S(1)}, f32[4,128]{1,0:T(4,128)S(1)}, u32[]{:S(2)}, u32[]{:S(2)}) collective-permute-start(f32[4,128]{1,0:T(4,128)S(1)} %pad_maximum_fusion.4), channel_id=1, source_target_pairs={{0,16},{2,18},{4,20},{6,22},{8,24},{10,26},{12,28},{14,30},{16,0},... | collective-permute-start | bytes 6152 | tf_op jit(solution)/shard_map/ppermute | solution.py:21
  12.7 29.9 %collective-permute-start.1 = (f32[2,256,128]{2,1,0:T(8,128)S(1)}, f32[2,256,128]{2,1,0:T(8,128)S(1)}, u32[]{:S(2)}, u32[]{:S(2)}) collective-permute-start(f32[2,256,128]{2,1,0:T(8,128)S(1)} %pad_maximum_fusion), channel_id=1, source_target_pairs={{0,16},{2,18},{4,20},{6,22},{8,24},{10,26},{12,28},{14,30},{16,0},... | collective-permute-start | bytes 786440 | tf_op jit(solution)/shard_map/ppermute | solution.py:21
  15.6 5.0 %collective-permute-start.10 = (f32[256,128]{1,0:T(8,128)S(1)}, f32[256,128]{1,0:T(8,128)S(1)}, u32[]{:S(2)}, u32[]{:S(2)}) collective-permute-start(f32[256,128]{1,0:T(8,128)S(1)} %fusion.3), channel_id=1, source_target_pairs={{0,1},{1,0},{2,3},{3,2},{4,5},{5,4},{6,7},{7,6},{8,9},{9,8},{10,11... | collective-permute-start | bytes 393224 | tf_op jit(solution)/shard_map/ppermute | solution.py:21
  17.4 18.6 %collective-permute-start.8 = (f32[256,128]{1,0:T(8,128)S(1)}, f32[256,128]{1,0:T(8,128)S(1)}, u32[]{:S(2)}, u32[]{:S(2)}) collective-permute-start(f32[256,128]{1,0:T(8,128)S(1)} %fusion.9), channel_id=1, source_target_pairs={{0,16},{2,18},{4,20},{6,22},{8,24},{10,26},{12,28},{14,30},{16,0},... | collective-permute-start | bytes 393224 | tf_op jit(solution)/shard_map/ppermute | solution.py:21
  20.8 17.4 %collective-permute-start.11 = (f32[256,128]{1,0:T(8,128)S(1)}, f32[256,128]{1,0:T(8,128)S(1)}, u32[]{:S(2)}, u32[]{:S(2)}) collective-permute-start(f32[256,128]{1,0:T(8,128)S(1)} %fusion.14), channel_id=1, source_target_pairs={{0,16},{2,18},{4,20},{6,22},{8,24},{10,26},{12,28},{14,30},{16,0},... | collective-permute-start | bytes 393224 | tf_op jit(solution)/shard_map/ppermute | solution.py:21
  36.1 5.0 %collective-permute-start.9 = (f32[256,128]{1,0:T(8,128)S(1)}, f32[256,128]{1,0:T(8,128)S(1)}, u32[]{:S(2)}, u32[]{:S(2)}) collective-permute-start(f32[256,128]{1,0:T(8,128)S(1)} %add.85), channel_id=1, source_target_pairs={{0,8},{2,10},{4,12},{6,14},{8,0},{10,2},{12,4},{14,6},{16,24},{18,... | collective-permute-start | bytes 393224 | tf_op jit(solution)/shard_map/ppermute | solution.py:21
  36.1 9.2 %collective-permute-start.4 = (f32[2,256,128]{2,1,0:T(8,128)S(1)}, f32[2,256,128]{2,1,0:T(8,128)S(1)}, u32[]{:S(2)}, u32[]{:S(2)}) collective-permute-start(f32[2,256,128]{2,1,0:T(8,128)S(1)} %get-tuple-element.78), channel_id=1, source_target_pairs={{0,1},{1,0},{2,3},{3,2},{4,5},{5,4},{6,7},{7,6},{8,9},{9,8},{10,11... | collective-permute-start | bytes 786440 | tf_op jit(solution)/shard_map/ppermute | solution.py:21
  37.5 11.2 %collective-permute-start.3 = (f32[2,256,128]{2,1,0:T(8,128)S(1)}, f32[2,256,128]{2,1,0:T(8,128)S(1)}, u32[]{:S(2)}, u32[]{:S(2)}) collective-permute-start(f32[2,256,128]{2,1,0:T(8,128)S(1)} %get-tuple-element.79), channel_id=1, source_target_pairs={{0,1},{1,0},{2,3},{3,2},{4,5},{5,4},{6,7},{7,6},{8,9},{9,8},{10,11... | collective-permute-start | bytes 786440 | tf_op jit(solution)/shard_map/ppermute | solution.py:21
  41.1 11.6 %collective-permute-start.12 = (f32[512,128]{1,0:T(8,128)S(1)}, f32[512,128]{1,0:T(8,128)S(1)}, u32[]{:S(2)}, u32[]{:S(2)}) collective-permute-start(f32[512,128]{1,0:T(8,128)S(1)} %maximum_multiply_fusion.refs_0_), channel_id=1, source_target_pairs={{0,2},{2,0},{4,6},{6,4},{8,10},{10,8},{12,14},{14,12},{16,18},{18,... | collective-permute-start | bytes 786440 | tf_op jit(solution)/shard_map/ppermute | solution.py:21
  41.2 8.7 %collective-permute-start.13 = (f32[512,128]{1,0:T(8,128)S(1)}, f32[512,128]{1,0:T(8,128)S(1)}, u32[]{:S(2)}, u32[]{:S(2)}) collective-permute-start(f32[512,128]{1,0:T(8,128)S(1)} %maximum_multiply_fusion.refs_0_), channel_id=1, source_target_pairs={{0,4},{2,6},{4,0},{6,2},{8,12},{10,14},{12,8},{14,10},{16,20},{18,... | collective-permute-start | bytes 786440 | tf_op jit(solution)/shard_map/ppermute | solution.py:21
  42.7 23.3 %collective-permute-start.17 = (f32[512,128]{1,0:T(8,128)S(1)}, f32[512,128]{1,0:T(8,128)S(1)}, u32[]{:S(2)}, u32[]{:S(2)}) collective-permute-start(f32[512,128]{1,0:T(8,128)S(1)} %add_multiply_fusion.4), channel_id=1, source_target_pairs={{0,8},{2,10},{4,12},{6,14},{8,0},{10,2},{12,4},{14,6},{16,24},{18,... | collective-permute-start | bytes 786440 | tf_op jit(solution)/shard_map/ppermute | solution.py:21
  49.9 2.8 %collective-permute-start.14 = (f32[512,128]{1,0:T(8,128)S(1)}, f32[512,128]{1,0:T(8,128)S(1)}, u32[]{:S(2)}, u32[]{:S(2)}) collective-permute-start(f32[512,128]{1,0:T(8,128)S(1)} %collective-permute-done.13.refs_2_), channel_id=1, source_target_pairs={{0,2},{2,0},{4,6},{6,4},{8,10},{10,8},{12,14},{14,12},{16,18},{18,... | collective-permute-start | bytes 786440 | tf_op jit(solution)/shard_map/ppermute | solution.py:21
  50.0 15.9 %collective-permute-start.18 = (f32[512,128]{1,0:T(8,128)S(1)}, f32[512,128]{1,0:T(8,128)S(1)}, u32[]{:S(2)}, u32[]{:S(2)}) collective-permute-start(f32[512,128]{1,0:T(8,128)S(1)} %multiply_add_fusion), channel_id=1, source_target_pairs={{0,16},{2,18},{4,20},{6,22},{8,24},{10,26},{12,28},{14,30},{16,0},... | collective-permute-start | bytes 786440 | tf_op jit(solution)/shard_map/ppermute | solution.py:21
  66.0 27.3 %collective-permute-start.20 = (f32[512,128]{1,0:T(8,128)S(1)}, f32[512,128]{1,0:T(8,128)S(1)}, u32[]{:S(2)}, u32[]{:S(2)}) collective-permute-start(f32[512,128]{1,0:T(8,128)S(1)} %add_multiply_fusion.1.refs_2_), channel_id=1, source_target_pairs={{0,2},{2,0},{4,6},{6,4},{8,10},{10,8},{12,14},{14,12},{16,18},{18,... | collective-permute-start | bytes 786440 | tf_op jit(solution)/shard_map/ppermute | solution.py:21
  66.3 20.5 %collective-permute-start.22 = (f32[512,128]{1,0:T(8,128)S(1)}, f32[512,128]{1,0:T(8,128)S(1)}, u32[]{:S(2)}, u32[]{:S(2)}) collective-permute-start(f32[512,128]{1,0:T(8,128)S(1)} %add_multiply_fusion.1.refs_2_), channel_id=1, source_target_pairs={{0,4},{2,6},{4,0},{6,2},{8,12},{10,14},{12,8},{14,10},{16,20},{18,... | collective-permute-start | bytes 786440 | tf_op jit(solution)/shard_map/ppermute | solution.py:21
  67.8 13.7 %collective-permute-start.15 = (f32[512,128]{1,0:T(8,128)S(1)}, f32[512,128]{1,0:T(8,128)S(1)}, u32[]{:S(2)}, u32[]{:S(2)}) collective-permute-start(f32[512,128]{1,0:T(8,128)S(1)} %broadcast_multiply_fusion), channel_id=1, source_target_pairs={{0,8},{2,10},{4,12},{6,14},{8,0},{10,2},{12,4},{14,6},{16,24},{18,... | collective-permute-start | bytes 786440 | tf_op jit(solution)/shard_map/ppermute | solution.py:21
  68.3 14.6 %collective-permute-start.16 = (f32[512,128]{1,0:T(8,128)S(1)}, f32[512,128]{1,0:T(8,128)S(1)}, u32[]{:S(2)}, u32[]{:S(2)}) collective-permute-start(f32[512,128]{1,0:T(8,128)S(1)} %multiply_add_fusion.1), channel_id=1, source_target_pairs={{0,16},{2,18},{4,20},{6,22},{8,24},{10,26},{12,28},{14,30},{16,0},... | collective-permute-start | bytes 786440 | tf_op jit(solution)/shard_map/ppermute | solution.py:21
  70.2 23.1 %collective-permute-start.21 = (f32[512,128]{1,0:T(8,128)S(1)}, f32[512,128]{1,0:T(8,128)S(1)}, u32[]{:S(2)}, u32[]{:S(2)}) collective-permute-start(f32[512,128]{1,0:T(8,128)S(1)} %add_multiply_fusion.refs_3_), channel_id=1, source_target_pairs={{0,2},{2,0},{4,6},{6,4},{8,10},{10,8},{12,14},{14,12},{16,18},{18,... | collective-permute-start | bytes 786440 | tf_op jit(solution)/shard_map/ppermute | solution.py:21
  81.4 7.4 %collective-permute-start.23 = (f32[512,128]{1,0:T(8,128)S(1)}, f32[512,128]{1,0:T(8,128)S(1)}, u32[]{:S(2)}, u32[]{:S(2)}) collective-permute-start(f32[512,128]{1,0:T(8,128)S(1)} %add_multiply_fusion.refs_3_), channel_id=1, source_target_pairs={{0,4},{2,6},{4,0},{6,2},{8,12},{10,14},{12,8},{14,10},{16,20},{18,... | collective-permute-start | bytes 786440 | tf_op jit(solution)/shard_map/ppermute | solution.py:21
  83.0 10.2 %collective-permute-start.19 = (f32[512,128]{1,0:T(8,128)S(1)}, f32[512,128]{1,0:T(8,128)S(1)}, u32[]{:S(2)}, u32[]{:S(2)}) collective-permute-start(f32[512,128]{1,0:T(8,128)S(1)} %pad_maximum_fusion.3), channel_id=1, source_target_pairs={{0,1},{2,3},{4,5},{6,7},{8,9},{10,11},{12,13},{14,15},{16,17},{18,... | collective-permute-start | bytes 786440 | tf_op jit(solution)/shard_map/ppermute | solution.py:321
  86.7 6.6 %collective-permute-start.24 = (f32[512,128]{1,0:T(8,128)S(1)}, f32[512,128]{1,0:T(8,128)S(1)}, u32[]{:S(2)}, u32[]{:S(2)}) collective-permute-start(f32[512,128]{1,0:T(8,128)S(1)} %collective-permute-done.22.refs_6_), channel_id=1, source_target_pairs={{0,2},{2,0},{4,6},{6,4},{8,10},{10,8},{12,14},{14,12},{16,18},{18,... | collective-permute-start | bytes 786440 | tf_op jit(solution)/shard_map/ppermute | solution.py:21
  88.8 4.5 %collective-permute-start.25 = (f32[512,128]{1,0:T(8,128)S(1)}, f32[512,128]{1,0:T(8,128)S(1)}, u32[]{:S(2)}, u32[]{:S(2)}) collective-permute-start(f32[512,128]{1,0:T(8,128)S(1)} %collective-permute-done.23.refs_7_), channel_id=1, source_target_pairs={{0,2},{2,0},{4,6},{6,4},{8,10},{10,8},{12,14},{14,12},{16,18},{18,... | collective-permute-start | bytes 786440 | tf_op jit(solution)/shard_map/ppermute | solution.py:21
